TPU v7x, 32 devices: a whole 2x2x4 slice. The times are simulated.
32 devices in a mesh: grp: 4 (over y, x), seq: 8 (over z, core).
Axes of the slice: x: 2, y: 2, z: 4, core: 2. Of those that a mesh axis runs over, the one named last changes fastest.
Arguments:
- tokens: bfloat16 [32, 832, 1024], P('grp', 'seq'), may hold values from -6 to 6
- counts: int32 [32, 8], P('grp', 'seq'), may hold values from 1 to 104, as said below
- w_qkv: bfloat16 [1024, 3072], P(('grp', 'seq')), may hold values from -0.1875 to 0.1875
- bias_q: bfloat16 [1024], P(('grp', 'seq')), may hold values from -3 to 3
- bias_v: bfloat16 [1024], P(('grp', 'seq')), may hold values from -3 to 3
- w_out: bfloat16 [1024, 1024], P(('grp', 'seq')), may hold values from -3.5 to 3.5
- bias_out: bfloat16 [1024], P(('grp', 'seq')), may hold values from -3 to 3
- w_up: bfloat16 [1024, 4096], P(('grp', 'seq')), may hold values from -0.1875 to 0.1875
- bias_up: bfloat16 [4096], P(('grp', 'seq')), may hold values from -3 to 3
- w_down: bfloat16 [4096, 1024], P(('grp', 'seq')), may hold values from -0.09375 to 0.09375
- bias_down: bfloat16 [1024], P(('grp', 'seq')), may hold values from -3 to 3
- gain_one: bfloat16 [1024], P(('grp', 'seq')), may hold values from 0.099609375 to 1.8984375
- shift_one: bfloat16 [1024], P(('grp', 'seq')), may hold values from -3 to 3
- gain_two: bfloat16 [1024], P(('grp', 'seq')), may hold values from 0.099609375 to 1.8984375
- shift_two: bfloat16 [1024], P(('grp', 'seq')), may hold values from -3 to 3
- cotangent: bfloat16 [32, 832, 1024], P('grp', 'seq'), may hold values from -6 to 6
Outputs:
- result: bfloat16 [32, 832, 1024], P('grp', 'seq')
- grad_tokens: float32 [32, 832, 1024], P('grp', 'seq')
- grad_w_qkv: float32 [1024, 3072], P(('grp', 'seq'))
- grad_bias_q: float32 [1024], P(('grp', 'seq'))
- grad_bias_v: float32 [1024], P(('grp', 'seq'))
- grad_w_out: float32 [1024, 1024], P(('grp', 'seq'))
- grad_bias_out: float32 [1024], P(('grp', 'seq'))
- grad_w_up: float32 [1024, 4096], P(('grp', 'seq'))
- grad_bias_up: float32 [4096], P(('grp', 'seq'))
- grad_w_down: float32 [4096, 1024], P(('grp', 'seq'))
- grad_bias_down: float32 [1024], P(('grp', 'seq'))
- grad_gain_one: float32 [1024], P(('grp', 'seq'))
- grad_shift_one: float32 [1024], P(('grp', 'seq'))
- grad_gain_two: float32 [1024], P(('grp', 'seq'))
- grad_shift_two: float32 [1024], P(('grp', 'seq'))
Inputs may be any that keep to these rules, and one draw needn't show every extreme that they name: For each image the counts over the 8 devices of its group sum to 577, and one device holds exactly 104 of its tokens.
All inputs are finite; a program needn't handle non-finite values.
Results may differ from a plain program's by a relative error of at most 0.014.
Values may be sent and summed in bfloat16 or wider, within the bound.
No kernel may reach another device: no remote copies, remote signals or barrier semaphores. Data moves between devices by JAX's collectives and lax.ppermute only.
A program may use at most 264 MiB of HBM per device.

v0:
```python
import jax
import jax.numpy as jnp
from jax import lax
from jax.sharding import PartitionSpec as P

H = 16
HD = 64


EPSILON = 1e-06
NEGATIVE = -1e30


def norm_rows(values, gain_vec, shift_vec):
    row_mean = jnp.mean(values, axis=-1, keepdims=True)
    centred = values - row_mean
    row_var = jnp.mean(centred * centred, axis=-1, keepdims=True)
    return centred * lax.rsqrt(row_var + EPSILON) * gain_vec + shift_vec


def gelu_exact(values):
    return jax.nn.gelu(values, approximate=False)


def dot_float(left, right):
    return jnp.dot(left, right, preferred_element_type=jnp.float32)


def contract_rows(left, right):
    return lax.dot_general(
        left, right, (((0,), (0,)), ((), ())), preferred_element_type=jnp.float32
    )


def contract_cols(left, right):
    return lax.dot_general(
        left, right, (((1,), (1,)), ((), ())), preferred_element_type=jnp.float32
    )


def split_heads(array):
    return array.reshape(array.shape[0], array.shape[1], H, HD)


def masked_scores(query_heads, key_heads, key_valid, score_scale):
    raw_scores = jnp.einsum(
        "iqhd,ikhd->ihqk", query_heads, key_heads, preferred_element_type=jnp.float32
    )
    raw_scores = raw_scores * score_scale
    return jnp.where(key_valid[:, None, None, :] > 0, raw_scores, NEGATIVE)


def shards(
    tokens,
    counts,
    w_qkv,
    bias_q,
    bias_v,
    w_out,
    bias_out,
    w_up,
    bias_up,
    w_down,
    bias_down,
    gain_one,
    shift_one,
    gain_two,
    shift_two,
    cotangent,
):
    image_count, slot_count, model_width = tokens.shape
    token_count = image_count * slot_count
    score_scale = HD ** (-0.5)
    slot_index = lax.broadcasted_iota(jnp.int32, (image_count, slot_count), 1)
    valid_slots = (slot_index < counts).astype(jnp.float32)
    valid_rows = valid_slots.reshape(token_count, 1)
    (
        full_qkv,
        full_bq,
        full_bv,
        full_out,
        full_bo,
        full_up,
        full_bu,
        full_down,
        full_bd,
        full_g1,
        full_s1,
        full_g2,
        full_s2,
    ) = (
        lax.all_gather(w_qkv, ("grp", "seq"), axis=0, tiled=True),
        lax.all_gather(bias_q, ("grp", "seq"), axis=0, tiled=True),
        lax.all_gather(bias_v, ("grp", "seq"), axis=0, tiled=True),
        lax.all_gather(w_out, ("grp", "seq"), axis=0, tiled=True),
        lax.all_gather(bias_out, ("grp", "seq"), axis=0, tiled=True),
        lax.all_gather(w_up, ("grp", "seq"), axis=0, tiled=True),
        lax.all_gather(bias_up, ("grp", "seq"), axis=0, tiled=True),
        lax.all_gather(w_down, ("grp", "seq"), axis=0, tiled=True),
        lax.all_gather(bias_down, ("grp", "seq"), axis=0, tiled=True),
        lax.all_gather(gain_one, ("grp", "seq"), axis=0, tiled=True),
        lax.all_gather(shift_one, ("grp", "seq"), axis=0, tiled=True),
        lax.all_gather(gain_two, ("grp", "seq"), axis=0, tiled=True),
        lax.all_gather(shift_two, ("grp", "seq"), axis=0, tiled=True),
    )
    tokens_f = tokens.reshape(token_count, model_width).astype(jnp.float32)
    normed_f, norm_one_pull = jax.vjp(
        norm_rows, tokens_f, full_g1.astype(jnp.float32), full_s1.astype(jnp.float32)
    )
    normed = normed_f.astype(jnp.bfloat16)
    joined = dot_float(normed, full_qkv)
    query_rows = (joined[:, :model_width] + full_bq.astype(jnp.float32)).astype(jnp.bfloat16)
    key_rows = joined[:, model_width : 2 * model_width].astype(jnp.bfloat16)
    value_rows = (joined[:, 2 * model_width :] + full_bv.astype(jnp.float32)).astype(jnp.bfloat16)
    key_local = key_rows.reshape(image_count, slot_count, model_width)
    value_local = value_rows.reshape(image_count, slot_count, model_width)
    valid_low = valid_slots.astype(jnp.bfloat16)
    key_all, value_all, valid_all = (
        lax.all_gather(key_local, "seq", axis=1, tiled=True),
        lax.all_gather(value_local, "seq", axis=1, tiled=True),
        lax.all_gather(valid_low, "seq", axis=1, tiled=True),
    )
    query_heads = query_rows.reshape(image_count, slot_count, H, HD)
    scores = masked_scores(query_heads, split_heads(key_all), valid_all, score_scale)
    row_top = jnp.max(scores, axis=-1, keepdims=True)
    exponent = jnp.exp(scores - row_top)
    row_total = jnp.sum(exponent, axis=-1, keepdims=True)
    soft_weights = exponent / row_total
    mixed_heads = jnp.einsum(
        "ihqk,ikhd->iqhd",
        soft_weights.astype(jnp.bfloat16),
        split_heads(value_all),
        preferred_element_type=jnp.float32,
    )
    mixed_rows = mixed_heads.reshape(token_count, model_width).astype(jnp.bfloat16)
    residual = tokens_f + dot_float(mixed_rows, full_out) + full_bo.astype(jnp.float32)
    normed_two_f, norm_two_pull = jax.vjp(
        norm_rows, residual, full_g2.astype(jnp.float32), full_s2.astype(jnp.float32)
    )
    normed_two = normed_two_f.astype(jnp.bfloat16)
    hidden = dot_float(normed_two, full_up) + full_bu.astype(jnp.float32)
    active_f, gelu_pull = jax.vjp(gelu_exact, hidden)
    active = active_f.astype(jnp.bfloat16)
    output = dot_float(active, full_down) + full_bd.astype(jnp.float32)
    result = ((residual + output) * valid_rows).astype(jnp.bfloat16).reshape(tokens.shape)
    full_qkv, full_out, full_up, full_down = (
        lax.all_gather(w_qkv, ("grp", "seq"), axis=0, tiled=True),
        lax.all_gather(w_out, ("grp", "seq"), axis=0, tiled=True),
        lax.all_gather(w_up, ("grp", "seq"), axis=0, tiled=True),
        lax.all_gather(w_down, ("grp", "seq"), axis=0, tiled=True),
    )
    key_all, value_all, valid_all = (
        lax.all_gather(key_local, "seq", axis=1, tiled=True),
        lax.all_gather(value_local, "seq", axis=1, tiled=True),
        lax.all_gather(valid_low, "seq", axis=1, tiled=True),
    )
    cotan_rows = cotangent.reshape(token_count, model_width).astype(jnp.float32) * valid_rows
    cotan_low = cotan_rows.astype(jnp.bfloat16)
    grad_w_down = contract_rows(active, cotan_low)
    grad_bias_down = jnp.sum(cotan_low.astype(jnp.float32), axis=0)
    grad_active = contract_cols(cotan_low, full_down)
    (grad_hidden,) = gelu_pull(grad_active)
    hidden_low = grad_hidden.astype(jnp.bfloat16)
    grad_w_up = contract_rows(normed_two, hidden_low)
    grad_bias_up = jnp.sum(hidden_low.astype(jnp.float32), axis=0)
    grad_normed_two = contract_cols(hidden_low, full_up)
    grad_residual, grad_gain_two, grad_shift_two = norm_two_pull(grad_normed_two)
    grad_residual = grad_residual + cotan_rows
    residual_low = grad_residual.astype(jnp.bfloat16)
    grad_w_out = contract_rows(mixed_rows, residual_low)
    grad_bias_out = jnp.sum(residual_low.astype(jnp.float32), axis=0)
    grad_mixed = contract_cols(residual_low, full_out).astype(jnp.bfloat16)
    grad_mixed_heads = grad_mixed.reshape(image_count, slot_count, H, HD)
    key_heads = split_heads(key_all)
    value_heads = split_heads(value_all)
    scores = masked_scores(query_heads, key_heads, valid_all, score_scale)
    soft_weights = jnp.exp(scores - row_top) / row_total
    grad_soft = jnp.einsum(
        "iqhd,ikhd->ihqk", grad_mixed_heads, value_heads, preferred_element_type=jnp.float32
    )
    row_delta = jnp.sum(soft_weights * grad_soft, axis=-1, keepdims=True)
    grad_scores = (soft_weights * (grad_soft - row_delta)).astype(jnp.bfloat16)
    grad_query = jnp.einsum(
        "ihqk,ikhd->iqhd", grad_scores, key_heads, preferred_element_type=jnp.float32
    )
    grad_query = (grad_query * score_scale).astype(jnp.bfloat16).reshape(token_count, model_width)
    query_all, mixed_all = (
        lax.all_gather(
            query_rows.reshape(image_count, slot_count, model_width), "seq", axis=1, tiled=True
        ),
        lax.all_gather(
            grad_mixed.reshape(image_count, slot_count, model_width), "seq", axis=1, tiled=True
        ),
    )
    top_all, total_all, delta_all = (
        lax.all_gather(row_top, "seq", axis=2, tiled=True),
        lax.all_gather(row_total, "seq", axis=2, tiled=True),
        lax.all_gather(row_delta, "seq", axis=2, tiled=True),
    )
    query_all_heads = split_heads(query_all)
    mixed_all_heads = split_heads(mixed_all)
    own_scores = masked_scores(query_all_heads, split_heads(key_local), valid_slots, score_scale)
    own_soft = jnp.exp(own_scores - top_all) / total_all
    own_grad_soft = jnp.einsum(
        "iqhd,ikhd->ihqk",
        mixed_all_heads,
        split_heads(value_local),
        preferred_element_type=jnp.float32,
    )
    own_grad_scores = (own_soft * (own_grad_soft - delta_all)).astype(jnp.bfloat16)
    value_grad = jnp.einsum(
        "ihqk,iqhd->ikhd",
        own_soft.astype(jnp.bfloat16),
        mixed_all_heads,
        preferred_element_type=jnp.float32,
    )
    value_grad = value_grad.reshape(image_count, slot_count, model_width)
    key_grad = jnp.einsum(
        "ihqk,iqhd->ikhd", own_grad_scores, query_all_heads, preferred_element_type=jnp.float32
    )
    key_grad = (key_grad * score_scale).reshape(image_count, slot_count, model_width)
    key_low = key_grad.reshape(token_count, model_width).astype(jnp.bfloat16)
    value_low = value_grad.reshape(token_count, model_width).astype(jnp.bfloat16)
    grad_joined = jnp.concatenate([grad_query, key_low, value_low], axis=1)
    grad_w_qkv = contract_rows(normed, grad_joined)
    grad_bias_q = jnp.sum(grad_query.astype(jnp.float32), axis=0)
    grad_bias_v = jnp.sum(value_low.astype(jnp.float32), axis=0)
    grad_normed = contract_cols(grad_joined, full_qkv)
    grad_tokens_norm, grad_gain_one, grad_shift_one = norm_one_pull(grad_normed)
    grad_tokens = (grad_residual + grad_tokens_norm).reshape(tokens.shape)
    (
        sum_qkv,
        sum_bq,
        sum_bv,
        sum_out,
        sum_bo,
        sum_up,
        sum_bu,
        sum_down,
        sum_bd,
        sum_g1,
        sum_s1,
        sum_g2,
        sum_s2,
    ) = (
        lax.psum_scatter(grad_w_qkv, ("grp", "seq"), scatter_dimension=0, tiled=True),
        lax.psum_scatter(grad_bias_q, ("grp", "seq"), scatter_dimension=0, tiled=True),
        lax.psum_scatter(grad_bias_v, ("grp", "seq"), scatter_dimension=0, tiled=True),
        lax.psum_scatter(grad_w_out, ("grp", "seq"), scatter_dimension=0, tiled=True),
        lax.psum_scatter(grad_bias_out, ("grp", "seq"), scatter_dimension=0, tiled=True),
        lax.psum_scatter(grad_w_up, ("grp", "seq"), scatter_dimension=0, tiled=True),
        lax.psum_scatter(grad_bias_up, ("grp", "seq"), scatter_dimension=0, tiled=True),
        lax.psum_scatter(grad_w_down, ("grp", "seq"), scatter_dimension=0, tiled=True),
        lax.psum_scatter(grad_bias_down, ("grp", "seq"), scatter_dimension=0, tiled=True),
        lax.psum_scatter(grad_gain_one, ("grp", "seq"), scatter_dimension=0, tiled=True),
        lax.psum_scatter(grad_shift_one, ("grp", "seq"), scatter_dimension=0, tiled=True),
        lax.psum_scatter(grad_gain_two, ("grp", "seq"), scatter_dimension=0, tiled=True),
        lax.psum_scatter(grad_shift_two, ("grp", "seq"), scatter_dimension=0, tiled=True),
    )
    return (
        result,
        grad_tokens,
        sum_qkv,
        sum_bq,
        sum_bv,
        sum_out,
        sum_bo,
        sum_up,
        sum_bu,
        sum_down,
        sum_bd,
        sum_g1,
        sum_s1,
        sum_g2,
        sum_s2,
    )


def solution(mesh):
    in_specs = (
        P("grp", "seq", None),
        P("grp", "seq"),
        P(("grp", "seq"), None),
        P(("grp", "seq")),
        P(("grp", "seq")),
        P(("grp", "seq"), None),
        P(("grp", "seq")),
        P(("grp", "seq"), None),
        P(("grp", "seq")),
        P(("grp", "seq"), None),
        P(("grp", "seq")),
        P(("grp", "seq")),
        P(("grp", "seq")),
        P(("grp", "seq")),
        P(("grp", "seq")),
        P("grp", "seq", None),
    )
    out_specs = (
        P("grp", "seq", None),
        P("grp", "seq", None),
        P(("grp", "seq"), None),
        P(("grp", "seq")),
        P(("grp", "seq")),
        P(("grp", "seq"), None),
        P(("grp", "seq")),
        P(("grp", "seq"), None),
        P(("grp", "seq")),
        P(("grp", "seq"), None),
        P(("grp", "seq")),
        P(("grp", "seq")),
        P(("grp", "seq")),
        P(("grp", "seq")),
        P(("grp", "seq")),
    )
    return jax.shard_map(shards, mesh=mesh, in_specs=in_specs, out_specs=out_specs, check_vma=False)
```

profile of v0, /device:TPU:0, one launch (start us, length us, event | category | flops | bytes accessed | tf_op | source)
XLA Modules:
  0.0 1532.8 jit_solution(886901765680803790)
XLA Ops:
  16.5 42.5 %all-reduce.18 = (bf16[1024]{0:T(1024)(128)(2,1)S(1)}, bf16[1024]{0:T(1024)(128)(2,1)S(1)}, bf16[1024]{0:T(1024)(128)(2,1)S(1)}, bf16[1024]{0:T(1024)(128)(2,1)S...) all-reduce(bf16[1024]{0:T(1024)(128)(2,1)S(1)} %dynamic-update-slic, ...), channel_id=1, replica_groups=mesh['grp'=4,'seq'=8] {'grp','seq'}, use_global_device_ids=true, to_apply=%add.1 | all-reduce | flops 8192 | bytes 32768
  66.4 16.9 %all-gather.14.cloned.1.call-done = bf16[1024,3072]{1,0:T(8,128)(2,1)} async-done(((bf16[32,3072]{1,0:T(8,128)(2,1)}), bf16[1024,3072]{1,0:T(8,128)(2,1)}) %all-gather.14.cloned.1.call-update) | async-done | bytes 6291472 | tf_op jit(solution)/shard_map/all_gather | solution.py:92
  104.1 14.7 all-gather.3
  119.1 37.4 %all-gather.4 = bf16[32,1,128]{2,1,0:T(2,128)(2,1)S(1)} all-gather(bf16[1,1,128]{2,1,0:T(2,128)(2,1)S(1)} %bitcast.115), channel_id=1, replica_groups=mesh['grp'=4,'seq'=8] {'grp','seq'}, dimensions={0}, use_global_device_ids=true | all-gather | bytes 8448 | tf_op jit(solution)/shard_map/all_gather | solution.py:98
  162.4 58.1 %all-gather.18.cloned.1.call-done = bf16[8,832,1024]{2,1,0:T(8,128)(2,1)} async-done(((bf16[8,104,1024]{2,1,0:T(8,128)(2,1)}), bf16[8,832,1024]{2,1,0:T(8,128)(2,1)}) %all-gather.18.cloned.1.call-update) | async-done | bytes 13631504 | tf_op jit(solution)/shard_map/all_gather | solution.py:119
  220.5 19.7 %copy.103 = bf16[8,832,1024]{1,2,0:T(8,128)(2,1)} copy(bf16[8,832,1024]{2,1,0:T(8,128)(2,1)} %all-gather.18.cloned.1.call-done) | data formatting | bytes 27262976 | tf_op jit(solution)/shard_map/all_gather | solution.py:119
  240.2 22.1 %fusion = (f32[8,16,104]{2,1,0:T(8,128)S(1)}, f32[8,16,104,832]{3,2,1,0:T(8,128)}) fusion(pred[8,832]{1,0:T(8,128)(4,1)S(1)} %bitcast.108, bf16[8,832,16,64]{1,3,2,0:T(8,128)(2,1)} %bitcast.96, bf16[8,104,16,64]{3,2,1,0:T(8,128)(2,1)S(1)} %copy-done.10), kind=kOutput, calls=%fused_computation.6 | convolution fusion | flops 1450888192 | bytes 59697664 | tf_op jit(solution)/shard_map/iqhd,ikhd->ihqk/dot_general | solution.py:46
  262.3 16.2 %fusion.2 = f32[8,16,104]{2,1,0:T(8,128)S(1)} fusion(f32[8,16,104,832]{3,2,1,0:T(8,128)} %get-tuple-element.53, f32[8,16,104]{2,1,0:T(8,128)S(1)} %get-tuple-element.52, pred[8,832]{1,0:T(8,128)(4,1)S(1)} %bitcast.109), kind=kLoop, calls=%fused_computation.8 | loop fusion | flops 44289024 | bytes 44415488 | tf_op jit(solution)/shard_map/reduce_sum | solution.py:127
  278.5 67.7 %all-gather.16.cloned.1.call-done = bf16[8,832,1024]{2,1,0:T(8,128)(2,1)} async-done(((bf16[8,104,1024]{2,1,0:T(8,128)(2,1)}), bf16[8,832,1024]{2,1,0:T(8,128)(2,1)}) %all-gather.16.cloned.1.call-update) | async-done | bytes 13631504 | tf_op jit(solution)/shard_map/all_gather | solution.py:120
  346.2 19.5 %copy.100 = bf16[8,832,1024]{1,2,0:T(8,128)(2,1)} copy(bf16[8,832,1024]{2,1,0:T(8,128)(2,1)} %all-gather.16.cloned.1.call-done) | data formatting | bytes 27262976 | tf_op jit(solution)/shard_map/all_gather | solution.py:120
  365.7 23.7 %convert_bitcast_fusion = bf16[8,104,16,64]{1,3,2,0:T(8,128)(2,1)} fusion(bf16[8,832,16,64]{1,3,2,0:T(8,128)(2,1)} %bitcast.103, f32[8,16,104,832]{3,2,1,0:T(8,128)} %get-tuple-element.53, f32[8,16,104]{2,1,0:T(8,128)S(1)} %fusion.2, f32[8,16,104]{2,1,0:T(8,128)S(1)} %get-tuple-element.52, pred[8,832]{1,0:T(8,128)(4,1)S(1)} %bitcast.110), kind=kOutput, calls=%fused_computation.77 | convolution fusion | flops 1473904640 | bytes 59750912 | tf_op jit(solution)/shard_map/ihqk,ikhd->iqhd/dot_general | solution.py:129
  410.1 72.7 %all-gather.22.cloned.1.call-done = bf16[1024,4096]{1,0:T(8,128)(2,1)} async-done(((bf16[32,4096]{1,0:T(8,128)(2,1)}), bf16[1024,4096]{1,0:T(8,128)(2,1)}) %all-gather.22.cloned.1.call-update) | async-done | bytes 8388624 | tf_op jit(solution)/shard_map/all_gather | solution.py:97
  482.7 14.4 fusion.47
  497.1 64.5 %all-gather.24.cloned.1.call-done = bf16[4096,1024]{1,0:T(8,128)(2,1)} async-done(((bf16[128,1024]{1,0:T(8,128)(2,1)}), bf16[4096,1024]{1,0:T(8,128)(2,1)}) %all-gather.24.cloned.1.call-update) | async-done | bytes 8388624 | tf_op jit(solution)/shard_map/all_gather | solution.py:99
  561.6 43.3 %convert_reduce_fusion = (f32[4096]{0:T(1024)}, bf16[832,4096]{1,0:T(8,128)(2,1)S(1)}, f32[832,4096]{1,0:T(8,128)}) fusion(f32[832,4096]{1,0:T(8,128)} %fusion.47, f32[4096]{0:T(1024)S(1)} %bitcast.113, bf16[832,1024]{1,0:T(8,128)(2,1)} %fusion.30, bf16[4096,1024]{1,0:T(8,128)(2,1)} %all-gather.24.cloned.1.call-done), kind=kOutput, calls=%fused_computation.20 | convolution fusion | flops 7234908160 | bytes 44204032 | tf_op jit(solution)/shard_map/dot_general | solution.py:36
  627.7 15.1 fusion.46
  681.7 40.8 %multiply_reduce_fusion = (f32[8,16,104]{2,1,0:T(8,128)S(1)}, f32[8,16,104,832]{3,2,1,0:T(8,128)}) fusion(f32[8,16,104]{2,1,0:T(8,128)S(1)} %copy-done.26, f32[8,16,104]{2,1,0:T(8,128)S(1)} %copy-done.22, f32[8,16,104,832]{3,2,1,0:T(8,128)} %get-tuple-element.53, pred[8,832]{1,0:T(8,128)(4,1)S(1)} %bitcast.111, bf16[8,832,16,64]{1,3,2,0:T(8,128)(2,1)} %bitcast.104, ...), kind=kOutput, calls=%fused_computation.3 | convolution fusion | flops 1484114944 | bytes 104106496 | tf_op jit(solution)/shard_map/iqhd,ikhd->ihqk/dot_general | solution.py:178
  723.4 39.1 %convert_reduce_fusion.2 = (f32[16,64]{1,0:T(8,128)}, bf16[8,104,16,64]{1,3,2,0:T(8,128)(2,1)}) fusion(bf16[8,832,16,64]{1,3,2,0:T(8,128)(2,1)} %bitcast.97, f32[8,16,104,832]{3,2,1,0:T(8,128)} %get-tuple-element.56, f32[8,16,104]{2,1,0:T(8,128)S(1)} %get-tuple-element.55, f32[8,16,104]{2,1,0:T(8,128)S(1)} %copy-done.26, f32[8,16,104]{2,1,0:T(8,128)S(1)} %copy-done.22, ...), kind=kOutput, calls=%fused_computation.39 | convolution fusion | flops 1498610688 | bytes 104110592 | tf_op jit(solution)/shard_map/ihqk,ikhd->iqhd/dot_general | solution.py:183
  768.6 60.8 %all-gather.1 = f32[8,16,832]{1,0,2:T(8,128)S(1)} all-gather(f32[8,16,104]{1,0,2:T(8,128)} %copy.114), channel_id=3, replica_groups=mesh['grp'=4,'seq'=8] {'seq'}, dimensions={2}, use_global_device_ids=true | all-gather | bytes 479232 | tf_op jit(solution)/shard_map/all_gather | solution.py:197
  831.7 43.9 %all-gather = f32[8,16,832]{1,0,2:T(8,128)S(1)} all-gather(f32[8,16,104]{1,0,2:T(8,128)} %copy.112), channel_id=2, replica_groups=mesh['grp'=4,'seq'=8] {'seq'}, dimensions={2}, use_global_device_ids=true | all-gather | bytes 479232 | tf_op jit(solution)/shard_map/all_gather | solution.py:196
  877.7 46.2 %all-gather.2 = f32[8,16,832]{1,0,2:T(8,128)S(1)} all-gather(f32[8,16,104]{1,0,2:T(8,128)} %copy.119), channel_id=4, replica_groups=mesh['grp'=4,'seq'=8] {'seq'}, dimensions={2}, use_global_device_ids=true | all-gather | bytes 479232 | tf_op jit(solution)/shard_map/all_gather | solution.py:198
  926.0 19.5 %copy.109 = bf16[8,832,1024]{1,2,0:T(8,128)(2,1)} copy(bf16[8,832,1024]{2,1,0:T(8,128)(2,1)} %all-gather.26.cloned.1.call-done) | data formatting | bytes 27262976 | tf_op jit(solution)/shard_map/all_gather | solution.py:188
  947.0 24.0 %exponential_divide_fusion = f32[8,16,832,104]{2,3,1,0:T(8,128)} fusion(f32[8,16,832]{2,1,0:T(8,128)S(1)} %copy-done.23, f32[8,16,832]{2,1,0:T(8,128)S(1)} %copy-done.24, pred[8,104]{1,0:T(8,128)(4,1)S(1)} %copy-done.55, bf16[8,832,16,64]{1,3,2,0:T(8,128)(2,1)} %bitcast.98, bf16[8,104,16,64]{3,2,1,0:T(8,128)(2,1)} %reshape.265), kind=kOutput, calls=%fused_computation.1 | convolution fusion | flops 1461977088 | bytes 60490560 | tf_op jit(solution)/shard_map/iqhd,ikhd->ihqk/dot_general | solution.py:46
  971.0 19.6 %copy.116 = bf16[8,832,1024]{1,2,0:T(8,128)(2,1)} copy(bf16[8,832,1024]{2,1,0:T(8,128)(2,1)} %all-gather.28.cloned.1.call-done) | data formatting | bytes 27262976 | tf_op jit(solution)/shard_map/all_gather | solution.py:191
  990.6 30.9 %fusion.31 = bf16[8,104,16,64]{1,3,2,0:T(8,128)(2,1)} fusion(bf16[8,832,16,64]{1,3,2,0:T(8,128)(2,1)} %bitcast.99, f32[8,16,832,104]{2,3,1,0:T(8,128)} %exponential_divide_fusion, f32[8,16,832]{2,1,0:T(8,128)} %copy.120, bf16[8,832,16,64]{1,3,2,0:T(8,128)(2,1)} %bitcast.94, bf16[8,104,16,64]{3,2,1,0:T(8,128)(2,1)S(1)} %copy-done.9), kind=kOutput, calls=%fused_computation.76 | convolution fusion | flops 2870280192 | bytes 75399168 | tf_op jit(solution)/shard_map/ihqk,iqhd->ikhd/dot_general | solution.py:218
  1027.7 22.6 %convert_reduce_fusion.1 = (f32[16,64]{1,0:T(8,128)S(1)}, bf16[8,16,64,104]{3,2,1,0:T(8,128)(2,1)S(1)}) fusion(bf16[8,832,16,64]{1,3,2,0:T(8,128)(2,1)} %bitcast.95, f32[8,16,832,104]{2,3,1,0:T(8,128)} %exponential_divide_fusion), kind=kOutput, calls=%fused_computation.38 | convolution fusion | flops 1431305216 | bytes 59641856 | tf_op jit(solution)/shard_map/ihqk,iqhd->ikhd/dot_general | solution.py:211
  1076.8 12.7 multiply_convert_fusion.8
  1089.7 13.2 fusion.50
  1102.9 42.0 %all-reduce.17 = (f32[1024]{0:T(1024)S(1)}, f32[1024]{0:T(1024)S(1)}, f32[1024]{0:T(1024)S(1)}, f32[4096]{0:T(1024)S(1)}, f32[1024]{0:T(1024)S(1)}, /*index=5*/f...) all-reduce(f32[1024]{0:T(1024)S(1)} %reduce_sum.218, ...), channel_id=6, replica_groups=mesh['grp'=4,'seq'=8] {'grp','seq'}, use_global_device_ids=true, to_apply=%region_13.14.clone | all-reduce | flops 12288 | bytes 98304
  1162.8 15.9 %reduce-scatter.9.cloned.1.call-done = f32[32,4096]{1,0:T(8,128)} async-done(((f32[1024,4096]{1,0:T(8,128)}), f32[32,4096]{1,0:T(8,128)}) %reduce-scatter.9.cloned.1.call-update) | async-done | bytes 524304 | tf_op jit(solution)/shard_map/reduce_scatter | solution.py:251
  1178.7 187.3 %reduce-scatter.11.cloned.1.call-done = f32[128,1024]{1,0:T(8,128)} async-done(((f32[4096,1024]{1,0:T(8,128)}), f32[128,1024]{1,0:T(8,128)}) %reduce-scatter.11.cloned.1.call-update) | async-done | bytes 524304 | tf_op jit(solution)/shard_map/reduce_scatter | solution.py:253
  1366.0 159.5 %reduce-scatter.5.cloned.1.call-done = f32[32,3072]{1,0:T(8,128)} async-done(((f32[1024,3072]{1,0:T(8,128)}), f32[32,3072]{1,0:T(8,128)}) %reduce-scatter.5.cloned.1.call-update) | async-done | bytes 393232 | tf_op jit(solution)/shard_map/reduce_scatter | solution.py:246
  (245 shorter events, 191.2 us)
Async XLA Ops:
  7.2 76.1 %all-gather.14.cloned.1.call-start = ((), (), s32[]{:S(2)}) async-start(), calls=%async_computation.4 | async-start | bytes 6488064 | tf_op jit(solution)/shard_map/all_gather | solution.py:92
  7.9 212.6 %all-gather.18.cloned.1.call-start = ((), (), s32[]{:S(2)}) async-start(), calls=%async_computation.6 | async-start | bytes 15335424 | tf_op jit(solution)/shard_map/all_gather | solution.py:119
  9.8 81.0 %copy-start.41 = (f32[832]{0:T(1024)}, f32[832]{0:T(1024)S(1)}, u32[]{:S(2)}) copy-start(f32[832]{0:T(1024)S(1)} %div.61) | copy-start | bytes 9988
  59.1 31.7 %copy-start.43 = (f32[1024]{0:T(1024)}, f32[1024]{0:T(1024)S(1)}, u32[]{:S(2)}) copy-start(f32[1024]{0:T(1024)S(1)} %convert_element_type.169) | copy-start | bytes 12292
  66.4 24.4 %copy-start.17 = (bf16[832,1024]{1,0:T(8,128)(2,1)}, bf16[832,1024]{1,0:T(8,128)(2,1)S(1)}, u32[]{:S(2)}) copy-start(bf16[832,1024]{1,0:T(8,128)(2,1)S(1)} %get-tuple-element.48) | copy-start | bytes 5111812
  96.2 249.9 %all-gather.16.cloned.1.call-start = ((), (), s32[]{:S(2)}) async-start(), calls=%async_computation.5 | async-start | bytes 15335424 | tf_op jit(solution)/shard_map/all_gather | solution.py:120
  96.3 22.7 %copy-start.56 = (bf16[128]{0:T(256)(128)(2,1)S(1)}, bf16[128]{0:T(256)(128)(2,1)}, u32[]{:S(2)}) copy-start(bf16[128]{0:T(256)(128)(2,1)} %param.24) | copy-start | bytes 772
  96.3 60.7 %copy-start.4 = (bf16[8,104,1024]{2,1,0:T(8,128)(2,1)S(1)}, bf16[8,104,1024]{2,1,0:T(8,128)(2,1)}, u32[]{:S(2)}) copy-start(bf16[8,104,1024]{2,1,0:T(8,128)(2,1)} %param.31) | copy-start | bytes 5111812
  101.7 60.4 %copy-start.6 = (bf16[832,1024]{1,0:T(8,128)(2,1)}, bf16[832,1024]{1,0:T(8,128)(2,1)S(1)}, u32[]{:S(2)}) copy-start(bf16[832,1024]{1,0:T(8,128)(2,1)S(1)} %get-tuple-element.45) | copy-start | bytes 5111812
  101.7 302.0 %all-gather.20.cloned.1.call-start = ((), (), s32[]{:S(2)}) async-start(), calls=%async_computation.7 | async-start | bytes 2162688 | tf_op jit(solution)/shard_map/all_gather | solution.py:95
  102.3 380.4 %all-gather.22.cloned.1.call-start = ((), (), s32[]{:S(2)}) async-start(), calls=%async_computation.8 | async-start | bytes 8650752 | tf_op jit(solution)/shard_map/all_gather | solution.py:97
  102.9 458.7 %all-gather.24.cloned.1.call-start = ((), (), s32[]{:S(2)}) async-start(), calls=%async_computation.9 | async-start | bytes 8650752 | tf_op jit(solution)/shard_map/all_gather | solution.py:99
  103.5 822.6 %all-gather.26.cloned.1.call-start = ((), (), s32[]{:S(2)}) async-start(), calls=%async_computation.10 | async-start | bytes 15335424 | tf_op jit(solution)/shard_map/all_gather | solution.py:188
  118.9 246.8 %copy-start.19 = (pred[832,8]{0,1:T(8,128)(4,1)}, pred[832,8]{0,1:T(8,128)(4,1)S(1)}, u32[]{:S(2)}) copy-start(pred[832,8]{0,1:T(8,128)(4,1)S(1)} %reshape.262) | copy-start | bytes 19972
  119.0 121.2 %copy-start.27 = (f32[832]{0:T(1024)}, f32[832]{0:T(1024)S(1)}, u32[]{:S(2)}) copy-start(f32[832]{0:T(1024)S(1)} %reshape.232) | copy-start | bytes 9988
  119.0 508.7 %copy-start.30 = (f32[1024]{0:T(1024)}, f32[1024]{0:T(1024)S(1)}, u32[]{:S(2)}) copy-start(f32[1024]{0:T(1024)S(1)} %convert_element_type.182) | copy-start | bytes 12292
  119.0 363.7 %copy-start.52 = (f32[1024]{0:T(1024)}, f32[1024]{0:T(1024)S(1)}, u32[]{:S(2)}) copy-start(f32[1024]{0:T(1024)S(1)} %convert_element_type.184) | copy-start | bytes 12292
  162.1 78.1 %copy-start.10 = (bf16[8,104,16,64]{3,2,1,0:T(8,128)(2,1)S(1)}, bf16[8,104,16,64]{3,2,1,0:T(8,128)(2,1)}, u32[]{:S(2)}) copy-start(bf16[8,104,16,64]{3,2,1,0:T(8,128)(2,1)} %reshape.263) | copy-start | bytes 5111812
  162.1 808.9 %all-gather.28.cloned.1.call-start = ((), (), s32[]{:S(2)}) async-start(), calls=%async_computation.11 | async-start | bytes 15335424 | tf_op jit(solution)/shard_map/all_gather | solution.py:191
  262.3 103.4 %copy-start.21 = (f32[8,16,104]{2,1,0:T(8,128)}, f32[8,16,104]{2,1,0:T(8,128)S(1)}, u32[]{:S(2)}) copy-start(f32[8,16,104]{2,1,0:T(8,128)S(1)} %get-tuple-element.52) | copy-start | bytes 159748
  278.5 87.2 %copy-start.25 = (f32[8,16,104]{2,1,0:T(8,128)}, f32[8,16,104]{2,1,0:T(8,128)S(1)}, u32[]{:S(2)}) copy-start(f32[8,16,104]{2,1,0:T(8,128)S(1)} %fusion.2) | copy-start | bytes 159748
  408.3 219.4 %copy-start.2 = (f32[832,1024]{1,0:T(8,128)}, f32[832,1024]{1,0:T(8,128)S(1)}, u32[]{:S(2)}) copy-start(f32[832,1024]{1,0:T(8,128)S(1)} %bitcast_add_fusion) | copy-start | bytes 10223620
  410.1 151.5 %copy-start.32 = (f32[32,1,128]{2,1,0:T(1,128)S(1)}, f32[32,1,128]{2,1,0:T(1,128)}, u32[]{:S(2)}) copy-start(f32[32,1,128]{2,1,0:T(1,128)} %convert_element_type.219) | copy-start | bytes 49156
  561.6 43.3 %copy-start.58 = (bf16[1024,4096]{1,0:T(8,128)(2,1)S(1)}, bf16[1024,4096]{1,0:T(8,128)(2,1)}, u32[]{:S(2)}) copy-start(bf16[1024,4096]{1,0:T(8,128)(2,1)} %all-gather.22.cloned.1.call-done) | copy-start | bytes 25165828
  621.2 541.7 %reduce-scatter.7.cloned.1.call-start = ((), (), s32[]{:S(2)}) async-start(), calls=%async_computation.13 | async-start | bytes 4325376 | tf_op jit(solution)/shard_map/reduce_scatter | solution.py:249
  627.7 551.0 %reduce-scatter.9.cloned.1.call-start = ((), (), s32[]{:S(2)}) async-start(), calls=%async_computation.14 | async-start | bytes 17301504 | tf_op jit(solution)/shard_map/reduce_scatter | solution.py:251
  642.8 723.1 %reduce-scatter.11.cloned.1.call-start = ((), (), s32[]{:S(2)}) async-start(), calls=%async_computation.15 | async-start | bytes 17301504 | tf_op jit(solution)/shard_map/reduce_scatter | solution.py:253
  667.5 858.0 %reduce-scatter.5.cloned.1.call-start = ((), (), s32[]{:S(2)}) async-start(), calls=%async_computation.12 | async-start | bytes 12976128 | tf_op jit(solution)/shard_map/reduce_scatter | solution.py:246
  926.0 21.0 %copy-start.23 = (f32[8,16,832]{2,1,0:T(8,128)S(1)}, f32[8,16,832]{2,1,0:T(8,128)}, u32[]{:S(2)}) copy-start(f32[8,16,832]{2,1,0:T(8,128)} %copy.115) | copy-start | bytes 1277956
  926.0 21.0 %copy-start.24 = (f32[8,16,832]{2,1,0:T(8,128)S(1)}, f32[8,16,832]{2,1,0:T(8,128)}, u32[]{:S(2)}) copy-start(f32[8,16,832]{2,1,0:T(8,128)} %copy.113) | copy-start | bytes 1277956
  926.0 21.0 %copy-start.55 = (pred[8,104]{1,0:T(8,128)(4,1)S(1)}, pred[8,104]{1,0:T(8,128)(4,1)}, u32[]{:S(2)}) copy-start(pred[8,104]{1,0:T(8,128)(4,1)} %get-tuple-element.49) | copy-start | bytes 2500
  1089.7 59.9 %copy-start.40 = (f32[832]{0:T(1024)S(1)}, f32[832]{0:T(1024)}, u32[]{:S(2)}) copy-start(f32[832]{0:T(1024)} %copy-done.39) | copy-start | bytes 9988
  (41 other events, 293.8 us)
Sparse Core Ops, SparseCore 0:
  11.0 72.2 all-gather.13
  96.4 124.0 all-gather.17
  222.7 123.4 all-gather.15
  349.0 54.6 all-gather.19
  406.6 76.1 all-gather.21
  485.6 75.9 all-gather.23
  563.2 123.9 all-gather.25
  688.7 150.7 all-gather.27
  842.4 148.6 reduce-scatter.6
  993.8 184.8 reduce-scatter.8
  1181.6 184.3 reduce-scatter.10
  1372.4 153.0 reduce-scatter.4
where the time goes:
time: 1540 us; the launch traced here: 1530 us
  waiting for transfers between devices  653 us (42%)
  matrix products  356 us (23%)
  blocking collectives  287 us (19%)
  local copies, waits for them, and re-layouts  160 us (10%)
  other arithmetic  60.7 us (4%)
    reduce_scatter x1, waiting for transfers between devices, shards(): lax.psum_scatter(grad_w_down, ('grp', 'seq'), scatter_dimension=0, tiled=...  187 us
    reduce_scatter x1, waiting for transfers between devices, shards(): lax.psum_scatter(grad_w_qkv, ('grp', 'seq'), scatter_dimension=0, tiled=T...  160 us
    unnamed x2, blocking collectives  84.6 us
    all_gather x1, waiting for transfers between devices, shards(): lax.all_gather(w_up, ('grp', 'seq'), axis=0, tiled=True)  72.7 us
    dot_general x4, matrix products, contract_cols(): lax.dot_general(left, right, (((1,), (1,)), ((), ())), preferred_element_...  68.2 us
    all_gather x1, waiting for transfers between devices, shards(): lax.all_gather(value_local, 'seq', axis=1, tiled=True)  67.7 us
    all_gather x1, waiting for transfers between devices, shards(): lax.all_gather(w_down, ('grp', 'seq'), axis=0, tiled=True)  64.5 us
    all_gather x1, blocking collectives, shards(): lax.all_gather(row_total, 'seq', axis=2, tiled=True)  60.8 us
  transfers between devices with their start and end apart: 12, of which 9 were waited for; matrix products, arithmetic and copies ran while one was open for 36% of the time, Pallas kernels for 0%

commit v1 on v0

v1 whole, which is shorter than its diff:
```python
import jax
import jax.numpy as jnp
import numpy as np
from jax import lax
from jax.experimental import pallas as pl
from jax.experimental.pallas import tpu as pltpu
from jax.sharding import Mesh
from jax.sharding import PartitionSpec as P

H = 16
HD = 64
LENGTH = 577
PACKED = 592
EPSILON = 1e-06
NEGATIVE = -1e30
ABSENT = 100.0
SMALL = 128
AXES = ("gy", "gx", "sz", "sc")

bf16 = jnp.bfloat16
f32 = jnp.float32


def norm_rows(values, gain_vec, shift_vec):
    row_mean = jnp.mean(values, axis=-1, keepdims=True)
    centred = values - row_mean
    row_var = jnp.mean(centred * centred, axis=-1, keepdims=True)
    return centred * lax.rsqrt(row_var + EPSILON) * gain_vec + shift_vec


def gelu_exact(values):
    return jax.nn.gelu(values, approximate=False)


def dot_float(left, right):
    return jnp.dot(left, right, preferred_element_type=f32)


def contract_rows(left, right):
    return lax.dot_general(left, right, (((0,), (0,)), ((), ())), preferred_element_type=f32)


def contract_cols(left, right):
    return lax.dot_general(left, right, (((1,), (1,)), ((), ())), preferred_element_type=f32)


def shifted(array, axis, size, step):
    return lax.ppermute(array, axis, [(i, (i + step) % size) for i in range(size)])


def pick(array, index, axis):
    return lax.dynamic_index_in_dim(array, index, axis, keepdims=False)


class Ring:
    def __init__(self, sizes):
        self.sizes = dict(zip(AXES, sizes))
        self.count = int(np.prod(sizes))

    def place(self):
        return {axis: lax.axis_index(axis) for axis in AXES}

    def others(self, array, axis):
        size = self.sizes[axis]
        return [shifted(array, axis, size, step) for step in range(1, size)]

    def gather(self, shard):
        rows, width = shard.shape
        cut = rows // 2
        columns = [shard] + self.others(shard, "sz")
        near, far = [], []
        halves = []
        for part in range(2):
            piece = jnp.stack([c[part * cut : (part + 1) * cut] for c in columns])
            halves.append([piece, ("gx", "gy") if part == 0 else ("gy", "gx")])
        first = [[piece] + self.others(piece, order[0]) for piece, order in halves]
        first = [jnp.stack(group) for group in first]
        first = lax.optimization_barrier(tuple(first))
        second = [self.others(group, order[1]) for group, (_, order) in zip(first, halves)]
        sources = []
        for part in range(2):
            order = halves[part][1]
            plane = [first[part]] + second[part]
            for turn in range(2):
                for step, group in enumerate(plane):
                    if turn:
                        group = shifted(group, "sc", 2, 1)
                    sources.append((group, part, order, turn, step))
        return self.assemble(sources, rows, width)

    def assemble(self, sources, rows, width):
        place = self.place()
        sizes = self.sizes
        cut = rows // 2
        targets = []
        arrays = []
        for group, part, order, turn, step in sources:
            inner, depth = group.shape[:2]
            arrays.append(group.reshape(inner * depth, cut, width))
            for one in range(inner):
                for k in range(depth):
                    at = dict(place)
                    at["sc"] = (place["sc"] - turn) % 2
                    at[order[1]] = (place[order[1]] - step) % sizes[order[1]]
                    at[order[0]] = (place[order[0]] - one) % sizes[order[0]]
                    at["sz"] = (place["sz"] - k) % sizes["sz"]
                    index = at["gy"]
                    for axis in AXES[1:]:
                        index = index * sizes[axis] + at[axis]
                    targets.append(index * 2 + part)
        table = jnp.stack(targets).astype(jnp.int32)
        total = len(targets)
        blocks = [a.shape[0] for a in arrays]

        def body(table_ref, *refs):
            ins, out, sems = refs[: len(blocks)], refs[-2], refs[-1]
            copies = []
            n = 0
            for ref, count in zip(ins, blocks):
                for k in range(count):
                    copies.append(pltpu.make_async_copy(ref.at[k], out.at[table_ref[n]], sems.at[n]))
                    n += 1
            for copy in copies:
                copy.start()
            for copy in copies:
                copy.wait()

        out = pl.pallas_call(
            body,
            out_shape=jax.ShapeDtypeStruct((total, cut, width), bf16),
            grid_spec=pltpu.PrefetchScalarGridSpec(
                num_scalar_prefetch=1,
                grid=(1,),
                in_specs=[pl.BlockSpec(memory_space=pl.ANY)] * len(blocks),
                out_specs=pl.BlockSpec(memory_space=pl.ANY),
                scratch_shapes=[pltpu.SemaphoreType.DMA((total,))],
            ),
            name="assemble",
        )(table, *arrays)
        return out.reshape(total * cut, width)

    def add(self, *arrays):
        total = arrays[0].astype(f32)
        for array in arrays[1:]:
            total = total + array.astype(f32)
        return total

    def fold(self, array, axis, at, low=True):
        size = self.sizes[axis]
        own = pick(array, at[axis], 0)
        came = [shifted(pick(array, (at[axis] + k) % size, 0), axis, size, k) for k in range(1, size)]
        total = self.add(own, *came)
        return total.astype(bf16) if low else total

    def scatter(self, grads):
        width = grads.shape[-1]
        rows = grads.shape[0] // self.count
        cut = rows // 2
        at = self.place()
        sizes = self.sizes
        grads = grads.reshape(sizes["gy"], sizes["gx"], sizes["sz"], 2, rows, width)
        own = pick(grads, at["sc"], 3)
        came = shifted(pick(grads, 1 - at["sc"], 3), "sc", 2, 1)
        total = self.add(own, came).astype(bf16)
        upper = total[:, :, :, :cut]
        lower = jnp.swapaxes(total[:, :, :, cut:], 0, 1)
        upper = self.fold(upper, "gy", at)
        lower = self.fold(lower, "gx", at)
        upper = self.fold(upper, "gx", at)
        lower = self.fold(lower, "gy", at)
        both = jnp.concatenate([upper, lower], axis=1)
        return self.fold(both, "sz", at, low=False)


def head_mask(part):
    lane = lax.broadcasted_iota(jnp.int32, (1, 2 * HD), 1)
    return (lane // HD == part).astype(bf16)


def soft_rows(query, key):
    scores = contract_cols(query, key) * (HD**-0.5)
    lane = lax.broadcasted_iota(jnp.int32, scores.shape, 1)
    scores = jnp.where(lane < LENGTH, scores, NEGATIVE)
    exponent = jnp.exp(scores - jnp.max(scores, axis=-1, keepdims=True))
    return exponent * (1.0 / jnp.sum(exponent, axis=-1, keepdims=True))


def mix_body(q_ref, k_ref, v_ref, o_ref):
    query, key, value = q_ref[...], k_ref[...], v_ref[...]
    total = None
    for part in range(2):
        mask = head_mask(part)
        soft = soft_rows(query * mask, key).astype(bf16)
        mixed = dot_float(soft, value * mask)
        total = mixed if total is None else total + mixed
    o_ref[...] = total.astype(bf16)


def attend(qkv):
    pairs = H // 2
    spec = lambda shift: pl.BlockSpec((PACKED, 2 * HD), lambda i, s=shift: (0, i + s))
    return pl.pallas_call(
        mix_body,
        out_shape=jax.ShapeDtypeStruct((PACKED, H * HD), bf16),
        grid=(pairs,),
        in_specs=[spec(0), spec(pairs), spec(2 * pairs)],
        out_specs=spec(0),
        compiler_params=pltpu.CompilerParams(vmem_limit_bytes=50 * 2**20),
        name="attend",
    )(qkv, qkv, qkv)


def mix_back_body(q_ref, k_ref, v_ref, g_ref, dq_ref, dk_ref, dv_ref):
    query, key, value, grad = q_ref[...], k_ref[...], v_ref[...], g_ref[...]
    scale = HD**-0.5
    sums = None
    for part in range(2):
        mask = head_mask(part)
        soft = soft_rows(query * mask, key)
        grad_part = grad * mask
        grad_soft = contract_cols(grad_part, value)
        delta = jnp.sum(soft * grad_soft, axis=-1, keepdims=True)
        grad_scores = (soft * (grad_soft - delta)).astype(bf16)
        terms = (
            dot_float(grad_scores, key * mask),
            contract_rows(grad_scores, query * mask),
            contract_rows(soft.astype(bf16), grad_part),
        )
        sums = terms if sums is None else tuple(a + b for a, b in zip(sums, terms))
    dq_ref[...] = (sums[0] * scale).astype(bf16)
    dk_ref[...] = (sums[1] * scale).astype(bf16)
    dv_ref[...] = sums[2].astype(bf16)


def attend_back(qkv, grad_mixed):
    pairs = H // 2
    spec = lambda shift: pl.BlockSpec((PACKED, 2 * HD), lambda i, s=shift: (0, i + s))
    return pl.pallas_call(
        mix_back_body,
        out_shape=[jax.ShapeDtypeStruct((PACKED, H * HD), bf16)] * 3,
        grid=(pairs,),
        in_specs=[spec(0), spec(pairs), spec(2 * pairs), spec(0)],
        out_specs=[spec(0)] * 3,
        compiler_params=pltpu.CompilerParams(vmem_limit_bytes=50 * 2**20),
        name="attend_back",
    )(qkv, qkv, qkv, grad_mixed)


def layer(ring, tokens, counts, w_qkv, bias_q, bias_v, w_out, bias_out, w_up, bias_up, w_down, bias_down, gain_one, shift_one, gain_two, shift_two, cotangent):
    images, slots, width = tokens.shape
    group = ring.sizes["sz"] * ring.sizes["sc"]
    twins = group // images
    rows = w_qkv.shape[0]
    wide = w_down.shape[0] // rows
    ff = w_up.shape[1]

    slot = lax.broadcasted_iota(jnp.int32, (images, slots, 1), 1)
    marked = jnp.where(slot < counts[:, :, None], tokens, jnp.asarray(ABSENT, bf16))

    def exchange(array):
        if twins > 1:
            array = jnp.repeat(array, twins, axis=0)
        return lax.all_to_all(array, ("sz", "sc"), 0, 0, tiled=True).reshape(group * slots, width)

    def exchange_back(array):
        array = lax.all_to_all(array.reshape(group, slots, width), ("sz", "sc"), 0, 0, tiled=True)
        return array[::twins] if twins > 1 else array

    image_slots = exchange(marked)
    cot_slots = exchange(cotangent)

    small = [bias_q, bias_v, bias_out, bias_down, gain_one, shift_one, gain_two, shift_two]
    small = jnp.stack(small + list(bias_up.reshape(wide, rows)), axis=1)
    small = jnp.pad(small, ((0, 0), (0, SMALL - small.shape[1])))
    gathered = ring.gather(jnp.concatenate([w_qkv, small], axis=1))
    full_qkv = gathered[:, : 3 * width]
    vectors = gathered[:, 3 * width :].astype(f32)
    bq, bv, bo, bd, g1, s1, g2, s2 = [vectors[:, k] for k in range(8)]
    bu = jnp.swapaxes(vectors[:, 8 : 8 + wide].reshape(ring.count, rows, wide), 1, 2).reshape(ff)
    gathered = ring.gather(jnp.concatenate([w_out, w_up], axis=1))
    full_out, full_up = gathered[:, :width], gathered[:, width:]
    full_down = ring.gather(w_down.reshape(rows, wide * width)).reshape(ff, width)

    here = (image_slots[:, :1].astype(f32) < 0.5 * ABSENT).reshape(group, slots)
    held = jnp.sum(here.astype(f32), axis=1)
    before = jnp.sum(jnp.where(np.tril(np.ones((group, group), bool), -1), held[None, :], 0.0), axis=1)
    rank = before[:, None] + lax.broadcasted_iota(jnp.int32, (group, slots), 1).astype(f32)
    rank = jnp.where(here, rank, -1.0).reshape(1, group * slots).astype(jnp.int32)
    packing = (rank == lax.broadcasted_iota(jnp.int32, (PACKED, group * slots), 0)).astype(bf16)
    tokens_f = dot_float(packing, image_slots)
    grad_low = dot_float(packing, cot_slots).astype(bf16)

    normed_f, norm_one_pull = jax.vjp(norm_rows, tokens_f, g1, s1)
    normed = normed_f.astype(bf16)
    qkv_bias = jnp.concatenate([bq, jnp.zeros((width,), f32), bv])
    qkv = (dot_float(normed, full_qkv) + qkv_bias).astype(bf16)
    mixed = attend(qkv)
    residual = tokens_f + dot_float(mixed, full_out) + bo
    normed_two_f, norm_two_pull = jax.vjp(norm_rows, residual, g2, s2)
    normed_two = normed_two_f.astype(bf16)
    hidden = dot_float(normed_two, full_up) + bu
    active_f, gelu_pull = jax.vjp(gelu_exact, hidden)
    active = active_f.astype(bf16)
    result = (residual + dot_float(active, full_down) + bd).astype(bf16)
    result = exchange_back(contract_rows(packing, result).astype(bf16))

    grad_y = grad_low.astype(f32)
    if twins > 1:
        share = (lax.axis_index(("sz", "sc")) % twins == 0).astype(f32)
    else:
        share = None

    def mine(array):
        return array if share is None else array * share

    grad_w_down = mine(contract_rows(active, grad_low)).astype(bf16).reshape(width, wide * width)
    sum_down = ring.scatter(grad_w_down).reshape(wide * rows, width)
    grad_bd = jnp.sum(grad_y, axis=0)
    (grad_hidden,) = gelu_pull(contract_cols(grad_low, full_down))
    hidden_low = grad_hidden.astype(bf16)
    grad_bu = jnp.sum(hidden_low.astype(f32), axis=0)
    grad_w_up = mine(contract_rows(normed_two, hidden_low)).astype(bf16)
    grad_residual, grad_g2, grad_s2 = norm_two_pull(contract_cols(hidden_low, full_up))
    grad_residual = grad_residual + grad_y
    residual_low = grad_residual.astype(bf16)
    grad_w_out = mine(contract_rows(mixed, residual_low)).astype(bf16)
    sums = ring.scatter(jnp.concatenate([grad_w_out, grad_w_up], axis=1))
    sum_out, sum_up = sums[:, :width], sums[:, width:]
    grad_bo = jnp.sum(residual_low.astype(f32), axis=0)
    grad_mixed = contract_cols(residual_low, full_out).astype(bf16)
    grad_joined = jnp.concatenate(attend_back(qkv, grad_mixed), axis=1)
    grad_w_qkv = mine(contract_rows(normed, grad_joined)).astype(bf16)
    joined_sum = jnp.sum(grad_joined.astype(f32), axis=0)
    grad_bq, grad_bv = joined_sum[:width], joined_sum[2 * width :]
    grad_tokens, grad_g1, grad_s1 = norm_one_pull(contract_cols(grad_joined, full_qkv))
    grad_tokens = (grad_tokens + grad_residual).astype(bf16)
    grad_tokens = exchange_back(contract_rows(packing, grad_tokens).astype(bf16)).astype(f32)

    small = [grad_bq, grad_bv, grad_bo, grad_bd, grad_g1, grad_s1, grad_g2, grad_s2]
    grad_bu = jnp.swapaxes(grad_bu.reshape(ring.count, wide, rows), 1, 2).reshape(width, wide)
    small = jnp.concatenate([jnp.stack(small, axis=1), grad_bu], axis=1)
    small = mine(jnp.pad(small, ((0, 0), (0, SMALL - small.shape[1])))).astype(bf16)
    sums = ring.scatter(jnp.concatenate([grad_w_qkv, small], axis=1))
    sum_qkv = sums[:, : 3 * width]
    vectors = sums[:, 3 * width :]
    sum_bq, sum_bv, sum_bo, sum_bd, sum_g1, sum_s1, sum_g2, sum_s2 = [vectors[:, k] for k in range(8)]
    sum_bu = jnp.swapaxes(vectors[:, 8 : 8 + wide], 0, 1).reshape(wide * rows)
    return (result, grad_tokens, sum_qkv, sum_bq, sum_bv, sum_out, sum_bo, sum_up, sum_bu, sum_down, sum_bd, sum_g1, sum_s1, sum_g2, sum_s2)


def solution(mesh):
    n_grp, n_seq = mesh.shape["grp"], mesh.shape["seq"]
    sizes = (n_grp // 2, 2, n_seq // 2, 2)
    fine = Mesh(mesh.devices.reshape(sizes), AXES)
    ring = Ring(sizes)
    grp, seq = AXES[:2], AXES[2:]
    by_token = P(grp, seq, None)
    rows, vec = P(AXES, None), P(AXES)
    in_specs = (by_token, P(grp, seq), rows, vec, vec, rows, vec, rows, vec, rows, vec, vec, vec, vec, vec, by_token)
    out_specs = (by_token, by_token, rows, vec, vec, rows, vec, rows, vec, rows, vec, vec, vec, vec, vec)

    def shards(*args):
        return layer(ring, *args)

    return jax.shard_map(shards, mesh=fine, in_specs=in_specs, out_specs=out_specs, check_vma=False)
```

time: 1540 us -> 1440 us (0.935)
  Pallas kernels: 0 us -> 828 us
  waiting for transfers between devices: 653 us -> 220 us
  blocking collectives: 287 us -> 0 us
  matrix products: 356 us -> 117 us
  starting transfers between devices: 0.69 us -> 103 us
  local copies, waits for them, and re-layouts: 160 us -> 93.9 us
    pallas_call x0 -> x5, Pallas kernels: none -> 828 us  [the longest x3 777 us: assemble(): pl.pallas_call(body, out_shape=jax.ShapeDtypeStruct((total, cut, width),...]
    reduce_scatter x4 -> x0, waiting for transfers between devices: 363 us -> none  [the longest x1 187 us: shards(): lax.psum_scatter(grad_w_down, ('grp', 'seq'), scatter_dimension=0, tiled=...]
    all_gather x8 -> x0, waiting for transfers between devices: 288 us -> none  [the longest x1 72.7 us: shards(): lax.all_gather(w_up, ('grp', 'seq'), axis=0, tiled=True)]
    dot_general x11 -> x5, matrix products: 242 us -> 21.5 us  [dot_float(): return jnp.dot(left, right, preferred_element_type=f32)]
    all_gather x5 -> x0, blocking collectives: 203 us -> none  [the longest x1 60.8 us: shards(): lax.all_gather(row_total, 'seq', axis=2, tiled=True)]
    ppermute x0 -> x57, waiting for transfers between devices: none -> 196 us  [shifted(): lax.ppermute(array, axis, [(i, (i + step) % size) for i in range(size)])]
    all_gather x7 -> x0, local copies, waits for them, and re-layouts: 84.8 us -> none  [the longest x1 19.7 us: shards(): lax.all_gather(key_local, 'seq', axis=1, tiled=True)]
    unnamed x2 -> x0, blocking collectives: 84.6 us -> none
  transfers between devices with their start and end apart: 12 -> 61, of which waited for: 9 -> 27; matrix products, arithmetic and copies ran while one was open for 36% -> 9% of each run, Pallas kernels for 0% -> 33%
where the time goes in v1:
time: 1440 us; the launch traced here: 1430 us
  Pallas kernels  828 us (58%)
  waiting for transfers between devices  220 us (15%)
  matrix products  117 us (8%)
  starting transfers between devices  103 us (7%)
  local copies, waits for them, and re-layouts  93.9 us (7%)
  other arithmetic  62.2 us (4%)
    pallas_call x3, Pallas kernels, assemble(): pl.pallas_call(body, out_shape=jax.ShapeDtypeStruct((total, cut, width),...  777 us
    ppermute x57, waiting for transfers between devices, shifted(): lax.ppermute(array, axis, [(i, (i + step) % size) for i in range(size)])  196 us
    ppermute x57, starting transfers between devices, shifted(): lax.ppermute(array, axis, [(i, (i + step) % size) for i in range(size)])  77.9 us
    dot_general x6, matrix products, contract_rows(): lax.dot_general(left, right, (((0,), (0,)), ((), ())), preferred_element_...  50.8 us
    dot_general x4, matrix products, contract_cols(): lax.dot_general(left, right, (((1,), (1,)), ((), ())), preferred_element_...  45 us
    pallas_call x1, Pallas kernels, attend_back(): pl.pallas_call(mix_back_body, out_shape=[jax.ShapeDtypeStruct((PACKED, H...  31.8 us
  transfers between devices with their start and end apart: 61, of which 27 were waited for; matrix products, arithmetic and copies ran while one was open for 9% of the time, Pallas kernels for 33%

profile of v1, /device:TPU:0, one launch (start us, length us, event | category | flops | bytes accessed | tf_op | source)
XLA Modules:
  0.0 1425.9 jit_solution(203856610695063624)
XLA Ops:
  23.2 13.6 collective-permute-done
  36.9 17.9 %collective-permute-start.1 = (bf16[32,3200]{1,0:T(8,128)(2,1)S(1)}, bf16[32,3200]{1,0:T(8,128)(2,1)S(1)}, u32[]{:S(2)}, u32[]{:S(2)}) collective-permute-start(bf16[32,3200]{1,0:T(8,128)(2,1)S(1)} %fusion.79), channel_id=1, source_target_pairs={{0,4},{2,6},{4,0},{6,2},{1,5},{3,7},{5,1},{7,3},{8,12},{10,14},{12... | collective-permute-start | bytes 614408 | tf_op jit(solution)/shard_map/ppermute | solution.py:48
  54.8 32.0 %collective-permute-done.1 = bf16[32,3200]{1,0:T(8,128)(2,1)S(1)} collective-permute-done((bf16[32,3200]{1,0:T(8,128)(2,1)S(1)}, bf16[32,3200]{1,0:T(8,128)(2,1)S(1)}, u32[]{:S(2)}, u32[]{:S(2)}) %collective-permute-start.1) | collective-permute-done | bytes 204832 | tf_op jit(solution)/shard_map/ppermute | solution.py:48
  101.4 8.2 collective-permute-done.12
  115.4 7.3 collective-permute-done.25
  124.4 12.3 collective-permute-done.14
  140.0 16.0 %collective-permute-done.5 = bf16[2,4,16,3200]{3,2,1,0:T(8,128)(2,1)S(1)} collective-permute-done((bf16[2,4,16,3200]{3,2,1,0:T(8,128)(2,1)S(1)}, bf16[2,4,16,3200]{3,2,1,0:T(8,128)(2,1)S(1)}, u32[]{:S(2)}, u32[]{:S(2)}) %collective-permute-start.5) | collective-permute-done | bytes 819232 | tf_op jit(solution)/shard_map/ppermute | solution.py:48
  160.5 17.0 %collective-permute-done.27 = bf16[2,4,16,4096]{3,2,1,0:T(8,128)(2,1)} collective-permute-done((bf16[2,4,16,4096]{3,2,1,0:T(8,128)(2,1)S(1)}, bf16[2,4,16,4096]{3,2,1,0:T(8,128)(2,1)}, u32[]{:S(2)}, u32[]{:S(2)}) %collective-permute-start.27) | collective-permute-done | bytes 1048608 | tf_op jit(solution)/shard_map/ppermute | solution.py:48
  186.1 200.9 %assemble.3 = bf16[64,16,3200]{2,1,0:T(8,128)(2,1)} custom-call(s32[64]{0:T(128)} %stack.592.table_ref, bf16[8,16,3200]{2,1,0:T(8,128)(2,1)} %bitcast.341, bf16[8,16,3200]{2,1,0:T(8,128)(2,1)} %bitcast.347, bf16[8,16,3200]{2,1,0:T(8,128)(2,1)} %bitcast.349, bf16[8,16,3200]{2,1,0:T(8,128)(2,1)} %bitcast.351, bf16[8,16,3200]{2,1,0:T(8,128)(2,1)} %bitcast.340, ...), custom_call_target="tpu_custom_call" | custom-call | tf_op jit(solution)/shard_map/assemble/pallas_call | solution.py:128
  391.5 10.6 all-to-all-start.2
  404.2 256.5 %assemble.5 = bf16[64,16,4096]{2,1,0:T(8,128)(2,1)} custom-call(s32[64]{0:T(128)} %stack.592.table_ref, bf16[8,16,4096]{2,1,0:T(8,128)(2,1)} %bitcast.338, bf16[8,16,4096]{2,1,0:T(8,128)(2,1)} %bitcast.139.refs_1_, bf16[8,16,4096]{2,1,0:T(8,128)(2,1)} %bitcast.344, bf16[8,16,4096]{2,1,0:T(8,128)(2,1)} %bitcast.346, bf16[8,16,4096]{2,1,0:T(8,128)(2,1)} %bitcast.339, ...), custom_call_target="tpu_custom_call" | custom-call | tf_op jit(solution)/shard_map/assemble/pallas_call | solution.py:128
  660.7 13.9 reshape_reshape.6
  681.0 5.8 add_convert_fusion.1.q_ref.k_ref.v_ref
  686.8 18.6 %attend.1 = bf16[592,1024]{1,0:T(8,128)(2,1)S(1)} custom-call(bf16[592,3072]{1,0:T(8,128)(2,1)} %add_convert_fusion.1.q_ref.k_ref.v_ref, bf16[592,3072]{1,0:T(8,128)(2,1)} %add_convert_fusion.1.q_ref.k_ref.v_ref, bf16[592,3072]{1,0:T(8,128)(2,1)} %add_convert_fusion.1.q_ref.k_ref.v_ref), custom_call_target="tpu_custom_call" | custom-call | tf_op jit(solution)/shard_map/attend/pallas_call | solution.py:202
  708.8 320.0 %assemble.4 = bf16[64,16,5120]{2,1,0:T(8,128)(2,1)} custom-call(s32[64]{0:T(128)} %stack.592.table_ref, bf16[8,16,5120]{2,1,0:T(8,128)(2,1)} %bitcast.115.refs_0_, bf16[8,16,5120]{2,1,0:T(8,128)(2,1)} %bitcast.116.refs_1_, bf16[8,16,5120]{2,1,0:T(8,128)(2,1)} %bitcast.117.refs_2_, bf16[8,16,5120]{2,1,0:T(8,128)(2,1)} %bitcast.118.refs_3_, ...), custom_call_target="tpu_custom_call" | custom-call | tf_op jit(solution)/shard_map/assemble/pallas_call | solution.py:128
  1040.3 31.3 %fusion.97 = (bf16[4096]{0:T(1024)(128)(2,1)S(1)}, bf16[592,4096]{1,0:T(8,128)(2,1)}, f32[592,4096]{1,0:T(8,128)}) fusion(f32[592,4096]{1,0:T(8,128)S(1)} %fusion.11, f32[4096]{0:T(1024)S(1)} %add.2065, bf16[592,1024]{1,0:T(8,128)(2,1)S(1)} %fusion.40, bf16[4096,1024]{1,0:T(8,128)(2,1)} %reshape_reshape.6), kind=kOutput, calls=%fused_computation.258 | convolution fusion | flops 5145489408 | bytes 33873920 | tf_op jit(solution)/shard_map/dot_general | solution.py:44
  1071.6 12.3 convolution_convert_fusion
  1084.0 5.7 multiply_reduce_fusion
  1095.4 31.8 %attend_back.1 = (bf16[592,1024]{1,0:T(8,128)(2,1)S(1)}, bf16[592,1024]{1,0:T(8,128)(2,1)S(1)}, bf16[592,1024]{1,0:T(8,128)(2,1)S(1)}) custom-call(bf16[592,3072]{1,0:T(8,128)(2,1)} %add_convert_fusion.1.q_ref.k_ref.v_ref, bf16[592,3072]{1,0:T(8,128)(2,1)} %add_convert_fusion.1.q_ref.k_ref.v_ref, bf16[592,3072]{1,0:T(8,128)(2,1)} %add_convert_fusion.1.q_ref.k_ref.v_ref, ...), custom_call_target="tpu_custom_call" | custom-call | tf_op jit(solution)/shard_map/attend_back/pallas_call | solution.py:238
  1129.0 7.4 convolution_convert_fusion.2
  1142.0 11.1 multiply_convert_fusion
  1153.1 11.5 convolution_convert_fusion.1
  1164.6 13.9 reshape_reshape.7
  1212.4 9.6 pad_maximum_fusion
  1222.0 13.3 fusion.33
  1249.7 9.2 constant_dynamic-slice_fusion.1
  1267.9 17.9 %all-to-all-done.1 = bf16[8,104,1024]{2,1,0:T(8,128)(2,1)} async-done(((bf16[8,104,1024]{2,1,0:T(8,128)(2,1)}), bf16[8,104,1024]{2,1,0:T(8,128)(2,1)}, u32[]{:S(2)}, u32[]{:S(2)}) %all-to-all-start.1) | async-done | bytes 1703968 | tf_op jit(solution)/shard_map/all_to_all | solution.py:266
  1289.4 17.7 %collective-permute-done.34 = bf16[2,4,16,3200]{3,2,1,0:T(8,128)(2,1)S(1)} collective-permute-done((bf16[2,4,16,3200]{3,2,1,0:T(8,128)(2,1)S(1)}, bf16[2,4,16,3200]{3,2,1,0:T(8,128)(2,1)S(1)}, u32[]{:S(2)}, u32[]{:S(2)}) %collective-permute-start.34) | collective-permute-done | bytes 819232 | tf_op jit(solution)/shard_map/ppermute | solution.py:48
  1342.9 6.1 collective-permute-done.50
  1371.5 13.8 collective-permute-done.44
  1391.3 7.6 collective-permute-done.45
  1413.2 7.1 collective-permute-done.47
  (365 shorter events, 245.8 us)
Async XLA Ops:
  1.8 92.2 %collective-permute-start.22 = (bf16[32,4096]{1,0:T(8,128)(2,1)S(1)}, bf16[32,4096]{1,0:T(8,128)(2,1)}, u32[]{:S(2)}, u32[]{:S(2)}) collective-permute-start(bf16[32,4096]{1,0:T(8,128)(2,1)S(1)} %reshape.353), channel_id=1, source_target_pairs={{0,2},{2,4},{4,6},{6,0},{1,3},{3,5},{5,7},{7,1},{8,10},{10,12},{12... | collective-permute-start | bytes 786440 | tf_op jit(solution)/shard_map/ppermute | solution.py:48
  4.8 92.5 %collective-permute-start.23 = (bf16[32,4096]{1,0:T(8,128)(2,1)S(1)}, bf16[32,4096]{1,0:T(8,128)(2,1)S(1)}, u32[]{:S(2)}, u32[]{:S(2)}) collective-permute-start(bf16[32,4096]{1,0:T(8,128)(2,1)S(1)} %reshape.353), channel_id=1, source_target_pairs={{0,4},{2,6},{4,0},{6,2},{1,5},{3,7},{5,1},{7,3},{8,12},{10,14},{12... | collective-permute-start | bytes 786440 | tf_op jit(solution)/shard_map/ppermute | solution.py:48
  7.4 91.6 %collective-permute-start.24 = (bf16[32,4096]{1,0:T(8,128)(2,1)S(1)}, bf16[32,4096]{1,0:T(8,128)(2,1)S(1)}, u32[]{:S(2)}, u32[]{:S(2)}) collective-permute-start(bf16[32,4096]{1,0:T(8,128)(2,1)S(1)} %reshape.353), channel_id=1, source_target_pairs={{0,6},{2,0},{4,2},{6,4},{1,7},{3,1},{5,3},{7,5},{8,14},{10,8},{12,... | collective-permute-start | bytes 786440 | tf_op jit(solution)/shard_map/ppermute | solution.py:48
  10.6 90.2 %collective-permute-start.11 = (bf16[32,5120]{1,0:T(8,128)(2,1)S(1)}, bf16[32,5120]{1,0:T(8,128)(2,1)S(1)}, u32[]{:S(2)}, u32[]{:S(2)}) collective-permute-start(bf16[32,5120]{1,0:T(8,128)(2,1)S(1)} %constant_dynamic-update-slice_fusion), channel_id=1, source_target_pairs={{0,2},{2,4},{4,6},{6,0},{1,3},{3,5},{5,7},{7,1},{8,10},{10,12},{12... | collective-permute-start | bytes 983048 | tf_op jit(solution)/shard_map/ppermute | solution.py:48
  17.8 373.7 %all-to-all-start = ((bf16[8,104,1024]{2,1,0:T(8,128)(2,1)}), bf16[8,104,1024]{2,1,0:T(8,128)(2,1)}, u32[]{:S(2)}, u32[]{:S(2)}) async-start(bf16[8,104,1024]{2,1,0:T(8,128)(2,1)} %broadcast_select_fusion), calls=%async_computation | async-start | bytes 3407872 | tf_op jit(solution)/shard_map/all_to_all | solution.py:263
  36.9 49.9 %collective-permute-start.1 = (bf16[32,3200]{1,0:T(8,128)(2,1)S(1)}, bf16[32,3200]{1,0:T(8,128)(2,1)S(1)}, u32[]{:S(2)}, u32[]{:S(2)}) collective-permute-start(bf16[32,3200]{1,0:T(8,128)(2,1)S(1)} %fusion.79), channel_id=1, source_target_pairs={{0,4},{2,6},{4,0},{6,2},{1,5},{3,7},{5,1},{7,3},{8,12},{10,14},{12... | collective-permute-start | bytes 614408 | tf_op jit(solution)/shard_map/ppermute | solution.py:48
  113.8 42.2 %collective-permute-start.5 = (bf16[2,4,16,3200]{3,2,1,0:T(8,128)(2,1)S(1)}, bf16[2,4,16,3200]{3,2,1,0:T(8,128)(2,1)S(1)}, u32[]{:S(2)}, u32[]{:S(2)}) collective-permute-start(bf16[2,4,16,3200]{3,2,1,0:T(8,128)(2,1)S(1)} %pad_maximum_fusion.5), channel_id=1, source_target_pairs={{0,16},{16,0},{1,17},{17,1},{2,18},{18,2},{3,19},{19,3},{4,20},{20... | collective-permute-start | bytes 2457608 | tf_op jit(solution)/shard_map/ppermute | solution.py:48
  122.7 33.3 %collective-permute-start.8 = (bf16[2,4,16,3200]{3,2,1,0:T(8,128)(2,1)S(1)}, bf16[2,4,16,3200]{3,2,1,0:T(8,128)(2,1)S(1)}, u32[]{:S(2)}, u32[]{:S(2)}) collective-permute-start(bf16[2,4,16,3200]{3,2,1,0:T(8,128)(2,1)S(1)} %pad_maximum_fusion.6), channel_id=1, source_target_pairs={{0,8},{8,0},{1,9},{9,1},{2,10},{10,2},{3,11},{11,3},{4,12},{12,4},... | collective-permute-start | bytes 2457608 | tf_op jit(solution)/shard_map/ppermute | solution.py:48
  124.4 34.4 %collective-permute-start.6 = (bf16[2,4,16,3200]{3,2,1,0:T(8,128)(2,1)S(1)}, bf16[2,4,16,3200]{3,2,1,0:T(8,128)(2,1)S(1)}, u32[]{:S(2)}, u32[]{:S(2)}) collective-permute-start(bf16[2,4,16,3200]{3,2,1,0:T(8,128)(2,1)S(1)} %pad_maximum_fusion.5), channel_id=1, source_target_pairs={{0,1},{1,0},{2,3},{3,2},{4,5},{5,4},{6,7},{7,6},{8,9},{9,8},{10,11... | collective-permute-start | bytes 2457608 | tf_op jit(solution)/shard_map/ppermute | solution.py:48
  138.5 39.1 %collective-permute-start.27 = (bf16[2,4,16,4096]{3,2,1,0:T(8,128)(2,1)S(1)}, bf16[2,4,16,4096]{3,2,1,0:T(8,128)(2,1)}, u32[]{:S(2)}, u32[]{:S(2)}) collective-permute-start(bf16[2,4,16,4096]{3,2,1,0:T(8,128)(2,1)S(1)} %pad_maximum_fusion.3), channel_id=1, source_target_pairs={{0,16},{16,0},{1,17},{17,1},{2,18},{18,2},{3,19},{19,3},{4,20},{20... | collective-permute-start | bytes 3145736 | tf_op jit(solution)/shard_map/ppermute | solution.py:48
  156.0 27.2 %collective-permute-start.28 = (bf16[2,4,16,4096]{3,2,1,0:T(8,128)(2,1)S(1)}, bf16[2,4,16,4096]{3,2,1,0:T(8,128)(2,1)S(1)}, u32[]{:S(2)}, u32[]{:S(2)}) collective-permute-start(bf16[2,4,16,4096]{3,2,1,0:T(8,128)(2,1)S(1)} %pad_maximum_fusion.3), channel_id=1, source_target_pairs={{0,1},{1,0},{2,3},{3,2},{4,5},{5,4},{6,7},{7,6},{8,9},{9,8},{10,11... | collective-permute-start | bytes 3145736 | tf_op jit(solution)/shard_map/ppermute | solution.py:48
  177.5 225.2 %collective-permute-start.16 = (bf16[2,4,16,5120]{3,2,1,0:T(8,128)(2,1)}, bf16[2,4,16,5120]{3,2,1,0:T(8,128)(2,1)}, u32[]{:S(2)}, u32[]{:S(2)}) collective-permute-start(bf16[2,4,16,5120]{3,2,1,0:T(8,128)(2,1)} %pad_maximum_fusion.1), channel_id=1, source_target_pairs={{0,16},{16,0},{1,17},{17,1},{2,18},{18,2},{3,19},{19,3},{4,20},{20... | collective-permute-start | bytes 3932168 | tf_op jit(solution)/shard_map/ppermute | solution.py:48
  181.7 221.1 %collective-permute-start.19 = (bf16[2,4,16,5120]{3,2,1,0:T(8,128)(2,1)}, bf16[2,4,16,5120]{3,2,1,0:T(8,128)(2,1)}, u32[]{:S(2)}, u32[]{:S(2)}) collective-permute-start(bf16[2,4,16,5120]{3,2,1,0:T(8,128)(2,1)} %pad_maximum_fusion.2), channel_id=1, source_target_pairs={{0,8},{8,0},{1,9},{9,1},{2,10},{10,2},{3,11},{11,3},{4,12},{12,4},... | collective-permute-start | bytes 3932168 | tf_op jit(solution)/shard_map/ppermute | solution.py:48
  183.2 218.9 %collective-permute-start.31 = (bf16[2,4,16,4096]{3,2,1,0:T(8,128)(2,1)S(1)}, bf16[2,4,16,4096]{3,2,1,0:T(8,128)(2,1)S(1)}, u32[]{:S(2)}, u32[]{:S(2)}) collective-permute-start(bf16[2,4,16,4096]{3,2,1,0:T(8,128)(2,1)S(1)} %pad_maximum_fusion.4), channel_id=1, source_target_pairs={{0,1},{1,0},{2,3},{3,2},{4,5},{5,4},{6,7},{7,6},{8,9},{9,8},{10,11... | collective-permute-start | bytes 3145736 | tf_op jit(solution)/shard_map/ppermute | solution.py:48
  184.2 219.0 %collective-permute-start.29 = (bf16[2,4,16,4096]{3,2,1,0:T(8,128)(2,1)}, bf16[2,4,16,4096]{3,2,1,0:T(8,128)(2,1)S(1)}, u32[]{:S(2)}, u32[]{:S(2)}) collective-permute-start(bf16[2,4,16,4096]{3,2,1,0:T(8,128)(2,1)} %collective-permute-done.27), channel_id=1, source_target_pairs={{0,1},{1,0},{2,3},{3,2},{4,5},{5,4},{6,7},{7,6},{8,9},{9,8},{10,11... | collective-permute-start | bytes 3145736 | tf_op jit(solution)/shard_map/ppermute | solution.py:48
  184.2 219.1 %collective-permute-start.32 = (bf16[2,4,16,4096]{3,2,1,0:T(8,128)(2,1)}, bf16[2,4,16,4096]{3,2,1,0:T(8,128)(2,1)}, u32[]{:S(2)}, u32[]{:S(2)}) collective-permute-start(bf16[2,4,16,4096]{3,2,1,0:T(8,128)(2,1)} %collective-permute-done.30), channel_id=1, source_target_pairs={{0,1},{1,0},{2,3},{3,2},{4,5},{5,4},{6,7},{7,6},{8,9},{9,8},{10,11... | collective-permute-start | bytes 3145736 | tf_op jit(solution)/shard_map/ppermute | solution.py:48
  391.5 314.0 %all-to-all-start.2 = ((bf16[8,104,1024]{2,1,0:T(8,128)(2,1)}), bf16[8,104,1024]{2,1,0:T(8,128)(2,1)}, u32[]{:S(2)}, u32[]{:S(2)}) async-start(bf16[8,104,1024]{2,1,0:T(8,128)(2,1)} %param.32), calls=%async_computation.2 | async-start | bytes 3407872 | tf_op jit(solution)/shard_map/all_to_all | solution.py:263
  402.1 306.7 %collective-permute-start.17 = (bf16[2,4,16,5120]{3,2,1,0:T(8,128)(2,1)}, bf16[2,4,16,5120]{3,2,1,0:T(8,128)(2,1)}, u32[]{:S(2)}, u32[]{:S(2)}) collective-permute-start(bf16[2,4,16,5120]{3,2,1,0:T(8,128)(2,1)} %pad_maximum_fusion.1), channel_id=1, source_target_pairs={{0,1},{1,0},{2,3},{3,2},{4,5},{5,4},{6,7},{7,6},{8,9},{9,8},{10,11... | collective-permute-start | bytes 3932168 | tf_op jit(solution)/shard_map/ppermute | solution.py:48
  402.7 306.1 %collective-permute-start.20 = (bf16[2,4,16,5120]{3,2,1,0:T(8,128)(2,1)}, bf16[2,4,16,5120]{3,2,1,0:T(8,128)(2,1)}, u32[]{:S(2)}, u32[]{:S(2)}) collective-permute-start(bf16[2,4,16,5120]{3,2,1,0:T(8,128)(2,1)} %pad_maximum_fusion.2), channel_id=1, source_target_pairs={{0,1},{1,0},{2,3},{3,2},{4,5},{5,4},{6,7},{7,6},{8,9},{9,8},{10,11... | collective-permute-start | bytes 3932168 | tf_op jit(solution)/shard_map/ppermute | solution.py:48
  402.8 306.0 %collective-permute-start.18 = (bf16[2,4,16,5120]{3,2,1,0:T(8,128)(2,1)}, bf16[2,4,16,5120]{3,2,1,0:T(8,128)(2,1)}, u32[]{:S(2)}, u32[]{:S(2)}) collective-permute-start(bf16[2,4,16,5120]{3,2,1,0:T(8,128)(2,1)} %collective-permute-done.16), channel_id=1, source_target_pairs={{0,1},{1,0},{2,3},{3,2},{4,5},{5,4},{6,7},{7,6},{8,9},{9,8},{10,11... | collective-permute-start | bytes 3932168 | tf_op jit(solution)/shard_map/ppermute | solution.py:48
  403.2 305.6 %collective-permute-start.21 = (bf16[2,4,16,5120]{3,2,1,0:T(8,128)(2,1)}, bf16[2,4,16,5120]{3,2,1,0:T(8,128)(2,1)}, u32[]{:S(2)}, u32[]{:S(2)}) collective-permute-start(bf16[2,4,16,5120]{3,2,1,0:T(8,128)(2,1)} %collective-permute-done.19), channel_id=1, source_target_pairs={{0,1},{1,0},{2,3},{3,2},{4,5},{5,4},{6,7},{7,6},{8,9},{9,8},{10,11... | collective-permute-start | bytes 3932168 | tf_op jit(solution)/shard_map/ppermute | solution.py:48
  1188.4 56.7 %collective-permute-start.33 = (bf16[2,2,4,32,3200]{4,3,2,0,1:T(8,128)(2,1)}, bf16[2,2,4,32,3200]{4,3,2,0,1:T(8,128)(2,1)}, u32[]{:S(2)}, u32[]{:S(2)}) collective-permute-start(bf16[2,2,4,32,3200]{4,3,2,0,1:T(8,128)(2,1)} %bitcast.321), channel_id=1, source_target_pairs={{0,1},{1,0},{2,3},{3,2},{4,5},{5,4},{6,7},{7,6},{8,9},{9,8},{10,11... | collective-permute-start | bytes 9830408 | tf_op jit(solution)/shard_map/ppermute | solution.py:48
  1195.2 45.5 %all-to-all-start.3 = ((bf16[8,104,1024]{2,1,0:T(8,128)(2,1)}), bf16[8,104,1024]{2,1,0:T(8,128)(2,1)}, u32[]{:S(2)}, u32[]{:S(2)}) async-start(bf16[8,104,1024]{2,1,0:T(8,128)(2,1)} %bitcast.343), calls=%async_computation.3 | async-start | bytes 3407872 | tf_op jit(solution)/shard_map/all_to_all | solution.py:266
  1204.8 103.2 %collective-permute-start.49 = (bf16[2,2,4,32,4096]{4,3,2,1,0:T(8,128)(2,1)}, bf16[2,2,4,32,4096]{4,3,2,1,0:T(8,128)(2,1)}, u32[]{:S(2)}, u32[]{:S(2)}) collective-permute-start(bf16[2,2,4,32,4096]{4,3,2,1,0:T(8,128)(2,1)} %dynamic-slice_bitcast_fusion), channel_id=1, source_target_pairs={{0,1},{1,0},{2,3},{3,2},{4,5},{5,4},{6,7},{7,6},{8,9},{9,8},{10,11... | collective-permute-start | bytes 12582920 | tf_op jit(solution)/shard_map/ppermute | solution.py:48
  1240.7 45.1 %all-to-all-start.1 = ((bf16[8,104,1024]{2,1,0:T(8,128)(2,1)}), bf16[8,104,1024]{2,1,0:T(8,128)(2,1)}, u32[]{:S(2)}, u32[]{:S(2)}) async-start(bf16[8,104,1024]{2,1,0:T(8,128)(2,1)} %bitcast.342), calls=%async_computation.1 | async-start | bytes 3407872 | tf_op jit(solution)/shard_map/all_to_all | solution.py:266
  1249.1 38.3 %collective-permute-start.36 = (bf16[2,4,16,3200]{3,2,1,0:T(8,128)(2,1)}, bf16[2,4,16,3200]{3,2,1,0:T(8,128)(2,1)}, u32[]{:S(2)}, u32[]{:S(2)}) collective-permute-start(bf16[2,4,16,3200]{3,2,1,0:T(8,128)(2,1)} %dynamic-slice_bitcast_fusion.5), channel_id=1, source_target_pairs={{0,8},{8,0},{1,9},{9,1},{2,10},{10,2},{3,11},{11,3},{4,12},{12,4},... | collective-permute-start | bytes 2457608 | tf_op jit(solution)/shard_map/ppermute | solution.py:48
  1264.2 87.7 %collective-permute-start.41 = (bf16[2,2,4,32,5120]{4,3,2,0,1:T(8,128)(2,1)}, bf16[2,2,4,32,5120]{4,3,2,0,1:T(8,128)(2,1)}, u32[]{:S(2)}, u32[]{:S(2)}) collective-permute-start(bf16[2,2,4,32,5120]{4,3,2,0,1:T(8,128)(2,1)} %bitcast.320), channel_id=1, source_target_pairs={{0,1},{1,0},{2,3},{3,2},{4,5},{5,4},{6,7},{7,6},{8,9},{9,8},{10,11... | collective-permute-start | bytes 15728648 | tf_op jit(solution)/shard_map/ppermute | solution.py:48
  1356.8 28.4 %collective-permute-start.44 = (bf16[2,4,16,5120]{3,2,1,0:T(8,128)(2,1)S(1)}, bf16[2,4,16,5120]{3,2,1,0:T(8,128)(2,1)S(1)}, u32[]{:S(2)}, u32[]{:S(2)}) collective-permute-start(bf16[2,4,16,5120]{3,2,1,0:T(8,128)(2,1)S(1)} %dynamic-slice_bitcast_fusion.1), channel_id=1, source_target_pairs={{0,8},{8,0},{1,9},{9,1},{2,10},{10,2},{3,11},{11,3},{4,12},{12,4},... | collective-permute-start | bytes 3932168 | tf_op jit(solution)/shard_map/ppermute | solution.py:48
  1357.8 31.8 %collective-permute-start.42 = (bf16[2,4,16,5120]{3,2,1,0:T(8,128)(2,1)S(1)}, bf16[2,4,16,5120]{3,2,1,0:T(8,128)(2,1)S(1)}, u32[]{:S(2)}, u32[]{:S(2)}) collective-permute-start(bf16[2,4,16,5120]{3,2,1,0:T(8,128)(2,1)S(1)} %dynamic-slice_bitcast_fusion.2), channel_id=1, source_target_pairs={{0,16},{16,0},{1,17},{17,1},{2,18},{18,2},{3,19},{19,3},{4,20},{20... | collective-permute-start | bytes 3932168 | tf_op jit(solution)/shard_map/ppermute | solution.py:48
  1365.6 38.2 %collective-permute-start.54 = (bf16[32,4096]{1,0:T(8,128)(2,1)S(1)}, bf16[32,4096]{1,0:T(8,128)(2,1)S(1)}, u32[]{:S(2)}, u32[]{:S(2)}) collective-permute-start(bf16[32,4096]{1,0:T(8,128)(2,1)S(1)} %get-tuple-element.70), channel_id=1, source_target_pairs={{0,2},{2,4},{4,6},{6,0},{1,3},{3,5},{5,7},{7,1},{8,10},{10,12},{12... | collective-permute-start | bytes 786440 | tf_op jit(solution)/shard_map/ppermute | solution.py:48
  1365.7 40.9 %collective-permute-start.55 = (bf16[32,4096]{1,0:T(8,128)(2,1)S(1)}, bf16[32,4096]{1,0:T(8,128)(2,1)S(1)}, u32[]{:S(2)}, u32[]{:S(2)}) collective-permute-start(bf16[32,4096]{1,0:T(8,128)(2,1)S(1)} %get-tuple-element.71), channel_id=1, source_target_pairs={{0,4},{2,6},{4,0},{6,2},{1,5},{3,7},{5,1},{7,3},{8,12},{10,14},{12... | collective-permute-start | bytes 786440 | tf_op jit(solution)/shard_map/ppermute | solution.py:48
  1368.6 38.0 %collective-permute-start.56 = (bf16[32,4096]{1,0:T(8,128)(2,1)S(1)}, bf16[32,4096]{1,0:T(8,128)(2,1)S(1)}, u32[]{:S(2)}, u32[]{:S(2)}) collective-permute-start(bf16[32,4096]{1,0:T(8,128)(2,1)S(1)} %get-tuple-element.72), channel_id=1, source_target_pairs={{0,6},{2,0},{4,2},{6,4},{1,7},{3,1},{5,3},{7,5},{8,14},{10,8},{12,... | collective-permute-start | bytes 786440 | tf_op jit(solution)/shard_map/ppermute | solution.py:48
  (83 other events, 2393.0 us)

commit v2 on v1

v2 whole, which is shorter than its diff:
```python
import jax
import jax.numpy as jnp
import numpy as np
from jax import lax
from jax.experimental import pallas as pl
from jax.experimental.pallas import tpu as pltpu
from jax.sharding import Mesh
from jax.sharding import PartitionSpec as P

H = 16
HD = 64
LENGTH = 577
PACKED = 592
EPSILON = 1e-06
NEGATIVE = -1e30
ABSENT = 100.0
SMALL = 128
AXES = ("gy", "gx", "sz", "sc")
ORDERS = (("gx", "gy"), ("gy", "gx"))

bf16 = jnp.bfloat16
f32 = jnp.float32


def norm_rows(values, gain_vec, shift_vec):
    row_mean = jnp.mean(values, axis=-1, keepdims=True)
    centred = values - row_mean
    row_var = jnp.mean(centred * centred, axis=-1, keepdims=True)
    return centred * lax.rsqrt(row_var + EPSILON) * gain_vec + shift_vec


def dot_float(left, right):
    return jnp.dot(left, right, preferred_element_type=f32)


def contract_rows(left, right):
    return lax.dot_general(left, right, (((0,), (0,)), ((), ())), preferred_element_type=f32)


def contract_cols(left, right):
    return lax.dot_general(left, right, (((1,), (1,)), ((), ())), preferred_element_type=f32)


def shifted(array, axis, size, step):
    return lax.ppermute(array, axis, [(i, (i + step) % size) for i in range(size)])


def pick(array, index, axis):
    return lax.dynamic_index_in_dim(array, index, axis, keepdims=False)


class Ring:
    def __init__(self, sizes):
        self.sizes = dict(zip(AXES, sizes))
        self.count = int(np.prod(sizes))

    def place(self):
        return {axis: lax.axis_index(axis) for axis in AXES}

    def others(self, array, axis):
        size = self.sizes[axis]
        return [shifted(array, axis, size, step) for step in range(1, size)]

    def along(self, shard):
        cut = shard.shape[0] // 2
        columns = [shard] + self.others(shard, "sz")
        return [jnp.stack([c[:cut] for c in columns]), jnp.stack([c[cut:] for c in columns])]

    def across(self, halves):
        return [jnp.stack([half] + self.others(half, order[0])) for half, order in zip(halves, ORDERS)]

    def plane(self, halves):
        return [[half] + self.others(half, order[1]) for half, order in zip(halves, ORDERS)]

    def cores(self, planes):
        sources = []
        for part, arrays in enumerate(planes):
            for turn in range(2):
                for step, group in enumerate(arrays):
                    if turn:
                        group = shifted(group, "sc", 2, 1)
                    sources.append((group, part, turn, step))
        return sources

    def assemble(self, sources, widths):
        place = self.place()
        sizes = self.sizes
        cut, width = sources[0][0].shape[-2:]
        targets = []
        arrays = []
        for group, part, turn, step in sources:
            order = ORDERS[part]
            inner, depth = group.shape[:2]
            arrays.append(group.reshape(inner * depth, cut, width))
            for one in range(inner):
                for k in range(depth):
                    at = dict(place)
                    at["sc"] = (place["sc"] - turn) % 2
                    at[order[1]] = (place[order[1]] - step) % sizes[order[1]]
                    at[order[0]] = (place[order[0]] - one) % sizes[order[0]]
                    at["sz"] = (place["sz"] - k) % sizes["sz"]
                    index = at["gy"]
                    for axis in AXES[1:]:
                        index = index * sizes[axis] + at[axis]
                    targets.append(index * 2 + part)
        table = jnp.stack(targets).astype(jnp.int32)
        total = len(targets)
        blocks = [a.shape[0] for a in arrays]
        starts = np.concatenate([[0], np.cumsum(widths)])

        def body(table_ref, *refs):
            ins = refs[: len(blocks)]
            outs = refs[len(blocks) : -3]
            held, came, left = refs[-3:]
            arrivals = []
            n = 0
            for ref, count in zip(ins, blocks):
                for k in range(count):
                    arrivals.append(pltpu.make_async_copy(ref.at[k], held.at[n], came.at[n]))
                    n += 1
            for copy in arrivals:
                copy.start()
            departures = []
            for n, copy in enumerate(arrivals):
                copy.wait()
                for i, out in enumerate(outs):
                    window = held.at[n, :, pl.ds(int(starts[i]), widths[i])]
                    leave = pltpu.make_async_copy(window, out.at[table_ref[n]], left.at[n, i])
                    leave.start()
                    departures.append(leave)
            for copy in departures:
                copy.wait()

        outs = pl.pallas_call(
            body,
            out_shape=[jax.ShapeDtypeStruct((total, cut, w), bf16) for w in widths],
            grid_spec=pltpu.PrefetchScalarGridSpec(
                num_scalar_prefetch=1,
                grid=(1,),
                in_specs=[pl.BlockSpec(memory_space=pl.ANY)] * len(blocks),
                out_specs=[pl.BlockSpec(memory_space=pl.ANY)] * len(widths),
                scratch_shapes=[
                    pltpu.VMEM((total, cut, width), bf16),
                    pltpu.SemaphoreType.DMA((total,)),
                    pltpu.SemaphoreType.DMA((total, len(widths))),
                ],
            ),
            compiler_params=pltpu.CompilerParams(vmem_limit_bytes=50 * 2**20),
            name="assemble",
        )(table, *arrays)
        return [out.reshape(total * cut, w) for out, w in zip(outs, widths)]

    def add(self, *arrays):
        total = arrays[0].astype(f32)
        for array in arrays[1:]:
            total = total + array.astype(f32)
        return total

    def fold(self, array, axis, at, low=True):
        size = self.sizes[axis]
        own = pick(array, at[axis], 0)
        came = [shifted(pick(array, (at[axis] + k) % size, 0), axis, size, k) for k in range(1, size)]
        total = self.add(own, *came)
        return total.astype(bf16) if low else total

    def between(self, grads):
        at = self.place()
        sizes = self.sizes
        sums = []
        for array in grads:
            array = array.reshape(sizes["gy"], sizes["gx"], sizes["sz"], 2, array.shape[0] // self.count, array.shape[-1])
            own = pick(array, at["sc"], 3)
            came = shifted(pick(array, 1 - at["sc"], 3), "sc", 2, 1)
            sums.append((own, came))
        return sums

    def halves(self, sums):
        total = [self.add(own, came).astype(bf16) for own, came in sums]
        total = total[0] if len(total) == 1 else jnp.concatenate(total, axis=-1)
        cut = total.shape[3] // 2
        return total[:, :, :, :cut], jnp.swapaxes(total[:, :, :, cut:], 0, 1)

    def inward(self, pair):
        at = self.place()
        return self.fold(pair[0], "gy", at), self.fold(pair[1], "gx", at)

    def inward_more(self, pair):
        at = self.place()
        return self.fold(pair[0], "gx", at), self.fold(pair[1], "gy", at)

    def down(self, pair):
        return self.fold(jnp.concatenate(pair, axis=1), "sz", self.place(), low=False)


def tie(*values):
    return lax.optimization_barrier(values)


def room(mib=50):
    return pltpu.CompilerParams(vmem_limit_bytes=mib * 2**20)


def of_head(part):
    return lax.broadcasted_iota(jnp.int32, (1, 2 * HD), 1) // HD == part


def mask_tail(scores, fill):
    start = LENGTH // 8 * 8
    row = lax.broadcasted_iota(jnp.int32, (PACKED - start, PACKED), 0)
    tail = jnp.where(row < LENGTH - start, scores[start:], fill)
    return jnp.concatenate([scores[:start], tail], axis=0)


def flip(array):
    return array.astype(f32).T.astype(bf16)


def attend_body(q_ref, k_ref, v_ref, o_ref, l_ref):
    query, key = q_ref[...] * jnp.asarray(HD**-0.5, bf16), k_ref[...]
    value_t = flip(v_ref[...])
    mixed, logs = [], []
    for part in range(2):
        scores = contract_cols(jnp.where(of_head(part), key, 0), query)
        scores = mask_tail(scores, NEGATIVE)
        top = jnp.max(scores, axis=0, keepdims=True)
        exponent = jnp.exp(scores - top)
        total = jnp.sum(exponent, axis=0, keepdims=True)
        out = dot_float(value_t[HD * part : HD * (part + 1)], exponent.astype(bf16))
        mixed.append(out * (1.0 / total))
        logs.append(top + jnp.log(total))
    o_ref[...] = jnp.concatenate(mixed, axis=0).T.astype(bf16)
    l_ref[...] = jnp.concatenate(logs + [jnp.zeros((6, PACKED), f32)], axis=0)


PAIR = (PACKED, 2 * HD)
PAIRS = H // 2


def pair_spec(shift=0):
    return pl.BlockSpec(PAIR, lambda i: (0, i + shift))


LOG_SPEC = pl.BlockSpec((8, PACKED), lambda i: (i, 0))


def attend(qkv):
    return pl.pallas_call(
        attend_body,
        out_shape=[
            jax.ShapeDtypeStruct((PACKED, H * HD), bf16),
            jax.ShapeDtypeStruct((8 * PAIRS, PACKED), f32),
        ],
        grid=(PAIRS,),
        in_specs=[pair_spec(), pair_spec(PAIRS), pair_spec(2 * PAIRS)],
        out_specs=[pair_spec(), LOG_SPEC],
        compiler_params=room(),
        name="attend",
    )(qkv, qkv, qkv)


def attend_back_body(q_ref, k_ref, v_ref, o_ref, l_ref, g_ref, dq_ref, dk_ref, dv_ref):
    scale = jnp.asarray(HD**-0.5, bf16)
    query, key, value, grad = q_ref[...] * scale, k_ref[...], v_ref[...], g_ref[...]
    product = (grad.astype(f32) * o_ref[...].astype(f32)).T
    key_t = flip(key)
    grad_query, grad_key, grad_value = [], [], []
    for part in range(2):
        mask = of_head(part)
        delta = jnp.sum(product[HD * part : HD * (part + 1)], axis=0, keepdims=True)
        scores = contract_cols(jnp.where(mask, key, 0), query)
        soft = mask_tail(jnp.exp(scores - l_ref[part : part + 1]), 0.0)
        grad_soft = contract_cols(jnp.where(mask, value, 0), grad)
        grad_scores = (soft * (grad_soft - delta)).astype(bf16)
        grad_value.append(dot_float(soft.astype(bf16), grad))
        grad_key.append(dot_float(grad_scores, query))
        grad_query.append(dot_float(key_t[HD * part : HD * (part + 1)], grad_scores))
    first = of_head(0)
    dq_ref[...] = (jnp.concatenate(grad_query, axis=0).T * HD**-0.5).astype(bf16)
    dk_ref[...] = jnp.where(first, grad_key[0], grad_key[1]).astype(bf16)
    dv_ref[...] = jnp.where(first, grad_value[0], grad_value[1]).astype(bf16)


def attend_back(qkv, mixed, logs, grad_mixed):
    return pl.pallas_call(
        attend_back_body,
        out_shape=[jax.ShapeDtypeStruct((PACKED, H * HD), bf16)] * 3,
        grid=(PAIRS,),
        in_specs=[pair_spec(), pair_spec(PAIRS), pair_spec(2 * PAIRS), pair_spec(), LOG_SPEC, pair_spec()],
        out_specs=[pair_spec()] * 3,
        compiler_params=room(),
        name="attend_back",
    )(qkv, qkv, qkv, mixed, logs, grad_mixed)


def rise_body(x_ref, w_ref, b_ref, active_ref, slope_ref):
    hidden = dot_float(x_ref[...], w_ref[...]) + b_ref[...]
    share = 0.5 * (1.0 + lax.erf(hidden * np.float32(np.sqrt(0.5))))
    active_ref[...] = (hidden * share).astype(bf16)
    bell = jnp.exp(hidden * hidden * -0.5) * np.float32(1.0 / np.sqrt(2.0 * np.pi))
    slope_ref[...] = share + hidden * bell


def rise(normed, weights, bias):
    width, ff = weights.shape
    step = 1024
    return pl.pallas_call(
        rise_body,
        out_shape=[jax.ShapeDtypeStruct((PACKED, ff), bf16), jax.ShapeDtypeStruct((PACKED, ff), f32)],
        grid=(ff // step,),
        in_specs=[
            pl.BlockSpec((PACKED, width), lambda i: (0, 0)),
            pl.BlockSpec((width, step), lambda i: (0, i)),
            pl.BlockSpec((1, step), lambda i: (0, i)),
        ],
        out_specs=[pl.BlockSpec((PACKED, step), lambda i: (0, i))] * 2,
        compiler_params=room(),
        name="rise",
    )(normed, weights, bias.reshape(1, ff))


def layer(ring, tokens, counts, w_qkv, bias_q, bias_v, w_out, bias_out, w_up, bias_up, w_down, bias_down, gain_one, shift_one, gain_two, shift_two, cotangent):
    images, slots, width = tokens.shape
    group = ring.sizes["sz"] * ring.sizes["sc"]
    twins = group // images
    rows = w_qkv.shape[0]
    wide = w_down.shape[0] // rows
    ff = w_up.shape[1]

    slot = lax.broadcasted_iota(jnp.int32, (images, slots, 1), 1)
    marked = jnp.where(slot < counts[:, :, None], tokens, jnp.asarray(ABSENT, bf16))

    def exchange(array):
        if twins > 1:
            array = jnp.repeat(array, twins, axis=0)
        return lax.all_to_all(array, ("sz", "sc"), 0, 0, tiled=True).reshape(group * slots, width)

    def exchange_back(array):
        array = lax.all_to_all(array.reshape(group, slots, width), ("sz", "sc"), 0, 0, tiled=True)
        return array[::twins] if twins > 1 else array

    small = [bias_q, bias_v, bias_out, bias_down, gain_one, shift_one, gain_two, shift_two]
    small = jnp.stack(small + list(bias_up.reshape(wide, rows)), axis=1)
    small = jnp.pad(small, ((0, 0), (0, SMALL - small.shape[1])))

    def arrays_of(sources):
        return [source[0] for source in sources]

    def with_arrays(sources, arrays):
        return [(array,) + source[1:] for array, source in zip(arrays, sources)]

    one = ring.along(jnp.concatenate([w_qkv, small], axis=1))
    two = jnp.concatenate([w_out, w_up], axis=1)
    one, two, marked = tie(one, two, marked)
    one = ring.across(one)
    two = ring.along(two)
    one, two, marked = tie(one, two, marked)
    image_slots = exchange(marked)
    one = ring.plane(one)
    one, two = tie(one, two)
    full_qkv, vectors = ring.assemble(ring.cores(one), [3 * width, SMALL])
    two = ring.across(two)
    image_slots, two, full_qkv, vectors, three = tie(image_slots, two, full_qkv, vectors, w_down)

    two = ring.plane(two)
    three = ring.along(three)
    vectors = vectors.astype(f32)
    bq, bv, bo, bd, g1, s1, g2, s2 = [vectors[:, k] for k in range(8)]
    bu = jnp.swapaxes(vectors[:, 8 : 8 + wide].reshape(ring.count, rows, wide), 1, 2).reshape(ff)
    here = (image_slots[:, :1].astype(f32) < 0.5 * ABSENT).reshape(group, slots)
    held = jnp.sum(here.astype(f32), axis=1)
    before = jnp.sum(jnp.where(np.tril(np.ones((group, group), bool), -1), held[None, :], 0.0), axis=1)
    rank = before[:, None] + lax.broadcasted_iota(jnp.int32, (group, slots), 1).astype(f32)
    rank = jnp.where(here, rank, -1.0).reshape(1, group * slots).astype(jnp.int32)
    packing = (rank == lax.broadcasted_iota(jnp.int32, (PACKED, group * slots), 0)).astype(bf16)
    tokens_f = dot_float(packing, image_slots)
    normed_f, norm_one_pull = jax.vjp(norm_rows, tokens_f, g1, s1)
    normed = normed_f.astype(bf16)
    qkv_bias = jnp.concatenate([bq, jnp.zeros((width,), f32), bv])
    qkv = (dot_float(normed, full_qkv) + qkv_bias).astype(bf16)
    two, three, qkv, cotangent = tie(two, three, qkv, cotangent)

    two = ring.cores(two)
    three = ring.across(three)
    cot_slots = exchange(cotangent)
    mixed, logs = attend(qkv)
    traded, three, mixed = tie(arrays_of(two), three, mixed)

    three = ring.plane(three)
    full_out, full_up = ring.assemble(with_arrays(two, traded), [width, ff])
    residual = tokens_f + dot_float(mixed, full_out) + bo
    normed_two_f, norm_two_pull = jax.vjp(norm_rows, residual, g2, s2)
    normed_two = normed_two_f.astype(bf16)
    active, slope = rise(normed_two, full_up, bu)
    three, active, cot_slots = tie(three, active, cot_slots)

    three = ring.cores(three)
    grad_low = dot_float(packing, cot_slots).astype(bf16)
    grad_y = grad_low.astype(f32)
    if twins > 1:
        share = (lax.axis_index(("sz", "sc")) % twins == 0).astype(f32)
    else:
        share = None

    def mine(array):
        return array if share is None else array * share

    grad_w_down = mine(contract_rows(active, grad_low)).astype(bf16)
    sum_down = ring.between([grad_w_down])
    (full_down,) = ring.assemble(three, [width])
    result = (residual + dot_float(active, full_down) + bd).astype(bf16)
    result = contract_rows(packing, result).astype(bf16)
    grad_bd = jnp.sum(grad_y, axis=0)
    grad_hidden = contract_cols(grad_low, full_down) * slope
    hidden_low = grad_hidden.astype(bf16)
    sum_down, hidden_low, result = tie(sum_down, hidden_low, result)

    result = exchange_back(result)
    sum_down = ring.inward(ring.halves(sum_down))
    grad_bu = jnp.sum(hidden_low.astype(f32), axis=0)
    grad_w_up = mine(contract_rows(normed_two, hidden_low)).astype(bf16)
    grad_residual, grad_g2, grad_s2 = norm_two_pull(contract_cols(hidden_low, full_up))
    grad_residual = grad_residual + grad_y
    residual_low = grad_residual.astype(bf16)
    sum_down, grad_w_up, residual_low = tie(sum_down, grad_w_up, residual_low)

    sum_down = ring.inward_more(sum_down)
    sum_up = ring.between([grad_w_up])
    grad_w_out = mine(contract_rows(mixed, residual_low)).astype(bf16)
    grad_bo = jnp.sum(residual_low.astype(f32), axis=0)
    grad_mixed = contract_cols(residual_low, full_out).astype(bf16)
    sum_out = ring.between([grad_w_out])
    sum_down, sum_up, sum_out, grad_mixed, result = tie(sum_down, sum_up, sum_out, grad_mixed, result)

    sum_up = ring.inward(ring.halves(sum_up))
    sum_down = ring.down(sum_down)
    grads = attend_back(qkv, mixed, logs, grad_mixed)
    sum_down, sum_up, grads = tie(sum_down, sum_up, grads)

    sum_up = ring.inward_more(sum_up)
    sum_out = ring.inward(ring.halves(sum_out))
    grad_joined = jnp.concatenate(grads, axis=1)
    grad_w_qkv = mine(contract_rows(normed, grad_joined)).astype(bf16)
    sum_qkv = ring.between([grad_w_qkv])
    joined_sum = jnp.sum(grad_joined.astype(f32), axis=0)
    grad_bq, grad_bv = joined_sum[:width], joined_sum[2 * width :]
    grad_tokens, grad_g1, grad_s1 = norm_one_pull(contract_cols(grad_joined, full_qkv))
    grad_tokens = (grad_tokens + grad_residual).astype(bf16)
    grad_tokens = contract_rows(packing, grad_tokens).astype(bf16)
    small = [grad_bq, grad_bv, grad_bo, grad_bd, grad_g1, grad_s1, grad_g2, grad_s2]
    grad_bu = jnp.swapaxes(grad_bu.reshape(ring.count, wide, rows), 1, 2).reshape(width, wide)
    small = jnp.concatenate([jnp.stack(small, axis=1), grad_bu], axis=1)
    small = mine(jnp.pad(small, ((0, 0), (0, SMALL - small.shape[1])))).astype(bf16)
    sum_small = ring.between([small])
    sum_qkv, sum_small, sum_up, sum_out, grad_tokens = tie(sum_qkv, sum_small, sum_up, sum_out, grad_tokens)

    sum_qkv = ring.inward(ring.halves(sum_qkv + sum_small))
    sum_up = ring.down(sum_up)
    sum_out = ring.inward_more(sum_out)
    grad_tokens = exchange_back(grad_tokens).astype(f32)
    sum_qkv, sum_out, sum_up = tie(sum_qkv, sum_out, sum_up)

    sum_out = ring.down(sum_out)
    sums = ring.down(ring.inward_more(sum_qkv))
    sum_qkv = sums[:, : 3 * width]
    vectors = sums[:, 3 * width :]
    sum_bq, sum_bv, sum_bo, sum_bd, sum_g1, sum_s1, sum_g2, sum_s2 = [vectors[:, k] for k in range(8)]
    sum_bu = jnp.swapaxes(vectors[:, 8 : 8 + wide], 0, 1).reshape(wide * rows)
    return (result, grad_tokens, sum_qkv, sum_bq, sum_bv, sum_out, sum_bo, sum_up, sum_bu, sum_down, sum_bd, sum_g1, sum_s1, sum_g2, sum_s2)


def solution(mesh):
    n_grp, n_seq = mesh.shape["grp"], mesh.shape["seq"]
    sizes = (n_grp // 2, 2, n_seq // 2, 2)
    fine = Mesh(mesh.devices.reshape(sizes), AXES)
    ring = Ring(sizes)
    grp, seq = AXES[:2], AXES[2:]
    by_token = P(grp, seq, None)
    rows, vec = P(AXES, None), P(AXES)
    in_specs = (by_token, P(grp, seq), rows, vec, vec, rows, vec, rows, vec, rows, vec, vec, vec, vec, vec, by_token)
    out_specs = (by_token, by_token, rows, vec, vec, rows, vec, rows, vec, rows, vec, vec, vec, vec, vec)

    def shards(*args):
        return layer(ring, *args)

    return jax.shard_map(shards, mesh=fine, in_specs=in_specs, out_specs=out_specs, check_vma=False)
```

time: 1440 us -> 621 us (0.43)
  Pallas kernels: 828 us -> 80.7 us
  local copies, waits for them, and re-layouts: 93.9 us -> 60.3 us
  matrix products: 117 us -> 91.5 us
  starting transfers between devices: 103 us -> 88.2 us
    pallas_call x5 -> x6, Pallas kernels: 828 us -> 80.7 us  [the longest x3 32.1 us: assemble(): pl.pallas_call(body, out_shape=[jax.ShapeDtypeStruct((total, cut, w), bf1...]
    another operation x15 -> x13, local copies, waits for them, and re-layouts: 29.2 us -> 0.33 us  [the longest x12 0.23 us: along(): jnp.stack([c[cut:] for c in columns])]
    ppermute x57 -> x66, waiting for transfers between devices: 196 us -> 212 us  [shifted(): lax.ppermute(array, axis, [(i, (i + step) % size) for i in range(size)])]
    dynamic_slice x4 -> x12, local copies, waits for them, and re-layouts: 16.9 us -> 31.9 us  [pick(): return lax.dynamic_index_in_dim(array, index, axis, keepdims=False)]
    dot_general x4, matrix products: 45 us -> 30.3 us  [contract_cols(): lax.dot_general(left, right, (((1,), (1,)), ((), ())), preferred_element_...]
    ppermute x57 -> x66, starting transfers between devices: 77.9 us -> 70 us  [shifted(): lax.ppermute(array, axis, [(i, (i + step) % size) for i in range(size)])]
  transfers between devices with their start and end apart: 61 -> 70, of which waited for: 27 -> 23; matrix products, arithmetic and copies ran while one was open for 9% -> 23% of each run, Pallas kernels for 33% -> 13%
where the time goes in v2:
time: 621 us; the launch traced here: 611 us
  waiting for transfers between devices  225 us (36%)
  matrix products  91.5 us (15%)
  starting transfers between devices  88.2 us (14%)
  Pallas kernels  80.7 us (13%)
  other arithmetic  63.3 us (10%)
  local copies, waits for them, and re-layouts  60.3 us (10%)
    ppermute x66, waiting for transfers between devices, shifted(): lax.ppermute(array, axis, [(i, (i + step) % size) for i in range(size)])  212 us
    ppermute x66, starting transfers between devices, shifted(): lax.ppermute(array, axis, [(i, (i + step) % size) for i in range(size)])  70 us
    dot_general x6, matrix products, contract_rows(): lax.dot_general(left, right, (((0,), (0,)), ((), ())), preferred_element_...  46.2 us
    pallas_call x3, Pallas kernels, assemble(): pl.pallas_call(body, out_shape=[jax.ShapeDtypeStruct((total, cut, w), bf1...  32.1 us
    dynamic_slice x12, local copies, waits for them, and re-layouts, pick(): return lax.dynamic_index_in_dim(array, index, axis, keepdims=False)  31.9 us
    dot_general x4, matrix products, contract_cols(): lax.dot_general(left, right, (((1,), (1,)), ((), ())), preferred_element_...  30.3 us
    pallas_call x1, Pallas kernels, attend_back(): pl.pallas_call(attend_back_body, out_shape=[jax.ShapeDtypeStruct((PACKED,...  21.6 us
    dot_general x4, matrix products, dot_float(): return jnp.dot(left, right, preferred_element_type=f32)  15.1 us
  transfers between devices with their start and end apart: 70, of which 23 were waited for; matrix products, arithmetic and copies ran while one was open for 23% of the time, Pallas kernels for 13%

profile of v2, /device:TPU:0, one launch (start us, length us, event | category | flops | bytes accessed | tf_op | source)
XLA Modules:
  0.0 611.1 jit_solution(6702706780865577468)
XLA Ops:
  3.4 5.1 collective-permute-start.2
  14.1 11.8 %collective-permute-done.1 = bf16[32,3200]{1,0:T(8,128)(2,1)S(1)} collective-permute-done((bf16[32,3200]{1,0:T(8,128)(2,1)S(1)}, bf16[32,3200]{1,0:T(8,128)(2,1)S(1)}, u32[]{:S(2)}, u32[]{:S(2)}) %collective-permute-start.1) | collective-permute-done | bytes 204832 | tf_op jit(solution)/shard_map/ppermute | solution.py:45
  35.0 22.1 %collective-permute-done.6 = bf16[32,5120]{1,0:T(8,128)(2,1)S(1)} collective-permute-done((bf16[32,5120]{1,0:T(8,128)(2,1)S(1)}, bf16[32,5120]{1,0:T(8,128)(2,1)S(1)}, u32[]{:S(2)}, u32[]{:S(2)}) %collective-permute-start.6) | collective-permute-done | bytes 327712 | tf_op jit(solution)/shard_map/ppermute | solution.py:45
  66.6 17.5 %collective-permute-done.8 = bf16[2,4,16,3200]{3,2,1,0:T(8,128)(2,1)S(1)} collective-permute-done((bf16[2,4,16,3200]{3,2,1,0:T(8,128)(2,1)S(1)}, bf16[2,4,16,3200]{3,2,1,0:T(8,128)(2,1)S(1)}, u32[]{:S(2)}, u32[]{:S(2)}) %collective-permute-start.8) | collective-permute-done | bytes 819232 | tf_op jit(solution)/shard_map/ppermute | solution.py:45
  88.3 13.2 %collective-permute-done.10 = bf16[4,16,5120]{2,1,0:T(8,128)(2,1)S(1)} collective-permute-done((bf16[4,16,5120]{2,1,0:T(8,128)(2,1)S(1)}, bf16[4,16,5120]{2,1,0:T(8,128)(2,1)S(1)}, u32[]{:S(2)}, u32[]{:S(2)}) %collective-permute-start.10) | collective-permute-done | bytes 655392 | tf_op jit(solution)/shard_map/ppermute | solution.py:45
  107.2 10.7 %assemble.3 = (bf16[64,16,3072]{2,1,0:T(8,128)(2,1)}, bf16[64,16,128]{2,1,0:T(8,128)(2,1)S(1)}) custom-call(s32[64]{0:T(128)S(1)} %stack.633.table_ref, bf16[8,16,3200]{2,1,0:T(8,128)(2,1)S(1)} %bitcast.367, bf16[8,16,3200]{2,1,0:T(8,128)(2,1)S(1)} %bitcast.369, bf16[8,16,3200]{2,1,0:T(8,128)(2,1)S(1)} %bitcast.370, bf16[8,16,3200]{2,1,0:T(8,128)(2,1)S(1)} %bitcast.371, ...), custom_call_target="tpu_custom_call" | custom-call | tf_op jit(solution)/shard_map/assemble/pallas_call | solution.py:134
  132.9 5.8 add_convert_fusion.2.q_ref.k_ref.v_ref
  140.0 7.6 %collective-permute-done.18 = bf16[128,1024]{1,0:T(8,128)(2,1)S(1)} collective-permute-done((bf16[128,1024]{1,0:T(8,128)(2,1)S(1)}, bf16[128,1024]{1,0:T(8,128)(2,1)S(1)}, u32[]{:S(2)}, u32[]{:S(2)}) %collective-permute-start.18) | collective-permute-done | bytes 262176 | tf_op jit(solution)/shard_map/ppermute | solution.py:45
  147.8 9.2 %collective-permute-done.16 = bf16[2,4,16,5120]{3,2,1,0:T(8,128)(2,1)} collective-permute-done((bf16[2,4,16,5120]{3,2,1,0:T(8,128)(2,1)S(1)}, bf16[2,4,16,5120]{3,2,1,0:T(8,128)(2,1)}, u32[]{:S(2)}, u32[]{:S(2)}) %collective-permute-start.16) | collective-permute-done | bytes 1310752 | tf_op jit(solution)/shard_map/ppermute | solution.py:45
  164.5 12.8 %collective-permute-done.25 = bf16[4,64,1024]{2,1,0:T(8,128)(2,1)S(1)} collective-permute-done((bf16[4,64,1024]{2,1,0:T(8,128)(2,1)S(1)}, bf16[4,64,1024]{2,1,0:T(8,128)(2,1)S(1)}, u32[]{:S(2)}, u32[]{:S(2)}) %collective-permute-start.25) | collective-permute-done | bytes 524320 | tf_op jit(solution)/shard_map/ppermute | solution.py:45
  179.1 14.0 %attend.1 = (bf16[592,1024]{1,0:T(8,128)(2,1)S(1)}, f32[64,592]{1,0:T(8,128)S(1)}) custom-call(bf16[592,3072]{1,0:T(8,128)(2,1)} %add_convert_fusion.2.q_ref.k_ref.v_ref, bf16[592,3072]{1,0:T(8,128)(2,1)} %add_convert_fusion.2.q_ref.k_ref.v_ref, bf16[592,3072]{1,0:T(8,128)(2,1)} %add_convert_fusion.2.q_ref.k_ref.v_ref), custom_call_target="tpu_custom_call" | custom-call | tf_op jit(solution)/shard_map/attend/pallas_call | solution.py:247
  198.8 11.2 %assemble.4 = (bf16[64,16,1024]{2,1,0:T(8,128)(2,1)}, bf16[64,16,4096]{2,1,0:T(8,128)(2,1)}) custom-call(s32[64]{0:T(128)S(1)} %stack.633.table_ref, bf16[8,16,5120]{2,1,0:T(8,128)(2,1)S(1)} %bitcast.365, bf16[8,16,5120]{2,1,0:T(8,128)(2,1)} %bitcast.129.refs_1_, bf16[8,16,5120]{2,1,0:T(8,128)(2,1)} %bitcast.130.refs_2_, ...), custom_call_target="tpu_custom_call" | custom-call | tf_op jit(solution)/shard_map/assemble/pallas_call | solution.py:134
  214.1 13.1 %rise.1 = (bf16[592,4096]{1,0:T(8,128)(2,1)}, f32[592,4096]{1,0:T(8,128)}) custom-call(bf16[592,1024]{1,0:T(8,128)(2,1)S(1)} %add_convert_fusion.6.x_ref, bf16[1024,4096]{1,0:T(8,128)(2,1)} %bitcast.378, f32[1,4096]{1,0:T(1,128)S(1)} %reshape_reshape.3.b_ref), custom_call_target="tpu_custom_call" | custom-call | tf_op jit(solution)/shard_map/rise/pallas_call | solution.py:306
  231.4 9.4 %convolution_convert_fusion.1 = bf16[4096,1024]{1,0:T(8,128)(2,1)} fusion(bf16[592,4096]{1,0:T(8,128)(2,1)S(1)} %copy-done.48, bf16[592,1024]{1,0:T(8,128)(2,1)S(1)} %get-tuple-element.291), kind=kOutput, calls=%fused_computation.4 | convolution fusion | flops 4970250240 | bytes 14450688 | tf_op jit(solution)/shard_map/dot_general | solution.py:37
  240.9 7.0 %constant_dynamic-slice_fusion.6 = (bf16[2,2,4,1,128,1024]{5,4,3,2,1,0:T(8,128)(2,1)S(1)}, bf16[2,2,4,1,128,1024]{5,4,3,2,1,0:T(8,128)(2,1)}) fusion(bf16[2,2,4,2,128,1024]{5,4,3,2,1,0:T(8,128)(2,1)} %bitcast.383, s32[]{:T(128)S(6)} %select_n.1751, s32[]{:T(128)S(6)} %select_n.1750), kind=kLoop, calls=%fused_computation.209 | loop fusion | bytes 16777224 | tf_op jit(solution)/shard_map/jit(dynamic_index_in_dim)/dynamic_slice | solution.py:49
  250.6 4.8 copy.107
  255.5 10.1 %assemble.5 = bf16[64,64,1024]{2,1,0:T(8,128)(2,1)} custom-call(s32[64]{0:T(128)S(1)} %stack.633.table_ref, bf16[8,64,1024]{2,1,0:T(8,128)(2,1)S(1)} %bitcast.366, bf16[8,64,1024]{2,1,0:T(8,128)(2,1)S(1)} %bitcast.368, bf16[8,64,1024]{2,1,0:T(8,128)(2,1)} %bitcast.148.refs_2_, bf16[8,64,1024]{2,1,0:T(8,128)(2,1)} %bitcast.149.refs_3_, ...), custom_call_target="tpu_custom_call" | custom-call | tf_op jit(solution)/shard_map/assemble/pallas_call | solution.py:134
  265.6 11.9 %multiply_convert_fusion = bf16[592,4096]{1,0:T(8,128)(2,1)} fusion(f32[592,4096]{1,0:T(8,128)} %get-tuple-element.160, bf16[592,1024]{1,0:T(8,128)(2,1)S(1)} %copy-done.31, bf16[4096,1024]{1,0:T(8,128)(2,1)} %bitcast.376), kind=kOutput, calls=%fused_computation | convolution fusion | flops 4970905600 | bytes 24150016 | tf_op jit(solution)/shard_map/dot_general | solution.py:41
  277.5 13.1 %fusion.8 = bf16[832,1024]{1,0:T(8,128)(2,1)} fusion(s32[832]{0:T(1024)S(1)} %select_convert_fusion, f32[592,1024]{1,0:T(8,128)} %copy-done.4, bf16[592,4096]{1,0:T(8,128)(2,1)} %get-tuple-element.154, bf16[4096,1024]{1,0:T(8,128)(2,1)} %bitcast.377, f32[1024]{0:T(1024)S(1)} %bitcast.418), kind=kOutput, calls=%fused_computation.47 | convolution fusion | flops 5977949184 | bytes 17374464 | tf_op jit(solution)/shard_map/dot_general | solution.py:37
  290.6 10.2 %multiply_reduce_fusion.1 = (bf16[1024]{0:T(1024)(128)(2,1)S(1)}, f32[592]{0:T(1024)S(1)}, bf16[1024]{0:T(1024)(128)(2,1)S(1)}, f32[592,1024]{1,0:T(8,128)S(1)}) fusion(f32[592,1024]{1,0:T(8,128)} %copy-done.4, f32[592]{0:T(1024)S(1)} %fusion.54, f32[592]{0:T(1024)S(1)} %broadcast_multiply_fusion, f32[1024]{0:T(1024)S(1)} %bitcast.407, ...), kind=kOutput, calls=%fused_computation.20 | convolution fusion | flops 4970903040 | bytes 18103232 | tf_op jit(solution)/shard_map/dot_general | solution.py:41
  300.8 9.4 %convolution_convert_fusion = bf16[1024,4096]{1,0:T(8,128)(2,1)} fusion(bf16[592,1024]{1,0:T(8,128)(2,1)S(1)} %add_convert_fusion.6.x_ref, bf16[592,4096]{1,0:T(8,128)(2,1)S(1)} %copy-done.18), kind=kOutput, calls=%fused_computation.3 | convolution fusion | flops 4970250240 | bytes 14450688 | tf_op jit(solution)/shard_map/dot_general | solution.py:37
  320.3 20.6 %collective-permute-done.34 = bf16[2,4,64,1024]{3,2,1,0:T(8,128)(2,1)S(1)} collective-permute-done((bf16[2,4,64,1024]{3,2,1,0:T(8,128)(2,1)S(1)}, bf16[2,4,64,1024]{3,2,1,0:T(8,128)(2,1)S(1)}, u32[]{:S(2)}, u32[]{:S(2)}) %collective-permute-start.34) | collective-permute-done | bytes 1048608 | tf_op jit(solution)/shard_map/ppermute | solution.py:45
  348.9 4.9 all-to-all-start.2
  381.7 12.8 %all-to-all-done.2 = bf16[8,104,1024]{2,1,0:T(8,128)(2,1)S(1)} async-done(((bf16[8,104,1024]{2,1,0:T(8,128)(2,1)}), bf16[8,104,1024]{2,1,0:T(8,128)(2,1)S(1)}, u32[]{:S(2)}, u32[]{:S(2)}) %all-to-all-start.2) | async-done | bytes 1703968 | tf_op jit(solution)/shard_map/all_to_all | solution.py:338
  409.1 21.6 %attend_back.1 = (bf16[592,1024]{1,0:T(8,128)(2,1)S(1)}, bf16[592,1024]{1,0:T(8,128)(2,1)S(1)}, bf16[592,1024]{1,0:T(8,128)(2,1)S(1)}) custom-call(bf16[592,3072]{1,0:T(8,128)(2,1)} %add_convert_fusion.2.q_ref.k_ref.v_ref, bf16[592,3072]{1,0:T(8,128)(2,1)} %add_convert_fusion.2.q_ref.k_ref.v_ref, bf16[592,3072]{1,0:T(8,128)(2,1)} %add_convert_fusion.2.q_ref.k_ref.v_ref, ...), custom_call_target="tpu_custom_call" | custom-call | tf_op jit(solution)/shard_map/attend_back/pallas_call | solution.py:284
  441.1 19.2 %collective-permute-done.44 = bf16[2,4,16,4096]{3,2,1,0:T(8,128)(2,1)S(1)} collective-permute-done((bf16[2,4,16,4096]{3,2,1,0:T(8,128)(2,1)S(1)}, bf16[2,4,16,4096]{3,2,1,0:T(8,128)(2,1)S(1)}, u32[]{:S(2)}, u32[]{:S(2)}) %collective-permute-start.44) | collective-permute-done | bytes 1048608 | tf_op jit(solution)/shard_map/ppermute | solution.py:45
  464.6 5.7 multiply_reduce_fusion
  473.1 7.9 %convolution_convert_fusion.2 = bf16[1024,3072]{1,0:T(8,128)(2,1)S(1)} fusion(bf16[592,3072]{1,0:T(8,128)(2,1)} %copy-done.17, f32[592,1024]{1,0:T(8,128)S(1)} %copy-done.10, f32[1024]{0:T(1024)S(1)} %bitcast.417, f32[1024]{0:T(1024)S(1)} %bitcast.411, f32[592]{0:T(1024)S(1)} %fusion.53, f32[592]{0:T(1024)S(1)} %broadcast_multiply_fusion.1), kind=kOutput, calls=%fused_computation.7 | convolution fusion | flops 3730718720 | bytes 12366464 | tf_op jit(solution)/shard_map/dot_general | solution.py:37
  520.7 25.8 %collective-permute-done.55 = bf16[32,4096]{1,0:T(8,128)(2,1)S(1)} collective-permute-done((bf16[32,4096]{1,0:T(8,128)(2,1)S(1)}, bf16[32,4096]{1,0:T(8,128)(2,1)S(1)}, u32[]{:S(2)}, u32[]{:S(2)}) %collective-permute-start.55) | collective-permute-done | bytes 262176 | tf_op jit(solution)/shard_map/ppermute | solution.py:45
  548.0 23.0 %collective-permute-done.56 = bf16[32,4096]{1,0:T(8,128)(2,1)S(1)} collective-permute-done((bf16[32,4096]{1,0:T(8,128)(2,1)S(1)}, bf16[32,4096]{1,0:T(8,128)(2,1)S(1)}, u32[]{:S(2)}, u32[]{:S(2)}) %collective-permute-start.56) | collective-permute-done | bytes 262176 | tf_op jit(solution)/shard_map/ppermute | solution.py:45
  578.9 8.0 %collective-permute-done.59 = bf16[4,16,3200]{2,1,0:T(8,128)(2,1)S(1)} collective-permute-done((bf16[4,16,3200]{2,1,0:T(8,128)(2,1)S(1)}, bf16[4,16,3200]{2,1,0:T(8,128)(2,1)S(1)}, u32[]{:S(2)}, u32[]{:S(2)}) %collective-permute-start.59) | collective-permute-done | bytes 409632 | tf_op jit(solution)/shard_map/ppermute | solution.py:45
  597.7 5.8 collective-permute-done.61
  (402 shorter events, 223.4 us)
Async XLA Ops:
  26.3 30.7 %collective-permute-start.6 = (bf16[32,5120]{1,0:T(8,128)(2,1)S(1)}, bf16[32,5120]{1,0:T(8,128)(2,1)S(1)}, u32[]{:S(2)}, u32[]{:S(2)}) collective-permute-start(bf16[32,5120]{1,0:T(8,128)(2,1)S(1)} %pad_maximum_fusion.12), channel_id=1, source_target_pairs={{0,4},{2,6},{4,0},{6,2},{1,5},{3,7},{5,1},{7,3},{8,12},{10,14},{12... | collective-permute-start | bytes 983048 | tf_op jit(solution)/shard_map/ppermute | solution.py:45
  29.0 28.1 %collective-permute-start.5 = (bf16[32,5120]{1,0:T(8,128)(2,1)S(1)}, bf16[32,5120]{1,0:T(8,128)(2,1)S(1)}, u32[]{:S(2)}, u32[]{:S(2)}) collective-permute-start(bf16[32,5120]{1,0:T(8,128)(2,1)S(1)} %pad_maximum_fusion.12), channel_id=1, source_target_pairs={{0,2},{2,4},{4,6},{6,0},{1,3},{3,5},{5,7},{7,1},{8,10},{10,12},{12... | collective-permute-start | bytes 983048 | tf_op jit(solution)/shard_map/ppermute | solution.py:45
  31.0 27.2 %collective-permute-start.3 = (bf16[4,16,3200]{2,1,0:T(8,128)(2,1)S(1)}, bf16[4,16,3200]{2,1,0:T(8,128)(2,1)S(1)}, u32[]{:S(2)}, u32[]{:S(2)}) collective-permute-start(bf16[4,16,3200]{2,1,0:T(8,128)(2,1)S(1)} %get-tuple-element.108), channel_id=1, source_target_pairs={{0,8},{8,0},{1,9},{9,1},{2,10},{10,2},{3,11},{11,3},{4,12},{12,4},... | collective-permute-start | bytes 1228808 | tf_op jit(solution)/shard_map/ppermute | solution.py:45
  32.5 25.8 %collective-permute-start.4 = (bf16[4,16,3200]{2,1,0:T(8,128)(2,1)S(1)}, bf16[4,16,3200]{2,1,0:T(8,128)(2,1)S(1)}, u32[]{:S(2)}, u32[]{:S(2)}) collective-permute-start(bf16[4,16,3200]{2,1,0:T(8,128)(2,1)S(1)} %get-tuple-element.109), channel_id=1, source_target_pairs={{0,16},{16,0},{1,17},{17,1},{2,18},{18,2},{3,19},{19,3},{4,20},{20... | collective-permute-start | bytes 1228808 | tf_op jit(solution)/shard_map/ppermute | solution.py:45
  59.3 58.7 %all-to-all-start = ((bf16[8,104,1024]{2,1,0:T(8,128)(2,1)}), bf16[8,104,1024]{2,1,0:T(8,128)(2,1)}, u32[]{:S(2)}, u32[]{:S(2)}) async-start(bf16[8,104,1024]{2,1,0:T(8,128)(2,1)} %broadcast_select_fusion), calls=%async_computation | async-start | bytes 3407872 | tf_op jit(solution)/shard_map/all_to_all | solution.py:335
  126.8 30.2 %collective-permute-start.16 = (bf16[2,4,16,5120]{3,2,1,0:T(8,128)(2,1)S(1)}, bf16[2,4,16,5120]{3,2,1,0:T(8,128)(2,1)}, u32[]{:S(2)}, u32[]{:S(2)}) collective-permute-start(bf16[2,4,16,5120]{3,2,1,0:T(8,128)(2,1)S(1)} %pad_maximum_fusion), channel_id=1, source_target_pairs={{0,16},{16,0},{1,17},{17,1},{2,18},{18,2},{3,19},{19,3},{4,20},{20... | collective-permute-start | bytes 3932168 | tf_op jit(solution)/shard_map/ppermute | solution.py:45
  127.3 30.1 %collective-permute-start.17 = (bf16[2,4,16,5120]{3,2,1,0:T(8,128)(2,1)}, bf16[2,4,16,5120]{3,2,1,0:T(8,128)(2,1)}, u32[]{:S(2)}, u32[]{:S(2)}) collective-permute-start(bf16[2,4,16,5120]{3,2,1,0:T(8,128)(2,1)} %pad_maximum_fusion.1), channel_id=1, source_target_pairs={{0,8},{8,0},{1,9},{9,1},{2,10},{10,2},{3,11},{11,3},{4,12},{12,4},... | collective-permute-start | bytes 3932168 | tf_op jit(solution)/shard_map/ppermute | solution.py:45
  157.4 69.9 %all-to-all-start.1 = ((bf16[8,104,1024]{2,1,0:T(8,128)(2,1)}), bf16[8,104,1024]{2,1,0:T(8,128)(2,1)}, u32[]{:S(2)}, u32[]{:S(2)}) async-start(bf16[8,104,1024]{2,1,0:T(8,128)(2,1)} %param.32), calls=%async_computation.1 | async-start | bytes 3407872 | tf_op jit(solution)/shard_map/all_to_all | solution.py:335
  161.9 34.8 %collective-permute-start.21 = (bf16[2,4,16,5120]{3,2,1,0:T(8,128)(2,1)S(1)}, bf16[2,4,16,5120]{3,2,1,0:T(8,128)(2,1)}, u32[]{:S(2)}, u32[]{:S(2)}) collective-permute-start(bf16[2,4,16,5120]{3,2,1,0:T(8,128)(2,1)S(1)} %pad_maximum_fusion), channel_id=1, source_target_pairs={{0,1},{1,0},{2,3},{3,2},{4,5},{5,4},{6,7},{7,6},{8,9},{9,8},{10,11... | collective-permute-start | bytes 3932168 | tf_op jit(solution)/shard_map/ppermute | solution.py:45
  162.4 34.3 %collective-permute-start.22 = (bf16[2,4,16,5120]{3,2,1,0:T(8,128)(2,1)}, bf16[2,4,16,5120]{3,2,1,0:T(8,128)(2,1)}, u32[]{:S(2)}, u32[]{:S(2)}) collective-permute-start(bf16[2,4,16,5120]{3,2,1,0:T(8,128)(2,1)} %collective-permute-done.16), channel_id=1, source_target_pairs={{0,1},{1,0},{2,3},{3,2},{4,5},{5,4},{6,7},{7,6},{8,9},{9,8},{10,11... | collective-permute-start | bytes 3932168 | tf_op jit(solution)/shard_map/ppermute | solution.py:45
  162.5 34.2 %collective-permute-start.23 = (bf16[2,4,16,5120]{3,2,1,0:T(8,128)(2,1)}, bf16[2,4,16,5120]{3,2,1,0:T(8,128)(2,1)}, u32[]{:S(2)}, u32[]{:S(2)}) collective-permute-start(bf16[2,4,16,5120]{3,2,1,0:T(8,128)(2,1)} %pad_maximum_fusion.1), channel_id=1, source_target_pairs={{0,1},{1,0},{2,3},{3,2},{4,5},{5,4},{6,7},{7,6},{8,9},{9,8},{10,11... | collective-permute-start | bytes 3932168 | tf_op jit(solution)/shard_map/ppermute | solution.py:45
  162.9 33.8 %collective-permute-start.24 = (bf16[2,4,16,5120]{3,2,1,0:T(8,128)(2,1)}, bf16[2,4,16,5120]{3,2,1,0:T(8,128)(2,1)}, u32[]{:S(2)}, u32[]{:S(2)}) collective-permute-start(bf16[2,4,16,5120]{3,2,1,0:T(8,128)(2,1)} %collective-permute-done.17), channel_id=1, source_target_pairs={{0,1},{1,0},{2,3},{3,2},{4,5},{5,4},{6,7},{7,6},{8,9},{9,8},{10,11... | collective-permute-start | bytes 3932168 | tf_op jit(solution)/shard_map/ppermute | solution.py:45
  196.8 30.5 %collective-permute-start.27 = (bf16[2,4,64,1024]{3,2,1,0:T(8,128)(2,1)S(1)}, bf16[2,4,64,1024]{3,2,1,0:T(8,128)(2,1)S(1)}, u32[]{:S(2)}, u32[]{:S(2)}) collective-permute-start(bf16[2,4,64,1024]{3,2,1,0:T(8,128)(2,1)S(1)} %pad_maximum_fusion.2), channel_id=1, source_target_pairs={{0,16},{16,0},{1,17},{17,1},{2,18},{18,2},{3,19},{19,3},{4,20},{20... | collective-permute-start | bytes 3145736 | tf_op jit(solution)/shard_map/ppermute | solution.py:45
  197.3 29.9 %collective-permute-start.28 = (bf16[2,4,64,1024]{3,2,1,0:T(8,128)(2,1)}, bf16[2,4,64,1024]{3,2,1,0:T(8,128)(2,1)}, u32[]{:S(2)}, u32[]{:S(2)}) collective-permute-start(bf16[2,4,64,1024]{3,2,1,0:T(8,128)(2,1)} %pad_maximum_fusion.3), channel_id=1, source_target_pairs={{0,8},{8,0},{1,9},{9,1},{2,10},{10,2},{3,11},{11,3},{4,12},{12,4},... | collective-permute-start | bytes 3145736 | tf_op jit(solution)/shard_map/ppermute | solution.py:45
  230.3 25.1 %collective-permute-start.30 = (bf16[2,4,64,1024]{3,2,1,0:T(8,128)(2,1)S(1)}, bf16[2,4,64,1024]{3,2,1,0:T(8,128)(2,1)}, u32[]{:S(2)}, u32[]{:S(2)}) collective-permute-start(bf16[2,4,64,1024]{3,2,1,0:T(8,128)(2,1)S(1)} %pad_maximum_fusion.2), channel_id=1, source_target_pairs={{0,1},{1,0},{2,3},{3,2},{4,5},{5,4},{6,7},{7,6},{8,9},{9,8},{10,11... | collective-permute-start | bytes 3145736 | tf_op jit(solution)/shard_map/ppermute | solution.py:45
  250.5 40.1 %collective-permute-start.29 = (bf16[2,2,4,128,1024]{4,3,2,0,1:T(8,128)(2,1)}, bf16[2,2,4,128,1024]{4,3,2,0,1:T(8,128)(2,1)}, u32[]{:S(2)}, u32[]{:S(2)}) collective-permute-start(bf16[2,2,4,128,1024]{4,3,2,0,1:T(8,128)(2,1)} %bitcast.359), channel_id=1, source_target_pairs={{0,1},{1,0},{2,3},{3,2},{4,5},{5,4},{6,7},{7,6},{8,9},{9,8},{10,11... | collective-permute-start | bytes 12582920 | tf_op jit(solution)/shard_map/ppermute | solution.py:45
  315.3 25.6 %collective-permute-start.34 = (bf16[2,4,64,1024]{3,2,1,0:T(8,128)(2,1)S(1)}, bf16[2,4,64,1024]{3,2,1,0:T(8,128)(2,1)S(1)}, u32[]{:S(2)}, u32[]{:S(2)}) collective-permute-start(bf16[2,4,64,1024]{3,2,1,0:T(8,128)(2,1)S(1)} %dynamic-slice_bitcast_fusion.3), channel_id=1, source_target_pairs={{0,16},{16,0},{1,17},{17,1},{2,18},{18,2},{3,19},{19,3},{4,20},{20... | collective-permute-start | bytes 3145736 | tf_op jit(solution)/shard_map/ppermute | solution.py:45
  317.0 25.4 %collective-permute-start.35 = (bf16[2,4,64,1024]{3,2,1,0:T(8,128)(2,1)S(1)}, bf16[2,4,64,1024]{3,2,1,0:T(8,128)(2,1)S(1)}, u32[]{:S(2)}, u32[]{:S(2)}) collective-permute-start(bf16[2,4,64,1024]{3,2,1,0:T(8,128)(2,1)S(1)} %dynamic-slice_bitcast_fusion.2), channel_id=1, source_target_pairs={{0,8},{8,0},{1,9},{9,1},{2,10},{10,2},{3,11},{11,3},{4,12},{12,4},... | collective-permute-start | bytes 3145736 | tf_op jit(solution)/shard_map/ppermute | solution.py:45
  348.9 45.5 %collective-permute-start.38 = (bf16[2,2,4,32,4096]{4,3,2,0,1:T(8,128)(2,1)}, bf16[2,2,4,32,4096]{4,3,2,0,1:T(8,128)(2,1)}, u32[]{:S(2)}, u32[]{:S(2)}) collective-permute-start(bf16[2,2,4,32,4096]{4,3,2,0,1:T(8,128)(2,1)} %bitcast.357), channel_id=1, source_target_pairs={{0,1},{1,0},{2,3},{3,2},{4,5},{5,4},{6,7},{7,6},{8,9},{9,8},{10,11... | collective-permute-start | bytes 12582920 | tf_op jit(solution)/shard_map/ppermute | solution.py:45
  348.9 45.5 %all-to-all-start.2 = ((bf16[8,104,1024]{2,1,0:T(8,128)(2,1)}), bf16[8,104,1024]{2,1,0:T(8,128)(2,1)S(1)}, u32[]{:S(2)}, u32[]{:S(2)}) async-start(bf16[8,104,1024]{2,1,0:T(8,128)(2,1)} %bitcast.392), calls=%async_computation.2 | async-start | bytes 3407872 | tf_op jit(solution)/shard_map/all_to_all | solution.py:338
  396.7 36.3 %collective-permute-start.40 = (bf16[128,1024]{1,0:T(8,128)(2,1)}, bf16[128,1024]{1,0:T(8,128)(2,1)}, u32[]{:S(2)}, u32[]{:S(2)}) collective-permute-start(bf16[128,1024]{1,0:T(8,128)(2,1)} %get-tuple-element.236), channel_id=1, source_target_pairs={{0,2},{2,4},{4,6},{6,0},{1,3},{3,5},{5,7},{7,1},{8,10},{10,12},{12... | collective-permute-start | bytes 786440 | tf_op jit(solution)/shard_map/ppermute | solution.py:45
  396.7 37.8 %collective-permute-start.42 = (bf16[128,1024]{1,0:T(8,128)(2,1)S(1)}, bf16[128,1024]{1,0:T(8,128)(2,1)}, u32[]{:S(2)}, u32[]{:S(2)}) collective-permute-start(bf16[128,1024]{1,0:T(8,128)(2,1)S(1)} %get-tuple-element.237), channel_id=1, source_target_pairs={{0,6},{2,0},{4,2},{6,4},{1,7},{3,1},{5,3},{7,5},{8,14},{10,8},{12,... | collective-permute-start | bytes 786440 | tf_op jit(solution)/shard_map/ppermute | solution.py:45
  400.7 33.8 %collective-permute-start.41 = (bf16[128,1024]{1,0:T(8,128)(2,1)S(1)}, bf16[128,1024]{1,0:T(8,128)(2,1)}, u32[]{:S(2)}, u32[]{:S(2)}) collective-permute-start(bf16[128,1024]{1,0:T(8,128)(2,1)S(1)} %get-tuple-element.238), channel_id=1, source_target_pairs={{0,4},{2,6},{4,0},{6,2},{1,5},{3,7},{5,1},{7,3},{8,12},{10,14},{12... | collective-permute-start | bytes 786440 | tf_op jit(solution)/shard_map/ppermute | solution.py:45
  402.6 28.1 %collective-permute-start.49 = (bf16[2,4,16,1024]{3,2,1,0:T(8,128)(2,1)S(1)}, bf16[2,4,16,1024]{3,2,1,0:T(8,128)(2,1)}, u32[]{:S(2)}, u32[]{:S(2)}) collective-permute-start(bf16[2,4,16,1024]{3,2,1,0:T(8,128)(2,1)S(1)} %dynamic-slice_bitcast_fusion.15), channel_id=1, source_target_pairs={{0,16},{16,0},{1,17},{17,1},{2,18},{18,2},{3,19},{19,3},{4,20},{20... | collective-permute-start | bytes 786440 | tf_op jit(solution)/shard_map/ppermute | solution.py:45
  408.3 32.5 %collective-permute-start.43 = (bf16[2,4,16,4096]{3,2,1,0:T(8,128)(2,1)S(1)}, bf16[2,4,16,4096]{3,2,1,0:T(8,128)(2,1)S(1)}, u32[]{:S(2)}, u32[]{:S(2)}) collective-permute-start(bf16[2,4,16,4096]{3,2,1,0:T(8,128)(2,1)S(1)} %dynamic-slice_bitcast_fusion.1), channel_id=1, source_target_pairs={{0,16},{16,0},{1,17},{17,1},{2,18},{18,2},{3,19},{19,3},{4,20},{20... | collective-permute-start | bytes 3145736 | tf_op jit(solution)/shard_map/ppermute | solution.py:45
  433.0 27.2 %collective-permute-start.44 = (bf16[2,4,16,4096]{3,2,1,0:T(8,128)(2,1)S(1)}, bf16[2,4,16,4096]{3,2,1,0:T(8,128)(2,1)S(1)}, u32[]{:S(2)}, u32[]{:S(2)}) collective-permute-start(bf16[2,4,16,4096]{3,2,1,0:T(8,128)(2,1)S(1)} %dynamic-slice_bitcast_fusion), channel_id=1, source_target_pairs={{0,8},{8,0},{1,9},{9,1},{2,10},{10,2},{3,11},{11,3},{4,12},{12,4},... | collective-permute-start | bytes 3145736 | tf_op jit(solution)/shard_map/ppermute | solution.py:45
  503.6 102.3 %all-to-all-start.3 = ((bf16[8,104,1024]{2,1,0:T(8,128)(2,1)}), bf16[8,104,1024]{2,1,0:T(8,128)(2,1)}, u32[]{:S(2)}, u32[]{:S(2)}) async-start(bf16[8,104,1024]{2,1,0:T(8,128)(2,1)} %bitcast.391), calls=%async_computation.3 | async-start | bytes 3407872 | tf_op jit(solution)/shard_map/all_to_all | solution.py:338
  513.8 32.7 %collective-permute-start.55 = (bf16[32,4096]{1,0:T(8,128)(2,1)S(1)}, bf16[32,4096]{1,0:T(8,128)(2,1)S(1)}, u32[]{:S(2)}, u32[]{:S(2)}) collective-permute-start(bf16[32,4096]{1,0:T(8,128)(2,1)S(1)} %get-tuple-element.231), channel_id=1, source_target_pairs={{0,2},{2,4},{4,6},{6,0},{1,3},{3,5},{5,7},{7,1},{8,10},{10,12},{12... | collective-permute-start | bytes 786440 | tf_op jit(solution)/shard_map/ppermute | solution.py:45
  515.7 32.3 %collective-permute-start.57 = (bf16[32,4096]{1,0:T(8,128)(2,1)S(1)}, bf16[32,4096]{1,0:T(8,128)(2,1)S(1)}, u32[]{:S(2)}, u32[]{:S(2)}) collective-permute-start(bf16[32,4096]{1,0:T(8,128)(2,1)S(1)} %get-tuple-element.232), channel_id=1, source_target_pairs={{0,6},{2,0},{4,2},{6,4},{1,7},{3,1},{5,3},{7,5},{8,14},{10,8},{12,... | collective-permute-start | bytes 786440 | tf_op jit(solution)/shard_map/ppermute | solution.py:45
  517.7 53.4 %collective-permute-start.56 = (bf16[32,4096]{1,0:T(8,128)(2,1)S(1)}, bf16[32,4096]{1,0:T(8,128)(2,1)S(1)}, u32[]{:S(2)}, u32[]{:S(2)}) collective-permute-start(bf16[32,4096]{1,0:T(8,128)(2,1)S(1)} %get-tuple-element.233), channel_id=1, source_target_pairs={{0,4},{2,6},{4,0},{6,2},{1,5},{3,7},{5,1},{7,3},{8,12},{10,14},{12... | collective-permute-start | bytes 786440 | tf_op jit(solution)/shard_map/ppermute | solution.py:45
  518.8 53.2 %collective-permute-start.52 = (bf16[2,4,16,3200]{3,2,1,0:T(8,128)(2,1)S(1)}, bf16[2,4,16,3200]{3,2,1,0:T(8,128)(2,1)S(1)}, u32[]{:S(2)}, u32[]{:S(2)}) collective-permute-start(bf16[2,4,16,3200]{3,2,1,0:T(8,128)(2,1)S(1)} %copy-done.37), channel_id=1, source_target_pairs={{0,8},{8,0},{1,9},{9,1},{2,10},{10,2},{3,11},{11,3},{4,12},{12,4},... | collective-permute-start | bytes 2457608 | tf_op jit(solution)/shard_map/ppermute | solution.py:45
  519.4 52.8 %collective-permute-start.51 = (bf16[2,4,16,3200]{3,2,1,0:T(8,128)(2,1)S(1)}, bf16[2,4,16,3200]{3,2,1,0:T(8,128)(2,1)S(1)}, u32[]{:S(2)}, u32[]{:S(2)}) collective-permute-start(bf16[2,4,16,3200]{3,2,1,0:T(8,128)(2,1)S(1)} %dynamic-slice_bitcast_fusion.4), channel_id=1, source_target_pairs={{0,16},{16,0},{1,17},{17,1},{2,18},{18,2},{3,19},{19,3},{4,20},{20... | collective-permute-start | bytes 2457608 | tf_op jit(solution)/shard_map/ppermute | solution.py:45
  (94 other events, 1045.1 us)

commit v3 on v2

v3 whole, which is shorter than its diff:
```python
import jax
import jax.numpy as jnp
import numpy as np
from jax import lax
from jax.experimental import pallas as pl
from jax.experimental.pallas import tpu as pltpu
from jax.sharding import Mesh
from jax.sharding import PartitionSpec as P

H = 16
HD = 64
LENGTH = 577
PACKED = 592
EPSILON = 1e-06
NEGATIVE = -1e30
ABSENT = 100.0
SMALL = 256
AXES = ("gy", "gx", "sz", "sc")
ORDERS = (("gx", "gy"), ("gy", "gx"))

bf16 = jnp.bfloat16
f32 = jnp.float32


def norm_rows(values, gain_vec, shift_vec):
    row_mean = jnp.mean(values, axis=-1, keepdims=True)
    centred = values - row_mean
    row_var = jnp.mean(centred * centred, axis=-1, keepdims=True)
    return centred * lax.rsqrt(row_var + EPSILON) * gain_vec + shift_vec


def dot_float(left, right):
    return jnp.dot(left, right, preferred_element_type=f32)


def contract_rows(left, right):
    return lax.dot_general(left, right, (((0,), (0,)), ((), ())), preferred_element_type=f32)


def contract_cols(left, right):
    return lax.dot_general(left, right, (((1,), (1,)), ((), ())), preferred_element_type=f32)


def room(mib=50):
    return pltpu.CompilerParams(vmem_limit_bytes=mib * 2**20)


HINT = 0.02


def cost(flops, bytes_accessed, transcendentals=0):
    return pl.CostEstimate(
        flops=int(HINT * flops), bytes_accessed=int(HINT * bytes_accessed), transcendentals=int(HINT * transcendentals)
    )


def shifted(array, axis, size, step):
    return lax.ppermute(array, axis, [(i, (i + step) % size) for i in range(size)])


def pick(array, index, axis):
    return lax.dynamic_index_in_dim(array, index, axis, keepdims=False)


class Ring:
    def __init__(self, sizes):
        self.sizes = dict(zip(AXES, sizes))
        self.count = int(np.prod(sizes))

    def place(self):
        return {axis: lax.axis_index(axis) for axis in AXES}

    def others(self, array, axis):
        size = self.sizes[axis]
        return [shifted(array, axis, size, step) for step in range(1, size)]

    def others_from(self, array, axis, steps):
        size = self.sizes[axis]
        return [shifted(array, axis, size, step) for step in steps]

    def along(self, shard, columns):
        cut = shard.shape[0] // 2
        size = self.sizes["sz"]
        columns = [shard] + [columns[k] for k in range(1, size)]
        here = lax.axis_index("sz")
        ordered = [lax.select_n((here - k) % size, *columns) if size > 2 else jnp.where(here == k, *columns) for k in range(size)]
        return [jnp.stack([c[:cut] for c in ordered]), jnp.stack([c[cut:] for c in ordered])]

    def spread(self, shard, steps):
        return {k: shifted(shard, "sz", self.sizes["sz"], k) for k in steps}

    def across(self, halves):
        return [jnp.stack([half] + self.others(half, order[0])) for half, order in zip(halves, ORDERS)]

    def plane(self, halves):
        return [self.others(half, order[1]) for half, order in zip(halves, ORDERS)]

    def to_core(self, groups):
        return [[shifted(group, "sc", 2, 1) for group in part] for part in groups]

    def sources(self, first, traded_first, second, traded_second):
        found = []
        for part in range(2):
            kinds = ([first[part]] + second[part], traded_first[part] + traded_second[part])
            for turn, groups in enumerate(kinds):
                found += [(group, part, turn, step) for step, group in enumerate(groups)]
        return found

    def assemble(self, sources, widths):
        place = self.place()
        sizes = self.sizes
        cut, width = sources[0][0].shape[-2:]
        depth = sizes["sz"]
        planes, kinds, parts, arrays, counts = [], [], [], [], []
        for group, part, turn, step in sources:
            order = ORDERS[part]
            arrays.append(group)
            counts.append(group.shape[0])
            for one in range(group.shape[0]):
                at = {order[1]: (place[order[1]] - step) % sizes[order[1]], order[0]: (place[order[0]] - one) % sizes[order[0]]}
                planes.append(at["gy"] * sizes["gx"] + at["gx"])
                kinds.append((place["sc"] - turn) % 2)
                parts.append(part)
        table = jnp.stack(planes + kinds).astype(jnp.int32)
        many = len(planes)
        starts = np.concatenate([[0], np.cumsum(widths)])

        def body(table_ref, *refs):
            ins = refs[: len(counts)]
            outs = refs[len(counts) : -3]
            held, came, left = refs[-3:]
            arrivals = []
            for ref, count in zip(ins, counts):
                for k in range(count):
                    n = len(arrivals)
                    arrivals.append(pltpu.make_async_copy(ref.at[k], held.at[n], came.at[n]))
            for copy in arrivals:
                copy.start()
            departures = []
            for n, copy in enumerate(arrivals):
                copy.wait()
                for i, out in enumerate(outs):
                    window = held.at[n, :, :, pl.ds(int(starts[i]), widths[i])]
                    target = out.at[table_ref[n], :, table_ref[many + n], parts[n]]
                    leave = pltpu.make_async_copy(window, target, left.at[n, i])
                    leave.start()
                    departures.append(leave)
            for copy in departures:
                copy.wait()

        planes_all = sizes["gy"] * sizes["gx"]
        outs = pl.pallas_call(
            body,
            out_shape=[jax.ShapeDtypeStruct((planes_all, depth, 2, 2, cut, w), bf16) for w in widths],
            grid_spec=pltpu.PrefetchScalarGridSpec(
                num_scalar_prefetch=1,
                grid=(1,),
                in_specs=[pl.BlockSpec(memory_space=pl.ANY)] * len(counts),
                out_specs=[pl.BlockSpec(memory_space=pl.ANY)] * len(widths),
                scratch_shapes=[
                    pltpu.VMEM((many, depth, cut, width), bf16),
                    pltpu.SemaphoreType.DMA((many,)),
                    pltpu.SemaphoreType.DMA((many, len(widths))),
                ],
            ),
            compiler_params=room(),
            cost_estimate=cost(0, 4 * self.count * 2 * cut * width),
            name="assemble",
        )(table, *arrays)
        return [out.reshape(self.count * 2 * cut, w) for out, w in zip(outs, widths)]

    def far(self, device):
        place = self.place()
        sizes = self.sizes
        index, out = device, {}
        for axis in AXES[::-1]:
            out[axis] = (index % sizes[axis] - place[axis]) % sizes[axis]
            index = index // sizes[axis]
        return ((out["sc"] * sizes["gy"] + out["gy"]) * sizes["gx"] + out["gx"]) * sizes["sz"] + out["sz"]

    def by_distance(self, array):
        tokens, width = array.shape
        block = width // self.count
        half = width // 2
        row = lax.broadcasted_iota(jnp.int32, (width, 1), 0)
        target = self.far(row // block) * block + row % block

        def body(x_ref, t_ref, o_ref):
            columns = lax.broadcasted_iota(jnp.int32, (width, half), 1) + half * pl.program_id(0)
            pick_columns = jnp.where(t_ref[...] == columns, 1.0, 0.0).astype(bf16)
            o_ref[0] = dot_float(x_ref[...], pick_columns).astype(bf16)

        return pl.pallas_call(
            body,
            out_shape=jax.ShapeDtypeStruct((2, tokens, half), bf16),
            grid=(2,),
            in_specs=[pl.BlockSpec((tokens, width), lambda i: (0, 0)), pl.BlockSpec((width, 1), lambda i: (0, 0))],
            out_specs=pl.BlockSpec((1, tokens, half), lambda i: (i, 0, 0)),
            compiler_params=room(),
            cost_estimate=cost(2 * tokens * width * width, 4 * tokens * width),
            name="by_distance",
        )(array, target)

    def blocks_for(self, array, twins):
        place = self.place()
        size = self.sizes["sz"]
        out = []
        for turn in range(2):
            found = [((place["sz"] + k) % size * 2 + (place["sc"] + turn) % 2) // twins for k in range(size)]
            out.append(jnp.stack([pick(array, image, 0) for image in found]))
        return out

    def paired(self, stay, came):
        return [jnp.stack([stay[k], came[k]]) for k in range(self.sizes["sz"])]

    def send(self, pieces, steps, sign=1):
        return {k: shifted(pieces[k], "sz", self.sizes["sz"], sign * k) for k in steps}

    def images_of(self, own, came, images, twins):
        place = self.place()
        size = self.sizes["sz"]
        both = jnp.stack([jnp.stack(own), came])
        both = both.reshape((2 * size,) + both.shape[2:])
        out = []
        for image in range(images):
            device = image * twins
            out.append(pick(both, (device % 2 - place["sc"]) % 2 * size + (device // 2 - place["sz"]) % size, 0))
        return jnp.stack(out)

    def swap(self, sent):
        return shifted(sent, "sc", 2, 1)

    def reshaped(self, out):
        sizes = self.sizes
        return out.reshape(sizes["gy"], sizes["gx"], sizes["sz"], out.shape[0] // (self.count // 2), out.shape[1])

    def kept(self, left, right, share, came):
        cut = left.shape[2] // (self.count // 2) // 2
        if cut % 16 == 0:
            return weight_grad(left, 0, right, share, came, self.sizes)
        return self.ready(self.reshaped(weight_grad(left, 0, right, share, came)))

    def toward(self, arrays, axis):
        size = self.sizes[axis]
        return [arrays[0]] + [shifted(arrays[k], axis, size, k) for k in range(1, size)]

    def ready(self, sums):
        cut = sums.shape[3] // 2
        upper = [sums[k, :, :, :cut] for k in range(self.sizes["gy"])]
        lower = [sums[:, k, :, cut:] for k in range(self.sizes["gx"])]
        return upper, lower

    def first(self, pair):
        return self.toward(pair[0], "gy"), self.toward(pair[1], "gx")

    def again(self, pair):
        return tuple(
            [total([t[k] for t in terms]).astype(bf16) for k in range(self.sizes[axis])]
            for terms, axis in zip(pair, ("gx", "gy"))
        )

    def second(self, pair):
        return self.toward(pair[0], "gx"), self.toward(pair[1], "gy")

    def last(self, pair):
        return [
            jnp.concatenate([total([t[k] for t in terms]) for terms in pair], axis=0).astype(bf16)
            for k in range(self.sizes["sz"])
        ]

    def third(self, parts):
        return self.toward(parts, "sz")


def weight_grad(left, kind, right, share, came=None, sizes=None):
    tokens, columns = right.shape
    rows = left.shape[2]
    tiled = rows > 512
    parts = 1
    if sizes is not None:
        ny, nx, nz = sizes["gy"], sizes["gx"], sizes["sz"]
        parts = ny * nx
        block = rows // (parts * nz)
        cut = block // 2
    if tiled:
        tall, broad = rows // (parts if sizes is not None else rows // 512), columns
        steps = rows // tall
        at = lambda i: (i, 0)
        left_at, right_at = (lambda i: (kind, 0, i)), (lambda i: (0, 0))
    else:
        tall, broad = rows, next(w for w in (1024, 768, 512, 128) if columns % w == 0)
        steps = columns // broad
        at = lambda i: (0, i)
        left_at, right_at = (lambda i: (kind, 0, 0)), (lambda i: (0, i))
    others = [] if came is None else [came.reshape(rows, columns)]
    if share is not None:
        others.append(share.reshape(1, 1))
    given = 2 + len(others)

    def body(*refs):
        outs = refs[given:]
        out = contract_rows(refs[0][0], refs[1][...])
        if share is not None:
            out = out * refs[given - 1][...]
        if came is not None:
            out = out + refs[2][...].astype(f32)
        if sizes is None:
            outs[0][...] = out.astype(bf16)
        elif tiled:
            i = pl.program_id(0)
            out = out.astype(bf16).reshape(nz, block, broad)
            for k in range(ny):

                @pl.when(i // nx == k)
                def _(k=k):
                    outs[k][0] = out[:, :cut]

            for k in range(nx):

                @pl.when(i % nx == k)
                def _(k=k):
                    outs[ny + k][0] = out[:, cut:]

        else:
            out = out.astype(bf16).reshape(ny, nx, nz, block, broad)
            for k in range(ny):
                outs[k][...] = out[k, :, :, :cut]
            for k in range(nx):
                outs[ny + k][...] = out[:, k, :, cut:]

    specs = [pl.BlockSpec((1, tokens, tall), left_at), pl.BlockSpec((tokens, broad), right_at)]
    if came is not None:
        specs.append(pl.BlockSpec((tall, broad), at))
    if share is not None:
        specs.append(pl.BlockSpec((1, 1), lambda i: (0, 0)))
    if sizes is None:
        shapes, out_specs = [(rows, columns)], [pl.BlockSpec((tall, broad), at)]
    else:
        shapes = [(nx, nz, cut, columns)] * ny + [(ny, nz, cut, columns)] * nx
        if tiled:
            out_specs = [
                pl.BlockSpec((1, nz, cut, broad), lambda i, k=k: (jnp.clip(i - k * nx, 0, nx - 1), 0, 0, 0)) for k in range(ny)
            ]
            out_specs += [pl.BlockSpec((1, nz, cut, broad), lambda i, k=k: (jnp.maximum(i - k, 0) // nx, 0, 0, 0)) for k in range(nx)]
        else:
            out_specs = [pl.BlockSpec(shape[:3] + (broad,), lambda i: (0, 0, 0, i)) for shape in shapes]
    outs = pl.pallas_call(
        body,
        out_shape=[jax.ShapeDtypeStruct(shape, bf16) for shape in shapes],
        grid=(steps,),
        in_specs=specs,
        out_specs=out_specs,
        compiler_params=room(),
        cost_estimate=cost(2 * tokens * rows * columns, 4 * rows * columns),
        name="weight_grad",
    )(left, right, *others)
    return outs[0] if sizes is None else (outs[:ny], outs[ny:])


def total(arrays):
    out = arrays[0].astype(f32)
    for array in arrays[1:]:
        out = out + array.astype(f32)
    return out


def tie(*values):
    return lax.optimization_barrier(values)


def of_head(part):
    return lax.broadcasted_iota(jnp.int32, (1, 2 * HD), 1) // HD == part


def mask_tail(scores, fill):
    start = LENGTH // 8 * 8
    row = lax.broadcasted_iota(jnp.int32, (PACKED - start, PACKED), 0)
    tail = jnp.where(row < LENGTH - start, scores[start:], fill)
    return jnp.concatenate([scores[:start], tail], axis=0)


def flip(array):
    return array.astype(f32).T.astype(bf16)


def attend_body(q_ref, k_ref, v_ref, o_ref, l_ref):
    query, key = q_ref[...] * jnp.asarray(HD**-0.5, bf16), k_ref[...]
    value_t = flip(v_ref[...])
    mixed, logs = [], []
    for part in range(2):
        scores = contract_cols(jnp.where(of_head(part), key, 0), query)
        scores = mask_tail(scores, NEGATIVE)
        top = jnp.max(scores, axis=0, keepdims=True)
        exponent = jnp.exp(scores - top)
        total = jnp.sum(exponent, axis=0, keepdims=True)
        out = dot_float(value_t[HD * part : HD * (part + 1)], exponent.astype(bf16))
        mixed.append(out * (1.0 / total))
        logs.append(top + jnp.log(total))
    o_ref[...] = jnp.concatenate(mixed, axis=0).T.astype(bf16)
    l_ref[...] = jnp.concatenate(logs + [jnp.zeros((6, PACKED), f32)], axis=0)


PAIR = (PACKED, 2 * HD)
PAIRS = H // 2
CUT = PAIRS // 2


def kind_spec(kind, base=0):
    return pl.BlockSpec(PAIR, lambda i: (0, (i + base) // CUT * 3 * CUT + (i + base) % CUT + kind * CUT))


def pair_spec(base=0):
    return pl.BlockSpec(PAIR, lambda i: (0, i + base))


def log_spec(base=0):
    return pl.BlockSpec((8, PACKED), lambda i: (i + base, 0))


def halved(array):
    return array.reshape(-1, 3, 2, H * HD // 2).swapaxes(1, 2).reshape(array.shape)


def whole(array):
    return array.reshape(-1, 2, 3, H * HD // 2).swapaxes(1, 2).reshape(array.shape)


def attend(qkv):
    return pl.pallas_call(
        attend_body,
        out_shape=[
            jax.ShapeDtypeStruct((PACKED, H * HD), bf16),
            jax.ShapeDtypeStruct((8 * PAIRS, PACKED), f32),
        ],
        grid=(PAIRS,),
        in_specs=[kind_spec(0), kind_spec(1), kind_spec(2)],
        out_specs=[pair_spec(), log_spec()],
        compiler_params=room(),
        cost_estimate=cost(12e9, 8 * qkv.size, PACKED * PACKED * H),
        name="attend",
    )(qkv, qkv, qkv)


def attend_back_body(q_ref, k_ref, v_ref, l_ref, g_ref, d_ref, s_ref):
    scale = jnp.asarray(HD**-0.5, bf16)
    query, key, value, grad = q_ref[...] * scale, k_ref[...], v_ref[...], g_ref[...]
    key_t = flip(key)
    grad_query, grad_key, grad_value = [], [], []
    for part in range(2):
        mask = of_head(part)
        scores = contract_cols(jnp.where(mask, key, 0), query)
        soft = mask_tail(jnp.exp(scores - l_ref[part : part + 1]), 0.0)
        grad_soft = contract_cols(jnp.where(mask, value, 0), grad)
        delta = jnp.sum(soft * grad_soft, axis=0, keepdims=True)
        grad_scores = (soft * (grad_soft - delta)).astype(bf16)
        grad_value.append(dot_float(soft.astype(bf16), grad))
        grad_key.append(dot_float(grad_scores, query))
        grad_query.append(dot_float(key_t[HD * part : HD * (part + 1)], grad_scores))
    first = of_head(0)
    grads = (
        jnp.concatenate(grad_query, axis=0).T * HD**-0.5,
        jnp.where(first, grad_key[0], grad_key[1]),
        jnp.where(first, grad_value[0], grad_value[1]),
    )
    for kind, array in enumerate(grads):
        start = pl.multiple_of((pl.program_id(0) + kind * CUT) * 2 * HD, 2 * HD)
        low = array.astype(bf16)
        d_ref[:, pl.ds(start, 2 * HD)] = low
        s_ref[:, pl.ds(start, 2 * HD)] = jnp.sum(low.astype(f32), axis=0, keepdims=True)


def attend_back(qkv, logs, grad_mixed, half):
    base = half * CUT
    shape = (PACKED, 3 * CUT * 2 * HD)
    return pl.pallas_call(
        attend_back_body,
        out_shape=[jax.ShapeDtypeStruct(shape, bf16), jax.ShapeDtypeStruct((1, shape[1]), f32)],
        grid=(CUT,),
        in_specs=[kind_spec(0, base), kind_spec(1, base), kind_spec(2, base), log_spec(base), pair_spec(base)],
        out_specs=[pl.BlockSpec(shape, lambda i: (0, 0)), pl.BlockSpec((1, shape[1]), lambda i: (0, 0))],
        compiler_params=room(),
        cost_estimate=cost(12e9, 8 * qkv.size, PACKED * PACKED * H // 2),
        name="attend_back",
    )(qkv, qkv, qkv, logs, grad_mixed)


def rise(normed, weights, bias, ranks):
    width, ff = weights.shape
    step = ff // 4
    count = ranks.shape[0]
    block = ff // count
    inside = step // block
    whole_tiles = block % 128 == 0

    def body(rank_ref, x_ref, w_ref, b_ref, active_ref, slope_ref, *rest):
        i = pl.program_id(0)
        hidden = dot_float(x_ref[...], w_ref[...]) + b_ref[...]
        share = 0.5 * (1.0 + lax.erf(hidden * np.float32(np.sqrt(0.5))))
        active = (hidden * share).astype(bf16)
        active_ref[...] = active
        bell = jnp.exp(hidden * hidden * -0.5) * np.float32(1.0 / np.sqrt(2.0 * np.pi))
        slope_ref[...] = share + hidden * bell
        if not whole_tiles:
            return
        far_ref, held, sems = rest
        held[i % 2] = active

        def copies(turn):
            out = []
            for k in range(inside):
                rank = rank_ref[turn * inside + k]
                start = pl.multiple_of(rank % (count // 2) * block, block)
                window = held.at[turn % 2, :, pl.ds(k * block, block)]
                out.append(pltpu.make_async_copy(window, far_ref.at[rank // (count // 2), :, pl.ds(start, block)], sems.at[turn % 2, k]))
            return out

        for copy in copies(i):
            copy.start()

        @pl.when(i > 0)
        def _():
            for copy in copies(i - 1):
                copy.wait()

        @pl.when(i == 3)
        def _():
            for copy in copies(i):
                copy.wait()

    shapes = [jax.ShapeDtypeStruct((PACKED, ff), bf16), jax.ShapeDtypeStruct((PACKED, ff), f32)]
    specs = [pl.BlockSpec((PACKED, step), lambda i, t: (0, i))] * 2
    scratch = []
    if whole_tiles:
        shapes.append(jax.ShapeDtypeStruct((2, PACKED, ff // 2), bf16))
        specs.append(pl.BlockSpec(memory_space=pl.ANY))
        scratch = [pltpu.VMEM((2, PACKED, step), bf16), pltpu.SemaphoreType.DMA((2, inside))]
    outs = pl.pallas_call(
        body,
        out_shape=shapes,
        grid_spec=pltpu.PrefetchScalarGridSpec(
            num_scalar_prefetch=1,
            grid=(4,),
            in_specs=[
                pl.BlockSpec((PACKED, width), lambda i, t: (0, 0)),
                pl.BlockSpec((width, step), lambda i, t: (0, i)),
                pl.BlockSpec((1, step), lambda i, t: (0, i)),
            ],
            out_specs=specs,
            scratch_shapes=scratch,
        ),
        compiler_params=room(),
        cost_estimate=cost(12e9, 30e6, PACKED * ff * 2),
        name="rise",
    )(ranks, normed, weights, bias.reshape(1, ff))
    return outs if whole_tiles else (outs[0], outs[1], None)


def fall_body(g_ref, w_ref, slope_ref, out_ref, sum_ref):
    grad = (contract_cols(g_ref[...], w_ref[...]) * slope_ref[...]).astype(bf16)
    out_ref[...] = grad
    sum_ref[...] = jnp.sum(grad.astype(f32), axis=0, keepdims=True)


def fall(grads, weights, slope):
    ff, width = weights.shape
    step = ff // 4
    return pl.pallas_call(
        fall_body,
        out_shape=[jax.ShapeDtypeStruct((PACKED, ff), bf16), jax.ShapeDtypeStruct((1, ff), f32)],
        grid=(4,),
        in_specs=[
            pl.BlockSpec((PACKED, width), lambda i: (0, 0)),
            pl.BlockSpec((step, width), lambda i: (i, 0)),
            pl.BlockSpec((PACKED, step), lambda i: (0, i)),
        ],
        out_specs=[pl.BlockSpec((PACKED, step), lambda i: (0, i)), pl.BlockSpec((1, step), lambda i: (0, i))],
        compiler_params=room(),
        cost_estimate=cost(10e9, 25e6),
        name="fall",
    )(grads, weights, slope)


def project_body(x_ref, w_ref, b_ref, out_ref):
    out_ref[...] = (dot_float(x_ref[...], w_ref[...]) + b_ref[...]).astype(bf16)


def project(left, weights, bias):
    width, columns = weights.shape
    step = columns // 3
    return pl.pallas_call(
        project_body,
        out_shape=jax.ShapeDtypeStruct((PACKED, columns), bf16),
        grid=(3,),
        in_specs=[
            pl.BlockSpec((PACKED, width), lambda i: (0, 0)),
            pl.BlockSpec((width, step), lambda i: (0, i)),
            pl.BlockSpec((1, step), lambda i: (0, i)),
        ],
        out_specs=pl.BlockSpec((PACKED, step), lambda i: (0, i)),
        compiler_params=room(),
        cost_estimate=cost(6e9, 12e6),
        name="project",
    )(left, weights, bias.reshape(1, columns))


def row(vector):
    return vector.reshape(1, -1)


def fixed(shape):
    return pl.BlockSpec(shape, lambda i: (0,) * len(shape))


def seed(weights, vectors, long):
    rows, width = weights.shape
    half = width // 6

    def body(w_ref, *refs):
        out_ref = refs[-1]
        for k in range(6):
            out_ref[:, k * half : (k + 1) * half] = w_ref[:, pl.ds((k % 3 * 2 + k // 3) * half, half)]
        out_ref[:, width:] = jnp.zeros((rows, SMALL), bf16)
        for k in range(len(vectors)):
            out_ref[k : k + 1, width : width + rows] = refs[k][...]
        out_ref[0:1, width + 128 : width + 128 + long.shape[0]] = refs[len(vectors)][...]

    return pl.pallas_call(
        body,
        out_shape=jax.ShapeDtypeStruct((rows, width + SMALL), bf16),
        cost_estimate=cost(0, 1e6),
        name="seed",
    )(weights, *[row(v) for v in vectors], row(long))


def pack_norm_body(p_ref, x_ref, g_ref, s_ref, t_ref, n_ref):
    tokens = dot_float(p_ref[...], x_ref[...])
    t_ref[...] = tokens
    n_ref[...] = norm_rows(tokens, g_ref[...], s_ref[...]).astype(bf16)


def pack_norm(packing, slots, gain, shift):
    count, width = slots.shape
    half = PACKED // 2
    by_row = pl.BlockSpec((half, width), lambda i: (i, 0))
    return pl.pallas_call(
        pack_norm_body,
        out_shape=[jax.ShapeDtypeStruct((PACKED, width), f32), jax.ShapeDtypeStruct((PACKED, width), bf16)],
        grid=(2,),
        in_specs=[pl.BlockSpec((half, count), lambda i: (i, 0)), fixed((count, width)), fixed((1, width)), fixed((1, width))],
        out_specs=[by_row, by_row],
        compiler_params=room(),
        cost_estimate=cost(1e9, 8e6),
        name="pack_norm",
    )(packing, slots, row(gain), row(shift))


def pack_body(p_ref, x_ref, o_ref, s_ref):
    low = dot_float(p_ref[...], x_ref[...]).astype(bf16)
    o_ref[...] = low
    s_ref[...] = jnp.sum(low.astype(f32), axis=0, keepdims=True)


def pack(packing, slots):
    count, width = slots.shape
    half = width // 2
    return pl.pallas_call(
        pack_body,
        out_shape=[jax.ShapeDtypeStruct((PACKED, width), bf16), jax.ShapeDtypeStruct((1, width), f32)],
        grid=(2,),
        in_specs=[fixed((PACKED, count)), pl.BlockSpec((count, half), lambda i: (0, i))],
        out_specs=[pl.BlockSpec((PACKED, half), lambda i: (0, i)), pl.BlockSpec((1, half), lambda i: (0, i))],
        compiler_params=room(),
        cost_estimate=cost(1e9, 4e6),
        name="pack",
    )(packing, slots)


def out_norm_body(m_ref, w_ref, t_ref, b_ref, g_ref, s_ref, r_ref, n_ref):
    residual = t_ref[...] + dot_float(m_ref[...], w_ref[...]) + b_ref[...]
    r_ref[...] = residual
    n_ref[...] = norm_rows(residual, g_ref[...], s_ref[...]).astype(bf16)


def out_norm(mixed, weights, tokens, bias, gain, shift):
    width = weights.shape[1]
    half = PACKED // 2
    by_row = pl.BlockSpec((half, width), lambda i: (i, 0))
    vec = fixed((1, width))
    return pl.pallas_call(
        out_norm_body,
        out_shape=[jax.ShapeDtypeStruct((PACKED, width), f32), jax.ShapeDtypeStruct((PACKED, width), bf16)],
        grid=(2,),
        in_specs=[by_row, fixed(weights.shape), by_row, vec, vec, vec],
        out_specs=[by_row, by_row],
        compiler_params=room(),
        cost_estimate=cost(2e9, 8e6),
        name="out_norm",
    )(mixed, weights, tokens, row(bias), row(gain), row(shift))


def land_body(a_ref, w_ref, r_ref, b_ref, p_ref, o_ref, sum_ref):
    i = pl.program_id(0)
    part = dot_float(a_ref[...], w_ref[...])

    @pl.when(i == 0)
    def _():
        sum_ref[...] = part + r_ref[...] + b_ref[...]

    @pl.when(i > 0)
    def _():
        sum_ref[...] += part

    @pl.when(i == pl.num_programs(0) - 1)
    def _():
        o_ref[...] = contract_rows(p_ref[...], sum_ref[...].astype(bf16)).astype(bf16)


def land(active, weights, residual, bias, packing):
    ff, width = weights.shape
    step = ff // 4
    count = packing.shape[1]
    return pl.pallas_call(
        land_body,
        out_shape=jax.ShapeDtypeStruct((count, width), bf16),
        grid=(4,),
        in_specs=[
            pl.BlockSpec((PACKED, step), lambda i: (0, i)),
            pl.BlockSpec((step, width), lambda i: (i, 0)),
            fixed((PACKED, width)),
            fixed((1, width)),
            fixed((PACKED, count)),
        ],
        out_specs=fixed((count, width)),
        scratch_shapes=[pltpu.VMEM((PACKED, width), f32)],
        compiler_params=room(),
        cost_estimate=cost(6e9, 14e6),
        name="land",
    )(active, weights, residual, row(bias), packing)


def back_norm(grads, weights, values, gain, added, packing=None):
    width = weights.shape[0]
    step = weights.shape[1] // (4 if len(grads) == 1 else len(grads))
    steps = weights.shape[1] // step
    count = len(grads)

    def body(*refs):
        g_refs, (w_ref, x_ref, gain_ref, add_ref), rest = refs[:count], refs[count : count + 4], refs[count + 4 :]
        sum_ref = rest[-1]
        i = pl.program_id(0)
        for k, g_ref in enumerate(g_refs):

            @pl.when((i == k) if count > 1 else (i >= 0))
            def _(g_ref=g_ref, k=k):
                part = contract_cols(g_ref[...], w_ref[...])

                @pl.when(i == 0)
                def _():
                    sum_ref[...] = part

                @pl.when(i > 0)
                def _():
                    sum_ref[...] += part

        @pl.when(i == steps - 1)
        def _():
            back = sum_ref[...]
            values = x_ref[...]
            centred = values - jnp.mean(values, axis=-1, keepdims=True)
            scale = lax.rsqrt(jnp.mean(centred * centred, axis=-1, keepdims=True) + EPSILON)
            normed = centred * scale
            scaled = back * gain_ref[...]
            inner = jnp.mean(scaled * normed, axis=-1, keepdims=True)
            out = (scaled - jnp.mean(scaled, axis=-1, keepdims=True) - normed * inner) * scale + add_ref[...].astype(f32)
            low = out.astype(bf16)
            if packing is None:
                out_ref, low_ref, sums_ref = rest[:3]
                out_ref[...] = out
                low_ref[...] = low
            else:
                p_ref, low_ref, sums_ref = rest[:3]
                low_ref[...] = contract_rows(p_ref[...], low).astype(bf16)
            sums = [jnp.sum(a, axis=0, keepdims=True) for a in (back * normed, back, low.astype(f32))]
            sums_ref[...] = jnp.concatenate(sums + [jnp.zeros((5, width), f32)], axis=0)

    full = fixed((PACKED, width))
    if packing is None:
        shapes = [jax.ShapeDtypeStruct((PACKED, width), f32), jax.ShapeDtypeStruct((PACKED, width), bf16)]
        out_specs, more_specs, more = [full, full], [], []
    else:
        shapes = [jax.ShapeDtypeStruct((packing.shape[1], width), bf16)]
        out_specs, more_specs, more = [fixed(shapes[0].shape)], [fixed(packing.shape)], [packing]
    g_spec = fixed((PACKED, step)) if count > 1 else pl.BlockSpec((PACKED, step), lambda i: (0, i))
    return pl.pallas_call(
        body,
        out_shape=shapes + [jax.ShapeDtypeStruct((8, width), f32)],
        grid=(steps,),
        in_specs=[g_spec] * count + [pl.BlockSpec((width, step), lambda i: (0, i)), full, fixed((1, width)), full] + more_specs,
        out_specs=out_specs + [fixed((8, width))],
        scratch_shapes=[pltpu.VMEM((PACKED, width), f32)],
        compiler_params=room(),
        cost_estimate=cost(6e9, 20e6),
        name="back_norm",
    )(*grads, weights, values, row(gain), added, *more)


def back_project_body(g_ref, w_ref, o_ref):
    o_ref[...] = contract_cols(g_ref[...], w_ref[...]).astype(bf16)


def back_project(grads, weights):
    rows, width = weights.shape
    half = rows // 2
    return pl.pallas_call(
        back_project_body,
        out_shape=jax.ShapeDtypeStruct((PACKED, rows), bf16),
        grid=(2,),
        in_specs=[fixed((PACKED, width)), pl.BlockSpec((half, width), lambda i: (i, 0))],
        out_specs=pl.BlockSpec((PACKED, half), lambda i: (0, i)),
        compiler_params=room(),
        cost_estimate=cost(2e9, 5e6),
        name="back_project",
    )(grads, weights)


def layer(ring, tokens, counts, w_qkv, bias_q, bias_v, w_out, bias_out, w_up, bias_up, w_down, bias_down, gain_one, shift_one, gain_two, shift_two, cotangent):
    images, slots, width = tokens.shape
    group = ring.sizes["sz"] * ring.sizes["sc"]
    twins = group // images
    rows = w_qkv.shape[0]
    wide = w_down.shape[0] // rows
    ff = w_up.shape[1]

    slot = lax.broadcasted_iota(jnp.int32, (images, slots, 1), 1)
    marked = jnp.where(slot < counts[:, :, None], tokens, jnp.asarray(ABSENT, bf16))

    def back_on_device(pieces, own):
        pieces = [own] + [pieces[k] for k in range(1, depth)]
        came = ring.swap(jnp.stack([piece[1] for piece in pieces]))
        return ring.images_of([piece[0] for piece in pieces], came, images, twins)

    def slots_of(array):
        return array.reshape(depth, 2, slots, width)

    depth = ring.sizes["sz"]
    outer = [k for k in range(1, depth) if k in (1, depth - 1)]
    inner = [k for k in range(1, depth) if k not in outer]
    everything = list(range(1, depth))

    small = [bias_q, bias_v, bias_out, bias_down, gain_one, shift_one, gain_two, shift_two]

    def arrays_of(sources):
        return [source[0] for source in sources]

    def with_arrays(sources, arrays):
        return [(array,) + source[1:] for array, source in zip(arrays, sources)]

    one = seed(w_qkv, small, bias_up)
    column = ring.spread(one, everything)
    one = ring.along(one, column)
    two = jnp.concatenate([w_out, w_up], axis=1)
    one, two = tie(one, two)

    one = ring.across(one)
    column = ring.spread(two, outer)
    stay, go = ring.blocks_for(marked, twins)
    came = ring.swap(go)
    one, two, column, stay, came = tie(one, two, column, stay, came)

    one_more = ring.plane(one)
    one_core = ring.to_core([[half] for half in one])
    column.update(ring.spread(two, inner))
    two = ring.along(two, column)
    pieces = ring.paired(stay, came)
    one, one_more, one_core, two, pieces = tie(one, one_more, one_core, two, pieces)

    one_more_core = ring.to_core(one_more)
    two = ring.across(two)
    rest = ring.send(pieces, outer[:1])
    one, one_more, one_core, one_more_core, two, pieces = tie(one, one_more, one_core, one_more_core, two, pieces)

    two_more = ring.plane(two)
    rest.update(ring.send(pieces, everything[1:]))
    full_qkv, vectors = ring.assemble(ring.sources(one, one_core, one_more, one_more_core), [3 * width, SMALL])
    two, two_more, rest, full_qkv, vectors, three = tie(two, two_more, rest, full_qkv, vectors, w_down)

    column = ring.spread(three, outer)
    two_core = ring.to_core([[half] for half in two])
    image_slots = jnp.concatenate([pieces[0]] + [rest[k] for k in everything]).reshape(group * slots, width)
    vectors = vectors.reshape(ring.count, rows, SMALL).astype(f32)
    bu = vectors[:, 0, 128 : 128 + wide * rows].reshape(ff)
    bq, bv, bo, bd, g1, s1, g2, s2 = [vectors[:, k, :rows].reshape(width) for k in range(8)]
    here = (image_slots[:, :1].astype(f32) < 0.5 * ABSENT).reshape(group, slots)
    held = jnp.sum(here.astype(f32), axis=1)
    before = jnp.sum(jnp.where(np.tril(np.ones((group, group), bool), -1), held[None, :], 0.0), axis=1)
    rank = before[:, None] + lax.broadcasted_iota(jnp.int32, (group, slots), 1).astype(f32)
    rank = jnp.where(here, rank, -1.0).reshape(1, group * slots).astype(jnp.int32)
    packing = (rank == lax.broadcasted_iota(jnp.int32, (PACKED, group * slots), 0)).astype(bf16)
    tokens_f, normed = pack_norm(packing, image_slots, g1, s1)
    qkv_bias = halved(jnp.concatenate([bq, jnp.zeros((width,), f32), bv]))
    qkv = project(normed, full_qkv, qkv_bias)
    two_core, column, three, qkv = tie(two_core, column, three, qkv)

    column.update(ring.spread(three, inner))
    two_more_core = ring.to_core(two_more)
    stay, go = ring.blocks_for(cotangent, twins)
    came = ring.swap(go)
    mixed, logs = attend(qkv)
    three = ring.along(three, column)
    two_more_core, three, mixed, stay, came = tie(two_more_core, three, mixed, stay, came)

    three = ring.across(three)
    cot_pieces = ring.paired(stay, came)
    cot_rest = ring.send(cot_pieces, outer)
    full_out, full_up = ring.assemble(ring.sources(two, two_core, two_more, two_more_core), [width, ff])
    residual, normed_two = out_norm(mixed, full_out, tokens_f, bo, g2, s2)
    three, normed_two, cot_pieces, cot_rest = tie(three, normed_two, cot_pieces, cot_rest)

    three_more = ring.plane(three)
    three_core = ring.to_core([[half] for half in three])
    cot_rest.update(ring.send(cot_pieces, inner))
    ranks = ring.far(lax.broadcasted_iota(jnp.int32, (ring.count,), 0))
    active, slope, active_far = rise(normed_two, full_up, bu, ranks)
    if active_far is None:
        active_far = ring.by_distance(active)
    mixed_far = ring.by_distance(mixed)
    normed_far = ring.by_distance(normed)
    three_more, three_core, active, active_far, cot_rest = tie(three_more, three_core, active, active_far, cot_rest)

    three_more_core = ring.to_core(three_more)
    share = (lax.axis_index(("sz", "sc")) % twins == 0).astype(f32) if twins > 1 else None
    cot_slots = jnp.concatenate([cot_pieces[0]] + [cot_rest[k] for k in everything]).reshape(group * slots, width)
    grad_low, grad_bd = pack(packing, cot_slots)
    sent = weight_grad(active_far, 1, grad_low, share)
    three_more_core, sent, grad_low = tie(three_more_core, sent, grad_low)

    d = ring.swap(sent)
    (full_down,) = ring.assemble(ring.sources(three, three_core, three_more, three_more_core), [width])
    two_far = ring.by_distance(normed_two)
    d, full_down, two_far = tie(d, full_down, two_far)

    d = ring.kept(active_far, grad_low, share, d)
    result = slots_of(land(active, full_down, residual, bd, packing))
    d, result = tie(d, result)

    d = ring.first(d)
    back = ring.send(result, outer, -1)
    hidden_low, grad_bu = fall(grad_low, full_down, slope)
    sent = weight_grad(two_far, 1, hidden_low, share)
    d, sent, back = tie(d, sent, back)

    d = ring.again(d)
    d, sent = tie(d, sent)

    d = ring.second(d)
    u = ring.swap(sent)
    back.update(ring.send(result, inner, -1))
    grad_residual, residual_low, sums_two = back_norm([hidden_low], full_up, residual, g2, grad_low)
    d, u, residual_low, back = tie(d, u, residual_low, back)

    d = ring.last(d)
    u = ring.kept(two_far, hidden_low, share, u)
    sent = weight_grad(mixed_far, 1, residual_low, share)
    d, u, sent, residual_low = tie(d, u, sent, residual_low)

    u = ring.first(u)
    sent_out = sent
    d = ring.third(d)
    grad_mixed = back_project(residual_low, full_out)
    first_half, first_sums = attend_back(qkv, logs, grad_mixed, 0)
    sent = weight_grad(normed_far, 1, first_half, share)
    u, sent_out, sent, d, grad_mixed = tie(u, sent_out, sent, d, grad_mixed)

    u = ring.again(u)
    u, sent, sent_out, grad_mixed, back = tie(u, sent, sent_out, grad_mixed, back)

    u = ring.second(u)
    q = ring.swap(sent)
    o = ring.swap(sent_out)
    second_half, second_sums = attend_back(qkv, logs, grad_mixed, 1)
    u, q, o, second_half, back = tie(u, q, o, second_half, back)

    u = ring.last(u)
    u, q, o, second_half, back = tie(u, q, o, second_half, back)

    u = ring.third(u)
    result = back_on_device(back, result[0])
    q = ring.reshaped(weight_grad(normed_far, 0, first_half, share, q))
    o = ring.reshaped(weight_grad(mixed_far, 0, residual_low, share, o))
    q = ring.ready(jnp.concatenate([q, o], axis=-1))
    sent = weight_grad(normed_far, 1, second_half, share)
    q, sent, result, u = tie(q, sent, result, u)

    q = ring.first(q)
    r = ring.swap(sent)
    grad_tokens, sums_one = back_norm([first_half, second_half], full_qkv, tokens_f, g1, grad_residual, packing)
    grad_tokens = slots_of(grad_tokens)
    q, r, grad_tokens, sums_one = tie(q, r, grad_tokens, sums_one)

    q = ring.again(q)
    q, r, grad_tokens, sums_one = tie(q, r, grad_tokens, sums_one)

    back = ring.send(grad_tokens, everything, -1)
    q = ring.second(q)
    joined_sum = whole(jnp.concatenate([first_sums[0], second_sums[0]]))
    grad_bq, grad_bv = joined_sum[:width], joined_sum[2 * width :]
    small = [grad_bq, grad_bv, sums_two[2], grad_bd, sums_one[0], sums_one[1], sums_two[0], sums_two[1]]
    small = [array.reshape(ring.count, rows) for array in small] + [grad_bu.reshape(ring.count, wide * rows)]
    small = jnp.concatenate(small, axis=1)
    small = (small if share is None else small * share).astype(bf16)
    near_first = (ranks[None, :] == lax.broadcasted_iota(jnp.int32, (ring.count, 1), 0)).astype(bf16)
    small = dot_float(near_first, small).astype(bf16)
    small = jnp.pad(small, ((0, 0), (0, rows * SMALL - small.shape[1]))).reshape(2, ring.count // 2 * rows, SMALL)
    r = ring.reshaped(weight_grad(normed_far, 0, second_half, share, r))
    result = jnp.where(slot < counts[:, :, None], result, jnp.asarray(0, bf16))
    q, r, small, result = tie(q, r, small, result)

    came = ring.swap(small[1])
    q = ring.last(q)
    came, q, r = tie(came, q, r)

    small = ring.reshaped(total([small[0], came]).astype(bf16))
    r = ring.first(ring.ready(jnp.concatenate([r, small], axis=-1)))
    (r,) = tie(r)
    r = ring.second(ring.again(r))
    r, q, back = tie(r, q, back)

    r = ring.last(r)
    q = ring.third([jnp.concatenate(pair, axis=-1) for pair in zip(q, r)])
    grad_tokens = back_on_device(back, grad_tokens[0]).astype(f32)

    sum_down, sum_up = total(d), total(u)
    q = total(q)
    first_end, second_start, small_start = 3 * width // 2, 5 * width // 2, 4 * width
    sum_out = q[:, first_end:second_start]
    sum_qkv = whole(jnp.concatenate([q[:, :first_end], q[:, second_start:small_start]], axis=1))
    small = q[:, small_start:].reshape(rows * SMALL)
    sum_bq, sum_bv, sum_bo, sum_bd, sum_g1, sum_s1, sum_g2, sum_s2 = [small[k * rows : (k + 1) * rows] for k in range(8)]
    sum_bu = small[8 * rows : (8 + wide) * rows]
    return (result, grad_tokens, sum_qkv, sum_bq, sum_bv, sum_out, sum_bo, sum_up, sum_bu, sum_down, sum_bd, sum_g1, sum_s1, sum_g2, sum_s2)


def solution(mesh):
    n_grp, n_seq = mesh.shape["grp"], mesh.shape["seq"]
    sizes = (n_grp // 2, 2, n_seq // 2, 2)
    fine = Mesh(mesh.devices.reshape(sizes), AXES)
    ring = Ring(sizes)
    grp, seq = AXES[:2], AXES[2:]
    by_token = P(grp, seq, None)
    rows, vec = P(AXES, None), P(AXES)
    in_specs = (by_token, P(grp, seq), rows, vec, vec, rows, vec, rows, vec, rows, vec, vec, vec, vec, vec, by_token)
    out_specs = (by_token, by_token, rows, vec, vec, rows, vec, rows, vec, rows, vec, vec, vec, vec, vec)

    def shards(*args):
        return layer(ring, *args)

    return jax.shard_map(shards, mesh=fine, in_specs=in_specs, out_specs=out_specs, check_vma=False)
```

time: 621 us -> 527 us (0.85)
  Pallas kernels: 80.7 us -> 201 us
  matrix products: 91.5 us -> 0.13 us
  waiting for transfers between devices: 225 us -> 147 us
  local copies, waits for them, and re-layouts: 60.3 us -> 24.7 us
  other arithmetic: 63.3 us -> 46.7 us
  starting transfers between devices: 88.2 us -> 94.5 us
    pallas_call x5 -> x29, Pallas kernels: 66.8 us -> 187 us  [the longest x10 48.1 us: weight_grad(): pl.pallas_call(body, out_shape=[jax.ShapeDtypeStruct(shape, bf16) for sha...]
    dot_general x10 -> x0, matrix products: 76.4 us -> none  [the longest x6 46.2 us: contract_rows(): lax.dot_general(left, right, (((0,), (0,)), ((), ())), preferred_element_...]
    ppermute x66 -> x80, waiting for transfers between devices: 212 us -> 147 us  [shifted(): lax.ppermute(array, axis, [(i, (i + step) % size) for i in range(size)])]
    dynamic_slice x12 -> x1, local copies, waits for them, and re-layouts: 31.9 us -> 1.35 us  [pick(): return lax.dynamic_index_in_dim(array, index, axis, keepdims=False)]
    ppermute x66 -> x80, starting transfers between devices: 70 us -> 94.5 us  [shifted(): lax.ppermute(array, axis, [(i, (i + step) % size) for i in range(size)])]
    all_to_all x4 -> x0, starting transfers between devices: 18.2 us -> none  [the longest x2 9.33 us: exchange_back(): lax.all_to_all(array.reshape(group, slots, width), ('sz', 'sc'), 0, 0, ti...]
    convert_element_type x24 -> x12, other arithmetic: 29.3 us -> 13.5 us  [the longest x8 10.9 us: again(): total([t[k] for t in terms]).astype(bf16)]
    dot_general x4 -> x1, matrix products: 15.1 us -> 0.13 us  [dot_float(): return jnp.dot(left, right, preferred_element_type=f32)]
  transfers between devices with their start and end apart: 70 -> 80, of which waited for: 23 -> 29; matrix products, arithmetic and copies ran while one was open for 23% -> 8% of each run, Pallas kernels for 13% -> 32%
where the time goes in v3:
time: 527 us; the launch traced here: 517 us
  Pallas kernels  201 us (38%)
  waiting for transfers between devices  147 us (28%)
  starting transfers between devices  94.5 us (18%)
  other arithmetic  46.7 us (9%)
  local copies, waits for them, and re-layouts  24.7 us (5%)
    ppermute x80, waiting for transfers between devices, shifted(): lax.ppermute(array, axis, [(i, (i + step) % size) for i in range(size)])  147 us
    ppermute x80, starting transfers between devices, shifted(): lax.ppermute(array, axis, [(i, (i + step) % size) for i in range(size)])  94.5 us
    pallas_call x10, Pallas kernels, weight_grad(): pl.pallas_call(body, out_shape=[jax.ShapeDtypeStruct(shape, bf16) for sha...  48.1 us
    pallas_call x2, Pallas kernels, back_norm(): pl.pallas_call(body, out_shape=shapes + [jax.ShapeDtypeStruct((8, width),...  25.6 us
    pallas_call x2, Pallas kernels, attend_back(): pl.pallas_call(attend_back_body, out_shape=[jax.ShapeDtypeStruct(shape, b...  24.3 us
    pallas_call x3, Pallas kernels, assemble(): pl.pallas_call(body, out_shape=[jax.ShapeDtypeStruct((planes_all, depth,...  22.9 us
    pallas_call x1, Pallas kernels, rise(): pl.pallas_call(body, out_shape=shapes, grid_spec=pltpu.PrefetchScalarGrid...  15.5 us
    pallas_call x1, Pallas kernels, attend(): pl.pallas_call(attend_body, out_shape=[jax.ShapeDtypeStruct((PACKED, H *...  14.1 us
  transfers between devices with their start and end apart: 80, of which 29 were waited for; matrix products, arithmetic and copies ran while one was open for 8% of the time, Pallas kernels for 32%

profile of v3, /device:TPU:0, one launch (start us, length us, event | category | flops | bytes accessed | tf_op | source)
XLA Modules:
  0.0 517.4 jit_solution(10791170947344748602)
XLA Ops:
  2.4 5.0 collective-permute-start.2
  13.4 12.3 %collective-permute-done.1 = bf16[32,3328]{1,0:T(8,128)(2,1)S(1)} collective-permute-done((bf16[32,3328]{1,0:T(8,128)(2,1)}, bf16[32,3328]{1,0:T(8,128)(2,1)S(1)}, u32[]{:S(2)}, u32[]{:S(2)}) %collective-permute-start.1) | collective-permute-done | bytes 213024 | tf_op jit(solution)/shard_map/ppermute | solution.py:58
  36.9 6.1 %collective-permute-done.4 = bf16[4,16,3328]{2,1,0:T(8,128)(2,1)S(1)} collective-permute-done((bf16[4,16,3328]{2,1,0:T(8,128)(2,1)S(1)}, bf16[4,16,3328]{2,1,0:T(8,128)(2,1)S(1)}, u32[]{:S(2)}, u32[]{:S(2)}) %collective-permute-start.4) | collective-permute-done | bytes 426016 | tf_op jit(solution)/shard_map/ppermute | solution.py:58
  43.1 5.6 %collective-permute-done.5 = bf16[32,5120]{1,0:T(8,128)(2,1)S(1)} collective-permute-done((bf16[32,5120]{1,0:T(8,128)(2,1)S(1)}, bf16[32,5120]{1,0:T(8,128)(2,1)S(1)}, u32[]{:S(2)}, u32[]{:S(2)}) %collective-permute-start.5) | collective-permute-done | bytes 327712 | tf_op jit(solution)/shard_map/ppermute | solution.py:58
  55.0 11.7 %collective-permute-done.12 = bf16[32,5120]{1,0:T(8,128)(2,1)S(1)} collective-permute-done((bf16[32,5120]{1,0:T(8,128)(2,1)S(1)}, bf16[32,5120]{1,0:T(8,128)(2,1)S(1)}, u32[]{:S(2)}, u32[]{:S(2)}) %collective-permute-start.12) | collective-permute-done | bytes 327712 | tf_op jit(solution)/shard_map/ppermute | solution.py:58
  73.8 13.9 %collective-permute-done.15 = bf16[4,16,5120]{2,1,0:T(8,128)(2,1)S(1)} collective-permute-done((bf16[4,16,5120]{2,1,0:T(8,128)(2,1)S(1)}, bf16[4,16,5120]{2,1,0:T(8,128)(2,1)S(1)}, u32[]{:S(2)}, u32[]{:S(2)}) %collective-permute-start.15) | collective-permute-done | bytes 655392 | tf_op jit(solution)/shard_map/ppermute | solution.py:58
  99.7 7.0 %assemble.3 = (bf16[4,4,2,2,16,3072]{5,4,3,2,1,0:T(8,128)(2,1)}, bf16[4,4,2,2,16,256]{5,4,3,2,1,0:T(8,128)(2,1)S(1)}) custom-call(s32[32]{0:T(128)S(1)} %stack.202.table_ref, bf16[2,4,16,3328]{3,2,1,0:T(8,128)(2,1)S(1)} %pad_maximum_fusion.8.refs_0_, bf16[2,4,16,3328]{3,2,1,0:T(8,128)(2,1)S(1)} %copy-done.26, ...), custom_call_target="tpu_custom_call" | custom-call | bytes 272629 | tf_op jit(solution)/shard_map/assemble/pallas_call | solution.py:152
  107.8 15.1 %collective-permute-done.20 = bf16[2,104,1024]{2,1,0:T(8,128)(2,1)} collective-permute-done((bf16[2,104,1024]{2,1,0:T(8,128)(2,1)}, bf16[2,104,1024]{2,1,0:T(8,128)(2,1)}, u32[]{:S(2)}, u32[]{:S(2)}) %collective-permute-start.20) | collective-permute-done | bytes 426016 | tf_op jit(solution)/shard_map/ppermute | solution.py:58
  123.0 7.3 %collective-permute-start.25 = (bf16[128,1024]{1,0:T(8,128)(2,1)}, bf16[128,1024]{1,0:T(8,128)(2,1)}, u32[]{:S(2)}, u32[]{:S(2)}) collective-permute-start(bf16[128,1024]{1,0:T(8,128)(2,1)} %param.26), channel_id=1, source_target_pairs={{0,6},{2,0},{4,2},{6,4},{1,7},{3,1},{5,3},{7,5},{8,14},{10,8},{12,... | collective-permute-start | bytes 786440 | tf_op jit(solution)/shard_map/ppermute | solution.py:58
  141.8 8.0 %project.1.q_ref.k_ref.v_ref = bf16[592,3072]{1,0:T(8,128)(2,1)} custom-call(bf16[592,1024]{1,0:T(8,128)(2,1)S(1)} %get-tuple-element.300.x_ref, bf16[1024,3072]{1,0:T(8,128)(2,1)} %bitcast.274, f32[1,3072]{1,0:T(1,128)S(1)} %reshape_reshape.3.b_ref), custom_call_target="tpu_custom_call" | custom-call | flops 120000000 | bytes 240000 | tf_op jit(solution)/shard_map/project/pallas_call | solution.py:590
  154.2 14.1 %attend.1 = (bf16[592,1024]{1,0:T(8,128)(2,1)S(1)}, f32[64,592]{1,0:T(8,128)S(1)}) custom-call(bf16[592,3072]{1,0:T(8,128)(2,1)} %project.1.q_ref.k_ref.v_ref, bf16[592,3072]{1,0:T(8,128)(2,1)} %project.1.q_ref.k_ref.v_ref, bf16[592,3072]{1,0:T(8,128)(2,1)} %project.1.q_ref.k_ref.v_ref), custom_call_target="tpu_custom_call" | custom-call | flops 240000000 | bytes 290979 | tf_op jit(solution)/shard_map/attend/pallas_call | solution.py:429
  178.7 9.3 %assemble.4 = (bf16[4,4,2,2,16,1024]{5,4,3,2,1,0:T(8,128)(2,1)}, bf16[4,4,2,2,16,4096]{5,4,3,2,1,0:T(8,128)(2,1)}) custom-call(s32[32]{0:T(128)S(1)} %stack.202.table_ref, bf16[2,4,16,5120]{3,2,1,0:T(8,128)(2,1)S(1)} %pad_maximum_fusion.4.refs_0_, bf16[2,4,16,5120]{3,2,1,0:T(8,128)(2,1)} %collective-permute-done.17.refs_1_, ...), custom_call_target="tpu_custom_call" | custom-call | bytes 419430 | tf_op jit(solution)/shard_map/assemble/pallas_call | solution.py:152
  188.0 5.2 out_norm.1
  200.5 15.5 %rise.1 = (bf16[592,4096]{1,0:T(8,128)(2,1)}, f32[592,4096]{1,0:T(8,128)}, bf16[2,592,2048]{2,1,0:T(8,128)(2,1)}) custom-call(s32[32]{0:T(128)S(1)} %fusion.99.rank_ref, bf16[592,1024]{1,0:T(8,128)(2,1)S(1)} %get-tuple-element.327.x_ref, bf16[1024,4096]{1,0:T(8,128)(2,1)} %bitcast.272, f32[1,4096]{1,0:T(1,128)S(1)} %slice_bitcast_fusion.36.b_ref), custom_call_target="tpu_custom_call" | custom-call | flops 240000000 | bytes 600000 | tf_op jit(solution)/shard_map/rise/pallas_call | solution.py:537
  225.5 7.1 %weight_grad.10 = bf16[2048,1024]{1,0:T(8,128)(2,1)} custom-call(bf16[2,592,2048]{2,1,0:T(8,128)(2,1)} %get-tuple-element.334.refs_0_, bf16[592,1024]{1,0:T(8,128)(2,1)S(1)} %get-tuple-element.342.refs_1_.g_ref.refs_4_), custom_call_target="tpu_custom_call" | custom-call | flops 49660560 | bytes 167772 | tf_op jit(solution)/shard_map/weight_grad/pallas_call | solution.py:347
  237.7 6.6 %assemble.5 = bf16[4,4,2,2,64,1024]{5,4,3,2,1,0:T(8,128)(2,1)} custom-call(s32[32]{0:T(128)S(1)} %stack.202.table_ref, bf16[2,4,64,1024]{3,2,1,0:T(8,128)(2,1)S(1)} %copy-done.18, bf16[2,4,64,1024]{3,2,1,0:T(8,128)(2,1)S(1)} %copy-done.24, bf16[2,4,64,1024]{3,2,1,0:T(8,128)(2,1)S(1)} %copy-done.22, bf16[2,4,64,1024]{3,2,1,0:T(8,128)(2,1)} %copy-done.53, ...), custom_call_target="tpu_custom_call" | custom-call | bytes 335544 | tf_op jit(solution)/shard_map/assemble/pallas_call | solution.py:152
  244.4 7.7 %weight_grad.11 = (bf16[2,4,64,1024]{3,2,1,0:T(8,128)(2,1)S(1)}, bf16[2,4,64,1024]{3,2,1,0:T(8,128)(2,1)S(1)}, bf16[2,4,64,1024]{3,2,1,0:T(8,128)(2,1)S(1)}, bf16[2,4,64,1024]{3,2,1,0:T(8,128)(2,1)}) custom-call(bf16[2,592,2048]{2,1,0:T(8,128)(2,1)} %get-tuple-element.334.refs_0_, bf16[592,1024]{1,0:T(8,128)(2,1)} %copy-done, ...), custom_call_target="tpu_custom_call" | custom-call | flops 49660560 | bytes 167772 | tf_op jit(solution)/shard_map/weight_grad/pallas_call | solution.py:347
  252.1 11.4 %land.1 = bf16[832,1024]{1,0:T(8,128)(2,1)S(1)} custom-call(bf16[592,4096]{1,0:T(8,128)(2,1)} %get-tuple-element.353.a_ref, bf16[4096,1024]{1,0:T(8,128)(2,1)} %bitcast.270, f32[592,1024]{1,0:T(8,128)} %get-tuple-element.355.r_ref.refs_2_, f32[1,1024]{1,0:T(1,128)S(1)} %reshape_reshape_squeeze.29.b_ref, bf16[592,832]{1,0:T(8,128)(2,1)S(1)} %fusion.p_ref.refs_6_), custom_call_target="tpu_custom_call" | custom-call | flops 120000000 | bytes 280000 | tf_op jit(solution)/shard_map/land/pallas_call | solution.py:722
  270.3 11.1 %fall.1 = (bf16[592,4096]{1,0:T(8,128)(2,1)}, f32[1,4096]{1,0:T(1,128)S(1)}) custom-call(bf16[592,1024]{1,0:T(8,128)(2,1)S(1)} %copy-done.1, bf16[4096,1024]{1,0:T(8,128)(2,1)} %bitcast.271, f32[592,4096]{1,0:T(8,128)} %get-tuple-element.361.slope_ref), custom_call_target="tpu_custom_call" | custom-call | flops 200000000 | bytes 500000 | tf_op jit(solution)/shard_map/fall/pallas_call | solution.py:567
  281.4 7.2 %weight_grad.12 = bf16[512,4096]{1,0:T(8,128)(2,1)} custom-call(bf16[2,592,512]{2,1,0:T(8,128)(2,1)S(1)} %by_distance.4.refs_0_, bf16[592,4096]{1,0:T(8,128)(2,1)} %get-tuple-element.362.refs_1_.refs_0_), custom_call_target="tpu_custom_call" | custom-call | flops 49660560 | bytes 167772 | tf_op jit(solution)/shard_map/weight_grad/pallas_call | solution.py:347
  299.2 13.7 %back_norm.2 = (f32[592,1024]{1,0:T(8,128)}, bf16[592,1024]{1,0:T(8,128)(2,1)S(1)}, f32[8,1024]{1,0:T(8,128)S(1)}) custom-call(bf16[592,4096]{1,0:T(8,128)(2,1)} %get-tuple-element.362.refs_1_.refs_0_, bf16[1024,4096]{1,0:T(8,128)(2,1)} %bitcast.273, f32[592,1024]{1,0:T(8,128)} %get-tuple-element.355.r_ref.refs_2_, ...), custom_call_target="tpu_custom_call" | custom-call | flops 120000000 | bytes 400000 | tf_op jit(solution)/shard_map/back_norm/pallas_call | solution.py:794
  312.9 5.0 collective-permute-done.49
  318.7 7.6 %weight_grad.13 = (bf16[2,4,16,4096]{3,2,1,0:T(8,128)(2,1)S(1)}, bf16[2,4,16,4096]{3,2,1,0:T(8,128)(2,1)S(1)}, bf16[2,4,16,4096]{3,2,1,0:T(8,128)(2,1)S(1)}, bf16[2,4,16,4096]{3,2,1,0:T(8,128)(2,1)}) custom-call(bf16[2,592,512]{2,1,0:T(8,128)(2,1)} %copy-done.7, bf16[592,4096]{1,0:T(8,128)(2,1)} %get-tuple-element.362.refs_1_.refs_0_, ...), custom_call_target="tpu_custom_call" | custom-call | flops 49660560 | bytes 167772 | tf_op jit(solution)/shard_map/weight_grad/pallas_call | solution.py:347
  340.9 12.2 %attend_back.2 = (bf16[592,1536]{1,0:T(8,128)(2,1)S(1)}, f32[1,1536]{1,0:T(1,128)S(1)}) custom-call(bf16[592,3072]{1,0:T(8,128)(2,1)} %project.1.q_ref.k_ref.v_ref, bf16[592,3072]{1,0:T(8,128)(2,1)} %project.1.q_ref.k_ref.v_ref, bf16[592,3072]{1,0:T(8,128)(2,1)} %project.1.q_ref.k_ref.v_ref, f32[64,592]{1,0:T(8,128)S(1)} %copy-done.30, ...), custom_call_target="tpu_custom_call" | custom-call | flops 240000000 | bytes 290979 | tf_op jit(solution)/shard_map/attend_back/pallas_call | solution.py:475
  364.6 12.2 %attend_back.3 = (bf16[592,1536]{1,0:T(8,128)(2,1)S(1)}, f32[1,1536]{1,0:T(1,128)S(1)}) custom-call(bf16[592,3072]{1,0:T(8,128)(2,1)} %project.1.q_ref.k_ref.v_ref, bf16[592,3072]{1,0:T(8,128)(2,1)} %project.1.q_ref.k_ref.v_ref, bf16[592,3072]{1,0:T(8,128)(2,1)} %project.1.q_ref.k_ref.v_ref, f32[64,592]{1,0:T(8,128)S(1)} %copy-done.31, ...), custom_call_target="tpu_custom_call" | custom-call | flops 240000000 | bytes 290979 | tf_op jit(solution)/shard_map/attend_back/pallas_call | solution.py:475
  399.6 7.6 %collective-permute-done.61 = bf16[32,4096]{1,0:T(8,128)(2,1)S(1)} collective-permute-done((bf16[32,4096]{1,0:T(8,128)(2,1)S(1)}, bf16[32,4096]{1,0:T(8,128)(2,1)S(1)}, u32[]{:S(2)}, u32[]{:S(2)}) %collective-permute-start.61) | collective-permute-done | bytes 262176 | tf_op jit(solution)/shard_map/ppermute | solution.py:58
  413.4 11.9 %back_norm.3 = (bf16[832,1024]{1,0:T(8,128)(2,1)S(1)}, f32[8,1024]{1,0:T(8,128)S(1)}) custom-call(bf16[592,1536]{1,0:T(8,128)(2,1)} %copy-done.2, bf16[592,1536]{1,0:T(8,128)(2,1)} %copy-done.3, bf16[1024,3072]{1,0:T(8,128)(2,1)} %bitcast.275, f32[592,1024]{1,0:T(8,128)} %get-tuple-element.321.t_ref.refs_3_, ...), custom_call_target="tpu_custom_call" | custom-call | flops 120000000 | bytes 400000 | tf_op jit(solution)/shard_map/back_norm/pallas_call | solution.py:794
  446.9 5.5 %collective-permute-start.75 = (bf16[2,104,1024]{2,1,0:T(8,128)(2,1)S(1)}, bf16[2,104,1024]{2,1,0:T(8,128)(2,1)S(1)}, u32[]{:S(2)}, u32[]{:S(2)}) collective-permute-start(bf16[2,104,1024]{2,1,0:T(8,128)(2,1)S(1)} %get-tuple-element.536), channel_id=1, source_target_pairs={{0,2},{2,4},{4,6},{6,0},{1,3},{3,5},{5,7},{7,1},{8,10},{10,12},{12... | collective-permute-start | bytes 1277960 | tf_op jit(solution)/shard_map/ppermute | solution.py:58
  464.3 17.5 %collective-permute-done.74 = bf16[2,104,1024]{2,1,0:T(8,128)(2,1)S(1)} collective-permute-done((bf16[2,104,1024]{2,1,0:T(8,128)(2,1)S(1)}, bf16[2,104,1024]{2,1,0:T(8,128)(2,1)S(1)}, u32[]{:S(2)}, u32[]{:S(2)}) %collective-permute-start.74) | collective-permute-done | bytes 426016 | tf_op jit(solution)/shard_map/ppermute | solution.py:58
  482.0 9.9 %collective-permute-start.77 = (bf16[32,4352]{1,0:T(8,128)(2,1)S(1)}, bf16[32,4352]{1,0:T(8,128)(2,1)S(1)}, u32[]{:S(2)}, u32[]{:S(2)}) collective-permute-start(bf16[32,4352]{1,0:T(8,128)(2,1)S(1)} %maximum_maximum_fusion), channel_id=1, source_target_pairs={{0,2},{2,4},{4,6},{6,0},{1,3},{3,5},{5,7},{7,1},{8,10},{10,12},{12... | collective-permute-start | bytes 835592 | tf_op jit(solution)/shard_map/ppermute | solution.py:58
  494.9 5.5 %collective-permute-done.77 = bf16[32,4352]{1,0:T(8,128)(2,1)S(1)} collective-permute-done((bf16[32,4352]{1,0:T(8,128)(2,1)S(1)}, bf16[32,4352]{1,0:T(8,128)(2,1)S(1)}, u32[]{:S(2)}, u32[]{:S(2)}) %collective-permute-start.77) | collective-permute-done | bytes 278560 | tf_op jit(solution)/shard_map/ppermute | solution.py:58
  500.3 10.6 %collective-permute-done.78 = bf16[32,4352]{1,0:T(8,128)(2,1)S(1)} collective-permute-done((bf16[32,4352]{1,0:T(8,128)(2,1)S(1)}, bf16[32,4352]{1,0:T(8,128)(2,1)S(1)}, u32[]{:S(2)}, u32[]{:S(2)}) %collective-permute-start.78) | collective-permute-done | bytes 278560 | tf_op jit(solution)/shard_map/ppermute | solution.py:58
  (519 shorter events, 208.2 us)
Async XLA Ops:
  48.7 21.4 %collective-permute-start.8 = (bf16[2,4,16,3328]{3,2,1,0:T(8,128)(2,1)S(1)}, bf16[2,4,16,3328]{3,2,1,0:T(8,128)(2,1)S(1)}, u32[]{:S(2)}, u32[]{:S(2)}) collective-permute-start(bf16[2,4,16,3328]{3,2,1,0:T(8,128)(2,1)S(1)} %pad_maximum_fusion.8.refs_0_), channel_id=1, source_target_pairs={{0,16},{16,0},{1,17},{17,1},{2,18},{18,2},{3,19},{19,3},{4,20},{20... | collective-permute-start | bytes 2555912 | tf_op jit(solution)/shard_map/ppermute | solution.py:58
  50.4 21.1 %collective-permute-start.9 = (bf16[2,4,16,3328]{3,2,1,0:T(8,128)(2,1)S(1)}, bf16[2,4,16,3328]{3,2,1,0:T(8,128)(2,1)S(1)}, u32[]{:S(2)}, u32[]{:S(2)}) collective-permute-start(bf16[2,4,16,3328]{3,2,1,0:T(8,128)(2,1)S(1)} %pad_maximum_fusion.9.refs_4_), channel_id=1, source_target_pairs={{0,8},{8,0},{1,9},{9,1},{2,10},{10,2},{3,11},{11,3},{4,12},{12,4},... | collective-permute-start | bytes 2555912 | tf_op jit(solution)/shard_map/ppermute | solution.py:58
  91.6 31.4 %collective-permute-start.17 = (bf16[2,4,16,5120]{3,2,1,0:T(8,128)(2,1)S(1)}, bf16[2,4,16,5120]{3,2,1,0:T(8,128)(2,1)}, u32[]{:S(2)}, u32[]{:S(2)}) collective-permute-start(bf16[2,4,16,5120]{3,2,1,0:T(8,128)(2,1)S(1)} %pad_maximum_fusion.4.refs_0_), channel_id=1, source_target_pairs={{0,16},{16,0},{1,17},{17,1},{2,18},{18,2},{3,19},{19,3},{4,20},{20... | collective-permute-start | bytes 3932168 | tf_op jit(solution)/shard_map/ppermute | solution.py:58
  92.1 30.9 %collective-permute-start.18 = (bf16[2,4,16,5120]{3,2,1,0:T(8,128)(2,1)}, bf16[2,4,16,5120]{3,2,1,0:T(8,128)(2,1)}, u32[]{:S(2)}, u32[]{:S(2)}) collective-permute-start(bf16[2,4,16,5120]{3,2,1,0:T(8,128)(2,1)} %pad_maximum_fusion.5.refs_4_), channel_id=1, source_target_pairs={{0,8},{8,0},{1,9},{9,1},{2,10},{10,2},{3,11},{11,3},{4,12},{12,4},... | collective-permute-start | bytes 3932168 | tf_op jit(solution)/shard_map/ppermute | solution.py:58
  92.9 30.0 %collective-permute-start.20 = (bf16[2,104,1024]{2,1,0:T(8,128)(2,1)}, bf16[2,104,1024]{2,1,0:T(8,128)(2,1)}, u32[]{:S(2)}, u32[]{:S(2)}) collective-permute-start(bf16[2,104,1024]{2,1,0:T(8,128)(2,1)} %pad_maximum_fusion.26), channel_id=1, source_target_pairs={{0,4},{2,6},{4,0},{6,2},{1,5},{3,7},{5,1},{7,3},{8,12},{10,14},{12... | collective-permute-start | bytes 1277960 | tf_op jit(solution)/shard_map/ppermute | solution.py:58
  93.4 29.6 %collective-permute-start.21 = (bf16[2,104,1024]{2,1,0:T(8,128)(2,1)}, bf16[2,104,1024]{2,1,0:T(8,128)(2,1)}, u32[]{:S(2)}, u32[]{:S(2)}) collective-permute-start(bf16[2,104,1024]{2,1,0:T(8,128)(2,1)} %pad_maximum_fusion.27), channel_id=1, source_target_pairs={{0,6},{2,0},{4,2},{6,4},{1,7},{3,1},{5,3},{7,5},{8,14},{10,8},{12,... | collective-permute-start | bytes 1277960 | tf_op jit(solution)/shard_map/ppermute | solution.py:58
  123.0 26.9 %collective-permute-start.25 = (bf16[128,1024]{1,0:T(8,128)(2,1)}, bf16[128,1024]{1,0:T(8,128)(2,1)}, u32[]{:S(2)}, u32[]{:S(2)}) collective-permute-start(bf16[128,1024]{1,0:T(8,128)(2,1)} %param.26), channel_id=1, source_target_pairs={{0,6},{2,0},{4,2},{6,4},{1,7},{3,1},{5,3},{7,5},{8,14},{10,8},{12,... | collective-permute-start | bytes 786440 | tf_op jit(solution)/shard_map/ppermute | solution.py:58
  170.5 22.7 %collective-permute-start.30 = (bf16[4,64,1024]{2,1,0:T(8,128)(2,1)S(1)}, bf16[4,64,1024]{2,1,0:T(8,128)(2,1)S(1)}, u32[]{:S(2)}, u32[]{:S(2)}) collective-permute-start(bf16[4,64,1024]{2,1,0:T(8,128)(2,1)S(1)} %pad_maximum_fusion.19), channel_id=1, source_target_pairs={{0,8},{8,0},{1,9},{9,1},{2,10},{10,2},{3,11},{11,3},{4,12},{12,4},... | collective-permute-start | bytes 1572872 | tf_op jit(solution)/shard_map/ppermute | solution.py:58
  171.7 21.6 %collective-permute-start.31 = (bf16[4,64,1024]{2,1,0:T(8,128)(2,1)S(1)}, bf16[4,64,1024]{2,1,0:T(8,128)(2,1)S(1)}, u32[]{:S(2)}, u32[]{:S(2)}) collective-permute-start(bf16[4,64,1024]{2,1,0:T(8,128)(2,1)S(1)} %pad_maximum_fusion.20), channel_id=1, source_target_pairs={{0,16},{16,0},{1,17},{17,1},{2,18},{18,2},{3,19},{19,3},{4,20},{20... | collective-permute-start | bytes 1572872 | tf_op jit(solution)/shard_map/ppermute | solution.py:58
  176.3 20.5 %collective-permute-start.33 = (bf16[2,104,1024]{2,1,0:T(8,128)(2,1)S(1)}, bf16[2,104,1024]{2,1,0:T(8,128)(2,1)S(1)}, u32[]{:S(2)}, u32[]{:S(2)}) collective-permute-start(bf16[2,104,1024]{2,1,0:T(8,128)(2,1)S(1)} %pad_maximum_fusion.31), channel_id=1, source_target_pairs={{0,6},{2,0},{4,2},{6,4},{1,7},{3,1},{5,3},{7,5},{8,14},{10,8},{12,... | collective-permute-start | bytes 1277960 | tf_op jit(solution)/shard_map/ppermute | solution.py:58
  196.8 23.5 %collective-permute-start.36 = (bf16[2,4,64,1024]{3,2,1,0:T(8,128)(2,1)S(1)}, bf16[2,4,64,1024]{3,2,1,0:T(8,128)(2,1)S(1)}, u32[]{:S(2)}, u32[]{:S(2)}) collective-permute-start(bf16[2,4,64,1024]{3,2,1,0:T(8,128)(2,1)S(1)} %pad_maximum_fusion.6.refs_0_), channel_id=1, source_target_pairs={{0,1},{1,0},{2,3},{3,2},{4,5},{5,4},{6,7},{7,6},{8,9},{9,8},{10,11... | collective-permute-start | bytes 3145736 | tf_op jit(solution)/shard_map/ppermute | solution.py:58
  196.8 25.6 %collective-permute-start.34 = (bf16[2,4,64,1024]{3,2,1,0:T(8,128)(2,1)S(1)}, bf16[2,4,64,1024]{3,2,1,0:T(8,128)(2,1)S(1)}, u32[]{:S(2)}, u32[]{:S(2)}) collective-permute-start(bf16[2,4,64,1024]{3,2,1,0:T(8,128)(2,1)S(1)} %pad_maximum_fusion.6.refs_0_), channel_id=1, source_target_pairs={{0,16},{16,0},{1,17},{17,1},{2,18},{18,2},{3,19},{19,3},{4,20},{20... | collective-permute-start | bytes 3145736 | tf_op jit(solution)/shard_map/ppermute | solution.py:58
  197.3 25.1 %collective-permute-start.37 = (bf16[2,4,64,1024]{3,2,1,0:T(8,128)(2,1)S(1)}, bf16[2,4,64,1024]{3,2,1,0:T(8,128)(2,1)S(1)}, u32[]{:S(2)}, u32[]{:S(2)}) collective-permute-start(bf16[2,4,64,1024]{3,2,1,0:T(8,128)(2,1)S(1)} %pad_maximum_fusion.7.refs_4_), channel_id=1, source_target_pairs={{0,1},{1,0},{2,3},{3,2},{4,5},{5,4},{6,7},{7,6},{8,9},{9,8},{10,11... | collective-permute-start | bytes 3145736 | tf_op jit(solution)/shard_map/ppermute | solution.py:58
  197.5 25.3 %collective-permute-start.35 = (bf16[2,4,64,1024]{3,2,1,0:T(8,128)(2,1)S(1)}, bf16[2,4,64,1024]{3,2,1,0:T(8,128)(2,1)S(1)}, u32[]{:S(2)}, u32[]{:S(2)}) collective-permute-start(bf16[2,4,64,1024]{3,2,1,0:T(8,128)(2,1)S(1)} %pad_maximum_fusion.7.refs_4_), channel_id=1, source_target_pairs={{0,8},{8,0},{1,9},{9,1},{2,10},{10,2},{3,11},{11,3},{4,12},{12,4},... | collective-permute-start | bytes 3145736 | tf_op jit(solution)/shard_map/ppermute | solution.py:58
  198.4 21.8 %collective-permute-start.38 = (bf16[2,104,1024]{2,1,0:T(8,128)(2,1)S(1)}, bf16[2,104,1024]{2,1,0:T(8,128)(2,1)S(1)}, u32[]{:S(2)}, u32[]{:S(2)}) collective-permute-start(bf16[2,104,1024]{2,1,0:T(8,128)(2,1)S(1)} %pad_maximum_fusion.30), channel_id=1, source_target_pairs={{0,4},{2,6},{4,0},{6,2},{1,5},{3,7},{5,1},{7,3},{8,12},{10,14},{12... | collective-permute-start | bytes 1277960 | tf_op jit(solution)/shard_map/ppermute | solution.py:58
  263.5 25.7 %collective-permute-start.42 = (bf16[2,4,64,1024]{3,2,1,0:T(8,128)(2,1)S(1)}, bf16[2,4,64,1024]{3,2,1,0:T(8,128)(2,1)}, u32[]{:S(2)}, u32[]{:S(2)}) collective-permute-start(bf16[2,4,64,1024]{3,2,1,0:T(8,128)(2,1)S(1)} %get-tuple-element.357), channel_id=1, source_target_pairs={{0,16},{16,0},{1,17},{17,1},{2,18},{18,2},{3,19},{19,3},{4,20},{20... | collective-permute-start | bytes 3145736 | tf_op jit(solution)/shard_map/ppermute | solution.py:58
  265.1 25.3 %collective-permute-start.43 = (bf16[2,4,64,1024]{3,2,1,0:T(8,128)(2,1)S(1)}, bf16[2,4,64,1024]{3,2,1,0:T(8,128)(2,1)}, u32[]{:S(2)}, u32[]{:S(2)}) collective-permute-start(bf16[2,4,64,1024]{3,2,1,0:T(8,128)(2,1)S(1)} %copy-done.88), channel_id=1, source_target_pairs={{0,8},{8,0},{1,9},{9,1},{2,10},{10,2},{3,11},{11,3},{4,12},{12,4},... | collective-permute-start | bytes 3145736 | tf_op jit(solution)/shard_map/ppermute | solution.py:58
  266.0 22.5 %collective-permute-start.45 = (bf16[2,104,1024]{2,1,0:T(8,128)(2,1)S(1)}, bf16[2,104,1024]{2,1,0:T(8,128)(2,1)S(1)}, u32[]{:S(2)}, u32[]{:S(2)}) collective-permute-start(bf16[2,104,1024]{2,1,0:T(8,128)(2,1)S(1)} %get-tuple-element.542), channel_id=1, source_target_pairs={{0,2},{2,4},{4,6},{6,0},{1,3},{3,5},{5,7},{7,1},{8,10},{10,12},{12... | collective-permute-start | bytes 1277960 | tf_op jit(solution)/shard_map/ppermute | solution.py:58
  267.3 21.3 %collective-permute-start.44 = (bf16[2,104,1024]{2,1,0:T(8,128)(2,1)S(1)}, bf16[2,104,1024]{2,1,0:T(8,128)(2,1)S(1)}, u32[]{:S(2)}, u32[]{:S(2)}) collective-permute-start(bf16[2,104,1024]{2,1,0:T(8,128)(2,1)S(1)} %get-tuple-element.543), channel_id=1, source_target_pairs={{0,6},{2,0},{4,2},{6,4},{1,7},{3,1},{5,3},{7,5},{8,14},{10,8},{12,... | collective-permute-start | bytes 1277960 | tf_op jit(solution)/shard_map/ppermute | solution.py:58
  294.7 23.2 %collective-permute-start.48 = (bf16[512,4096]{1,0:T(8,128)(2,1)S(1)}, bf16[512,4096]{1,0:T(8,128)(2,1)}, u32[]{:S(2)}, u32[]{:S(2)}) collective-permute-start(bf16[512,4096]{1,0:T(8,128)(2,1)S(1)} %copy-done.37), channel_id=1, source_target_pairs={{0,1},{1,0},{2,3},{3,2},{4,5},{5,4},{6,7},{7,6},{8,9},{9,8},{10,11... | collective-permute-start | bytes 12582920 | tf_op jit(solution)/shard_map/ppermute | solution.py:58
  294.8 23.1 %collective-permute-start.46 = (bf16[4,64,1024]{2,1,0:T(8,128)(2,1)}, bf16[4,64,1024]{2,1,0:T(8,128)(2,1)S(1)}, u32[]{:S(2)}, u32[]{:S(2)}) collective-permute-start(bf16[4,64,1024]{2,1,0:T(8,128)(2,1)} %get-tuple-element.370), channel_id=1, source_target_pairs={{0,8},{8,0},{1,9},{9,1},{2,10},{10,2},{3,11},{11,3},{4,12},{12,4},... | collective-permute-start | bytes 1572872 | tf_op jit(solution)/shard_map/ppermute | solution.py:58
  295.8 22.2 %collective-permute-start.47 = (bf16[4,64,1024]{2,1,0:T(8,128)(2,1)S(1)}, bf16[4,64,1024]{2,1,0:T(8,128)(2,1)S(1)}, u32[]{:S(2)}, u32[]{:S(2)}) collective-permute-start(bf16[4,64,1024]{2,1,0:T(8,128)(2,1)S(1)} %get-tuple-element.372), channel_id=1, source_target_pairs={{0,16},{16,0},{1,17},{17,1},{2,18},{18,2},{3,19},{19,3},{4,20},{20... | collective-permute-start | bytes 1572872 | tf_op jit(solution)/shard_map/ppermute | solution.py:58
  296.3 21.6 %collective-permute-start.49 = (bf16[2,104,1024]{2,1,0:T(8,128)(2,1)S(1)}, bf16[2,104,1024]{2,1,0:T(8,128)(2,1)S(1)}, u32[]{:S(2)}, u32[]{:S(2)}) collective-permute-start(bf16[2,104,1024]{2,1,0:T(8,128)(2,1)S(1)} %get-tuple-element.541), channel_id=1, source_target_pairs={{0,4},{2,6},{4,0},{6,2},{1,5},{3,7},{5,1},{7,3},{8,12},{10,14},{12... | collective-permute-start | bytes 1277960 | tf_op jit(solution)/shard_map/ppermute | solution.py:58
  329.5 28.6 %collective-permute-start.50 = (bf16[2,4,16,4096]{3,2,1,0:T(8,128)(2,1)S(1)}, bf16[2,4,16,4096]{3,2,1,0:T(8,128)(2,1)S(1)}, u32[]{:S(2)}, u32[]{:S(2)}) collective-permute-start(bf16[2,4,16,4096]{3,2,1,0:T(8,128)(2,1)S(1)} %get-tuple-element.390), channel_id=1, source_target_pairs={{0,16},{16,0},{1,17},{17,1},{2,18},{18,2},{3,19},{19,3},{4,20},{20... | collective-permute-start | bytes 3145736 | tf_op jit(solution)/shard_map/ppermute | solution.py:58
  330.9 27.2 %collective-permute-start.51 = (bf16[2,4,16,4096]{3,2,1,0:T(8,128)(2,1)}, bf16[2,4,16,4096]{3,2,1,0:T(8,128)(2,1)S(1)}, u32[]{:S(2)}, u32[]{:S(2)}) collective-permute-start(bf16[2,4,16,4096]{3,2,1,0:T(8,128)(2,1)} %get-tuple-element.392), channel_id=1, source_target_pairs={{0,8},{8,0},{1,9},{9,1},{2,10},{10,2},{3,11},{11,3},{4,12},{12,4},... | collective-permute-start | bytes 3145736 | tf_op jit(solution)/shard_map/ppermute | solution.py:58
  332.1 26.0 %collective-permute-start.52 = (bf16[128,1024]{1,0:T(8,128)(2,1)S(1)}, bf16[128,1024]{1,0:T(8,128)(2,1)S(1)}, u32[]{:S(2)}, u32[]{:S(2)}) collective-permute-start(bf16[128,1024]{1,0:T(8,128)(2,1)S(1)} %pad_maximum_fusion.35), channel_id=1, source_target_pairs={{0,2},{2,4},{4,6},{6,0},{1,3},{3,5},{5,7},{7,1},{8,10},{10,12},{12... | collective-permute-start | bytes 786440 | tf_op jit(solution)/shard_map/ppermute | solution.py:58
  332.1 26.0 %collective-permute-start.53 = (bf16[128,1024]{1,0:T(8,128)(2,1)S(1)}, bf16[128,1024]{1,0:T(8,128)(2,1)S(1)}, u32[]{:S(2)}, u32[]{:S(2)}) collective-permute-start(bf16[128,1024]{1,0:T(8,128)(2,1)S(1)} %pad_maximum_fusion.36), channel_id=1, source_target_pairs={{0,4},{2,6},{4,0},{6,2},{1,5},{3,7},{5,1},{7,3},{8,12},{10,14},{12... | collective-permute-start | bytes 786440 | tf_op jit(solution)/shard_map/ppermute | solution.py:58
  334.6 23.4 %collective-permute-start.54 = (bf16[128,1024]{1,0:T(8,128)(2,1)S(1)}, bf16[128,1024]{1,0:T(8,128)(2,1)S(1)}, u32[]{:S(2)}, u32[]{:S(2)}) collective-permute-start(bf16[128,1024]{1,0:T(8,128)(2,1)S(1)} %pad_maximum_fusion.37), channel_id=1, source_target_pairs={{0,6},{2,0},{4,2},{6,4},{1,7},{3,1},{5,3},{7,5},{8,14},{10,8},{12,... | collective-permute-start | bytes 786440 | tf_op jit(solution)/shard_map/ppermute | solution.py:58
  452.4 29.4 %collective-permute-start.74 = (bf16[2,104,1024]{2,1,0:T(8,128)(2,1)S(1)}, bf16[2,104,1024]{2,1,0:T(8,128)(2,1)S(1)}, u32[]{:S(2)}, u32[]{:S(2)}) collective-permute-start(bf16[2,104,1024]{2,1,0:T(8,128)(2,1)S(1)} %get-tuple-element.537), channel_id=1, source_target_pairs={{0,4},{2,6},{4,0},{6,2},{1,5},{3,7},{5,1},{7,3},{8,12},{10,14},{12... | collective-permute-start | bytes 1277960 | tf_op jit(solution)/shard_map/ppermute | solution.py:58
  454.1 27.7 %collective-permute-start.73 = (bf16[2,104,1024]{2,1,0:T(8,128)(2,1)S(1)}, bf16[2,104,1024]{2,1,0:T(8,128)(2,1)S(1)}, u32[]{:S(2)}, u32[]{:S(2)}) collective-permute-start(bf16[2,104,1024]{2,1,0:T(8,128)(2,1)S(1)} %get-tuple-element.538), channel_id=1, source_target_pairs={{0,6},{2,0},{4,2},{6,4},{1,7},{3,1},{5,3},{7,5},{8,14},{10,8},{12,... | collective-permute-start | bytes 1277960 | tf_op jit(solution)/shard_map/ppermute | solution.py:58
  458.1 23.7 %collective-permute-start.71 = (bf16[4,16,1792]{2,1,0:T(8,128)(2,1)S(1)}, bf16[4,16,1792]{2,1,0:T(8,128)(2,1)S(1)}, u32[]{:S(2)}, u32[]{:S(2)}) collective-permute-start(bf16[4,16,1792]{2,1,0:T(8,128)(2,1)S(1)} %get-tuple-element.590), channel_id=1, source_target_pairs={{0,8},{8,0},{1,9},{9,1},{2,10},{10,2},{3,11},{11,3},{4,12},{12,4},... | collective-permute-start | bytes 688136 | tf_op jit(solution)/shard_map/ppermute | solution.py:58
  459.2 22.7 %collective-permute-start.72 = (bf16[4,16,1792]{2,1,0:T(8,128)(2,1)S(1)}, bf16[4,16,1792]{2,1,0:T(8,128)(2,1)S(1)}, u32[]{:S(2)}, u32[]{:S(2)}) collective-permute-start(bf16[4,16,1792]{2,1,0:T(8,128)(2,1)S(1)} %get-tuple-element.588), channel_id=1, source_target_pairs={{0,16},{16,0},{1,17},{17,1},{2,18},{18,2},{3,19},{19,3},{4,20},{20... | collective-permute-start | bytes 688136 | tf_op jit(solution)/shard_map/ppermute | solution.py:58
  (137 other events, 1399.2 us)

commit v4 on v3

--- a/solution.py
+++ b/solution.py
@@ -103,8 +103,22 @@
         for part in range(2):
             kinds = ([first[part]] + second[part], traded_first[part] + traded_second[part])
             for turn, groups in enumerate(kinds):
-                found += [(group, part, turn, step) for step, group in enumerate(groups)]
+                found += [(g, turn, [(part, step, one) for one in range(g.shape[0])]) for step, g in enumerate(groups)]
         return found
+
+    def flat(self, groups):
+        return jnp.concatenate([group for part in groups for group in part], axis=0)
+
+    def labels(self, far):
+        sizes = self.sizes
+        found = []
+        for part in range(2):
+            for step in range(1, sizes[ORDERS[part][1]]) if far else [0]:
+                found += [(part, step, one) for one in range(sizes[ORDERS[part][0]])]
+        return found
+
+    def flat_sources(self, near, near_core, far, far_core):
+        return [(near, 0, self.labels(False)), (far, 0, self.labels(True)), (near_core, 1, self.labels(False)), (far_core, 1, self.labels(True))]
 
     def assemble(self, sources, widths):
         place = self.place()
@@ -112,11 +126,11 @@
         cut, width = sources[0][0].shape[-2:]
         depth = sizes["sz"]
         planes, kinds, parts, arrays, counts = [], [], [], [], []
-        for group, part, turn, step in sources:
-            order = ORDERS[part]
+        for group, turn, labels in sources:
             arrays.append(group)
-            counts.append(group.shape[0])
-            for one in range(group.shape[0]):
+            counts.append(len(labels))
+            for part, step, one in labels:
+                order = ORDERS[part]
                 at = {order[1]: (place[order[1]] - step) % sizes[order[1]], order[0]: (place[order[0]] - one) % sizes[order[0]]}
                 planes.append(at["gy"] * sizes["gx"] + at["gx"])
                 kinds.append((place["sc"] - turn) % 2)
@@ -219,7 +233,7 @@
     def images_of(self, own, came, images, twins):
         place = self.place()
         size = self.sizes["sz"]
-        both = jnp.stack([jnp.stack(own), came])
+        both = jnp.stack([own, came])
         both = both.reshape((2 * size,) + both.shape[2:])
         out = []
         for image in range(images):
@@ -243,6 +257,9 @@
     def toward(self, arrays, axis):
         size = self.sizes[axis]
         return [arrays[0]] + [shifted(arrays[k], axis, size, k) for k in range(1, size)]
+
+    def toward_some(self, parts, steps):
+        return {k: shifted(parts[k], "sz", self.sizes["sz"], k) for k in steps}
 
     def ready(self, sums):
         cut = sums.shape[3] // 2
@@ -463,20 +480,20 @@
         jnp.where(first, grad_value[0], grad_value[1]),
     )
     for kind, array in enumerate(grads):
-        start = pl.multiple_of((pl.program_id(0) + kind * CUT) * 2 * HD, 2 * HD)
+        i = pl.program_id(0)
+        start = pl.multiple_of((i // CUT * 3 * CUT + i % CUT + kind * CUT) * 2 * HD, 2 * HD)
         low = array.astype(bf16)
         d_ref[:, pl.ds(start, 2 * HD)] = low
         s_ref[:, pl.ds(start, 2 * HD)] = jnp.sum(low.astype(f32), axis=0, keepdims=True)
 
 
-def attend_back(qkv, logs, grad_mixed, half):
-    base = half * CUT
-    shape = (PACKED, 3 * CUT * 2 * HD)
+def attend_back(qkv, logs, grad_mixed):
+    shape = qkv.shape
     return pl.pallas_call(
         attend_back_body,
         out_shape=[jax.ShapeDtypeStruct(shape, bf16), jax.ShapeDtypeStruct((1, shape[1]), f32)],
-        grid=(CUT,),
-        in_specs=[kind_spec(0, base), kind_spec(1, base), kind_spec(2, base), log_spec(base), pair_spec(base)],
+        grid=(PAIRS,),
+        in_specs=[kind_spec(0), kind_spec(1), kind_spec(2), log_spec(), pair_spec()],
         out_specs=[pl.BlockSpec(shape, lambda i: (0, 0)), pl.BlockSpec((1, shape[1]), lambda i: (0, 0))],
         compiler_params=room(),
         cost_estimate=cost(12e9, 8 * qkv.size, PACKED * PACKED * H // 2),
@@ -834,10 +851,9 @@
     slot = lax.broadcasted_iota(jnp.int32, (images, slots, 1), 1)
     marked = jnp.where(slot < counts[:, :, None], tokens, jnp.asarray(ABSENT, bf16))
 
-    def back_on_device(pieces, own):
-        pieces = [own] + [pieces[k] for k in range(1, depth)]
-        came = ring.swap(jnp.stack([piece[1] for piece in pieces]))
-        return ring.images_of([piece[0] for piece in pieces], came, images, twins)
+    def back_pieces(pieces, own):
+        pieces = jnp.stack([own] + [pieces[k] for k in everything])
+        return pieces[:, 0], ring.swap(pieces[:, 1])
 
     def slots_of(array):
         return array.reshape(depth, 2, slots, width)
@@ -857,35 +873,41 @@
 
     one = seed(w_qkv, small, bias_up)
     column = ring.spread(one, everything)
+    stay, go = ring.blocks_for(marked, twins)
+    came = ring.swap(go)
+    cot_stay, go = ring.blocks_for(cotangent, twins)
+    cot_came = ring.swap(go)
     one = ring.along(one, column)
     two = jnp.concatenate([w_out, w_up], axis=1)
-    one, two = tie(one, two)
+    one, two, stay, came, cot_stay, cot_came = tie(one, two, stay, came, cot_stay, cot_came)
 
     one = ring.across(one)
     column = ring.spread(two, outer)
-    stay, go = ring.blocks_for(marked, twins)
-    came = ring.swap(go)
-    one, two, column, stay, came = tie(one, two, column, stay, came)
+    pieces = ring.paired(stay, came)
+    cot_pieces = ring.paired(cot_stay, cot_came)
+    one, two, column, pieces, cot_pieces = tie(one, two, column, pieces, cot_pieces)
 
     one_more = ring.plane(one)
     one_core = ring.to_core([[half] for half in one])
     column.update(ring.spread(two, inner))
     two = ring.along(two, column)
-    pieces = ring.paired(stay, came)
-    one, one_more, one_core, two, pieces = tie(one, one_more, one_core, two, pieces)
+    one, one_more, one_core, two, pieces, cot_pieces = tie(one, one_more, one_core, two, pieces, cot_pieces)
 
     one_more_core = ring.to_core(one_more)
     two = ring.across(two)
     rest = ring.send(pieces, outer[:1])
-    one, one_more, one_core, one_more_core, two, pieces = tie(one, one_more, one_core, one_more_core, two, pieces)
-
+    one, one_more, one_core, one_more_core, two, pieces, three = tie(one, one_more, one_core, one_more_core, two, pieces, w_down)
+
+    two_near = ring.flat([[half] for half in two])
     two_more = ring.plane(two)
     rest.update(ring.send(pieces, everything[1:]))
     full_qkv, vectors = ring.assemble(ring.sources(one, one_core, one_more, one_more_core), [3 * width, SMALL])
-    two, two_more, rest, full_qkv, vectors, three = tie(two, two_more, rest, full_qkv, vectors, w_down)
-
-    column = ring.spread(three, outer)
-    two_core = ring.to_core([[half] for half in two])
+    two_more = ring.flat(two_more)
+    two_near, two_more, rest, full_qkv, vectors, three = tie(two_near, two_more, rest, full_qkv, vectors, three)
+
+    column = ring.spread(three, everything)
+    two_core = ring.swap(two_near)
+    two_more_core = ring.swap(two_more)
     image_slots = jnp.concatenate([pieces[0]] + [rest[k] for k in everything]).reshape(group * slots, width)
     vectors = vectors.reshape(ring.count, rows, SMALL).astype(f32)
     bu = vectors[:, 0, 128 : 128 + wide * rows].reshape(ff)
@@ -899,22 +921,16 @@
     tokens_f, normed = pack_norm(packing, image_slots, g1, s1)
     qkv_bias = halved(jnp.concatenate([bq, jnp.zeros((width,), f32), bv]))
     qkv = project(normed, full_qkv, qkv_bias)
-    two_core, column, three, qkv = tie(two_core, column, three, qkv)
-
-    column.update(ring.spread(three, inner))
-    two_more_core = ring.to_core(two_more)
-    stay, go = ring.blocks_for(cotangent, twins)
-    came = ring.swap(go)
     mixed, logs = attend(qkv)
     three = ring.along(three, column)
-    two_more_core, three, mixed, stay, came = tie(two_more_core, three, mixed, stay, came)
+    two_core, two_more_core, three, mixed = tie(two_core, two_more_core, three, mixed)
 
     three = ring.across(three)
-    cot_pieces = ring.paired(stay, came)
     cot_rest = ring.send(cot_pieces, outer)
-    full_out, full_up = ring.assemble(ring.sources(two, two_core, two_more, two_more_core), [width, ff])
+    full_out, full_up = ring.assemble(ring.flat_sources(two_near, two_core, two_more, two_more_core), [width, ff])
     residual, normed_two = out_norm(mixed, full_out, tokens_f, bo, g2, s2)
-    three, normed_two, cot_pieces, cot_rest = tie(three, normed_two, cot_pieces, cot_rest)
+    normed_far = ring.by_distance(normed)
+    three, normed_two, normed_far, cot_rest = tie(three, normed_two, normed_far, cot_rest)
 
     three_more = ring.plane(three)
     three_core = ring.to_core([[half] for half in three])
@@ -924,8 +940,10 @@
     if active_far is None:
         active_far = ring.by_distance(active)
     mixed_far = ring.by_distance(mixed)
-    normed_far = ring.by_distance(normed)
-    three_more, three_core, active, active_far, cot_rest = tie(three_more, three_core, active, active_far, cot_rest)
+    two_far = ring.by_distance(normed_two)
+    three, three_more, three_core, active, active_far, mixed_far, two_far, cot_rest = tie(
+        three, three_more, three_core, active, active_far, mixed_far, two_far, cot_rest
+    )
 
     three_more_core = ring.to_core(three_more)
     share = (lax.axis_index(("sz", "sc")) % twins == 0).astype(f32) if twins > 1 else None
@@ -936,8 +954,7 @@
 
     d = ring.swap(sent)
     (full_down,) = ring.assemble(ring.sources(three, three_core, three_more, three_more_core), [width])
-    two_far = ring.by_distance(normed_two)
-    d, full_down, two_far = tie(d, full_down, two_far)
+    d, full_down = tie(d, full_down)
 
     d = ring.kept(active_far, grad_low, share, d)
     result = slots_of(land(active, full_down, residual, bd, packing))
@@ -964,45 +981,28 @@
     d, u, sent, residual_low = tie(d, u, sent, residual_low)
 
     u = ring.first(u)
-    sent_out = sent
     d = ring.third(d)
     grad_mixed = back_project(residual_low, full_out)
-    first_half, first_sums = attend_back(qkv, logs, grad_mixed, 0)
-    sent = weight_grad(normed_far, 1, first_half, share)
-    u, sent_out, sent, d, grad_mixed = tie(u, sent_out, sent, d, grad_mixed)
+    sent_out = sent
+    grads, grad_sums = attend_back(qkv, logs, grad_mixed)
+    sent = weight_grad(normed_far, 1, grads, share)
+    u, sent_out, sent, d, grads = tie(u, sent_out, sent, d, grads)
 
     u = ring.again(u)
-    u, sent, sent_out, grad_mixed, back = tie(u, sent, sent_out, grad_mixed, back)
+    u, sent_out, sent, grads, back = tie(u, sent_out, sent, grads, back)
 
     u = ring.second(u)
+    o = ring.swap(sent_out)
     q = ring.swap(sent)
-    o = ring.swap(sent_out)
-    second_half, second_sums = attend_back(qkv, logs, grad_mixed, 1)
-    u, q, o, second_half, back = tie(u, q, o, second_half, back)
-
+    grad_tokens, sums_one = back_norm([grads], full_qkv, tokens_f, g1, grad_residual, packing)
+    grad_tokens = slots_of(grad_tokens)
+    u, o, q, grads, grad_tokens, sums_one, back, d = tie(u, o, q, grads, grad_tokens, sums_one, back, d)
+
+    sent_back = ring.send(grad_tokens, outer, -1)
+    q = ring.kept(normed_far, grads, share, q)
+    o = ring.reshaped(weight_grad(mixed_far, 0, residual_low, share, o))
     u = ring.last(u)
-    u, q, o, second_half, back = tie(u, q, o, second_half, back)
-
-    u = ring.third(u)
-    result = back_on_device(back, result[0])
-    q = ring.reshaped(weight_grad(normed_far, 0, first_half, share, q))
-    o = ring.reshaped(weight_grad(mixed_far, 0, residual_low, share, o))
-    q = ring.ready(jnp.concatenate([q, o], axis=-1))
-    sent = weight_grad(normed_far, 1, second_half, share)
-    q, sent, result, u = tie(q, sent, result, u)
-
-    q = ring.first(q)
-    r = ring.swap(sent)
-    grad_tokens, sums_one = back_norm([first_half, second_half], full_qkv, tokens_f, g1, grad_residual, packing)
-    grad_tokens = slots_of(grad_tokens)
-    q, r, grad_tokens, sums_one = tie(q, r, grad_tokens, sums_one)
-
-    q = ring.again(q)
-    q, r, grad_tokens, sums_one = tie(q, r, grad_tokens, sums_one)
-
-    back = ring.send(grad_tokens, everything, -1)
-    q = ring.second(q)
-    joined_sum = whole(jnp.concatenate([first_sums[0], second_sums[0]]))
+    joined_sum = whole(grad_sums[0])
     grad_bq, grad_bv = joined_sum[:width], joined_sum[2 * width :]
     small = [grad_bq, grad_bv, sums_two[2], grad_bd, sums_one[0], sums_one[1], sums_two[0], sums_two[1]]
     small = [array.reshape(ring.count, rows) for array in small] + [grad_bu.reshape(ring.count, wide * rows)]
@@ -1011,30 +1011,50 @@
     near_first = (ranks[None, :] == lax.broadcasted_iota(jnp.int32, (ring.count, 1), 0)).astype(bf16)
     small = dot_float(near_first, small).astype(bf16)
     small = jnp.pad(small, ((0, 0), (0, rows * SMALL - small.shape[1]))).reshape(2, ring.count // 2 * rows, SMALL)
-    r = ring.reshaped(weight_grad(normed_far, 0, second_half, share, r))
+    q, o, small, u, sent_back, grad_tokens, back, d = tie(q, o, small, u, sent_back, grad_tokens, back, d)
+
+    q = ring.first(q)
+    sent_back.update(ring.send(grad_tokens, inner, -1))
+    came = ring.swap(small[1])
+    own = jnp.stack([result[0]] + [back[k] for k in everything])
+    q, came, sent_back, u, back, d, own = tie(q, came, sent_back, u, back, d, own)
+
+    q = ring.again(q)
+    q, u, own, d = tie(q, u, own, d)
+
+    q = ring.second(q)
+    later = ring.toward_some(u, outer)
+    other = ring.swap(own[:, 1])
+    small = ring.reshaped(total([small[0], came]).astype(bf16))
+    o = ring.ready(jnp.concatenate([o, small], axis=-1))
+    q, later, other, o, u, own, d = tie(q, later, other, o, u, own, d)
+
+    q = ring.last(q)
+    q, o, u, d = tie(q, o, u, d)
+
+    o = ring.first(o)
+    later.update(ring.toward_some(u, inner))
+    result = ring.images_of(own[:, 0], other, images, twins)
     result = jnp.where(slot < counts[:, :, None], result, jnp.asarray(0, bf16))
-    q, r, small, result = tie(q, r, small, result)
-
-    came = ring.swap(small[1])
-    q = ring.last(q)
-    came, q, r = tie(came, q, r)
-
-    small = ring.reshaped(total([small[0], came]).astype(bf16))
-    r = ring.first(ring.ready(jnp.concatenate([r, small], axis=-1)))
-    (r,) = tie(r)
-    r = ring.second(ring.again(r))
-    r, q, back = tie(r, q, back)
-
-    r = ring.last(r)
-    q = ring.third([jnp.concatenate(pair, axis=-1) for pair in zip(q, r)])
-    grad_tokens = back_on_device(back, grad_tokens[0]).astype(f32)
+    o, later, result, q, d = tie(o, later, result, q, d)
+
+    o = ring.again(o)
+    o, q, d = tie(o, q, d)
+
+    q = ring.third(q)
+    o = ring.second(o)
+    u = [u[0]] + [later[k] for k in everything]
+    grad_tokens, came = back_pieces(sent_back, grad_tokens[0])
+    q, o, grad_tokens, came = tie(q, o, grad_tokens, came)
+
+    o = ring.third(ring.last(o))
+    grad_tokens = ring.images_of(grad_tokens, came, images, twins).astype(f32)
 
     sum_down, sum_up = total(d), total(u)
-    q = total(q)
-    first_end, second_start, small_start = 3 * width // 2, 5 * width // 2, 4 * width
-    sum_out = q[:, first_end:second_start]
-    sum_qkv = whole(jnp.concatenate([q[:, :first_end], q[:, second_start:small_start]], axis=1))
-    small = q[:, small_start:].reshape(rows * SMALL)
+    o = total(o)
+    sum_out = o[:, :width]
+    sum_qkv = whole(total(q))
+    small = o[:, width:].reshape(rows * SMALL)
     sum_bq, sum_bv, sum_bo, sum_bd, sum_g1, sum_s1, sum_g2, sum_s2 = [small[k * rows : (k + 1) * rows] for k in range(8)]
     sum_bu = small[8 * rows : (8 + wide) * rows]
     return (result, grad_tokens, sum_qkv, sum_bq, sum_bv, sum_out, sum_bo, sum_up, sum_bu, sum_down, sum_bd, sum_g1, sum_s1, sum_g2, sum_s2)

time: 527 us -> 505 us (0.958)
  waiting for transfers between devices: 147 us -> 117 us
  other arithmetic: 46.7 us -> 58.5 us
    ppermute x80, waiting for transfers between devices: 147 us -> 117 us  [shifted(): lax.ppermute(array, axis, [(i, (i + step) % size) for i in range(size)])]
    concatenate x4 -> x2, other arithmetic: 0.1 us -> 7.04 us  [flat(): return jnp.concatenate([group for part in groups for group in part], axis=0)]
    pallas_call x10 -> x8, Pallas kernels: 48.1 us -> 46.5 us  [weight_grad(): pl.pallas_call(body, out_shape=[jax.ShapeDtypeStruct(shape, bf16) for sha...]
    pallas_call x2 -> x1, Pallas kernels: 24.3 us -> 25.4 us  [attend_back(): pl.pallas_call(attend_back_body, out_shape=[jax.ShapeDtypeStruct(shape, b...]
    unnamed x194 -> x184, local copies, waits for them, and re-layouts: 13.4 us -> 13.6 us
  transfers between devices with their start and end apart: 80 -> 80, of which waited for: 29 -> 23; matrix products, arithmetic and copies ran while one was open for 8% -> 11% of each run, Pallas kernels for 32% -> 33%
where the time goes in v4:
time: 505 us; the launch traced here: 499 us
  Pallas kernels  200 us (40%)
  waiting for transfers between devices  117 us (23%)
  starting transfers between devices  93.9 us (19%)
  other arithmetic  58.5 us (12%)
  local copies, waits for them, and re-layouts  26.1 us (5%)
    ppermute x80, waiting for transfers between devices, shifted(): lax.ppermute(array, axis, [(i, (i + step) % size) for i in range(size)])  117 us
    ppermute x80, starting transfers between devices, shifted(): lax.ppermute(array, axis, [(i, (i + step) % size) for i in range(size)])  93.9 us
    pallas_call x8, Pallas kernels, weight_grad(): pl.pallas_call(body, out_shape=[jax.ShapeDtypeStruct(shape, bf16) for sha...  46.5 us
    pallas_call x1, Pallas kernels, attend_back(): pl.pallas_call(attend_back_body, out_shape=[jax.ShapeDtypeStruct(shape, b...  25.4 us
    pallas_call x2, Pallas kernels, back_norm(): pl.pallas_call(body, out_shape=shapes + [jax.ShapeDtypeStruct((8, width),...  25.2 us
    pallas_call x3, Pallas kernels, assemble(): pl.pallas_call(body, out_shape=[jax.ShapeDtypeStruct((planes_all, depth,...  22.1 us
    pallas_call x1, Pallas kernels, rise(): pl.pallas_call(body, out_shape=shapes, grid_spec=pltpu.PrefetchScalarGrid...  15.2 us
    pallas_call x1, Pallas kernels, attend(): pl.pallas_call(attend_body, out_shape=[jax.ShapeDtypeStruct((PACKED, H *...  14.1 us
  transfers between devices with their start and end apart: 80, of which 23 were waited for; matrix products, arithmetic and copies ran while one was open for 11% of the time, Pallas kernels for 33%

profile of v4, /device:TPU:0, one launch (start us, length us, event | category | flops | bytes accessed | tf_op | source)
XLA Modules:
  0.0 498.5 jit_solution(3194979742732372748)
XLA Ops:
  2.4 5.0 %collective-permute-start.2 = (bf16[32,3328]{1,0:T(8,128)(2,1)}, bf16[32,3328]{1,0:T(8,128)(2,1)}, u32[]{:S(2)}, u32[]{:S(2)}) collective-permute-start(bf16[32,3328]{1,0:T(8,128)(2,1)} %seed.1), channel_id=1, source_target_pairs={{0,6},{2,0},{4,2},{6,4},{1,7},{3,1},{5,3},{7,5},{8,14},{10,8},{12,... | collective-permute-start | bytes 638984 | tf_op jit(solution)/shard_map/ppermute | solution.py:58
  16.0 9.8 %collective-permute-done.1 = bf16[32,3328]{1,0:T(8,128)(2,1)} collective-permute-done((bf16[32,3328]{1,0:T(8,128)(2,1)}, bf16[32,3328]{1,0:T(8,128)(2,1)}, u32[]{:S(2)}, u32[]{:S(2)}) %collective-permute-start.1) | collective-permute-done | bytes 213024 | tf_op jit(solution)/shard_map/ppermute | solution.py:58
  40.9 4.5 collective-permute-done.7
  48.7 11.2 %collective-permute-done.13 = bf16[32,5120]{1,0:T(8,128)(2,1)S(1)} collective-permute-done((bf16[32,5120]{1,0:T(8,128)(2,1)S(1)}, bf16[32,5120]{1,0:T(8,128)(2,1)S(1)}, u32[]{:S(2)}, u32[]{:S(2)}) %collective-permute-start.13) | collective-permute-done | bytes 327712 | tf_op jit(solution)/shard_map/ppermute | solution.py:58
  60.4 6.4 %collective-permute-done.9.refs_1_ = bf16[2,4,16,3328]{3,2,1,0:T(8,128)(2,1)S(1)} collective-permute-done((bf16[2,4,16,3328]{3,2,1,0:T(8,128)(2,1)S(1)}, bf16[2,4,16,3328]{3,2,1,0:T(8,128)(2,1)S(1)}, u32[]{:S(2)}, u32[]{:S(2)}) %collective-permute-start.9) | collective-permute-done | bytes 852000 | tf_op jit(solution)/shard_map/ppermute | solution.py:58
  70.9 13.6 %collective-permute-done.16 = bf16[4,16,5120]{2,1,0:T(8,128)(2,1)S(1)} collective-permute-done((bf16[4,16,5120]{2,1,0:T(8,128)(2,1)S(1)}, bf16[4,16,5120]{2,1,0:T(8,128)(2,1)S(1)}, u32[]{:S(2)}, u32[]{:S(2)}) %collective-permute-start.16) | collective-permute-done | bytes 655392 | tf_op jit(solution)/shard_map/ppermute | solution.py:58
  95.8 7.0 %assemble.3 = (bf16[4,4,2,2,16,3072]{5,4,3,2,1,0:T(8,128)(2,1)}, bf16[4,4,2,2,16,256]{5,4,3,2,1,0:T(8,128)(2,1)S(1)}) custom-call(s32[32]{0:T(128)S(1)} %stack.422.table_ref, bf16[2,4,16,3328]{3,2,1,0:T(8,128)(2,1)S(1)} %pad_maximum_fusion.16.refs_0_, bf16[2,4,16,3328]{3,2,1,0:T(8,128)(2,1)S(1)} %collective-permute-done.9.refs_1_, ...), custom_call_target="tpu_custom_call" | custom-call | bytes 272629 | tf_op jit(solution)/shard_map/assemble/pallas_call | solution.py:166
  106.4 10.9 %collective-permute-done.18 = bf16[2,4,16,5120]{3,2,1,0:T(8,128)(2,1)} collective-permute-done((bf16[2,4,16,5120]{3,2,1,0:T(8,128)(2,1)}, bf16[2,4,16,5120]{3,2,1,0:T(8,128)(2,1)}, u32[]{:S(2)}, u32[]{:S(2)}) %collective-permute-start.18) | collective-permute-done | bytes 1310752 | tf_op jit(solution)/shard_map/ppermute | solution.py:58
  121.0 10.1 %collective-permute-start.27 = (bf16[128,1024]{1,0:T(8,128)(2,1)S(1)}, bf16[128,1024]{1,0:T(8,128)(2,1)S(1)}, u32[]{:S(2)}, u32[]{:S(2)}) collective-permute-start(bf16[128,1024]{1,0:T(8,128)(2,1)S(1)} %copy-done.67), channel_id=1, source_target_pairs={{0,6},{2,0},{4,2},{6,4},{1,7},{3,1},{5,3},{7,5},{8,14},{10,8},{12,... | collective-permute-start | bytes 786440 | tf_op jit(solution)/shard_map/ppermute | solution.py:58
  138.7 7.5 %project.1.q_ref.k_ref.v_ref = bf16[592,3072]{1,0:T(8,128)(2,1)} custom-call(bf16[592,1024]{1,0:T(8,128)(2,1)S(1)} %get-tuple-element.387.x_ref, bf16[1024,3072]{1,0:T(8,128)(2,1)} %bitcast.260, f32[1,3072]{1,0:T(1,128)S(1)} %reshape_reshape.3.b_ref), custom_call_target="tpu_custom_call" | custom-call | flops 120000000 | bytes 240000 | tf_op jit(solution)/shard_map/project/pallas_call | solution.py:607
  147.3 14.1 %attend.1 = (bf16[592,1024]{1,0:T(8,128)(2,1)S(1)}, f32[64,592]{1,0:T(8,128)S(1)}) custom-call(bf16[592,3072]{1,0:T(8,128)(2,1)} %project.1.q_ref.k_ref.v_ref, bf16[592,3072]{1,0:T(8,128)(2,1)} %project.1.q_ref.k_ref.v_ref, bf16[592,3072]{1,0:T(8,128)(2,1)} %project.1.q_ref.k_ref.v_ref), custom_call_target="tpu_custom_call" | custom-call | flops 240000000 | bytes 290979 | tf_op jit(solution)/shard_map/attend/pallas_call | solution.py:446
  175.3 8.4 %assemble.4 = (bf16[4,4,2,2,16,1024]{5,4,3,2,1,0:T(8,128)(2,1)S(1)}, bf16[4,4,2,2,16,4096]{5,4,3,2,1,0:T(8,128)(2,1)}) custom-call(s32[32]{0:T(128)S(1)} %stack.439.table_ref, bf16[4,4,16,5120]{3,2,1,0:T(8,128)(2,1)} %pad_maximum_fusion.refs_0_, bf16[4,4,16,5120]{3,2,1,0:T(8,128)(2,1)} %pad_maximum_fusion.1.refs_1_, ...), custom_call_target="tpu_custom_call" | custom-call | bytes 419430 | tf_op jit(solution)/shard_map/assemble/pallas_call | solution.py:166
  185.1 5.1 %out_norm.1 = (f32[592,1024]{1,0:T(8,128)}, bf16[592,1024]{1,0:T(8,128)(2,1)S(1)}) custom-call(bf16[592,1024]{1,0:T(8,128)(2,1)S(1)} %copy-done.14, bf16[1024,1024]{1,0:T(8,128)(2,1)} %bitcast.249, f32[592,1024]{1,0:T(8,128)} %get-tuple-element.396.t_ref.refs_2_, f32[1,1024]{1,0:T(1,128)S(1)} %reshape_reshape_squeeze.25.b_ref, ...), custom_call_target="tpu_custom_call" | custom-call | flops 40000000 | bytes 160000 | tf_op jit(solution)/shard_map/out_norm/pallas_call | solution.py:706
  200.7 15.2 %rise.1 = (bf16[592,4096]{1,0:T(8,128)(2,1)}, f32[592,4096]{1,0:T(8,128)}, bf16[2,592,2048]{2,1,0:T(8,128)(2,1)}) custom-call(s32[32]{0:T(128)S(1)} %fusion.92.rank_ref, bf16[592,1024]{1,0:T(8,128)(2,1)S(1)} %get-tuple-element.403.x_ref, bf16[1024,4096]{1,0:T(8,128)(2,1)} %bitcast.258, f32[1,4096]{1,0:T(1,128)S(1)} %slice_bitcast_fusion.36.b_ref), custom_call_target="tpu_custom_call" | custom-call | flops 240000000 | bytes 600000 | tf_op jit(solution)/shard_map/rise/pallas_call | solution.py:554
  223.3 7.1 %weight_grad.8 = bf16[2048,1024]{1,0:T(8,128)(2,1)} custom-call(bf16[2,592,2048]{2,1,0:T(8,128)(2,1)} %get-tuple-element.410.refs_0_, bf16[592,1024]{1,0:T(8,128)(2,1)S(1)} %get-tuple-element.418.refs_1_.g_ref.refs_4_), custom_call_target="tpu_custom_call" | custom-call | flops 49660560 | bytes 167772 | tf_op jit(solution)/shard_map/weight_grad/pallas_call | solution.py:364
  235.5 6.7 %assemble.5 = bf16[4,4,2,2,64,1024]{5,4,3,2,1,0:T(8,128)(2,1)} custom-call(s32[32]{0:T(128)S(1)} %stack.422.table_ref, bf16[2,4,64,1024]{3,2,1,0:T(8,128)(2,1)S(1)} %copy-done.16, bf16[2,4,64,1024]{3,2,1,0:T(8,128)(2,1)S(1)} %copy-done.22, bf16[2,4,64,1024]{3,2,1,0:T(8,128)(2,1)S(1)} %copy-done.20, bf16[2,4,64,1024]{3,2,1,0:T(8,128)(2,1)} %copy-done.46, ...), custom_call_target="tpu_custom_call" | custom-call | bytes 335544 | tf_op jit(solution)/shard_map/assemble/pallas_call | solution.py:166
  242.3 7.7 %weight_grad.9 = (bf16[2,4,64,1024]{3,2,1,0:T(8,128)(2,1)S(1)}, bf16[2,4,64,1024]{3,2,1,0:T(8,128)(2,1)S(1)}, bf16[2,4,64,1024]{3,2,1,0:T(8,128)(2,1)S(1)}, bf16[2,4,64,1024]{3,2,1,0:T(8,128)(2,1)}) custom-call(bf16[2,592,2048]{2,1,0:T(8,128)(2,1)} %get-tuple-element.410.refs_0_, bf16[592,1024]{1,0:T(8,128)(2,1)} %copy-done, ...), custom_call_target="tpu_custom_call" | custom-call | flops 49660560 | bytes 167772 | tf_op jit(solution)/shard_map/weight_grad/pallas_call | solution.py:364
  250.0 11.4 %land.1 = bf16[832,1024]{1,0:T(8,128)(2,1)S(1)} custom-call(bf16[592,4096]{1,0:T(8,128)(2,1)} %get-tuple-element.431.a_ref, bf16[4096,1024]{1,0:T(8,128)(2,1)} %bitcast.256, f32[592,1024]{1,0:T(8,128)} %get-tuple-element.433.r_ref.refs_2_, f32[1,1024]{1,0:T(1,128)S(1)} %reshape_reshape_squeeze.29.b_ref, bf16[592,832]{1,0:T(8,128)(2,1)S(1)} %fusion.p_ref.refs_5_), custom_call_target="tpu_custom_call" | custom-call | flops 120000000 | bytes 280000 | tf_op jit(solution)/shard_map/land/pallas_call | solution.py:739
  269.3 11.3 %fall.1 = (bf16[592,4096]{1,0:T(8,128)(2,1)}, f32[1,4096]{1,0:T(1,128)S(1)}) custom-call(bf16[592,1024]{1,0:T(8,128)(2,1)S(1)} %copy-done.1, bf16[4096,1024]{1,0:T(8,128)(2,1)} %bitcast.257, f32[592,4096]{1,0:T(8,128)} %get-tuple-element.439.slope_ref), custom_call_target="tpu_custom_call" | custom-call | flops 200000000 | bytes 500000 | tf_op jit(solution)/shard_map/fall/pallas_call | solution.py:584
  280.7 7.1 %weight_grad.10 = bf16[512,4096]{1,0:T(8,128)(2,1)} custom-call(bf16[2,592,512]{2,1,0:T(8,128)(2,1)S(1)} %copy-done.7, bf16[592,4096]{1,0:T(8,128)(2,1)} %get-tuple-element.440.refs_1_.refs_0_), custom_call_target="tpu_custom_call" | custom-call | flops 49660560 | bytes 167772 | tf_op jit(solution)/shard_map/weight_grad/pallas_call | solution.py:364
  294.0 13.3 %back_norm.2 = (f32[592,1024]{1,0:T(8,128)}, bf16[592,1024]{1,0:T(8,128)(2,1)S(1)}, f32[8,1024]{1,0:T(8,128)S(1)}) custom-call(bf16[592,4096]{1,0:T(8,128)(2,1)} %get-tuple-element.440.refs_1_.refs_0_, bf16[1024,4096]{1,0:T(8,128)(2,1)} %bitcast.259, f32[592,1024]{1,0:T(8,128)} %get-tuple-element.433.r_ref.refs_2_, ...), custom_call_target="tpu_custom_call" | custom-call | flops 120000000 | bytes 400000 | tf_op jit(solution)/shard_map/back_norm/pallas_call | solution.py:811
  307.3 7.8 %collective-permute-done.47 = bf16[2,104,1024]{2,1,0:T(8,128)(2,1)S(1)} collective-permute-done((bf16[2,104,1024]{2,1,0:T(8,128)(2,1)S(1)}, bf16[2,104,1024]{2,1,0:T(8,128)(2,1)S(1)}, u32[]{:S(2)}, u32[]{:S(2)}) %collective-permute-start.47) | collective-permute-done | bytes 426016 | tf_op jit(solution)/shard_map/ppermute | solution.py:58
  315.1 7.7 %weight_grad.11 = (bf16[2,4,16,4096]{3,2,1,0:T(8,128)(2,1)S(1)}, bf16[2,4,16,4096]{3,2,1,0:T(8,128)(2,1)S(1)}, bf16[2,4,16,4096]{3,2,1,0:T(8,128)(2,1)S(1)}, bf16[2,4,16,4096]{3,2,1,0:T(8,128)(2,1)}) custom-call(bf16[2,592,512]{2,1,0:T(8,128)(2,1)} %copy-done.6, bf16[592,4096]{1,0:T(8,128)(2,1)} %get-tuple-element.440.refs_1_.refs_0_, ...), custom_call_target="tpu_custom_call" | custom-call | flops 49660560 | bytes 167772 | tf_op jit(solution)/shard_map/weight_grad/pallas_call | solution.py:364
  335.6 25.4 %attend_back.1 = (bf16[592,3072]{1,0:T(8,128)(2,1)}, f32[1,3072]{1,0:T(1,128)S(1)}) custom-call(bf16[592,3072]{1,0:T(8,128)(2,1)} %project.1.q_ref.k_ref.v_ref, bf16[592,3072]{1,0:T(8,128)(2,1)} %project.1.q_ref.k_ref.v_ref, bf16[592,3072]{1,0:T(8,128)(2,1)} %project.1.q_ref.k_ref.v_ref, f32[64,592]{1,0:T(8,128)S(1)} %copy-done.28, ...), custom_call_target="tpu_custom_call" | custom-call | flops 240000000 | bytes 290979 | tf_op jit(solution)/shard_map/attend_back/pallas_call | solution.py:492
  361.0 6.0 %weight_grad.13 = bf16[512,3072]{1,0:T(8,128)(2,1)} custom-call(bf16[2,592,512]{2,1,0:T(8,128)(2,1)S(1)} %by_distance.3.refs_0_, bf16[592,3072]{1,0:T(8,128)(2,1)} %get-tuple-element.505.refs_1_.refs_0_), custom_call_target="tpu_custom_call" | custom-call | flops 37245420 | bytes 125829 | tf_op jit(solution)/shard_map/weight_grad/pallas_call | solution.py:364
  372.7 11.9 %back_norm.3 = (bf16[832,1024]{1,0:T(8,128)(2,1)S(1)}, f32[8,1024]{1,0:T(8,128)S(1)}) custom-call(bf16[592,3072]{1,0:T(8,128)(2,1)} %get-tuple-element.505.refs_1_.refs_0_, bf16[1024,3072]{1,0:T(8,128)(2,1)} %bitcast.261, f32[592,1024]{1,0:T(8,128)} %get-tuple-element.396.t_ref.refs_2_, f32[1,1024]{1,0:T(1,128)S(1)} %reshape_reshape_squeeze.23.g_ref.refs_3_, ...), custom_call_target="tpu_custom_call" | custom-call | flops 120000000 | bytes 400000 | tf_op jit(solution)/shard_map/back_norm/pallas_call | solution.py:811
  393.7 6.6 %weight_grad.14 = (bf16[2,4,16,3072]{3,2,1,0:T(8,128)(2,1)S(1)}, bf16[2,4,16,3072]{3,2,1,0:T(8,128)(2,1)}, bf16[2,4,16,3072]{3,2,1,0:T(8,128)(2,1)S(1)}, bf16[2,4,16,3072]{3,2,1,0:T(8,128)(2,1)}) custom-call(bf16[2,592,512]{2,1,0:T(8,128)(2,1)} %copy-done.2, bf16[592,3072]{1,0:T(8,128)(2,1)} %get-tuple-element.505.refs_1_.refs_0_, ...), custom_call_target="tpu_custom_call" | custom-call | flops 37245420 | bytes 125829 | tf_op jit(solution)/shard_map/weight_grad/pallas_call | solution.py:364
  406.0 4.8 collective-permute-done.57
  418.4 15.8 %collective-permute-done.62 = bf16[2,104,1024]{2,1,0:T(8,128)(2,1)} collective-permute-done((bf16[2,104,1024]{2,1,0:T(8,128)(2,1)}, bf16[2,104,1024]{2,1,0:T(8,128)(2,1)}, u32[]{:S(2)}, u32[]{:S(2)}) %collective-permute-start.62) | collective-permute-done | bytes 426016 | tf_op jit(solution)/shard_map/ppermute | solution.py:58
  458.4 7.7 %collective-permute-done.70 = bf16[32,4096]{1,0:T(8,128)(2,1)S(1)} collective-permute-done((bf16[32,4096]{1,0:T(8,128)(2,1)S(1)}, bf16[32,4096]{1,0:T(8,128)(2,1)S(1)}, u32[]{:S(2)}, u32[]{:S(2)}) %collective-permute-start.70) | collective-permute-done | bytes 262176 | tf_op jit(solution)/shard_map/ppermute | solution.py:58
  477.9 6.9 %collective-permute-done.72 = bf16[32,3072]{1,0:T(8,128)(2,1)S(1)} collective-permute-done((bf16[32,3072]{1,0:T(8,128)(2,1)S(1)}, bf16[32,3072]{1,0:T(8,128)(2,1)S(1)}, u32[]{:S(2)}, u32[]{:S(2)}) %collective-permute-start.72) | collective-permute-done | bytes 196640 | tf_op jit(solution)/shard_map/ppermute | solution.py:58
  484.9 4.7 collective-permute-start.77
  (498 shorter events, 196.7 us)
Async XLA Ops:
  87.8 29.5 %collective-permute-start.18 = (bf16[2,4,16,5120]{3,2,1,0:T(8,128)(2,1)}, bf16[2,4,16,5120]{3,2,1,0:T(8,128)(2,1)}, u32[]{:S(2)}, u32[]{:S(2)}) collective-permute-start(bf16[2,4,16,5120]{3,2,1,0:T(8,128)(2,1)} %pad_maximum_fusion.8), channel_id=1, source_target_pairs={{0,16},{16,0},{1,17},{17,1},{2,18},{18,2},{3,19},{19,3},{4,20},{20... | collective-permute-start | bytes 3932168 | tf_op jit(solution)/shard_map/ppermute | solution.py:58
  88.3 29.3 %collective-permute-start.19 = (bf16[2,4,16,5120]{3,2,1,0:T(8,128)(2,1)}, bf16[2,4,16,5120]{3,2,1,0:T(8,128)(2,1)}, u32[]{:S(2)}, u32[]{:S(2)}) collective-permute-start(bf16[2,4,16,5120]{3,2,1,0:T(8,128)(2,1)} %pad_maximum_fusion.9), channel_id=1, source_target_pairs={{0,8},{8,0},{1,9},{9,1},{2,10},{10,2},{3,11},{11,3},{4,12},{12,4},... | collective-permute-start | bytes 3932168 | tf_op jit(solution)/shard_map/ppermute | solution.py:58
  89.9 31.1 %collective-permute-start.20 = (bf16[2,104,1024]{2,1,0:T(8,128)(2,1)}, bf16[2,104,1024]{2,1,0:T(8,128)(2,1)S(1)}, u32[]{:S(2)}, u32[]{:S(2)}) collective-permute-start(bf16[2,104,1024]{2,1,0:T(8,128)(2,1)} %pad_maximum_fusion.25), channel_id=1, source_target_pairs={{0,2},{2,4},{4,6},{6,0},{1,3},{3,5},{5,7},{7,1},{8,10},{10,12},{12... | collective-permute-start | bytes 1277960 | tf_op jit(solution)/shard_map/ppermute | solution.py:58
  90.1 30.9 %collective-permute-start.21 = (bf16[2,104,1024]{2,1,0:T(8,128)(2,1)}, bf16[2,104,1024]{2,1,0:T(8,128)(2,1)S(1)}, u32[]{:S(2)}, u32[]{:S(2)}) collective-permute-start(bf16[2,104,1024]{2,1,0:T(8,128)(2,1)} %pad_maximum_fusion.26), channel_id=1, source_target_pairs={{0,4},{2,6},{4,0},{6,2},{1,5},{3,7},{5,1},{7,3},{8,12},{10,14},{12... | collective-permute-start | bytes 1277960 | tf_op jit(solution)/shard_map/ppermute | solution.py:58
  92.9 28.0 %collective-permute-start.22 = (bf16[2,104,1024]{2,1,0:T(8,128)(2,1)}, bf16[2,104,1024]{2,1,0:T(8,128)(2,1)S(1)}, u32[]{:S(2)}, u32[]{:S(2)}) collective-permute-start(bf16[2,104,1024]{2,1,0:T(8,128)(2,1)} %pad_maximum_fusion.27), channel_id=1, source_target_pairs={{0,6},{2,0},{4,2},{6,4},{1,7},{3,1},{5,3},{7,5},{8,14},{10,8},{12,... | collective-permute-start | bytes 1277960 | tf_op jit(solution)/shard_map/ppermute | solution.py:58
  121.0 40.4 %collective-permute-start.27 = (bf16[128,1024]{1,0:T(8,128)(2,1)S(1)}, bf16[128,1024]{1,0:T(8,128)(2,1)S(1)}, u32[]{:S(2)}, u32[]{:S(2)}) collective-permute-start(bf16[128,1024]{1,0:T(8,128)(2,1)S(1)} %copy-done.67), channel_id=1, source_target_pairs={{0,6},{2,0},{4,2},{6,4},{1,7},{3,1},{5,3},{7,5},{8,14},{10,8},{12,... | collective-permute-start | bytes 786440 | tf_op jit(solution)/shard_map/ppermute | solution.py:58
  131.1 33.2 %collective-permute-start.26 = (bf16[128,1024]{1,0:T(8,128)(2,1)S(1)}, bf16[128,1024]{1,0:T(8,128)(2,1)}, u32[]{:S(2)}, u32[]{:S(2)}) collective-permute-start(bf16[128,1024]{1,0:T(8,128)(2,1)S(1)} %copy-done.67), channel_id=1, source_target_pairs={{0,4},{2,6},{4,0},{6,2},{1,5},{3,7},{5,1},{7,3},{8,12},{10,14},{12... | collective-permute-start | bytes 786440 | tf_op jit(solution)/shard_map/ppermute | solution.py:58
  131.2 34.1 %collective-permute-start.25 = (bf16[128,1024]{1,0:T(8,128)(2,1)S(1)}, bf16[128,1024]{1,0:T(8,128)(2,1)}, u32[]{:S(2)}, u32[]{:S(2)}) collective-permute-start(bf16[128,1024]{1,0:T(8,128)(2,1)S(1)} %copy-done.67), channel_id=1, source_target_pairs={{0,2},{2,4},{4,6},{6,0},{1,3},{3,5},{5,7},{7,1},{8,10},{10,12},{12... | collective-permute-start | bytes 786440 | tf_op jit(solution)/shard_map/ppermute | solution.py:58
  132.9 34.6 %collective-permute-start.23 = (bf16[4,4,16,5120]{3,2,1,0:T(8,128)(2,1)}, bf16[4,4,16,5120]{3,2,1,0:T(8,128)(2,1)}, u32[]{:S(2)}, u32[]{:S(2)}) collective-permute-start(bf16[4,4,16,5120]{3,2,1,0:T(8,128)(2,1)} %pad_maximum_fusion.refs_0_), channel_id=1, source_target_pairs={{0,1},{1,0},{2,3},{3,2},{4,5},{5,4},{6,7},{7,6},{8,9},{9,8},{10,11... | collective-permute-start | bytes 7864328 | tf_op jit(solution)/shard_map/ppermute | solution.py:58
  132.9 34.6 %collective-permute-start.24 = (bf16[4,4,16,5120]{3,2,1,0:T(8,128)(2,1)}, bf16[4,4,16,5120]{3,2,1,0:T(8,128)(2,1)}, u32[]{:S(2)}, u32[]{:S(2)}) collective-permute-start(bf16[4,4,16,5120]{3,2,1,0:T(8,128)(2,1)} %pad_maximum_fusion.1.refs_1_), channel_id=1, source_target_pairs={{0,1},{1,0},{2,3},{3,2},{4,5},{5,4},{6,7},{7,6},{8,9},{9,8},{10,11... | collective-permute-start | bytes 7864328 | tf_op jit(solution)/shard_map/ppermute | solution.py:58
  161.4 31.8 %collective-permute-start.30 = (bf16[2,104,1024]{2,1,0:T(8,128)(2,1)}, bf16[2,104,1024]{2,1,0:T(8,128)(2,1)}, u32[]{:S(2)}, u32[]{:S(2)}) collective-permute-start(bf16[2,104,1024]{2,1,0:T(8,128)(2,1)} %pad_maximum_fusion.29), channel_id=1, source_target_pairs={{0,2},{2,4},{4,6},{6,0},{1,3},{3,5},{5,7},{7,1},{8,10},{10,12},{12... | collective-permute-start | bytes 1277960 | tf_op jit(solution)/shard_map/ppermute | solution.py:58
  164.3 28.9 %collective-permute-start.31 = (bf16[2,104,1024]{2,1,0:T(8,128)(2,1)}, bf16[2,104,1024]{2,1,0:T(8,128)(2,1)}, u32[]{:S(2)}, u32[]{:S(2)}) collective-permute-start(bf16[2,104,1024]{2,1,0:T(8,128)(2,1)} %pad_maximum_fusion.31), channel_id=1, source_target_pairs={{0,6},{2,0},{4,2},{6,4},{1,7},{3,1},{5,3},{7,5},{8,14},{10,8},{12,... | collective-permute-start | bytes 1277960 | tf_op jit(solution)/shard_map/ppermute | solution.py:58
  167.5 22.7 %collective-permute-start.28 = (bf16[4,64,1024]{2,1,0:T(8,128)(2,1)}, bf16[4,64,1024]{2,1,0:T(8,128)(2,1)}, u32[]{:S(2)}, u32[]{:S(2)}) collective-permute-start(bf16[4,64,1024]{2,1,0:T(8,128)(2,1)} %pad_maximum_fusion.20), channel_id=1, source_target_pairs={{0,8},{8,0},{1,9},{9,1},{2,10},{10,2},{3,11},{11,3},{4,12},{12,4},... | collective-permute-start | bytes 1572872 | tf_op jit(solution)/shard_map/ppermute | solution.py:58
  168.0 23.6 %collective-permute-start.29 = (bf16[4,64,1024]{2,1,0:T(8,128)(2,1)S(1)}, bf16[4,64,1024]{2,1,0:T(8,128)(2,1)}, u32[]{:S(2)}, u32[]{:S(2)}) collective-permute-start(bf16[4,64,1024]{2,1,0:T(8,128)(2,1)S(1)} %pad_maximum_fusion.21), channel_id=1, source_target_pairs={{0,16},{16,0},{1,17},{17,1},{2,18},{18,2},{3,19},{19,3},{4,20},{20... | collective-permute-start | bytes 1572872 | tf_op jit(solution)/shard_map/ppermute | solution.py:58
  193.2 24.3 %collective-permute-start.34 = (bf16[2,4,64,1024]{3,2,1,0:T(8,128)(2,1)S(1)}, bf16[2,4,64,1024]{3,2,1,0:T(8,128)(2,1)S(1)}, u32[]{:S(2)}, u32[]{:S(2)}) collective-permute-start(bf16[2,4,64,1024]{3,2,1,0:T(8,128)(2,1)S(1)} %pad_maximum_fusion.10.refs_0_), channel_id=1, source_target_pairs={{0,1},{1,0},{2,3},{3,2},{4,5},{5,4},{6,7},{7,6},{8,9},{9,8},{10,11... | collective-permute-start | bytes 3145736 | tf_op jit(solution)/shard_map/ppermute | solution.py:58
  193.3 25.6 %collective-permute-start.32 = (bf16[2,4,64,1024]{3,2,1,0:T(8,128)(2,1)S(1)}, bf16[2,4,64,1024]{3,2,1,0:T(8,128)(2,1)S(1)}, u32[]{:S(2)}, u32[]{:S(2)}) collective-permute-start(bf16[2,4,64,1024]{3,2,1,0:T(8,128)(2,1)S(1)} %pad_maximum_fusion.10.refs_0_), channel_id=1, source_target_pairs={{0,16},{16,0},{1,17},{17,1},{2,18},{18,2},{3,19},{19,3},{4,20},{20... | collective-permute-start | bytes 3145736 | tf_op jit(solution)/shard_map/ppermute | solution.py:58
  193.9 25.0 %collective-permute-start.35 = (bf16[2,4,64,1024]{3,2,1,0:T(8,128)(2,1)S(1)}, bf16[2,4,64,1024]{3,2,1,0:T(8,128)(2,1)S(1)}, u32[]{:S(2)}, u32[]{:S(2)}) collective-permute-start(bf16[2,4,64,1024]{3,2,1,0:T(8,128)(2,1)S(1)} %pad_maximum_fusion.11.refs_4_), channel_id=1, source_target_pairs={{0,1},{1,0},{2,3},{3,2},{4,5},{5,4},{6,7},{7,6},{8,9},{9,8},{10,11... | collective-permute-start | bytes 3145736 | tf_op jit(solution)/shard_map/ppermute | solution.py:58
  194.0 25.5 %collective-permute-start.33 = (bf16[2,4,64,1024]{3,2,1,0:T(8,128)(2,1)S(1)}, bf16[2,4,64,1024]{3,2,1,0:T(8,128)(2,1)}, u32[]{:S(2)}, u32[]{:S(2)}) collective-permute-start(bf16[2,4,64,1024]{3,2,1,0:T(8,128)(2,1)S(1)} %pad_maximum_fusion.11.refs_4_), channel_id=1, source_target_pairs={{0,8},{8,0},{1,9},{9,1},{2,10},{10,2},{3,11},{11,3},{4,12},{12,4},... | collective-permute-start | bytes 3145736 | tf_op jit(solution)/shard_map/ppermute | solution.py:58
  261.4 26.5 %collective-permute-start.40 = (bf16[2,4,64,1024]{3,2,1,0:T(8,128)(2,1)S(1)}, bf16[2,4,64,1024]{3,2,1,0:T(8,128)(2,1)}, u32[]{:S(2)}, u32[]{:S(2)}) collective-permute-start(bf16[2,4,64,1024]{3,2,1,0:T(8,128)(2,1)S(1)} %get-tuple-element.435), channel_id=1, source_target_pairs={{0,16},{16,0},{1,17},{17,1},{2,18},{18,2},{3,19},{19,3},{4,20},{20... | collective-permute-start | bytes 3145736 | tf_op jit(solution)/shard_map/ppermute | solution.py:58
  262.9 24.9 %collective-permute-start.41 = (bf16[2,4,64,1024]{3,2,1,0:T(8,128)(2,1)S(1)}, bf16[2,4,64,1024]{3,2,1,0:T(8,128)(2,1)}, u32[]{:S(2)}, u32[]{:S(2)}) collective-permute-start(bf16[2,4,64,1024]{3,2,1,0:T(8,128)(2,1)S(1)} %copy-done.83), channel_id=1, source_target_pairs={{0,8},{8,0},{1,9},{9,1},{2,10},{10,2},{3,11},{11,3},{4,12},{12,4},... | collective-permute-start | bytes 3145736 | tf_op jit(solution)/shard_map/ppermute | solution.py:58
  265.5 22.3 %collective-permute-start.43 = (bf16[2,104,1024]{2,1,0:T(8,128)(2,1)S(1)}, bf16[2,104,1024]{2,1,0:T(8,128)(2,1)S(1)}, u32[]{:S(2)}, u32[]{:S(2)}) collective-permute-start(bf16[2,104,1024]{2,1,0:T(8,128)(2,1)S(1)} %get-tuple-element.678), channel_id=1, source_target_pairs={{0,2},{2,4},{4,6},{6,0},{1,3},{3,5},{5,7},{7,1},{8,10},{10,12},{12... | collective-permute-start | bytes 1277960 | tf_op jit(solution)/shard_map/ppermute | solution.py:58
  291.5 23.6 %collective-permute-start.46 = (bf16[512,4096]{1,0:T(8,128)(2,1)S(1)}, bf16[512,4096]{1,0:T(8,128)(2,1)}, u32[]{:S(2)}, u32[]{:S(2)}) collective-permute-start(bf16[512,4096]{1,0:T(8,128)(2,1)S(1)} %copy-done.34), channel_id=1, source_target_pairs={{0,1},{1,0},{2,3},{3,2},{4,5},{5,4},{6,7},{7,6},{8,9},{9,8},{10,11... | collective-permute-start | bytes 12582920 | tf_op jit(solution)/shard_map/ppermute | solution.py:58
  291.6 23.5 %collective-permute-start.44 = (bf16[4,64,1024]{2,1,0:T(8,128)(2,1)S(1)}, bf16[4,64,1024]{2,1,0:T(8,128)(2,1)S(1)}, u32[]{:S(2)}, u32[]{:S(2)}) collective-permute-start(bf16[4,64,1024]{2,1,0:T(8,128)(2,1)S(1)} %get-tuple-element.448), channel_id=1, source_target_pairs={{0,8},{8,0},{1,9},{9,1},{2,10},{10,2},{3,11},{11,3},{4,12},{12,4},... | collective-permute-start | bytes 1572872 | tf_op jit(solution)/shard_map/ppermute | solution.py:58
  292.9 22.2 %collective-permute-start.45 = (bf16[4,64,1024]{2,1,0:T(8,128)(2,1)S(1)}, bf16[4,64,1024]{2,1,0:T(8,128)(2,1)S(1)}, u32[]{:S(2)}, u32[]{:S(2)}) collective-permute-start(bf16[4,64,1024]{2,1,0:T(8,128)(2,1)S(1)} %get-tuple-element.450), channel_id=1, source_target_pairs={{0,16},{16,0},{1,17},{17,1},{2,18},{18,2},{3,19},{19,3},{4,20},{20... | collective-permute-start | bytes 1572872 | tf_op jit(solution)/shard_map/ppermute | solution.py:58
  326.3 40.7 %collective-permute-start.48 = (bf16[2,4,16,4096]{3,2,1,0:T(8,128)(2,1)S(1)}, bf16[2,4,16,4096]{3,2,1,0:T(8,128)(2,1)S(1)}, u32[]{:S(2)}, u32[]{:S(2)}) collective-permute-start(bf16[2,4,16,4096]{3,2,1,0:T(8,128)(2,1)S(1)} %get-tuple-element.467), channel_id=1, source_target_pairs={{0,16},{16,0},{1,17},{17,1},{2,18},{18,2},{3,19},{19,3},{4,20},{20... | collective-permute-start | bytes 3145736 | tf_op jit(solution)/shard_map/ppermute | solution.py:58
  327.9 39.2 %collective-permute-start.49 = (bf16[2,4,16,4096]{3,2,1,0:T(8,128)(2,1)S(1)}, bf16[2,4,16,4096]{3,2,1,0:T(8,128)(2,1)S(1)}, u32[]{:S(2)}, u32[]{:S(2)}) collective-permute-start(bf16[2,4,16,4096]{3,2,1,0:T(8,128)(2,1)S(1)} %copy-done.82), channel_id=1, source_target_pairs={{0,8},{8,0},{1,9},{9,1},{2,10},{10,2},{3,11},{11,3},{4,12},{12,4},... | collective-permute-start | bytes 3145736 | tf_op jit(solution)/shard_map/ppermute | solution.py:58
  328.6 38.4 %collective-permute-start.50 = (bf16[128,1024]{1,0:T(8,128)(2,1)S(1)}, bf16[128,1024]{1,0:T(8,128)(2,1)S(1)}, u32[]{:S(2)}, u32[]{:S(2)}) collective-permute-start(bf16[128,1024]{1,0:T(8,128)(2,1)S(1)} %pad_maximum_fusion.35), channel_id=1, source_target_pairs={{0,2},{2,4},{4,6},{6,0},{1,3},{3,5},{5,7},{7,1},{8,10},{10,12},{12... | collective-permute-start | bytes 786440 | tf_op jit(solution)/shard_map/ppermute | solution.py:58
  328.6 38.4 %collective-permute-start.51 = (bf16[128,1024]{1,0:T(8,128)(2,1)S(1)}, bf16[128,1024]{1,0:T(8,128)(2,1)S(1)}, u32[]{:S(2)}, u32[]{:S(2)}) collective-permute-start(bf16[128,1024]{1,0:T(8,128)(2,1)S(1)} %pad_maximum_fusion.36), channel_id=1, source_target_pairs={{0,4},{2,6},{4,0},{6,2},{1,5},{3,7},{5,1},{7,3},{8,12},{10,14},{12... | collective-permute-start | bytes 786440 | tf_op jit(solution)/shard_map/ppermute | solution.py:58
  330.3 36.7 %collective-permute-start.52 = (bf16[128,1024]{1,0:T(8,128)(2,1)S(1)}, bf16[128,1024]{1,0:T(8,128)(2,1)S(1)}, u32[]{:S(2)}, u32[]{:S(2)}) collective-permute-start(bf16[128,1024]{1,0:T(8,128)(2,1)S(1)} %pad_maximum_fusion.37), channel_id=1, source_target_pairs={{0,6},{2,0},{4,2},{6,4},{1,7},{3,1},{5,3},{7,5},{8,14},{10,8},{12,... | collective-permute-start | bytes 786440 | tf_op jit(solution)/shard_map/ppermute | solution.py:58
  410.8 23.4 %collective-permute-start.59 = (bf16[2,4,16,3072]{3,2,1,0:T(8,128)(2,1)}, bf16[2,4,16,3072]{3,2,1,0:T(8,128)(2,1)}, u32[]{:S(2)}, u32[]{:S(2)}) collective-permute-start(bf16[2,4,16,3072]{3,2,1,0:T(8,128)(2,1)} %get-tuple-element.530), channel_id=1, source_target_pairs={{0,16},{16,0},{1,17},{17,1},{2,18},{18,2},{3,19},{19,3},{4,20},{20... | collective-permute-start | bytes 2359304 | tf_op jit(solution)/shard_map/ppermute | solution.py:58
  412.3 21.9 %collective-permute-start.60 = (bf16[2,4,16,3072]{3,2,1,0:T(8,128)(2,1)}, bf16[2,4,16,3072]{3,2,1,0:T(8,128)(2,1)}, u32[]{:S(2)}, u32[]{:S(2)}) collective-permute-start(bf16[2,4,16,3072]{3,2,1,0:T(8,128)(2,1)} %get-tuple-element.532), channel_id=1, source_target_pairs={{0,8},{8,0},{1,9},{9,1},{2,10},{10,2},{3,11},{11,3},{4,12},{12,4},... | collective-permute-start | bytes 2359304 | tf_op jit(solution)/shard_map/ppermute | solution.py:58
  449.2 24.1 %collective-permute-start.76 = (bf16[4,104,1024]{2,1,0:T(8,128)(2,1)S(1)}, bf16[4,104,1024]{2,1,0:T(8,128)(2,1)S(1)}, u32[]{:S(2)}, u32[]{:S(2)}) collective-permute-start(bf16[4,104,1024]{2,1,0:T(8,128)(2,1)S(1)} %get-tuple-element.672), channel_id=1, source_target_pairs={{0,1},{1,0},{2,3},{3,2},{4,5},{5,4},{6,7},{7,6},{8,9},{9,8},{10,11... | collective-permute-start | bytes 2555912 | tf_op jit(solution)/shard_map/ppermute | solution.py:58
  (132 other events, 1465.9 us)

commit v5 on v4

--- a/solution.py
+++ b/solution.py
@@ -117,8 +117,13 @@
                 found += [(part, step, one) for one in range(sizes[ORDERS[part][0]])]
         return found
 
-    def flat_sources(self, near, near_core, far, far_core):
-        return [(near, 0, self.labels(False)), (far, 0, self.labels(True)), (near_core, 1, self.labels(False)), (far_core, 1, self.labels(True))]
+    def near_flat_sources(self, near, near_core, second, traded_second):
+        found = [(near, 0, self.labels(False)), (near_core, 1, self.labels(False))]
+        for turn, groups in enumerate((second, traded_second)):
+            for part in range(2):
+                for step, g in enumerate(groups[part]):
+                    found.append((g, turn, [(part, step + 1, one) for one in range(g.shape[0])]))
+        return found
 
     def assemble(self, sources, widths):
         place = self.place()
@@ -192,12 +197,14 @@
             index = index // sizes[axis]
         return ((out["sc"] * sizes["gy"] + out["gy"]) * sizes["gx"] + out["gx"]) * sizes["sz"] + out["sz"]
 
-    def by_distance(self, array):
+    def target(self, width):
+        block = width // self.count
+        row = lax.broadcasted_iota(jnp.int32, (width, 1), 0)
+        return self.far(row // block) * block + row % block
+
+    def by_distance(self, array, target):
         tokens, width = array.shape
-        block = width // self.count
         half = width // 2
-        row = lax.broadcasted_iota(jnp.int32, (width, 1), 0)
-        target = self.far(row // block) * block + row % block
 
         def body(x_ref, t_ref, o_ref):
             columns = lax.broadcasted_iota(jnp.int32, (width, half), 1) + half * pl.program_id(0)
@@ -458,7 +465,17 @@
     )(qkv, qkv, qkv)
 
 
-def attend_back_body(q_ref, k_ref, v_ref, l_ref, g_ref, d_ref, s_ref):
+def attend_back_body(q_ref, k_ref, v_ref, l_ref, g_ref, *rest):
+    d_ref, s_ref = rest[-2:]
+    base = 0
+    if len(rest) == 4:
+        base = rest[0].shape[1]
+
+        @pl.when(pl.program_id(0) == 0)
+        def _():
+            d_ref[:, :base] = rest[0][...]
+            s_ref[:, :base] = rest[1][...]
+
     scale = jnp.asarray(HD**-0.5, bf16)
     query, key, value, grad = q_ref[...] * scale, k_ref[...], v_ref[...], g_ref[...]
     key_t = flip(key)
@@ -480,25 +497,26 @@
         jnp.where(first, grad_value[0], grad_value[1]),
     )
     for kind, array in enumerate(grads):
-        i = pl.program_id(0)
-        start = pl.multiple_of((i // CUT * 3 * CUT + i % CUT + kind * CUT) * 2 * HD, 2 * HD)
+        start = pl.multiple_of(base + (pl.program_id(0) + kind * CUT) * 2 * HD, 2 * HD)
         low = array.astype(bf16)
         d_ref[:, pl.ds(start, 2 * HD)] = low
         s_ref[:, pl.ds(start, 2 * HD)] = jnp.sum(low.astype(f32), axis=0, keepdims=True)
 
 
-def attend_back(qkv, logs, grad_mixed):
-    shape = qkv.shape
+def attend_back(qkv, logs, grad_mixed, before=()):
+    base = CUT if before else 0
+    width = qkv.shape[1] // (1 if before else 2)
     return pl.pallas_call(
         attend_back_body,
-        out_shape=[jax.ShapeDtypeStruct(shape, bf16), jax.ShapeDtypeStruct((1, shape[1]), f32)],
-        grid=(PAIRS,),
-        in_specs=[kind_spec(0), kind_spec(1), kind_spec(2), log_spec(), pair_spec()],
-        out_specs=[pl.BlockSpec(shape, lambda i: (0, 0)), pl.BlockSpec((1, shape[1]), lambda i: (0, 0))],
+        out_shape=[jax.ShapeDtypeStruct((PACKED, width), bf16), jax.ShapeDtypeStruct((1, width), f32)],
+        grid=(CUT,),
+        in_specs=[kind_spec(0, base), kind_spec(1, base), kind_spec(2, base), log_spec(base), pair_spec(base)]
+        + [pl.BlockSpec(array.shape, lambda i: (0, 0)) for array in before],
+        out_specs=[pl.BlockSpec((PACKED, width), lambda i: (0, 0)), pl.BlockSpec((1, width), lambda i: (0, 0))],
         compiler_params=room(),
         cost_estimate=cost(12e9, 8 * qkv.size, PACKED * PACKED * H // 2),
         name="attend_back",
-    )(qkv, qkv, qkv, logs, grad_mixed)
+    )(qkv, qkv, qkv, logs, grad_mixed, *before)
 
 
 def rise(normed, weights, bias, ranks):
@@ -885,29 +903,32 @@
     column = ring.spread(two, outer)
     pieces = ring.paired(stay, came)
     cot_pieces = ring.paired(cot_stay, cot_came)
-    one, two, column, pieces, cot_pieces = tie(one, two, column, pieces, cot_pieces)
+    one_near = ring.flat([[half] for half in one])
+    target = ring.target(width)
+    one, one_near, two, column, pieces, cot_pieces, target = tie(one, one_near, two, column, pieces, cot_pieces, target)
 
     one_more = ring.plane(one)
-    one_core = ring.to_core([[half] for half in one])
+    one_core = ring.swap(one_near)
+    rest = ring.send(pieces, outer[:1])
     column.update(ring.spread(two, inner))
     two = ring.along(two, column)
-    one, one_more, one_core, two, pieces, cot_pieces = tie(one, one_more, one_core, two, pieces, cot_pieces)
+    one_near, one_more, one_core, two, pieces, rest, cot_pieces = tie(one_near, one_more, one_core, two, pieces, rest, cot_pieces)
 
     one_more_core = ring.to_core(one_more)
     two = ring.across(two)
-    rest = ring.send(pieces, outer[:1])
-    one, one_more, one_core, one_more_core, two, pieces, three = tie(one, one_more, one_core, one_more_core, two, pieces, w_down)
-
-    two_near = ring.flat([[half] for half in two])
+    rest.update(ring.send(pieces, outer[1:]))
+    one_near, one_more, one_core, one_more_core, two, pieces, rest, three = tie(
+        one_near, one_more, one_core, one_more_core, two, pieces, rest, w_down
+    )
+
+    two_core = ring.to_core([[half] for half in two])
     two_more = ring.plane(two)
-    rest.update(ring.send(pieces, everything[1:]))
-    full_qkv, vectors = ring.assemble(ring.sources(one, one_core, one_more, one_more_core), [3 * width, SMALL])
-    two_more = ring.flat(two_more)
-    two_near, two_more, rest, full_qkv, vectors, three = tie(two_near, two_more, rest, full_qkv, vectors, three)
+    rest.update(ring.send(pieces, inner))
+    full_qkv, vectors = ring.assemble(ring.near_flat_sources(one_near, one_core, one_more, one_more_core), [3 * width, SMALL])
+    two, two_core, two_more, rest, full_qkv, vectors, three = tie(two, two_core, two_more, rest, full_qkv, vectors, three)
 
     column = ring.spread(three, everything)
-    two_core = ring.swap(two_near)
-    two_more_core = ring.swap(two_more)
+    two_more_core = ring.to_core(two_more)
     image_slots = jnp.concatenate([pieces[0]] + [rest[k] for k in everything]).reshape(group * slots, width)
     vectors = vectors.reshape(ring.count, rows, SMALL).astype(f32)
     bu = vectors[:, 0, 128 : 128 + wide * rows].reshape(ff)
@@ -923,13 +944,13 @@
     qkv = project(normed, full_qkv, qkv_bias)
     mixed, logs = attend(qkv)
     three = ring.along(three, column)
-    two_core, two_more_core, three, mixed = tie(two_core, two_more_core, three, mixed)
+    two_more_core, three, mixed = tie(two_more_core, three, mixed)
 
     three = ring.across(three)
     cot_rest = ring.send(cot_pieces, outer)
-    full_out, full_up = ring.assemble(ring.flat_sources(two_near, two_core, two_more, two_more_core), [width, ff])
+    full_out, full_up = ring.assemble(ring.sources(two, two_core, two_more, two_more_core), [width, ff])
     residual, normed_two = out_norm(mixed, full_out, tokens_f, bo, g2, s2)
-    normed_far = ring.by_distance(normed)
+    normed_far = ring.by_distance(normed, target)
     three, normed_two, normed_far, cot_rest = tie(three, normed_two, normed_far, cot_rest)
 
     three_more = ring.plane(three)
@@ -938,9 +959,9 @@
     ranks = ring.far(lax.broadcasted_iota(jnp.int32, (ring.count,), 0))
     active, slope, active_far = rise(normed_two, full_up, bu, ranks)
     if active_far is None:
-        active_far = ring.by_distance(active)
-    mixed_far = ring.by_distance(mixed)
-    two_far = ring.by_distance(normed_two)
+        active_far = ring.by_distance(active, ring.target(ff))
+    mixed_far = ring.by_distance(mixed, target)
+    two_far = ring.by_distance(normed_two, target)
     three, three_more, three_core, active, active_far, mixed_far, two_far, cot_rest = tie(
         three, three_more, three_core, active, active_far, mixed_far, two_far, cot_rest
     )
@@ -981,27 +1002,35 @@
     d, u, sent, residual_low = tie(d, u, sent, residual_low)
 
     u = ring.first(u)
-    d = ring.third(d)
+    gone = ring.toward_some(d, outer)
     grad_mixed = back_project(residual_low, full_out)
     sent_out = sent
-    grads, grad_sums = attend_back(qkv, logs, grad_mixed)
+    half_grads = attend_back(qkv, logs, grad_mixed)
+    u, sent_out, d, gone, grad_mixed, half_grads = tie(u, sent_out, d, gone, grad_mixed, half_grads)
+
+    u = ring.again(u)
+    u, sent_out, back, d, grad_mixed, half_grads = tie(u, sent_out, back, d, grad_mixed, half_grads)
+
+    u = ring.second(u)
+    gone.update(ring.toward_some(d, inner))
+    o = ring.swap(sent_out)
+    grads, grad_sums = attend_back(qkv, logs, grad_mixed, half_grads)
     sent = weight_grad(normed_far, 1, grads, share)
-    u, sent_out, sent, d, grads = tie(u, sent_out, sent, d, grads)
-
-    u = ring.again(u)
-    u, sent_out, sent, grads, back = tie(u, sent_out, sent, grads, back)
-
-    u = ring.second(u)
-    o = ring.swap(sent_out)
+    u, o, sent, grads, back, d, gone = tie(u, o, sent, grads, back, d, gone)
+    d = [d[0]] + [gone[k] for k in everything]
+
+    u = ring.last(u)
+    u, sent, grads = tie(u, sent, grads)
+
+    later = ring.toward_some(u, outer)
     q = ring.swap(sent)
     grad_tokens, sums_one = back_norm([grads], full_qkv, tokens_f, g1, grad_residual, packing)
     grad_tokens = slots_of(grad_tokens)
-    u, o, q, grads, grad_tokens, sums_one, back, d = tie(u, o, q, grads, grad_tokens, sums_one, back, d)
+    u, later, o, q, grads, grad_tokens, sums_one, back, d = tie(u, later, o, q, grads, grad_tokens, sums_one, back, d)
 
     sent_back = ring.send(grad_tokens, outer, -1)
     q = ring.kept(normed_far, grads, share, q)
     o = ring.reshaped(weight_grad(mixed_far, 0, residual_low, share, o))
-    u = ring.last(u)
     joined_sum = whole(grad_sums[0])
     grad_bq, grad_bv = joined_sum[:width], joined_sum[2 * width :]
     small = [grad_bq, grad_bv, sums_two[2], grad_bd, sums_one[0], sums_one[1], sums_two[0], sums_two[1]]
@@ -1017,27 +1046,22 @@
     sent_back.update(ring.send(grad_tokens, inner, -1))
     came = ring.swap(small[1])
     own = jnp.stack([result[0]] + [back[k] for k in everything])
-    q, came, sent_back, u, back, d, own = tie(q, came, sent_back, u, back, d, own)
+    other = ring.swap(own[:, 1])
+    q, came, sent_back, u, back, d, own, other = tie(q, came, sent_back, u, back, d, own, other)
 
     q = ring.again(q)
-    q, u, own, d = tie(q, u, own, d)
-
-    q = ring.second(q)
-    later = ring.toward_some(u, outer)
-    other = ring.swap(own[:, 1])
     small = ring.reshaped(total([small[0], came]).astype(bf16))
     o = ring.ready(jnp.concatenate([o, small], axis=-1))
-    q, later, other, o, u, own, d = tie(q, later, other, o, u, own, d)
-
-    q = ring.last(q)
-    q, o, u, d = tie(q, o, u, d)
-
+    q, o, u, own, d = tie(q, o, u, own, d)
+
+    q = ring.second(q)
     o = ring.first(o)
     later.update(ring.toward_some(u, inner))
     result = ring.images_of(own[:, 0], other, images, twins)
     result = jnp.where(slot < counts[:, :, None], result, jnp.asarray(0, bf16))
     o, later, result, q, d = tie(o, later, result, q, d)
 
+    q = ring.last(q)
     o = ring.again(o)
     o, q, d = tie(o, q, d)
 

time: 505 us -> 501 us (level)
  starting transfers between devices: 93.9 us -> 82.6 us
  local copies, waits for them, and re-layouts: 26.1 us -> 35.1 us
  other arithmetic: 58.5 us -> 50.8 us
  waiting for transfers between devices: 117 us -> 124 us
    ppermute x80 -> x81, starting transfers between devices: 93.9 us -> 82.6 us  [shifted(): lax.ppermute(array, axis, [(i, (i + step) % size) for i in range(size)])]
    unnamed x184 -> x188, local copies, waits for them, and re-layouts: 13.6 us -> 20.8 us
    ppermute x80 -> x81, waiting for transfers between devices: 117 us -> 124 us  [shifted(): lax.ppermute(array, axis, [(i, (i + step) % size) for i in range(size)])]
    concatenate x2 -> x1, other arithmetic: 7.04 us -> 0.22 us  [flat(): return jnp.concatenate([group for part in groups for group in part], axis=0)]
    pallas_call x1 -> x2, Pallas kernels: 25.4 us -> 26.4 us  [attend_back(): pl.pallas_call(attend_back_body, out_shape=[jax.ShapeDtypeStruct((PACKED,...]
  transfers between devices with their start and end apart: 80 -> 81, of which waited for: 23 -> 25; matrix products, arithmetic and copies ran while one was open for 11% -> 9% of each run, Pallas kernels for 33% -> 34%
where the time goes in v5:
time: 501 us; the launch traced here: 493 us
  Pallas kernels  197 us (39%)
  waiting for transfers between devices  124 us (25%)
  starting transfers between devices  82.6 us (16%)
  other arithmetic  50.8 us (10%)
  local copies, waits for them, and re-layouts  35.1 us (7%)
    ppermute x81, waiting for transfers between devices, shifted(): lax.ppermute(array, axis, [(i, (i + step) % size) for i in range(size)])  124 us
    ppermute x81, starting transfers between devices, shifted(): lax.ppermute(array, axis, [(i, (i + step) % size) for i in range(size)])  82.6 us
    pallas_call x8, Pallas kernels, weight_grad(): pl.pallas_call(body, out_shape=[jax.ShapeDtypeStruct(shape, bf16) for sha...  45.1 us
    pallas_call x2, Pallas kernels, attend_back(): pl.pallas_call(attend_back_body, out_shape=[jax.ShapeDtypeStruct((PACKED,...  26.4 us
    pallas_call x2, Pallas kernels, back_norm(): pl.pallas_call(body, out_shape=shapes + [jax.ShapeDtypeStruct((8, width),...  25.2 us
    pallas_call x3, Pallas kernels, assemble(): pl.pallas_call(body, out_shape=[jax.ShapeDtypeStruct((planes_all, depth,...  20.9 us
    unnamed x188, local copies, waits for them, and re-layouts  20.8 us
    pallas_call x1, Pallas kernels, rise(): pl.pallas_call(body, out_shape=shapes, grid_spec=pltpu.PrefetchScalarGrid...  15.4 us
  transfers between devices with their start and end apart: 81, of which 25 were waited for; matrix products, arithmetic and copies ran while one was open for 9% of the time, Pallas kernels for 34%

profile of v5, /device:TPU:0, one launch (start us, length us, event | category | flops | bytes accessed | tf_op | source)
XLA Modules:
  0.0 492.8 jit_solution(15906043890879788955)
XLA Ops:
  2.4 5.0 %collective-permute-start.2 = (bf16[32,3328]{1,0:T(8,128)(2,1)}, bf16[32,3328]{1,0:T(8,128)(2,1)}, u32[]{:S(2)}, u32[]{:S(2)}) collective-permute-start(bf16[32,3328]{1,0:T(8,128)(2,1)} %seed.1), channel_id=1, source_target_pairs={{0,6},{2,0},{4,2},{6,4},{1,7},{3,1},{5,3},{7,5},{8,14},{10,8},{12,... | collective-permute-start | bytes 638984 | tf_op jit(solution)/shard_map/ppermute | solution.py:58
  20.0 5.8 %collective-permute-done.1 = bf16[32,3328]{1,0:T(8,128)(2,1)} collective-permute-done((bf16[32,3328]{1,0:T(8,128)(2,1)}, bf16[32,3328]{1,0:T(8,128)(2,1)}, u32[]{:S(2)}, u32[]{:S(2)}) %collective-permute-start.1) | collective-permute-done | bytes 213024 | tf_op jit(solution)/shard_map/ppermute | solution.py:58
  48.6 20.4 %collective-permute-done.12 = bf16[32,5120]{1,0:T(8,128)(2,1)S(1)} collective-permute-done((bf16[32,5120]{1,0:T(8,128)(2,1)S(1)}, bf16[32,5120]{1,0:T(8,128)(2,1)S(1)}, u32[]{:S(2)}, u32[]{:S(2)}) %collective-permute-start.12) | collective-permute-done | bytes 327712 | tf_op jit(solution)/shard_map/ppermute | solution.py:58
  73.2 13.1 %collective-permute-done.16 = bf16[4,16,5120]{2,1,0:T(8,128)(2,1)S(1)} collective-permute-done((bf16[4,16,5120]{2,1,0:T(8,128)(2,1)S(1)}, bf16[4,16,5120]{2,1,0:T(8,128)(2,1)S(1)}, u32[]{:S(2)}, u32[]{:S(2)}) %collective-permute-start.16) | collective-permute-done | bytes 655392 | tf_op jit(solution)/shard_map/ppermute | solution.py:58
  98.7 5.4 %assemble.3 = (bf16[4,4,2,2,16,3072]{5,4,3,2,1,0:T(8,128)(2,1)}, bf16[4,4,2,2,16,256]{5,4,3,2,1,0:T(8,128)(2,1)S(1)}) custom-call(s32[32]{0:T(128)S(1)} %stack.422.table_ref, bf16[4,4,16,3328]{3,2,1,0:T(8,128)(2,1)} %copy-done.40, bf16[4,4,16,3328]{3,2,1,0:T(8,128)(2,1)} %copy-done.45, bf16[2,4,16,3328]{3,2,1,0:T(8,128)(2,1)S(1)} %collective-permute-done.9.refs_2_, ...), custom_call_target="tpu_custom_call" | custom-call | bytes 272629 | tf_op jit(solution)/shard_map/assemble/pallas_call | solution.py:171
  104.9 10.0 %collective-permute-done.23 = bf16[2,104,1024]{2,1,0:T(8,128)(2,1)} collective-permute-done((bf16[2,104,1024]{2,1,0:T(8,128)(2,1)}, bf16[2,104,1024]{2,1,0:T(8,128)(2,1)}, u32[]{:S(2)}, u32[]{:S(2)}) %collective-permute-start.23) | collective-permute-done | bytes 426016 | tf_op jit(solution)/shard_map/ppermute | solution.py:58
  114.9 5.9 %collective-permute-done.21.refs_1_ = bf16[2,4,16,5120]{3,2,1,0:T(8,128)(2,1)S(1)} collective-permute-done((bf16[2,4,16,5120]{3,2,1,0:T(8,128)(2,1)S(1)}, bf16[2,4,16,5120]{3,2,1,0:T(8,128)(2,1)S(1)}, u32[]{:S(2)}, u32[]{:S(2)}) %collective-permute-start.21) | collective-permute-done | bytes 1310752 | tf_op jit(solution)/shard_map/ppermute | solution.py:58
  135.6 7.6 %project.1.q_ref.k_ref.v_ref = bf16[592,3072]{1,0:T(8,128)(2,1)} custom-call(bf16[592,1024]{1,0:T(8,128)(2,1)S(1)} %get-tuple-element.381.x_ref, bf16[1024,3072]{1,0:T(8,128)(2,1)} %bitcast.260, f32[1,3072]{1,0:T(1,128)S(1)} %reshape_reshape.3.b_ref), custom_call_target="tpu_custom_call" | custom-call | flops 120000000 | bytes 240000 | tf_op jit(solution)/shard_map/project/pallas_call | solution.py:625
  144.2 14.1 %attend.1 = (bf16[592,1024]{1,0:T(8,128)(2,1)S(1)}, f32[64,592]{1,0:T(8,128)S(1)}) custom-call(bf16[592,3072]{1,0:T(8,128)(2,1)} %project.1.q_ref.k_ref.v_ref, bf16[592,3072]{1,0:T(8,128)(2,1)} %project.1.q_ref.k_ref.v_ref, bf16[592,3072]{1,0:T(8,128)(2,1)} %project.1.q_ref.k_ref.v_ref), custom_call_target="tpu_custom_call" | custom-call | flops 240000000 | bytes 290979 | tf_op jit(solution)/shard_map/attend/pallas_call | solution.py:453
  172.7 8.8 %assemble.4 = (bf16[4,4,2,2,16,1024]{5,4,3,2,1,0:T(8,128)(2,1)}, bf16[4,4,2,2,16,4096]{5,4,3,2,1,0:T(8,128)(2,1)}) custom-call(s32[32]{0:T(128)S(1)} %stack.439.table_ref, bf16[2,4,16,5120]{3,2,1,0:T(8,128)(2,1)S(1)} %copy-done.11, bf16[2,4,16,5120]{3,2,1,0:T(8,128)(2,1)S(1)} %copy-done.21, bf16[2,4,16,5120]{3,2,1,0:T(8,128)(2,1)} %collective-permute-done.19.refs_2_, ...), custom_call_target="tpu_custom_call" | custom-call | bytes 419430 | tf_op jit(solution)/shard_map/assemble/pallas_call | solution.py:171
  181.5 5.1 %out_norm.1 = (f32[592,1024]{1,0:T(8,128)}, bf16[592,1024]{1,0:T(8,128)(2,1)S(1)}) custom-call(bf16[592,1024]{1,0:T(8,128)(2,1)S(1)} %copy-done.15, bf16[1024,1024]{1,0:T(8,128)(2,1)} %bitcast.262, f32[592,1024]{1,0:T(8,128)} %get-tuple-element.394.t_ref.refs_2_, f32[1,1024]{1,0:T(1,128)S(1)} %reshape_reshape_squeeze.25.b_ref, ...), custom_call_target="tpu_custom_call" | custom-call | flops 40000000 | bytes 160000 | tf_op jit(solution)/shard_map/out_norm/pallas_call | solution.py:724
  197.4 15.4 %rise.1 = (bf16[592,4096]{1,0:T(8,128)(2,1)}, f32[592,4096]{1,0:T(8,128)}, bf16[2,592,2048]{2,1,0:T(8,128)(2,1)}) custom-call(s32[32]{0:T(128)S(1)} %fusion.92.rank_ref, bf16[592,1024]{1,0:T(8,128)(2,1)S(1)} %get-tuple-element.402.x_ref, bf16[1024,4096]{1,0:T(8,128)(2,1)} %bitcast.258, f32[1,4096]{1,0:T(1,128)S(1)} %slice_bitcast_fusion.36.b_ref), custom_call_target="tpu_custom_call" | custom-call | flops 240000000 | bytes 600000 | tf_op jit(solution)/shard_map/rise/pallas_call | solution.py:572
  220.6 7.1 %weight_grad.8 = bf16[2048,1024]{1,0:T(8,128)(2,1)} custom-call(bf16[2,592,2048]{2,1,0:T(8,128)(2,1)} %get-tuple-element.409.refs_0_, bf16[592,1024]{1,0:T(8,128)(2,1)S(1)} %get-tuple-element.417.refs_1_.g_ref.refs_4_), custom_call_target="tpu_custom_call" | custom-call | flops 49660560 | bytes 167772 | tf_op jit(solution)/shard_map/weight_grad/pallas_call | solution.py:371
  231.6 6.7 %assemble.5 = bf16[4,4,2,2,64,1024]{5,4,3,2,1,0:T(8,128)(2,1)} custom-call(s32[32]{0:T(128)S(1)} %stack.439.table_ref, bf16[2,4,64,1024]{3,2,1,0:T(8,128)(2,1)S(1)} %copy-done.17, bf16[2,4,64,1024]{3,2,1,0:T(8,128)(2,1)S(1)} %copy-done.25, bf16[2,4,64,1024]{3,2,1,0:T(8,128)(2,1)S(1)} %collective-permute-done.35.refs_2_, bf16[2,4,64,1024]{3,2,1,0:T(8,128)(2,1)} %copy-done.55, ...), custom_call_target="tpu_custom_call" | custom-call | bytes 335544 | tf_op jit(solution)/shard_map/assemble/pallas_call | solution.py:171
  238.3 7.7 %weight_grad.9 = (bf16[2,4,64,1024]{3,2,1,0:T(8,128)(2,1)S(1)}, bf16[2,4,64,1024]{3,2,1,0:T(8,128)(2,1)S(1)}, bf16[2,4,64,1024]{3,2,1,0:T(8,128)(2,1)S(1)}, bf16[2,4,64,1024]{3,2,1,0:T(8,128)(2,1)}) custom-call(bf16[2,592,2048]{2,1,0:T(8,128)(2,1)} %get-tuple-element.409.refs_0_, bf16[592,1024]{1,0:T(8,128)(2,1)} %copy-done, ...), custom_call_target="tpu_custom_call" | custom-call | flops 49660560 | bytes 167772 | tf_op jit(solution)/shard_map/weight_grad/pallas_call | solution.py:371
  246.0 11.4 %land.1 = bf16[832,1024]{1,0:T(8,128)(2,1)S(1)} custom-call(bf16[592,4096]{1,0:T(8,128)(2,1)} %get-tuple-element.430.a_ref, bf16[4096,1024]{1,0:T(8,128)(2,1)} %bitcast.256, f32[592,1024]{1,0:T(8,128)} %get-tuple-element.432.r_ref.refs_2_, f32[1,1024]{1,0:T(1,128)S(1)} %reshape_reshape_squeeze.29.b_ref, bf16[592,832]{1,0:T(8,128)(2,1)S(1)} %fusion.p_ref.refs_5_), custom_call_target="tpu_custom_call" | custom-call | flops 120000000 | bytes 280000 | tf_op jit(solution)/shard_map/land/pallas_call | solution.py:757
  260.3 4.2 collective-permute-start.43
  264.5 11.1 %fall.1 = (bf16[592,4096]{1,0:T(8,128)(2,1)}, f32[1,4096]{1,0:T(1,128)S(1)}) custom-call(bf16[592,1024]{1,0:T(8,128)(2,1)S(1)} %copy-done.1, bf16[4096,1024]{1,0:T(8,128)(2,1)} %bitcast.257, f32[592,4096]{1,0:T(8,128)} %get-tuple-element.438.slope_ref), custom_call_target="tpu_custom_call" | custom-call | flops 200000000 | bytes 500000 | tf_op jit(solution)/shard_map/fall/pallas_call | solution.py:602
  275.6 7.1 %weight_grad.10 = bf16[512,4096]{1,0:T(8,128)(2,1)} custom-call(bf16[2,592,512]{2,1,0:T(8,128)(2,1)S(1)} %copy-done.7, bf16[592,4096]{1,0:T(8,128)(2,1)} %get-tuple-element.439.refs_1_.refs_0_), custom_call_target="tpu_custom_call" | custom-call | flops 49660560 | bytes 167772 | tf_op jit(solution)/shard_map/weight_grad/pallas_call | solution.py:371
  289.6 13.2 %back_norm.2 = (f32[592,1024]{1,0:T(8,128)}, bf16[592,1024]{1,0:T(8,128)(2,1)S(1)}, f32[8,1024]{1,0:T(8,128)S(1)}) custom-call(bf16[592,4096]{1,0:T(8,128)(2,1)} %get-tuple-element.439.refs_1_.refs_0_, bf16[1024,4096]{1,0:T(8,128)(2,1)} %bitcast.259, f32[592,1024]{1,0:T(8,128)} %get-tuple-element.432.r_ref.refs_2_, ...), custom_call_target="tpu_custom_call" | custom-call | flops 120000000 | bytes 400000 | tf_op jit(solution)/shard_map/back_norm/pallas_call | solution.py:829
  302.8 6.1 %collective-permute-done.48 = bf16[2,104,1024]{2,1,0:T(8,128)(2,1)S(1)} collective-permute-done((bf16[2,104,1024]{2,1,0:T(8,128)(2,1)S(1)}, bf16[2,104,1024]{2,1,0:T(8,128)(2,1)S(1)}, u32[]{:S(2)}, u32[]{:S(2)}) %collective-permute-start.48) | collective-permute-done | bytes 426016 | tf_op jit(solution)/shard_map/ppermute | solution.py:58
  309.7 7.5 %weight_grad.11 = (bf16[2,4,16,4096]{3,2,1,0:T(8,128)(2,1)S(1)}, bf16[2,4,16,4096]{3,2,1,0:T(8,128)(2,1)S(1)}, bf16[2,4,16,4096]{3,2,1,0:T(8,128)(2,1)S(1)}, bf16[2,4,16,4096]{3,2,1,0:T(8,128)(2,1)}) custom-call(bf16[2,592,512]{2,1,0:T(8,128)(2,1)} %copy-done.6, bf16[592,4096]{1,0:T(8,128)(2,1)} %get-tuple-element.439.refs_1_.refs_0_, ...), custom_call_target="tpu_custom_call" | custom-call | flops 49660560 | bytes 167772 | tf_op jit(solution)/shard_map/weight_grad/pallas_call | solution.py:371
  329.6 12.2 %attend_back.2 = (bf16[592,1536]{1,0:T(8,128)(2,1)S(1)}, f32[1,1536]{1,0:T(1,128)S(1)}) custom-call(bf16[592,3072]{1,0:T(8,128)(2,1)} %project.1.q_ref.k_ref.v_ref, bf16[592,3072]{1,0:T(8,128)(2,1)} %project.1.q_ref.k_ref.v_ref, bf16[592,3072]{1,0:T(8,128)(2,1)} %project.1.q_ref.k_ref.v_ref, f32[64,592]{1,0:T(8,128)S(1)} %copy-done.33, ...), custom_call_target="tpu_custom_call" | custom-call | flops 240000000 | bytes 290979 | tf_op jit(solution)/shard_map/attend_back/pallas_call | solution.py:509
  349.9 14.2 %attend_back.3 = (bf16[592,3072]{1,0:T(8,128)(2,1)}, f32[1,3072]{1,0:T(1,128)S(1)}) custom-call(bf16[592,3072]{1,0:T(8,128)(2,1)} %project.1.q_ref.k_ref.v_ref, bf16[592,3072]{1,0:T(8,128)(2,1)} %project.1.q_ref.k_ref.v_ref, bf16[592,3072]{1,0:T(8,128)(2,1)} %project.1.q_ref.k_ref.v_ref, f32[64,592]{1,0:T(8,128)S(1)} %copy-done.33, ...), custom_call_target="tpu_custom_call" | custom-call | flops 240000000 | bytes 290979 | tf_op jit(solution)/shard_map/attend_back/pallas_call | solution.py:509
  364.1 6.0 %weight_grad.13 = bf16[512,3072]{1,0:T(8,128)(2,1)} custom-call(bf16[2,592,512]{2,1,0:T(8,128)(2,1)S(1)} %by_distance.3.refs_0_, bf16[592,3072]{1,0:T(8,128)(2,1)} %get-tuple-element.530.refs_1_.refs_0_), custom_call_target="tpu_custom_call" | custom-call | flops 37245420 | bytes 125829 | tf_op jit(solution)/shard_map/weight_grad/pallas_call | solution.py:371
  377.7 11.9 %back_norm.3 = (bf16[832,1024]{1,0:T(8,128)(2,1)S(1)}, f32[8,1024]{1,0:T(8,128)S(1)}) custom-call(bf16[592,3072]{1,0:T(8,128)(2,1)} %get-tuple-element.530.refs_1_.refs_0_, bf16[1024,3072]{1,0:T(8,128)(2,1)} %bitcast.261, f32[592,1024]{1,0:T(8,128)} %get-tuple-element.394.t_ref.refs_2_, f32[1,1024]{1,0:T(1,128)S(1)} %reshape_reshape_squeeze.23.g_ref.refs_3_, ...), custom_call_target="tpu_custom_call" | custom-call | flops 120000000 | bytes 400000 | tf_op jit(solution)/shard_map/back_norm/pallas_call | solution.py:829
  400.1 6.4 %weight_grad.14 = (bf16[2,4,16,3072]{3,2,1,0:T(8,128)(2,1)S(1)}, bf16[2,4,16,3072]{3,2,1,0:T(8,128)(2,1)}, bf16[2,4,16,3072]{3,2,1,0:T(8,128)(2,1)S(1)}, bf16[2,4,16,3072]{3,2,1,0:T(8,128)(2,1)S(1)}) custom-call(bf16[2,592,512]{2,1,0:T(8,128)(2,1)} %copy-done.2, bf16[592,3072]{1,0:T(8,128)(2,1)} %get-tuple-element.530.refs_1_.refs_0_, ...), custom_call_target="tpu_custom_call" | custom-call | flops 37245420 | bytes 125829 | tf_op jit(solution)/shard_map/weight_grad/pallas_call | solution.py:371
  407.0 6.4 %collective-permute-done.60 = bf16[2,104,1024]{2,1,0:T(8,128)(2,1)} collective-permute-done((bf16[2,104,1024]{2,1,0:T(8,128)(2,1)}, bf16[2,104,1024]{2,1,0:T(8,128)(2,1)}, u32[]{:S(2)}, u32[]{:S(2)}) %collective-permute-start.60) | collective-permute-done | bytes 426016 | tf_op jit(solution)/shard_map/ppermute | solution.py:58
  421.8 17.1 %collective-permute-done.65 = bf16[2,104,1024]{2,1,0:T(8,128)(2,1)} collective-permute-done((bf16[2,104,1024]{2,1,0:T(8,128)(2,1)}, bf16[2,104,1024]{2,1,0:T(8,128)(2,1)}, u32[]{:S(2)}, u32[]{:S(2)}) %collective-permute-start.65) | collective-permute-done | bytes 426016 | tf_op jit(solution)/shard_map/ppermute | solution.py:58
  456.1 5.4 %collective-permute-done.70 = bf16[4,16,3072]{2,1,0:T(8,128)(2,1)S(1)} collective-permute-done((bf16[4,16,3072]{2,1,0:T(8,128)(2,1)S(1)}, bf16[4,16,3072]{2,1,0:T(8,128)(2,1)S(1)}, u32[]{:S(2)}, u32[]{:S(2)}) %collective-permute-start.70) | collective-permute-done | bytes 393248 | tf_op jit(solution)/shard_map/ppermute | solution.py:58
  473.6 5.0 %collective-permute-done.73 = bf16[32,3072]{1,0:T(8,128)(2,1)S(1)} collective-permute-done((bf16[32,3072]{1,0:T(8,128)(2,1)S(1)}, bf16[32,3072]{1,0:T(8,128)(2,1)S(1)}, u32[]{:S(2)}, u32[]{:S(2)}) %collective-permute-start.73) | collective-permute-done | bytes 196640 | tf_op jit(solution)/shard_map/ppermute | solution.py:58
  478.7 4.7 collective-permute-start.78
  (504 shorter events, 201.9 us)
Async XLA Ops:
  45.5 23.6 %collective-permute-start.12 = (bf16[32,5120]{1,0:T(8,128)(2,1)S(1)}, bf16[32,5120]{1,0:T(8,128)(2,1)S(1)}, u32[]{:S(2)}, u32[]{:S(2)}) collective-permute-start(bf16[32,5120]{1,0:T(8,128)(2,1)S(1)} %pad_maximum_fusion.32), channel_id=1, source_target_pairs={{0,4},{2,6},{4,0},{6,2},{1,5},{3,7},{5,1},{7,3},{8,12},{10,14},{12... | collective-permute-start | bytes 983048 | tf_op jit(solution)/shard_map/ppermute | solution.py:58
  45.5 24.1 %collective-permute-start.13 = (bf16[2,104,1024]{2,1,0:T(8,128)(2,1)S(1)}, bf16[2,104,1024]{2,1,0:T(8,128)(2,1)S(1)}, u32[]{:S(2)}, u32[]{:S(2)}) collective-permute-start(bf16[2,104,1024]{2,1,0:T(8,128)(2,1)S(1)} %pad_maximum_fusion.24), channel_id=1, source_target_pairs={{0,2},{2,4},{4,6},{6,0},{1,3},{3,5},{5,7},{7,1},{8,10},{10,12},{12... | collective-permute-start | bytes 1277960 | tf_op jit(solution)/shard_map/ppermute | solution.py:58
  45.6 23.9 %collective-permute-start.9 = (bf16[2,4,16,3328]{3,2,1,0:T(8,128)(2,1)S(1)}, bf16[2,4,16,3328]{3,2,1,0:T(8,128)(2,1)S(1)}, u32[]{:S(2)}, u32[]{:S(2)}) collective-permute-start(bf16[2,4,16,3328]{3,2,1,0:T(8,128)(2,1)S(1)} %pad_maximum_fusion.15), channel_id=1, source_target_pairs={{0,16},{16,0},{1,17},{17,1},{2,18},{18,2},{3,19},{19,3},{4,20},{20... | collective-permute-start | bytes 2555912 | tf_op jit(solution)/shard_map/ppermute | solution.py:58
  91.4 29.5 %collective-permute-start.21 = (bf16[2,4,16,5120]{3,2,1,0:T(8,128)(2,1)S(1)}, bf16[2,4,16,5120]{3,2,1,0:T(8,128)(2,1)S(1)}, u32[]{:S(2)}, u32[]{:S(2)}) collective-permute-start(bf16[2,4,16,5120]{3,2,1,0:T(8,128)(2,1)S(1)} %pad_maximum_fusion.7.refs_0_), channel_id=1, source_target_pairs={{0,16},{16,0},{1,17},{17,1},{2,18},{18,2},{3,19},{19,3},{4,20},{20... | collective-permute-start | bytes 3932168 | tf_op jit(solution)/shard_map/ppermute | solution.py:58
  92.9 28.0 %collective-permute-start.19 = (bf16[2,4,16,5120]{3,2,1,0:T(8,128)(2,1)S(1)}, bf16[2,4,16,5120]{3,2,1,0:T(8,128)(2,1)}, u32[]{:S(2)}, u32[]{:S(2)}) collective-permute-start(bf16[2,4,16,5120]{3,2,1,0:T(8,128)(2,1)S(1)} %pad_maximum_fusion.7.refs_0_), channel_id=1, source_target_pairs={{0,1},{1,0},{2,3},{3,2},{4,5},{5,4},{6,7},{7,6},{8,9},{9,8},{10,11... | collective-permute-start | bytes 3932168 | tf_op jit(solution)/shard_map/ppermute | solution.py:58
  92.9 31.5 %collective-permute-start.22 = (bf16[2,4,16,5120]{3,2,1,0:T(8,128)(2,1)}, bf16[2,4,16,5120]{3,2,1,0:T(8,128)(2,1)}, u32[]{:S(2)}, u32[]{:S(2)}) collective-permute-start(bf16[2,4,16,5120]{3,2,1,0:T(8,128)(2,1)} %pad_maximum_fusion.8.refs_4_), channel_id=1, source_target_pairs={{0,8},{8,0},{1,9},{9,1},{2,10},{10,2},{3,11},{11,3},{4,12},{12,4},... | collective-permute-start | bytes 3932168 | tf_op jit(solution)/shard_map/ppermute | solution.py:58
  93.6 30.8 %collective-permute-start.20 = (bf16[2,4,16,5120]{3,2,1,0:T(8,128)(2,1)}, bf16[2,4,16,5120]{3,2,1,0:T(8,128)(2,1)}, u32[]{:S(2)}, u32[]{:S(2)}) collective-permute-start(bf16[2,4,16,5120]{3,2,1,0:T(8,128)(2,1)} %pad_maximum_fusion.8.refs_4_), channel_id=1, source_target_pairs={{0,1},{1,0},{2,3},{3,2},{4,5},{5,4},{6,7},{7,6},{8,9},{9,8},{10,11... | collective-permute-start | bytes 3932168 | tf_op jit(solution)/shard_map/ppermute | solution.py:58
  126.1 32.3 %collective-permute-start.28 = (bf16[128,1024]{1,0:T(8,128)(2,1)S(1)}, bf16[128,1024]{1,0:T(8,128)(2,1)S(1)}, u32[]{:S(2)}, u32[]{:S(2)}) collective-permute-start(bf16[128,1024]{1,0:T(8,128)(2,1)S(1)} %copy-done.72), channel_id=1, source_target_pairs={{0,6},{2,0},{4,2},{6,4},{1,7},{3,1},{5,3},{7,5},{8,14},{10,8},{12,... | collective-permute-start | bytes 786440 | tf_op jit(solution)/shard_map/ppermute | solution.py:58
  126.2 32.2 %collective-permute-start.27 = (bf16[128,1024]{1,0:T(8,128)(2,1)S(1)}, bf16[128,1024]{1,0:T(8,128)(2,1)}, u32[]{:S(2)}, u32[]{:S(2)}) collective-permute-start(bf16[128,1024]{1,0:T(8,128)(2,1)S(1)} %copy-done.72), channel_id=1, source_target_pairs={{0,4},{2,6},{4,0},{6,2},{1,5},{3,7},{5,1},{7,3},{8,12},{10,14},{12... | collective-permute-start | bytes 786440 | tf_op jit(solution)/shard_map/ppermute | solution.py:58
  127.5 31.7 %collective-permute-start.26 = (bf16[128,1024]{1,0:T(8,128)(2,1)S(1)}, bf16[128,1024]{1,0:T(8,128)(2,1)}, u32[]{:S(2)}, u32[]{:S(2)}) collective-permute-start(bf16[128,1024]{1,0:T(8,128)(2,1)S(1)} %copy-done.72), channel_id=1, source_target_pairs={{0,2},{2,4},{4,6},{6,0},{1,3},{3,5},{5,7},{7,1},{8,10},{10,12},{12... | collective-permute-start | bytes 786440 | tf_op jit(solution)/shard_map/ppermute | solution.py:58
  131.6 29.9 %collective-permute-start.24 = (bf16[2,4,16,5120]{3,2,1,0:T(8,128)(2,1)}, bf16[2,4,16,5120]{3,2,1,0:T(8,128)(2,1)S(1)}, u32[]{:S(2)}, u32[]{:S(2)}) collective-permute-start(bf16[2,4,16,5120]{3,2,1,0:T(8,128)(2,1)} %copy-done.20), channel_id=1, source_target_pairs={{0,1},{1,0},{2,3},{3,2},{4,5},{5,4},{6,7},{7,6},{8,9},{9,8},{10,11... | collective-permute-start | bytes 3932168 | tf_op jit(solution)/shard_map/ppermute | solution.py:58
  131.6 29.9 %collective-permute-start.25 = (bf16[2,4,16,5120]{3,2,1,0:T(8,128)(2,1)}, bf16[2,4,16,5120]{3,2,1,0:T(8,128)(2,1)S(1)}, u32[]{:S(2)}, u32[]{:S(2)}) collective-permute-start(bf16[2,4,16,5120]{3,2,1,0:T(8,128)(2,1)} %collective-permute-done.22.refs_5_), channel_id=1, source_target_pairs={{0,1},{1,0},{2,3},{3,2},{4,5},{5,4},{6,7},{7,6},{8,9},{9,8},{10,11... | collective-permute-start | bytes 3932168 | tf_op jit(solution)/shard_map/ppermute | solution.py:58
  161.5 25.1 %collective-permute-start.29 = (bf16[4,64,1024]{2,1,0:T(8,128)(2,1)}, bf16[4,64,1024]{2,1,0:T(8,128)(2,1)}, u32[]{:S(2)}, u32[]{:S(2)}) collective-permute-start(bf16[4,64,1024]{2,1,0:T(8,128)(2,1)} %pad_maximum_fusion.19), channel_id=1, source_target_pairs={{0,8},{8,0},{1,9},{9,1},{2,10},{10,2},{3,11},{11,3},{4,12},{12,4},... | collective-permute-start | bytes 1572872 | tf_op jit(solution)/shard_map/ppermute | solution.py:58
  162.3 25.7 %collective-permute-start.30 = (bf16[4,64,1024]{2,1,0:T(8,128)(2,1)S(1)}, bf16[4,64,1024]{2,1,0:T(8,128)(2,1)}, u32[]{:S(2)}, u32[]{:S(2)}) collective-permute-start(bf16[4,64,1024]{2,1,0:T(8,128)(2,1)S(1)} %pad_maximum_fusion.20), channel_id=1, source_target_pairs={{0,16},{16,0},{1,17},{17,1},{2,18},{18,2},{3,19},{19,3},{4,20},{20... | collective-permute-start | bytes 1572872 | tf_op jit(solution)/shard_map/ppermute | solution.py:58
  162.8 26.8 %collective-permute-start.31 = (bf16[2,104,1024]{2,1,0:T(8,128)(2,1)}, bf16[2,104,1024]{2,1,0:T(8,128)(2,1)}, u32[]{:S(2)}, u32[]{:S(2)}) collective-permute-start(bf16[2,104,1024]{2,1,0:T(8,128)(2,1)} %pad_maximum_fusion.28), channel_id=1, source_target_pairs={{0,2},{2,4},{4,6},{6,0},{1,3},{3,5},{5,7},{7,1},{8,10},{10,12},{12... | collective-permute-start | bytes 1277960 | tf_op jit(solution)/shard_map/ppermute | solution.py:58
  163.1 26.5 %collective-permute-start.32 = (bf16[2,104,1024]{2,1,0:T(8,128)(2,1)}, bf16[2,104,1024]{2,1,0:T(8,128)(2,1)}, u32[]{:S(2)}, u32[]{:S(2)}) collective-permute-start(bf16[2,104,1024]{2,1,0:T(8,128)(2,1)} %pad_maximum_fusion.30), channel_id=1, source_target_pairs={{0,6},{2,0},{4,2},{6,4},{1,7},{3,1},{5,3},{7,5},{8,14},{10,8},{12,... | collective-permute-start | bytes 1277960 | tf_op jit(solution)/shard_map/ppermute | solution.py:58
  189.6 23.2 %collective-permute-start.35 = (bf16[2,4,64,1024]{3,2,1,0:T(8,128)(2,1)S(1)}, bf16[2,4,64,1024]{3,2,1,0:T(8,128)(2,1)S(1)}, u32[]{:S(2)}, u32[]{:S(2)}) collective-permute-start(bf16[2,4,64,1024]{3,2,1,0:T(8,128)(2,1)S(1)} %pad_maximum_fusion.9.refs_0_), channel_id=1, source_target_pairs={{0,1},{1,0},{2,3},{3,2},{4,5},{5,4},{6,7},{7,6},{8,9},{9,8},{10,11... | collective-permute-start | bytes 3145736 | tf_op jit(solution)/shard_map/ppermute | solution.py:58
  189.7 25.6 %collective-permute-start.33 = (bf16[2,4,64,1024]{3,2,1,0:T(8,128)(2,1)S(1)}, bf16[2,4,64,1024]{3,2,1,0:T(8,128)(2,1)S(1)}, u32[]{:S(2)}, u32[]{:S(2)}) collective-permute-start(bf16[2,4,64,1024]{3,2,1,0:T(8,128)(2,1)S(1)} %pad_maximum_fusion.9.refs_0_), channel_id=1, source_target_pairs={{0,16},{16,0},{1,17},{17,1},{2,18},{18,2},{3,19},{19,3},{4,20},{20... | collective-permute-start | bytes 3145736 | tf_op jit(solution)/shard_map/ppermute | solution.py:58
  191.2 24.0 %collective-permute-start.36 = (bf16[2,4,64,1024]{3,2,1,0:T(8,128)(2,1)S(1)}, bf16[2,4,64,1024]{3,2,1,0:T(8,128)(2,1)S(1)}, u32[]{:S(2)}, u32[]{:S(2)}) collective-permute-start(bf16[2,4,64,1024]{3,2,1,0:T(8,128)(2,1)S(1)} %pad_maximum_fusion.10.refs_4_), channel_id=1, source_target_pairs={{0,1},{1,0},{2,3},{3,2},{4,5},{5,4},{6,7},{7,6},{8,9},{9,8},{10,11... | collective-permute-start | bytes 3145736 | tf_op jit(solution)/shard_map/ppermute | solution.py:58
  191.4 25.4 %collective-permute-start.34 = (bf16[2,4,64,1024]{3,2,1,0:T(8,128)(2,1)S(1)}, bf16[2,4,64,1024]{3,2,1,0:T(8,128)(2,1)S(1)}, u32[]{:S(2)}, u32[]{:S(2)}) collective-permute-start(bf16[2,4,64,1024]{3,2,1,0:T(8,128)(2,1)S(1)} %pad_maximum_fusion.10.refs_4_), channel_id=1, source_target_pairs={{0,8},{8,0},{1,9},{9,1},{2,10},{10,2},{3,11},{11,3},{4,12},{12,4},... | collective-permute-start | bytes 3145736 | tf_op jit(solution)/shard_map/ppermute | solution.py:58
  257.4 25.4 %collective-permute-start.41 = (bf16[2,4,64,1024]{3,2,1,0:T(8,128)(2,1)S(1)}, bf16[2,4,64,1024]{3,2,1,0:T(8,128)(2,1)}, u32[]{:S(2)}, u32[]{:S(2)}) collective-permute-start(bf16[2,4,64,1024]{3,2,1,0:T(8,128)(2,1)S(1)} %get-tuple-element.434), channel_id=1, source_target_pairs={{0,16},{16,0},{1,17},{17,1},{2,18},{18,2},{3,19},{19,3},{4,20},{20... | collective-permute-start | bytes 3145736 | tf_op jit(solution)/shard_map/ppermute | solution.py:58
  258.0 25.6 %collective-permute-start.42 = (bf16[2,4,64,1024]{3,2,1,0:T(8,128)(2,1)S(1)}, bf16[2,4,64,1024]{3,2,1,0:T(8,128)(2,1)}, u32[]{:S(2)}, u32[]{:S(2)}) collective-permute-start(bf16[2,4,64,1024]{3,2,1,0:T(8,128)(2,1)S(1)} %copy-done.85), channel_id=1, source_target_pairs={{0,8},{8,0},{1,9},{9,1},{2,10},{10,2},{3,11},{11,3},{4,12},{12,4},... | collective-permute-start | bytes 3145736 | tf_op jit(solution)/shard_map/ppermute | solution.py:58
  260.3 22.5 %collective-permute-start.44 = (bf16[2,104,1024]{2,1,0:T(8,128)(2,1)S(1)}, bf16[2,104,1024]{2,1,0:T(8,128)(2,1)S(1)}, u32[]{:S(2)}, u32[]{:S(2)}) collective-permute-start(bf16[2,104,1024]{2,1,0:T(8,128)(2,1)S(1)} %get-tuple-element.670), channel_id=1, source_target_pairs={{0,2},{2,4},{4,6},{6,0},{1,3},{3,5},{5,7},{7,1},{8,10},{10,12},{12... | collective-permute-start | bytes 1277960 | tf_op jit(solution)/shard_map/ppermute | solution.py:58
  260.3 22.5 %collective-permute-start.43 = (bf16[2,104,1024]{2,1,0:T(8,128)(2,1)S(1)}, bf16[2,104,1024]{2,1,0:T(8,128)(2,1)S(1)}, u32[]{:S(2)}, u32[]{:S(2)}) collective-permute-start(bf16[2,104,1024]{2,1,0:T(8,128)(2,1)S(1)} %get-tuple-element.671), channel_id=1, source_target_pairs={{0,6},{2,0},{4,2},{6,4},{1,7},{3,1},{5,3},{7,5},{8,14},{10,8},{12,... | collective-permute-start | bytes 1277960 | tf_op jit(solution)/shard_map/ppermute | solution.py:58
  320.8 25.1 %collective-permute-start.49 = (bf16[2,4,16,4096]{3,2,1,0:T(8,128)(2,1)S(1)}, bf16[2,4,16,4096]{3,2,1,0:T(8,128)(2,1)S(1)}, u32[]{:S(2)}, u32[]{:S(2)}) collective-permute-start(bf16[2,4,16,4096]{3,2,1,0:T(8,128)(2,1)S(1)} %get-tuple-element.466), channel_id=1, source_target_pairs={{0,16},{16,0},{1,17},{17,1},{2,18},{18,2},{3,19},{19,3},{4,20},{20... | collective-permute-start | bytes 3145736 | tf_op jit(solution)/shard_map/ppermute | solution.py:58
  321.4 25.0 %collective-permute-start.50 = (bf16[2,4,16,4096]{3,2,1,0:T(8,128)(2,1)}, bf16[2,4,16,4096]{3,2,1,0:T(8,128)(2,1)S(1)}, u32[]{:S(2)}, u32[]{:S(2)}) collective-permute-start(bf16[2,4,16,4096]{3,2,1,0:T(8,128)(2,1)} %get-tuple-element.468), channel_id=1, source_target_pairs={{0,8},{8,0},{1,9},{9,1},{2,10},{10,2},{3,11},{11,3},{4,12},{12,4},... | collective-permute-start | bytes 3145736 | tf_op jit(solution)/shard_map/ppermute | solution.py:58
  346.9 23.2 %collective-permute-start.55 = (bf16[512,1024]{1,0:T(8,128)(2,1)S(1)}, bf16[512,1024]{1,0:T(8,128)(2,1)S(1)}, u32[]{:S(2)}, u32[]{:S(2)}) collective-permute-start(bf16[512,1024]{1,0:T(8,128)(2,1)S(1)} %weight_grad.12), channel_id=1, source_target_pairs={{0,1},{1,0},{2,3},{3,2},{4,5},{5,4},{6,7},{7,6},{8,9},{9,8},{10,11... | collective-permute-start | bytes 3145736 | tf_op jit(solution)/shard_map/ppermute | solution.py:58
  347.0 23.1 %collective-permute-start.53 = (bf16[4,16,4096]{2,1,0:T(8,128)(2,1)S(1)}, bf16[4,16,4096]{2,1,0:T(8,128)(2,1)S(1)}, u32[]{:S(2)}, u32[]{:S(2)}) collective-permute-start(bf16[4,16,4096]{2,1,0:T(8,128)(2,1)S(1)} %get-tuple-element.492), channel_id=1, source_target_pairs={{0,8},{8,0},{1,9},{9,1},{2,10},{10,2},{3,11},{11,3},{4,12},{12,4},... | collective-permute-start | bytes 1572872 | tf_op jit(solution)/shard_map/ppermute | solution.py:58
  414.6 24.2 %collective-permute-start.66 = (bf16[4,104,1024]{2,1,0:T(8,128)(2,1)}, bf16[4,104,1024]{2,1,0:T(8,128)(2,1)}, u32[]{:S(2)}, u32[]{:S(2)}) collective-permute-start(bf16[4,104,1024]{2,1,0:T(8,128)(2,1)} %slice_bitcast_fusion.2), channel_id=1, source_target_pairs={{0,1},{1,0},{2,3},{3,2},{4,5},{5,4},{6,7},{7,6},{8,9},{9,8},{10,11... | collective-permute-start | bytes 2555912 | tf_op jit(solution)/shard_map/ppermute | solution.py:58
  414.6 24.2 %collective-permute-start.62 = (bf16[2,4,16,3072]{3,2,1,0:T(8,128)(2,1)}, bf16[2,4,16,3072]{3,2,1,0:T(8,128)(2,1)}, u32[]{:S(2)}, u32[]{:S(2)}) collective-permute-start(bf16[2,4,16,3072]{3,2,1,0:T(8,128)(2,1)} %get-tuple-element.553), channel_id=1, source_target_pairs={{0,16},{16,0},{1,17},{17,1},{2,18},{18,2},{3,19},{19,3},{4,20},{20... | collective-permute-start | bytes 2359304 | tf_op jit(solution)/shard_map/ppermute | solution.py:58
  415.1 23.8 %collective-permute-start.63 = (bf16[2,4,16,3072]{3,2,1,0:T(8,128)(2,1)S(1)}, bf16[2,4,16,3072]{3,2,1,0:T(8,128)(2,1)}, u32[]{:S(2)}, u32[]{:S(2)}) collective-permute-start(bf16[2,4,16,3072]{3,2,1,0:T(8,128)(2,1)S(1)} %get-tuple-element.555), channel_id=1, source_target_pairs={{0,8},{8,0},{1,9},{9,1},{2,10},{10,2},{3,11},{11,3},{4,12},{12,4},... | collective-permute-start | bytes 2359304 | tf_op jit(solution)/shard_map/ppermute | solution.py:58
  456.1 22.5 %collective-permute-start.77 = (bf16[4,104,1024]{2,1,0:T(8,128)(2,1)S(1)}, bf16[4,104,1024]{2,1,0:T(8,128)(2,1)S(1)}, u32[]{:S(2)}, u32[]{:S(2)}) collective-permute-start(bf16[4,104,1024]{2,1,0:T(8,128)(2,1)S(1)} %get-tuple-element.664), channel_id=1, source_target_pairs={{0,1},{1,0},{2,3},{3,2},{4,5},{5,4},{6,7},{7,6},{8,9},{9,8},{10,11... | collective-permute-start | bytes 2555912 | tf_op jit(solution)/shard_map/ppermute | solution.py:58
  (135 other events, 1492.4 us)

commit v6 on v5

--- a/solution.py
+++ b/solution.py
@@ -982,7 +982,7 @@
     d, result = tie(d, result)
 
     d = ring.first(d)
-    back = ring.send(result, outer, -1)
+    back = ring.send(result, inner, -1)
     hidden_low, grad_bu = fall(grad_low, full_down, slope)
     sent = weight_grad(two_far, 1, hidden_low, share)
     d, sent, back = tie(d, sent, back)
@@ -992,7 +992,7 @@
 
     d = ring.second(d)
     u = ring.swap(sent)
-    back.update(ring.send(result, inner, -1))
+    back.update(ring.send(result, outer[:1], -1))
     grad_residual, residual_low, sums_two = back_norm([hidden_low], full_up, residual, g2, grad_low)
     d, u, residual_low, back = tie(d, u, residual_low, back)
 
@@ -1003,10 +1003,11 @@
 
     u = ring.first(u)
     gone = ring.toward_some(d, outer)
+    back.update(ring.send(result, outer[1:], -1))
     grad_mixed = back_project(residual_low, full_out)
     sent_out = sent
     half_grads = attend_back(qkv, logs, grad_mixed)
-    u, sent_out, d, gone, grad_mixed, half_grads = tie(u, sent_out, d, gone, grad_mixed, half_grads)
+    u, sent_out, d, gone, grad_mixed, half_grads, back = tie(u, sent_out, d, gone, grad_mixed, half_grads, back)
 
     u = ring.again(u)
     u, sent_out, back, d, grad_mixed, half_grads = tie(u, sent_out, back, d, grad_mixed, half_grads)

time: 501 us -> 497 us (level)
    unnamed x188 -> x184, local copies, waits for them, and re-layouts: 20.8 us -> 20.1 us
  transfers between devices with their start and end apart: 81 -> 81, of which waited for: 25 -> 26; matrix products, arithmetic and copies ran while one was open for 9% -> 9% of each run, Pallas kernels for 34% -> 34%
where the time goes in v6:
time: 497 us; the launch traced here: 489 us
  Pallas kernels  198 us (40%)
  waiting for transfers between devices  122 us (25%)
  starting transfers between devices  80 us (16%)
  other arithmetic  51.9 us (10%)
  local copies, waits for them, and re-layouts  34.3 us (7%)
    ppermute x81, waiting for transfers between devices, shifted(): lax.ppermute(array, axis, [(i, (i + step) % size) for i in range(size)])  122 us
    ppermute x81, starting transfers between devices, shifted(): lax.ppermute(array, axis, [(i, (i + step) % size) for i in range(size)])  80 us
    pallas_call x8, Pallas kernels, weight_grad(): pl.pallas_call(body, out_shape=[jax.ShapeDtypeStruct(shape, bf16) for sha...  45 us
    pallas_call x2, Pallas kernels, attend_back(): pl.pallas_call(attend_back_body, out_shape=[jax.ShapeDtypeStruct((PACKED,...  26.4 us
    pallas_call x2, Pallas kernels, back_norm(): pl.pallas_call(body, out_shape=shapes + [jax.ShapeDtypeStruct((8, width),...  25.2 us
    pallas_call x3, Pallas kernels, assemble(): pl.pallas_call(body, out_shape=[jax.ShapeDtypeStruct((planes_all, depth,...  20.9 us
    unnamed x184, local copies, waits for them, and re-layouts  20.1 us
    pallas_call x1, Pallas kernels, rise(): pl.pallas_call(body, out_shape=shapes, grid_spec=pltpu.PrefetchScalarGrid...  15.4 us
  transfers between devices with their start and end apart: 81, of which 26 were waited for; matrix products, arithmetic and copies ran while one was open for 9% of the time, Pallas kernels for 34%

profile of v6, /device:TPU:0, one launch (start us, length us, event | category | flops | bytes accessed | tf_op | source)
XLA Modules:
  0.0 489.0 jit_solution(1688217382562981769)
XLA Ops:
  2.4 5.0 %collective-permute-start.2 = (bf16[32,3328]{1,0:T(8,128)(2,1)}, bf16[32,3328]{1,0:T(8,128)(2,1)}, u32[]{:S(2)}, u32[]{:S(2)}) collective-permute-start(bf16[32,3328]{1,0:T(8,128)(2,1)} %seed.1), channel_id=1, source_target_pairs={{0,6},{2,0},{4,2},{6,4},{1,7},{3,1},{5,3},{7,5},{8,14},{10,8},{12,... | collective-permute-start | bytes 638984 | tf_op jit(solution)/shard_map/ppermute | solution.py:58
  20.0 5.8 %collective-permute-done.1 = bf16[32,3328]{1,0:T(8,128)(2,1)} collective-permute-done((bf16[32,3328]{1,0:T(8,128)(2,1)}, bf16[32,3328]{1,0:T(8,128)(2,1)}, u32[]{:S(2)}, u32[]{:S(2)}) %collective-permute-start.1) | collective-permute-done | bytes 213024 | tf_op jit(solution)/shard_map/ppermute | solution.py:58
  41.3 4.2 collective-permute-done.7
  48.6 20.4 %collective-permute-done.12 = bf16[32,5120]{1,0:T(8,128)(2,1)S(1)} collective-permute-done((bf16[32,5120]{1,0:T(8,128)(2,1)S(1)}, bf16[32,5120]{1,0:T(8,128)(2,1)S(1)}, u32[]{:S(2)}, u32[]{:S(2)}) %collective-permute-start.12) | collective-permute-done | bytes 327712 | tf_op jit(solution)/shard_map/ppermute | solution.py:58
  73.2 13.1 %collective-permute-done.16 = bf16[4,16,5120]{2,1,0:T(8,128)(2,1)S(1)} collective-permute-done((bf16[4,16,5120]{2,1,0:T(8,128)(2,1)S(1)}, bf16[4,16,5120]{2,1,0:T(8,128)(2,1)S(1)}, u32[]{:S(2)}, u32[]{:S(2)}) %collective-permute-start.16) | collective-permute-done | bytes 655392 | tf_op jit(solution)/shard_map/ppermute | solution.py:58
  98.7 5.4 %assemble.3 = (bf16[4,4,2,2,16,3072]{5,4,3,2,1,0:T(8,128)(2,1)}, bf16[4,4,2,2,16,256]{5,4,3,2,1,0:T(8,128)(2,1)S(1)}) custom-call(s32[32]{0:T(128)S(1)} %stack.422.table_ref, bf16[4,4,16,3328]{3,2,1,0:T(8,128)(2,1)} %copy-done.40, bf16[4,4,16,3328]{3,2,1,0:T(8,128)(2,1)} %copy-done.45, bf16[2,4,16,3328]{3,2,1,0:T(8,128)(2,1)S(1)} %collective-permute-done.9.refs_2_, ...), custom_call_target="tpu_custom_call" | custom-call | bytes 272629 | tf_op jit(solution)/shard_map/assemble/pallas_call | solution.py:171
  104.9 10.0 %collective-permute-done.23 = bf16[2,104,1024]{2,1,0:T(8,128)(2,1)} collective-permute-done((bf16[2,104,1024]{2,1,0:T(8,128)(2,1)}, bf16[2,104,1024]{2,1,0:T(8,128)(2,1)}, u32[]{:S(2)}, u32[]{:S(2)}) %collective-permute-start.23) | collective-permute-done | bytes 426016 | tf_op jit(solution)/shard_map/ppermute | solution.py:58
  114.9 6.0 %collective-permute-done.21.refs_1_ = bf16[2,4,16,5120]{3,2,1,0:T(8,128)(2,1)S(1)} collective-permute-done((bf16[2,4,16,5120]{3,2,1,0:T(8,128)(2,1)S(1)}, bf16[2,4,16,5120]{3,2,1,0:T(8,128)(2,1)S(1)}, u32[]{:S(2)}, u32[]{:S(2)}) %collective-permute-start.21) | collective-permute-done | bytes 1310752 | tf_op jit(solution)/shard_map/ppermute | solution.py:58
  135.6 7.5 %project.1.q_ref.k_ref.v_ref = bf16[592,3072]{1,0:T(8,128)(2,1)} custom-call(bf16[592,1024]{1,0:T(8,128)(2,1)S(1)} %get-tuple-element.382.x_ref, bf16[1024,3072]{1,0:T(8,128)(2,1)} %bitcast.260, f32[1,3072]{1,0:T(1,128)S(1)} %reshape_reshape.3.b_ref), custom_call_target="tpu_custom_call" | custom-call | flops 120000000 | bytes 240000 | tf_op jit(solution)/shard_map/project/pallas_call | solution.py:625
  144.2 14.1 %attend.1 = (bf16[592,1024]{1,0:T(8,128)(2,1)S(1)}, f32[64,592]{1,0:T(8,128)S(1)}) custom-call(bf16[592,3072]{1,0:T(8,128)(2,1)} %project.1.q_ref.k_ref.v_ref, bf16[592,3072]{1,0:T(8,128)(2,1)} %project.1.q_ref.k_ref.v_ref, bf16[592,3072]{1,0:T(8,128)(2,1)} %project.1.q_ref.k_ref.v_ref), custom_call_target="tpu_custom_call" | custom-call | flops 240000000 | bytes 290979 | tf_op jit(solution)/shard_map/attend/pallas_call | solution.py:453
  172.6 8.8 %assemble.4 = (bf16[4,4,2,2,16,1024]{5,4,3,2,1,0:T(8,128)(2,1)}, bf16[4,4,2,2,16,4096]{5,4,3,2,1,0:T(8,128)(2,1)}) custom-call(s32[32]{0:T(128)S(1)} %stack.439.table_ref, bf16[2,4,16,5120]{3,2,1,0:T(8,128)(2,1)S(1)} %copy-done.11, bf16[2,4,16,5120]{3,2,1,0:T(8,128)(2,1)S(1)} %copy-done.21, bf16[2,4,16,5120]{3,2,1,0:T(8,128)(2,1)} %collective-permute-done.19.refs_2_, ...), custom_call_target="tpu_custom_call" | custom-call | bytes 419430 | tf_op jit(solution)/shard_map/assemble/pallas_call | solution.py:171
  181.4 5.2 %out_norm.1 = (f32[592,1024]{1,0:T(8,128)}, bf16[592,1024]{1,0:T(8,128)(2,1)S(1)}) custom-call(bf16[592,1024]{1,0:T(8,128)(2,1)S(1)} %copy-done.15, bf16[1024,1024]{1,0:T(8,128)(2,1)} %bitcast.262, f32[592,1024]{1,0:T(8,128)} %get-tuple-element.395.t_ref.refs_2_, f32[1,1024]{1,0:T(1,128)S(1)} %reshape_reshape_squeeze.25.b_ref, ...), custom_call_target="tpu_custom_call" | custom-call | flops 40000000 | bytes 160000 | tf_op jit(solution)/shard_map/out_norm/pallas_call | solution.py:724
  197.3 15.4 %rise.1 = (bf16[592,4096]{1,0:T(8,128)(2,1)}, f32[592,4096]{1,0:T(8,128)}, bf16[2,592,2048]{2,1,0:T(8,128)(2,1)}) custom-call(s32[32]{0:T(128)S(1)} %fusion.92.rank_ref, bf16[592,1024]{1,0:T(8,128)(2,1)S(1)} %get-tuple-element.403.x_ref, bf16[1024,4096]{1,0:T(8,128)(2,1)} %bitcast.258, f32[1,4096]{1,0:T(1,128)S(1)} %slice_bitcast_fusion.36.b_ref), custom_call_target="tpu_custom_call" | custom-call | flops 240000000 | bytes 600000 | tf_op jit(solution)/shard_map/rise/pallas_call | solution.py:572
  220.5 7.1 %weight_grad.8 = bf16[2048,1024]{1,0:T(8,128)(2,1)} custom-call(bf16[2,592,2048]{2,1,0:T(8,128)(2,1)} %get-tuple-element.410.refs_0_, bf16[592,1024]{1,0:T(8,128)(2,1)S(1)} %get-tuple-element.418.refs_1_.g_ref.refs_4_), custom_call_target="tpu_custom_call" | custom-call | flops 49660560 | bytes 167772 | tf_op jit(solution)/shard_map/weight_grad/pallas_call | solution.py:371
  231.5 6.7 %assemble.5 = bf16[4,4,2,2,64,1024]{5,4,3,2,1,0:T(8,128)(2,1)} custom-call(s32[32]{0:T(128)S(1)} %stack.439.table_ref, bf16[2,4,64,1024]{3,2,1,0:T(8,128)(2,1)S(1)} %copy-done.17, bf16[2,4,64,1024]{3,2,1,0:T(8,128)(2,1)S(1)} %copy-done.25, bf16[2,4,64,1024]{3,2,1,0:T(8,128)(2,1)S(1)} %collective-permute-done.35.refs_2_, bf16[2,4,64,1024]{3,2,1,0:T(8,128)(2,1)} %copy-done.55, ...), custom_call_target="tpu_custom_call" | custom-call | bytes 335544 | tf_op jit(solution)/shard_map/assemble/pallas_call | solution.py:171
  238.2 7.7 %weight_grad.9 = (bf16[2,4,64,1024]{3,2,1,0:T(8,128)(2,1)S(1)}, bf16[2,4,64,1024]{3,2,1,0:T(8,128)(2,1)S(1)}, bf16[2,4,64,1024]{3,2,1,0:T(8,128)(2,1)S(1)}, bf16[2,4,64,1024]{3,2,1,0:T(8,128)(2,1)}) custom-call(bf16[2,592,2048]{2,1,0:T(8,128)(2,1)} %get-tuple-element.410.refs_0_, bf16[592,1024]{1,0:T(8,128)(2,1)} %copy-done, ...), custom_call_target="tpu_custom_call" | custom-call | flops 49660560 | bytes 167772 | tf_op jit(solution)/shard_map/weight_grad/pallas_call | solution.py:371
  245.9 11.4 %land.1 = bf16[832,1024]{1,0:T(8,128)(2,1)S(1)} custom-call(bf16[592,4096]{1,0:T(8,128)(2,1)} %get-tuple-element.431.a_ref, bf16[4096,1024]{1,0:T(8,128)(2,1)} %bitcast.256, f32[592,1024]{1,0:T(8,128)} %get-tuple-element.433.r_ref.refs_2_, f32[1,1024]{1,0:T(1,128)S(1)} %reshape_reshape_squeeze.29.b_ref, bf16[592,832]{1,0:T(8,128)(2,1)S(1)} %fusion.p_ref.refs_5_), custom_call_target="tpu_custom_call" | custom-call | flops 120000000 | bytes 280000 | tf_op jit(solution)/shard_map/land/pallas_call | solution.py:757
  260.3 11.4 %fall.1 = (bf16[592,4096]{1,0:T(8,128)(2,1)}, f32[1,4096]{1,0:T(1,128)S(1)}) custom-call(bf16[592,1024]{1,0:T(8,128)(2,1)S(1)} %copy-done.1, bf16[4096,1024]{1,0:T(8,128)(2,1)} %bitcast.257, f32[592,4096]{1,0:T(8,128)} %get-tuple-element.439.slope_ref), custom_call_target="tpu_custom_call" | custom-call | flops 200000000 | bytes 500000 | tf_op jit(solution)/shard_map/fall/pallas_call | solution.py:602
  271.8 7.1 %weight_grad.10 = bf16[512,4096]{1,0:T(8,128)(2,1)} custom-call(bf16[2,592,512]{2,1,0:T(8,128)(2,1)S(1)} %copy-done.7, bf16[592,4096]{1,0:T(8,128)(2,1)} %get-tuple-element.440.refs_1_.refs_0_), custom_call_target="tpu_custom_call" | custom-call | flops 49660560 | bytes 167772 | tf_op jit(solution)/shard_map/weight_grad/pallas_call | solution.py:371
  289.3 13.2 %back_norm.2 = (f32[592,1024]{1,0:T(8,128)}, bf16[592,1024]{1,0:T(8,128)(2,1)S(1)}, f32[8,1024]{1,0:T(8,128)S(1)}) custom-call(bf16[592,4096]{1,0:T(8,128)(2,1)} %get-tuple-element.440.refs_1_.refs_0_, bf16[1024,4096]{1,0:T(8,128)(2,1)} %bitcast.259, f32[592,1024]{1,0:T(8,128)} %get-tuple-element.433.r_ref.refs_2_, ...), custom_call_target="tpu_custom_call" | custom-call | flops 120000000 | bytes 400000 | tf_op jit(solution)/shard_map/back_norm/pallas_call | solution.py:829
  303.3 7.5 %weight_grad.11 = (bf16[2,4,16,4096]{3,2,1,0:T(8,128)(2,1)S(1)}, bf16[2,4,16,4096]{3,2,1,0:T(8,128)(2,1)S(1)}, bf16[2,4,16,4096]{3,2,1,0:T(8,128)(2,1)S(1)}, bf16[2,4,16,4096]{3,2,1,0:T(8,128)(2,1)}) custom-call(bf16[2,592,512]{2,1,0:T(8,128)(2,1)} %copy-done.6, bf16[592,4096]{1,0:T(8,128)(2,1)} %get-tuple-element.440.refs_1_.refs_0_, ...), custom_call_target="tpu_custom_call" | custom-call | flops 49660560 | bytes 167772 | tf_op jit(solution)/shard_map/weight_grad/pallas_call | solution.py:371
  324.7 12.2 %attend_back.2 = (bf16[592,1536]{1,0:T(8,128)(2,1)S(1)}, f32[1,1536]{1,0:T(1,128)S(1)}) custom-call(bf16[592,3072]{1,0:T(8,128)(2,1)} %project.1.q_ref.k_ref.v_ref, bf16[592,3072]{1,0:T(8,128)(2,1)} %project.1.q_ref.k_ref.v_ref, bf16[592,3072]{1,0:T(8,128)(2,1)} %project.1.q_ref.k_ref.v_ref, f32[64,592]{1,0:T(8,128)S(1)} %copy-done.33, ...), custom_call_target="tpu_custom_call" | custom-call | flops 240000000 | bytes 290979 | tf_op jit(solution)/shard_map/attend_back/pallas_call | solution.py:509
  344.2 14.2 %attend_back.3 = (bf16[592,3072]{1,0:T(8,128)(2,1)}, f32[1,3072]{1,0:T(1,128)S(1)}) custom-call(bf16[592,3072]{1,0:T(8,128)(2,1)} %project.1.q_ref.k_ref.v_ref, bf16[592,3072]{1,0:T(8,128)(2,1)} %project.1.q_ref.k_ref.v_ref, bf16[592,3072]{1,0:T(8,128)(2,1)} %project.1.q_ref.k_ref.v_ref, f32[64,592]{1,0:T(8,128)S(1)} %copy-done.33, ...), custom_call_target="tpu_custom_call" | custom-call | flops 240000000 | bytes 290979 | tf_op jit(solution)/shard_map/attend_back/pallas_call | solution.py:509
  358.4 6.0 %weight_grad.13 = bf16[512,3072]{1,0:T(8,128)(2,1)} custom-call(bf16[2,592,512]{2,1,0:T(8,128)(2,1)S(1)} %by_distance.3.refs_0_, bf16[592,3072]{1,0:T(8,128)(2,1)} %get-tuple-element.532.refs_1_.refs_0_), custom_call_target="tpu_custom_call" | custom-call | flops 37245420 | bytes 125829 | tf_op jit(solution)/shard_map/weight_grad/pallas_call | solution.py:371
  372.1 11.9 %back_norm.3 = (bf16[832,1024]{1,0:T(8,128)(2,1)S(1)}, f32[8,1024]{1,0:T(8,128)S(1)}) custom-call(bf16[592,3072]{1,0:T(8,128)(2,1)} %get-tuple-element.532.refs_1_.refs_0_, bf16[1024,3072]{1,0:T(8,128)(2,1)} %bitcast.261, f32[592,1024]{1,0:T(8,128)} %get-tuple-element.395.t_ref.refs_2_, f32[1,1024]{1,0:T(1,128)S(1)} %reshape_reshape_squeeze.23.g_ref.refs_3_, ...), custom_call_target="tpu_custom_call" | custom-call | flops 120000000 | bytes 400000 | tf_op jit(solution)/shard_map/back_norm/pallas_call | solution.py:829
  386.4 4.0 collective-permute-start.60
  394.5 6.3 %weight_grad.14 = (bf16[2,4,16,3072]{3,2,1,0:T(8,128)(2,1)S(1)}, bf16[2,4,16,3072]{3,2,1,0:T(8,128)(2,1)}, bf16[2,4,16,3072]{3,2,1,0:T(8,128)(2,1)S(1)}, bf16[2,4,16,3072]{3,2,1,0:T(8,128)(2,1)S(1)}) custom-call(bf16[2,592,512]{2,1,0:T(8,128)(2,1)} %copy-done.2, bf16[592,3072]{1,0:T(8,128)(2,1)} %get-tuple-element.532.refs_1_.refs_0_, ...), custom_call_target="tpu_custom_call" | custom-call | flops 37245420 | bytes 125829 | tf_op jit(solution)/shard_map/weight_grad/pallas_call | solution.py:371
  401.2 6.5 %collective-permute-done.60 = bf16[2,104,1024]{2,1,0:T(8,128)(2,1)} collective-permute-done((bf16[2,104,1024]{2,1,0:T(8,128)(2,1)}, bf16[2,104,1024]{2,1,0:T(8,128)(2,1)}, u32[]{:S(2)}, u32[]{:S(2)}) %collective-permute-start.60) | collective-permute-done | bytes 426016 | tf_op jit(solution)/shard_map/ppermute | solution.py:58
  417.0 17.2 %collective-permute-done.65 = bf16[2,104,1024]{2,1,0:T(8,128)(2,1)} collective-permute-done((bf16[2,104,1024]{2,1,0:T(8,128)(2,1)}, bf16[2,104,1024]{2,1,0:T(8,128)(2,1)}, u32[]{:S(2)}, u32[]{:S(2)}) %collective-permute-start.65) | collective-permute-done | bytes 426016 | tf_op jit(solution)/shard_map/ppermute | solution.py:58
  447.5 3.8 collective-permute-done.69
  451.4 6.3 %collective-permute-done.70 = bf16[4,16,3072]{2,1,0:T(8,128)(2,1)S(1)} collective-permute-done((bf16[4,16,3072]{2,1,0:T(8,128)(2,1)S(1)}, bf16[4,16,3072]{2,1,0:T(8,128)(2,1)S(1)}, u32[]{:S(2)}, u32[]{:S(2)}) %collective-permute-start.70) | collective-permute-done | bytes 393248 | tf_op jit(solution)/shard_map/ppermute | solution.py:58
  469.7 5.9 %collective-permute-done.73 = bf16[32,3072]{1,0:T(8,128)(2,1)S(1)} collective-permute-done((bf16[32,3072]{1,0:T(8,128)(2,1)S(1)}, bf16[32,3072]{1,0:T(8,128)(2,1)S(1)}, u32[]{:S(2)}, u32[]{:S(2)}) %collective-permute-start.73) | collective-permute-done | bytes 196640 | tf_op jit(solution)/shard_map/ppermute | solution.py:58
  (500 shorter events, 198.8 us)
Async XLA Ops:
  45.5 23.6 %collective-permute-start.12 = (bf16[32,5120]{1,0:T(8,128)(2,1)S(1)}, bf16[32,5120]{1,0:T(8,128)(2,1)S(1)}, u32[]{:S(2)}, u32[]{:S(2)}) collective-permute-start(bf16[32,5120]{1,0:T(8,128)(2,1)S(1)} %pad_maximum_fusion.32), channel_id=1, source_target_pairs={{0,4},{2,6},{4,0},{6,2},{1,5},{3,7},{5,1},{7,3},{8,12},{10,14},{12... | collective-permute-start | bytes 983048 | tf_op jit(solution)/shard_map/ppermute | solution.py:58
  45.5 24.1 %collective-permute-start.13 = (bf16[2,104,1024]{2,1,0:T(8,128)(2,1)S(1)}, bf16[2,104,1024]{2,1,0:T(8,128)(2,1)S(1)}, u32[]{:S(2)}, u32[]{:S(2)}) collective-permute-start(bf16[2,104,1024]{2,1,0:T(8,128)(2,1)S(1)} %pad_maximum_fusion.24), channel_id=1, source_target_pairs={{0,2},{2,4},{4,6},{6,0},{1,3},{3,5},{5,7},{7,1},{8,10},{10,12},{12... | collective-permute-start | bytes 1277960 | tf_op jit(solution)/shard_map/ppermute | solution.py:58
  45.6 23.9 %collective-permute-start.9 = (bf16[2,4,16,3328]{3,2,1,0:T(8,128)(2,1)S(1)}, bf16[2,4,16,3328]{3,2,1,0:T(8,128)(2,1)S(1)}, u32[]{:S(2)}, u32[]{:S(2)}) collective-permute-start(bf16[2,4,16,3328]{3,2,1,0:T(8,128)(2,1)S(1)} %pad_maximum_fusion.15), channel_id=1, source_target_pairs={{0,16},{16,0},{1,17},{17,1},{2,18},{18,2},{3,19},{19,3},{4,20},{20... | collective-permute-start | bytes 2555912 | tf_op jit(solution)/shard_map/ppermute | solution.py:58
  47.1 22.4 %collective-permute-start.10 = (bf16[2,4,16,3328]{3,2,1,0:T(8,128)(2,1)S(1)}, bf16[2,4,16,3328]{3,2,1,0:T(8,128)(2,1)S(1)}, u32[]{:S(2)}, u32[]{:S(2)}) collective-permute-start(bf16[2,4,16,3328]{3,2,1,0:T(8,128)(2,1)S(1)} %pad_maximum_fusion.16), channel_id=1, source_target_pairs={{0,8},{8,0},{1,9},{9,1},{2,10},{10,2},{3,11},{11,3},{4,12},{12,4},... | collective-permute-start | bytes 2555912 | tf_op jit(solution)/shard_map/ppermute | solution.py:58
  91.3 29.5 %collective-permute-start.21 = (bf16[2,4,16,5120]{3,2,1,0:T(8,128)(2,1)S(1)}, bf16[2,4,16,5120]{3,2,1,0:T(8,128)(2,1)S(1)}, u32[]{:S(2)}, u32[]{:S(2)}) collective-permute-start(bf16[2,4,16,5120]{3,2,1,0:T(8,128)(2,1)S(1)} %pad_maximum_fusion.7.refs_0_), channel_id=1, source_target_pairs={{0,16},{16,0},{1,17},{17,1},{2,18},{18,2},{3,19},{19,3},{4,20},{20... | collective-permute-start | bytes 3932168 | tf_op jit(solution)/shard_map/ppermute | solution.py:58
  92.9 28.0 %collective-permute-start.19 = (bf16[2,4,16,5120]{3,2,1,0:T(8,128)(2,1)S(1)}, bf16[2,4,16,5120]{3,2,1,0:T(8,128)(2,1)}, u32[]{:S(2)}, u32[]{:S(2)}) collective-permute-start(bf16[2,4,16,5120]{3,2,1,0:T(8,128)(2,1)S(1)} %pad_maximum_fusion.7.refs_0_), channel_id=1, source_target_pairs={{0,1},{1,0},{2,3},{3,2},{4,5},{5,4},{6,7},{7,6},{8,9},{9,8},{10,11... | collective-permute-start | bytes 3932168 | tf_op jit(solution)/shard_map/ppermute | solution.py:58
  92.9 31.5 %collective-permute-start.22 = (bf16[2,4,16,5120]{3,2,1,0:T(8,128)(2,1)}, bf16[2,4,16,5120]{3,2,1,0:T(8,128)(2,1)}, u32[]{:S(2)}, u32[]{:S(2)}) collective-permute-start(bf16[2,4,16,5120]{3,2,1,0:T(8,128)(2,1)} %pad_maximum_fusion.8.refs_4_), channel_id=1, source_target_pairs={{0,8},{8,0},{1,9},{9,1},{2,10},{10,2},{3,11},{11,3},{4,12},{12,4},... | collective-permute-start | bytes 3932168 | tf_op jit(solution)/shard_map/ppermute | solution.py:58
  93.6 30.8 %collective-permute-start.20 = (bf16[2,4,16,5120]{3,2,1,0:T(8,128)(2,1)}, bf16[2,4,16,5120]{3,2,1,0:T(8,128)(2,1)}, u32[]{:S(2)}, u32[]{:S(2)}) collective-permute-start(bf16[2,4,16,5120]{3,2,1,0:T(8,128)(2,1)} %pad_maximum_fusion.8.refs_4_), channel_id=1, source_target_pairs={{0,1},{1,0},{2,3},{3,2},{4,5},{5,4},{6,7},{7,6},{8,9},{9,8},{10,11... | collective-permute-start | bytes 3932168 | tf_op jit(solution)/shard_map/ppermute | solution.py:58
  126.1 32.2 %collective-permute-start.28 = (bf16[128,1024]{1,0:T(8,128)(2,1)S(1)}, bf16[128,1024]{1,0:T(8,128)(2,1)S(1)}, u32[]{:S(2)}, u32[]{:S(2)}) collective-permute-start(bf16[128,1024]{1,0:T(8,128)(2,1)S(1)} %copy-done.70), channel_id=1, source_target_pairs={{0,6},{2,0},{4,2},{6,4},{1,7},{3,1},{5,3},{7,5},{8,14},{10,8},{12,... | collective-permute-start | bytes 786440 | tf_op jit(solution)/shard_map/ppermute | solution.py:58
  126.2 32.2 %collective-permute-start.27 = (bf16[128,1024]{1,0:T(8,128)(2,1)S(1)}, bf16[128,1024]{1,0:T(8,128)(2,1)}, u32[]{:S(2)}, u32[]{:S(2)}) collective-permute-start(bf16[128,1024]{1,0:T(8,128)(2,1)S(1)} %copy-done.70), channel_id=1, source_target_pairs={{0,4},{2,6},{4,0},{6,2},{1,5},{3,7},{5,1},{7,3},{8,12},{10,14},{12... | collective-permute-start | bytes 786440 | tf_op jit(solution)/shard_map/ppermute | solution.py:58
  127.5 31.6 %collective-permute-start.26 = (bf16[128,1024]{1,0:T(8,128)(2,1)S(1)}, bf16[128,1024]{1,0:T(8,128)(2,1)}, u32[]{:S(2)}, u32[]{:S(2)}) collective-permute-start(bf16[128,1024]{1,0:T(8,128)(2,1)S(1)} %copy-done.70), channel_id=1, source_target_pairs={{0,2},{2,4},{4,6},{6,0},{1,3},{3,5},{5,7},{7,1},{8,10},{10,12},{12... | collective-permute-start | bytes 786440 | tf_op jit(solution)/shard_map/ppermute | solution.py:58
  131.6 29.9 %collective-permute-start.24 = (bf16[2,4,16,5120]{3,2,1,0:T(8,128)(2,1)}, bf16[2,4,16,5120]{3,2,1,0:T(8,128)(2,1)S(1)}, u32[]{:S(2)}, u32[]{:S(2)}) collective-permute-start(bf16[2,4,16,5120]{3,2,1,0:T(8,128)(2,1)} %copy-done.20), channel_id=1, source_target_pairs={{0,1},{1,0},{2,3},{3,2},{4,5},{5,4},{6,7},{7,6},{8,9},{9,8},{10,11... | collective-permute-start | bytes 3932168 | tf_op jit(solution)/shard_map/ppermute | solution.py:58
  131.6 29.8 %collective-permute-start.25 = (bf16[2,4,16,5120]{3,2,1,0:T(8,128)(2,1)}, bf16[2,4,16,5120]{3,2,1,0:T(8,128)(2,1)S(1)}, u32[]{:S(2)}, u32[]{:S(2)}) collective-permute-start(bf16[2,4,16,5120]{3,2,1,0:T(8,128)(2,1)} %collective-permute-done.22.refs_5_), channel_id=1, source_target_pairs={{0,1},{1,0},{2,3},{3,2},{4,5},{5,4},{6,7},{7,6},{8,9},{9,8},{10,11... | collective-permute-start | bytes 3932168 | tf_op jit(solution)/shard_map/ppermute | solution.py:58
  161.4 25.1 %collective-permute-start.29 = (bf16[4,64,1024]{2,1,0:T(8,128)(2,1)}, bf16[4,64,1024]{2,1,0:T(8,128)(2,1)}, u32[]{:S(2)}, u32[]{:S(2)}) collective-permute-start(bf16[4,64,1024]{2,1,0:T(8,128)(2,1)} %pad_maximum_fusion.19), channel_id=1, source_target_pairs={{0,8},{8,0},{1,9},{9,1},{2,10},{10,2},{3,11},{11,3},{4,12},{12,4},... | collective-permute-start | bytes 1572872 | tf_op jit(solution)/shard_map/ppermute | solution.py:58
  162.2 25.8 %collective-permute-start.30 = (bf16[4,64,1024]{2,1,0:T(8,128)(2,1)S(1)}, bf16[4,64,1024]{2,1,0:T(8,128)(2,1)}, u32[]{:S(2)}, u32[]{:S(2)}) collective-permute-start(bf16[4,64,1024]{2,1,0:T(8,128)(2,1)S(1)} %pad_maximum_fusion.20), channel_id=1, source_target_pairs={{0,16},{16,0},{1,17},{17,1},{2,18},{18,2},{3,19},{19,3},{4,20},{20... | collective-permute-start | bytes 1572872 | tf_op jit(solution)/shard_map/ppermute | solution.py:58
  162.7 26.8 %collective-permute-start.31 = (bf16[2,104,1024]{2,1,0:T(8,128)(2,1)}, bf16[2,104,1024]{2,1,0:T(8,128)(2,1)}, u32[]{:S(2)}, u32[]{:S(2)}) collective-permute-start(bf16[2,104,1024]{2,1,0:T(8,128)(2,1)} %pad_maximum_fusion.28), channel_id=1, source_target_pairs={{0,2},{2,4},{4,6},{6,0},{1,3},{3,5},{5,7},{7,1},{8,10},{10,12},{12... | collective-permute-start | bytes 1277960 | tf_op jit(solution)/shard_map/ppermute | solution.py:58
  163.0 26.5 %collective-permute-start.32 = (bf16[2,104,1024]{2,1,0:T(8,128)(2,1)}, bf16[2,104,1024]{2,1,0:T(8,128)(2,1)}, u32[]{:S(2)}, u32[]{:S(2)}) collective-permute-start(bf16[2,104,1024]{2,1,0:T(8,128)(2,1)} %pad_maximum_fusion.30), channel_id=1, source_target_pairs={{0,6},{2,0},{4,2},{6,4},{1,7},{3,1},{5,3},{7,5},{8,14},{10,8},{12,... | collective-permute-start | bytes 1277960 | tf_op jit(solution)/shard_map/ppermute | solution.py:58
  189.6 23.1 %collective-permute-start.35 = (bf16[2,4,64,1024]{3,2,1,0:T(8,128)(2,1)S(1)}, bf16[2,4,64,1024]{3,2,1,0:T(8,128)(2,1)S(1)}, u32[]{:S(2)}, u32[]{:S(2)}) collective-permute-start(bf16[2,4,64,1024]{3,2,1,0:T(8,128)(2,1)S(1)} %pad_maximum_fusion.9.refs_0_), channel_id=1, source_target_pairs={{0,1},{1,0},{2,3},{3,2},{4,5},{5,4},{6,7},{7,6},{8,9},{9,8},{10,11... | collective-permute-start | bytes 3145736 | tf_op jit(solution)/shard_map/ppermute | solution.py:58
  189.6 25.6 %collective-permute-start.33 = (bf16[2,4,64,1024]{3,2,1,0:T(8,128)(2,1)S(1)}, bf16[2,4,64,1024]{3,2,1,0:T(8,128)(2,1)S(1)}, u32[]{:S(2)}, u32[]{:S(2)}) collective-permute-start(bf16[2,4,64,1024]{3,2,1,0:T(8,128)(2,1)S(1)} %pad_maximum_fusion.9.refs_0_), channel_id=1, source_target_pairs={{0,16},{16,0},{1,17},{17,1},{2,18},{18,2},{3,19},{19,3},{4,20},{20... | collective-permute-start | bytes 3145736 | tf_op jit(solution)/shard_map/ppermute | solution.py:58
  191.2 24.0 %collective-permute-start.36 = (bf16[2,4,64,1024]{3,2,1,0:T(8,128)(2,1)S(1)}, bf16[2,4,64,1024]{3,2,1,0:T(8,128)(2,1)S(1)}, u32[]{:S(2)}, u32[]{:S(2)}) collective-permute-start(bf16[2,4,64,1024]{3,2,1,0:T(8,128)(2,1)S(1)} %pad_maximum_fusion.10.refs_4_), channel_id=1, source_target_pairs={{0,1},{1,0},{2,3},{3,2},{4,5},{5,4},{6,7},{7,6},{8,9},{9,8},{10,11... | collective-permute-start | bytes 3145736 | tf_op jit(solution)/shard_map/ppermute | solution.py:58
  191.4 25.4 %collective-permute-start.34 = (bf16[2,4,64,1024]{3,2,1,0:T(8,128)(2,1)S(1)}, bf16[2,4,64,1024]{3,2,1,0:T(8,128)(2,1)S(1)}, u32[]{:S(2)}, u32[]{:S(2)}) collective-permute-start(bf16[2,4,64,1024]{3,2,1,0:T(8,128)(2,1)S(1)} %pad_maximum_fusion.10.refs_4_), channel_id=1, source_target_pairs={{0,8},{8,0},{1,9},{9,1},{2,10},{10,2},{3,11},{11,3},{4,12},{12,4},... | collective-permute-start | bytes 3145736 | tf_op jit(solution)/shard_map/ppermute | solution.py:58
  257.3 25.2 %collective-permute-start.41 = (bf16[2,4,64,1024]{3,2,1,0:T(8,128)(2,1)S(1)}, bf16[2,4,64,1024]{3,2,1,0:T(8,128)(2,1)}, u32[]{:S(2)}, u32[]{:S(2)}) collective-permute-start(bf16[2,4,64,1024]{3,2,1,0:T(8,128)(2,1)S(1)} %get-tuple-element.435), channel_id=1, source_target_pairs={{0,16},{16,0},{1,17},{17,1},{2,18},{18,2},{3,19},{19,3},{4,20},{20... | collective-permute-start | bytes 3145736 | tf_op jit(solution)/shard_map/ppermute | solution.py:58
  257.9 24.9 %collective-permute-start.42 = (bf16[2,4,64,1024]{3,2,1,0:T(8,128)(2,1)S(1)}, bf16[2,4,64,1024]{3,2,1,0:T(8,128)(2,1)}, u32[]{:S(2)}, u32[]{:S(2)}) collective-permute-start(bf16[2,4,64,1024]{3,2,1,0:T(8,128)(2,1)S(1)} %copy-done.83), channel_id=1, source_target_pairs={{0,8},{8,0},{1,9},{9,1},{2,10},{10,2},{3,11},{11,3},{4,12},{12,4},... | collective-permute-start | bytes 3145736 | tf_op jit(solution)/shard_map/ppermute | solution.py:58
  314.5 25.3 %collective-permute-start.48 = (bf16[2,4,16,4096]{3,2,1,0:T(8,128)(2,1)S(1)}, bf16[2,4,16,4096]{3,2,1,0:T(8,128)(2,1)S(1)}, u32[]{:S(2)}, u32[]{:S(2)}) collective-permute-start(bf16[2,4,16,4096]{3,2,1,0:T(8,128)(2,1)S(1)} %get-tuple-element.466), channel_id=1, source_target_pairs={{0,16},{16,0},{1,17},{17,1},{2,18},{18,2},{3,19},{19,3},{4,20},{20... | collective-permute-start | bytes 3145736 | tf_op jit(solution)/shard_map/ppermute | solution.py:58
  315.0 24.8 %collective-permute-start.49 = (bf16[2,4,16,4096]{3,2,1,0:T(8,128)(2,1)}, bf16[2,4,16,4096]{3,2,1,0:T(8,128)(2,1)S(1)}, u32[]{:S(2)}, u32[]{:S(2)}) collective-permute-start(bf16[2,4,16,4096]{3,2,1,0:T(8,128)(2,1)} %get-tuple-element.468), channel_id=1, source_target_pairs={{0,8},{8,0},{1,9},{9,1},{2,10},{10,2},{3,11},{11,3},{4,12},{12,4},... | collective-permute-start | bytes 3145736 | tf_op jit(solution)/shard_map/ppermute | solution.py:58
  340.4 24.0 %collective-permute-start.55 = (bf16[512,1024]{1,0:T(8,128)(2,1)S(1)}, bf16[512,1024]{1,0:T(8,128)(2,1)S(1)}, u32[]{:S(2)}, u32[]{:S(2)}) collective-permute-start(bf16[512,1024]{1,0:T(8,128)(2,1)S(1)} %weight_grad.12), channel_id=1, source_target_pairs={{0,1},{1,0},{2,3},{3,2},{4,5},{5,4},{6,7},{7,6},{8,9},{9,8},{10,11... | collective-permute-start | bytes 3145736 | tf_op jit(solution)/shard_map/ppermute | solution.py:58
  340.5 23.9 %collective-permute-start.53 = (bf16[4,16,4096]{2,1,0:T(8,128)(2,1)S(1)}, bf16[4,16,4096]{2,1,0:T(8,128)(2,1)S(1)}, u32[]{:S(2)}, u32[]{:S(2)}) collective-permute-start(bf16[4,16,4096]{2,1,0:T(8,128)(2,1)S(1)} %get-tuple-element.494), channel_id=1, source_target_pairs={{0,8},{8,0},{1,9},{9,1},{2,10},{10,2},{3,11},{11,3},{4,12},{12,4},... | collective-permute-start | bytes 1572872 | tf_op jit(solution)/shard_map/ppermute | solution.py:58
  341.8 22.7 %collective-permute-start.54 = (bf16[4,16,4096]{2,1,0:T(8,128)(2,1)S(1)}, bf16[4,16,4096]{2,1,0:T(8,128)(2,1)S(1)}, u32[]{:S(2)}, u32[]{:S(2)}) collective-permute-start(bf16[4,16,4096]{2,1,0:T(8,128)(2,1)S(1)} %get-tuple-element.496), channel_id=1, source_target_pairs={{0,16},{16,0},{1,17},{17,1},{2,18},{18,2},{3,19},{19,3},{4,20},{20... | collective-permute-start | bytes 1572872 | tf_op jit(solution)/shard_map/ppermute | solution.py:58
  410.1 24.2 %collective-permute-start.66 = (bf16[4,104,1024]{2,1,0:T(8,128)(2,1)}, bf16[4,104,1024]{2,1,0:T(8,128)(2,1)}, u32[]{:S(2)}, u32[]{:S(2)}) collective-permute-start(bf16[4,104,1024]{2,1,0:T(8,128)(2,1)} %slice_bitcast_fusion.2), channel_id=1, source_target_pairs={{0,1},{1,0},{2,3},{3,2},{4,5},{5,4},{6,7},{7,6},{8,9},{9,8},{10,11... | collective-permute-start | bytes 2555912 | tf_op jit(solution)/shard_map/ppermute | solution.py:58
  410.1 24.2 %collective-permute-start.62 = (bf16[2,4,16,3072]{3,2,1,0:T(8,128)(2,1)}, bf16[2,4,16,3072]{3,2,1,0:T(8,128)(2,1)}, u32[]{:S(2)}, u32[]{:S(2)}) collective-permute-start(bf16[2,4,16,3072]{3,2,1,0:T(8,128)(2,1)} %get-tuple-element.555), channel_id=1, source_target_pairs={{0,16},{16,0},{1,17},{17,1},{2,18},{18,2},{3,19},{19,3},{4,20},{20... | collective-permute-start | bytes 2359304 | tf_op jit(solution)/shard_map/ppermute | solution.py:58
  410.6 23.7 %collective-permute-start.63 = (bf16[2,4,16,3072]{3,2,1,0:T(8,128)(2,1)S(1)}, bf16[2,4,16,3072]{3,2,1,0:T(8,128)(2,1)}, u32[]{:S(2)}, u32[]{:S(2)}) collective-permute-start(bf16[2,4,16,3072]{3,2,1,0:T(8,128)(2,1)S(1)} %get-tuple-element.557), channel_id=1, source_target_pairs={{0,8},{8,0},{1,9},{9,1},{2,10},{10,2},{3,11},{11,3},{4,12},{12,4},... | collective-permute-start | bytes 2359304 | tf_op jit(solution)/shard_map/ppermute | solution.py:58
  451.4 24.2 %collective-permute-start.77 = (bf16[4,104,1024]{2,1,0:T(8,128)(2,1)S(1)}, bf16[4,104,1024]{2,1,0:T(8,128)(2,1)S(1)}, u32[]{:S(2)}, u32[]{:S(2)}) collective-permute-start(bf16[4,104,1024]{2,1,0:T(8,128)(2,1)S(1)} %get-tuple-element.666), channel_id=1, source_target_pairs={{0,1},{1,0},{2,3},{3,2},{4,5},{5,4},{6,7},{7,6},{8,9},{9,8},{10,11... | collective-permute-start | bytes 2555912 | tf_op jit(solution)/shard_map/ppermute | solution.py:58
  (133 other events, 1447.3 us)

commit v7 on v6

--- a/solution.py
+++ b/solution.py
@@ -950,8 +950,7 @@
     cot_rest = ring.send(cot_pieces, outer)
     full_out, full_up = ring.assemble(ring.sources(two, two_core, two_more, two_more_core), [width, ff])
     residual, normed_two = out_norm(mixed, full_out, tokens_f, bo, g2, s2)
-    normed_far = ring.by_distance(normed, target)
-    three, normed_two, normed_far, cot_rest = tie(three, normed_two, normed_far, cot_rest)
+    three, normed_two, cot_rest = tie(three, normed_two, cot_rest)
 
     three_more = ring.plane(three)
     three_core = ring.to_core([[half] for half in three])
@@ -999,7 +998,7 @@
     d = ring.last(d)
     u = ring.kept(two_far, hidden_low, share, u)
     sent = weight_grad(mixed_far, 1, residual_low, share)
-    d, u, sent, residual_low = tie(d, u, sent, residual_low)
+    d, u, sent, residual_low, normed = tie(d, u, sent, residual_low, normed)
 
     u = ring.first(u)
     gone = ring.toward_some(d, outer)
@@ -1007,7 +1006,10 @@
     grad_mixed = back_project(residual_low, full_out)
     sent_out = sent
     half_grads = attend_back(qkv, logs, grad_mixed)
-    u, sent_out, d, gone, grad_mixed, half_grads, back = tie(u, sent_out, d, gone, grad_mixed, half_grads, back)
+    normed_far = ring.by_distance(normed, target)
+    u, sent_out, d, gone, grad_mixed, half_grads, back, normed_far = tie(
+        u, sent_out, d, gone, grad_mixed, half_grads, back, normed_far
+    )
 
     u = ring.again(u)
     u, sent_out, back, d, grad_mixed, half_grads = tie(u, sent_out, back, d, grad_mixed, half_grads)

time: 497 us -> 499 us (level); the launches traced: 489 us -> 497 us
  starting transfers between devices: 80 us -> 93.2 us
  waiting for transfers between devices: 122 us -> 117 us
    ppermute x81, starting transfers between devices: 80 us -> 93.2 us  [shifted(): lax.ppermute(array, axis, [(i, (i + step) % size) for i in range(size)])]
    unnamed x184 -> x168, local copies, waits for them, and re-layouts: 20.1 us -> 16.5 us
  transfers between devices with their start and end apart: 81 -> 81, of which waited for: 26 -> 27; matrix products, arithmetic and copies ran while one was open for 9% -> 9% of each run, Pallas kernels for 34% -> 34%
where the time goes in v7:
time: 499 us; the launch traced here: 497 us
  Pallas kernels  199 us (40%)
  waiting for transfers between devices  117 us (23%)
  starting transfers between devices  93.2 us (19%)
  other arithmetic  53.6 us (11%)
  local copies, waits for them, and re-layouts  30.7 us (6%)
    ppermute x81, waiting for transfers between devices, shifted(): lax.ppermute(array, axis, [(i, (i + step) % size) for i in range(size)])  117 us
    ppermute x81, starting transfers between devices, shifted(): lax.ppermute(array, axis, [(i, (i + step) % size) for i in range(size)])  93.2 us
    pallas_call x8, Pallas kernels, weight_grad(): pl.pallas_call(body, out_shape=[jax.ShapeDtypeStruct(shape, bf16) for sha...  45.8 us
    pallas_call x2, Pallas kernels, attend_back(): pl.pallas_call(attend_back_body, out_shape=[jax.ShapeDtypeStruct((PACKED,...  26.4 us
    pallas_call x2, Pallas kernels, back_norm(): pl.pallas_call(body, out_shape=shapes + [jax.ShapeDtypeStruct((8, width),...  25.3 us
    pallas_call x3, Pallas kernels, assemble(): pl.pallas_call(body, out_shape=[jax.ShapeDtypeStruct((planes_all, depth,...  20.8 us
    unnamed x168, local copies, waits for them, and re-layouts  16.5 us
    pallas_call x1, Pallas kernels, rise(): pl.pallas_call(body, out_shape=shapes, grid_spec=pltpu.PrefetchScalarGrid...  15.4 us
  transfers between devices with their start and end apart: 81, of which 27 were waited for; matrix products, arithmetic and copies ran while one was open for 9% of the time, Pallas kernels for 34%

profile of v7, /device:TPU:0, one launch (start us, length us, event | category | flops | bytes accessed | tf_op | source)
XLA Modules:
  0.0 496.5 jit_solution(5300701138557223165)
XLA Ops:
  2.4 5.0 %collective-permute-start.2 = (bf16[32,3328]{1,0:T(8,128)(2,1)}, bf16[32,3328]{1,0:T(8,128)(2,1)}, u32[]{:S(2)}, u32[]{:S(2)}) collective-permute-start(bf16[32,3328]{1,0:T(8,128)(2,1)} %seed.1), channel_id=1, source_target_pairs={{0,6},{2,0},{4,2},{6,4},{1,7},{3,1},{5,3},{7,5},{8,14},{10,8},{12,... | collective-permute-start | bytes 638984 | tf_op jit(solution)/shard_map/ppermute | solution.py:58
  20.0 5.8 %collective-permute-done.1 = bf16[32,3328]{1,0:T(8,128)(2,1)} collective-permute-done((bf16[32,3328]{1,0:T(8,128)(2,1)}, bf16[32,3328]{1,0:T(8,128)(2,1)}, u32[]{:S(2)}, u32[]{:S(2)}) %collective-permute-start.1) | collective-permute-done | bytes 213024 | tf_op jit(solution)/shard_map/ppermute | solution.py:58
  41.3 4.2 collective-permute-done.7
  48.6 20.4 %collective-permute-done.12 = bf16[32,5120]{1,0:T(8,128)(2,1)S(1)} collective-permute-done((bf16[32,5120]{1,0:T(8,128)(2,1)S(1)}, bf16[32,5120]{1,0:T(8,128)(2,1)S(1)}, u32[]{:S(2)}, u32[]{:S(2)}) %collective-permute-start.12) | collective-permute-done | bytes 327712 | tf_op jit(solution)/shard_map/ppermute | solution.py:58
  73.2 13.1 %collective-permute-done.16 = bf16[4,16,5120]{2,1,0:T(8,128)(2,1)S(1)} collective-permute-done((bf16[4,16,5120]{2,1,0:T(8,128)(2,1)S(1)}, bf16[4,16,5120]{2,1,0:T(8,128)(2,1)S(1)}, u32[]{:S(2)}, u32[]{:S(2)}) %collective-permute-start.16) | collective-permute-done | bytes 655392 | tf_op jit(solution)/shard_map/ppermute | solution.py:58
  98.6 5.4 %assemble.3 = (bf16[4,4,2,2,16,3072]{5,4,3,2,1,0:T(8,128)(2,1)}, bf16[4,4,2,2,16,256]{5,4,3,2,1,0:T(8,128)(2,1)S(1)}) custom-call(s32[32]{0:T(128)S(1)} %stack.422.table_ref, bf16[4,4,16,3328]{3,2,1,0:T(8,128)(2,1)} %copy-done.36, bf16[4,4,16,3328]{3,2,1,0:T(8,128)(2,1)} %copy-done.41, bf16[2,4,16,3328]{3,2,1,0:T(8,128)(2,1)S(1)} %collective-permute-done.9.refs_2_, ...), custom_call_target="tpu_custom_call" | custom-call | bytes 272629 | tf_op jit(solution)/shard_map/assemble/pallas_call | solution.py:171
  104.8 10.1 %collective-permute-done.23 = bf16[2,104,1024]{2,1,0:T(8,128)(2,1)} collective-permute-done((bf16[2,104,1024]{2,1,0:T(8,128)(2,1)}, bf16[2,104,1024]{2,1,0:T(8,128)(2,1)}, u32[]{:S(2)}, u32[]{:S(2)}) %collective-permute-start.23) | collective-permute-done | bytes 426016 | tf_op jit(solution)/shard_map/ppermute | solution.py:58
  114.9 6.0 %collective-permute-done.21.refs_1_ = bf16[2,4,16,5120]{3,2,1,0:T(8,128)(2,1)S(1)} collective-permute-done((bf16[2,4,16,5120]{3,2,1,0:T(8,128)(2,1)S(1)}, bf16[2,4,16,5120]{3,2,1,0:T(8,128)(2,1)S(1)}, u32[]{:S(2)}, u32[]{:S(2)}) %collective-permute-start.21) | collective-permute-done | bytes 1310752 | tf_op jit(solution)/shard_map/ppermute | solution.py:58
  127.5 13.8 %collective-permute-start.26 = (bf16[128,1024]{1,0:T(8,128)(2,1)S(1)}, bf16[128,1024]{1,0:T(8,128)(2,1)}, u32[]{:S(2)}, u32[]{:S(2)}) collective-permute-start(bf16[128,1024]{1,0:T(8,128)(2,1)S(1)} %copy-done.66), channel_id=1, source_target_pairs={{0,2},{2,4},{4,6},{6,0},{1,3},{3,5},{5,7},{7,1},{8,10},{10,12},{12... | collective-permute-start | bytes 786440 | tf_op jit(solution)/shard_map/ppermute | solution.py:58
  147.3 7.5 %project.1.q_ref.k_ref.v_ref = bf16[592,3072]{1,0:T(8,128)(2,1)} custom-call(bf16[592,1024]{1,0:T(8,128)(2,1)S(1)} %get-tuple-element.480.x_ref, bf16[1024,3072]{1,0:T(8,128)(2,1)} %bitcast.260, f32[1,3072]{1,0:T(1,128)S(1)} %reshape_reshape.3.b_ref), custom_call_target="tpu_custom_call" | custom-call | flops 120000000 | bytes 240000 | tf_op jit(solution)/shard_map/project/pallas_call | solution.py:625
  155.9 14.1 %attend.1 = (bf16[592,1024]{1,0:T(8,128)(2,1)S(1)}, f32[64,592]{1,0:T(8,128)S(1)}) custom-call(bf16[592,3072]{1,0:T(8,128)(2,1)} %project.1.q_ref.k_ref.v_ref, bf16[592,3072]{1,0:T(8,128)(2,1)} %project.1.q_ref.k_ref.v_ref, bf16[592,3072]{1,0:T(8,128)(2,1)} %project.1.q_ref.k_ref.v_ref), custom_call_target="tpu_custom_call" | custom-call | flops 240000000 | bytes 290979 | tf_op jit(solution)/shard_map/attend/pallas_call | solution.py:453
  179.9 8.8 %assemble.4 = (bf16[4,4,2,2,16,1024]{5,4,3,2,1,0:T(8,128)(2,1)}, bf16[4,4,2,2,16,4096]{5,4,3,2,1,0:T(8,128)(2,1)}) custom-call(s32[32]{0:T(128)S(1)} %stack.439.table_ref, bf16[2,4,16,5120]{3,2,1,0:T(8,128)(2,1)S(1)} %copy-done.9, bf16[2,4,16,5120]{3,2,1,0:T(8,128)(2,1)S(1)} %copy-done.19, bf16[2,4,16,5120]{3,2,1,0:T(8,128)(2,1)} %collective-permute-done.19.refs_2_, ...), custom_call_target="tpu_custom_call" | custom-call | bytes 419430 | tf_op jit(solution)/shard_map/assemble/pallas_call | solution.py:171
  188.7 5.1 %out_norm.1 = (f32[592,1024]{1,0:T(8,128)}, bf16[592,1024]{1,0:T(8,128)(2,1)S(1)}) custom-call(bf16[592,1024]{1,0:T(8,128)(2,1)S(1)} %copy-done.13, bf16[1024,1024]{1,0:T(8,128)(2,1)} %bitcast.262, f32[592,1024]{1,0:T(8,128)} %get-tuple-element.396.t_ref.refs_2_, f32[1,1024]{1,0:T(1,128)S(1)} %reshape_reshape_squeeze.25.b_ref, ...), custom_call_target="tpu_custom_call" | custom-call | flops 40000000 | bytes 160000 | tf_op jit(solution)/shard_map/out_norm/pallas_call | solution.py:724
  205.2 15.4 %rise.1 = (bf16[592,4096]{1,0:T(8,128)(2,1)}, f32[592,4096]{1,0:T(8,128)}, bf16[2,592,2048]{2,1,0:T(8,128)(2,1)}) custom-call(s32[32]{0:T(128)S(1)} %fusion.92.rank_ref, bf16[592,1024]{1,0:T(8,128)(2,1)S(1)} %get-tuple-element.402.x_ref, bf16[1024,4096]{1,0:T(8,128)(2,1)} %bitcast.258, f32[1,4096]{1,0:T(1,128)S(1)} %slice_bitcast_fusion.36.b_ref), custom_call_target="tpu_custom_call" | custom-call | flops 240000000 | bytes 600000 | tf_op jit(solution)/shard_map/rise/pallas_call | solution.py:572
  227.8 7.0 %weight_grad.8 = bf16[2048,1024]{1,0:T(8,128)(2,1)} custom-call(bf16[2,592,2048]{2,1,0:T(8,128)(2,1)} %get-tuple-element.410.refs_0_, bf16[592,1024]{1,0:T(8,128)(2,1)S(1)} %get-tuple-element.418.refs_1_.g_ref.refs_4_), custom_call_target="tpu_custom_call" | custom-call | flops 49660560 | bytes 167772 | tf_op jit(solution)/shard_map/weight_grad/pallas_call | solution.py:371
  238.7 6.7 %assemble.5 = bf16[4,4,2,2,64,1024]{5,4,3,2,1,0:T(8,128)(2,1)} custom-call(s32[32]{0:T(128)S(1)} %stack.439.table_ref, bf16[2,4,64,1024]{3,2,1,0:T(8,128)(2,1)S(1)} %copy-done.15, bf16[2,4,64,1024]{3,2,1,0:T(8,128)(2,1)S(1)} %copy-done.21, bf16[2,4,64,1024]{3,2,1,0:T(8,128)(2,1)S(1)} %collective-permute-done.35.refs_2_, bf16[2,4,64,1024]{3,2,1,0:T(8,128)(2,1)} %copy-done.51, ...), custom_call_target="tpu_custom_call" | custom-call | bytes 335544 | tf_op jit(solution)/shard_map/assemble/pallas_call | solution.py:171
  245.4 7.7 %weight_grad.9 = (bf16[2,4,64,1024]{3,2,1,0:T(8,128)(2,1)S(1)}, bf16[2,4,64,1024]{3,2,1,0:T(8,128)(2,1)S(1)}, bf16[2,4,64,1024]{3,2,1,0:T(8,128)(2,1)S(1)}, bf16[2,4,64,1024]{3,2,1,0:T(8,128)(2,1)}) custom-call(bf16[2,592,2048]{2,1,0:T(8,128)(2,1)} %get-tuple-element.410.refs_0_, bf16[592,1024]{1,0:T(8,128)(2,1)} %copy-done, ...), custom_call_target="tpu_custom_call" | custom-call | flops 49660560 | bytes 167772 | tf_op jit(solution)/shard_map/weight_grad/pallas_call | solution.py:371
  253.1 11.4 %land.1 = bf16[832,1024]{1,0:T(8,128)(2,1)S(1)} custom-call(bf16[592,4096]{1,0:T(8,128)(2,1)} %get-tuple-element.431.a_ref, bf16[4096,1024]{1,0:T(8,128)(2,1)} %bitcast.256, f32[592,1024]{1,0:T(8,128)} %get-tuple-element.433.r_ref.refs_2_, f32[1,1024]{1,0:T(1,128)S(1)} %reshape_reshape_squeeze.29.b_ref, bf16[592,832]{1,0:T(8,128)(2,1)S(1)} %fusion.p_ref.refs_5_), custom_call_target="tpu_custom_call" | custom-call | flops 120000000 | bytes 280000 | tf_op jit(solution)/shard_map/land/pallas_call | solution.py:757
  268.1 11.1 %fall.1 = (bf16[592,4096]{1,0:T(8,128)(2,1)}, f32[1,4096]{1,0:T(1,128)S(1)}) custom-call(bf16[592,1024]{1,0:T(8,128)(2,1)S(1)} %copy-done.1, bf16[4096,1024]{1,0:T(8,128)(2,1)} %bitcast.257, f32[592,4096]{1,0:T(8,128)} %get-tuple-element.439.slope_ref), custom_call_target="tpu_custom_call" | custom-call | flops 200000000 | bytes 500000 | tf_op jit(solution)/shard_map/fall/pallas_call | solution.py:602
  279.3 7.3 %weight_grad.10 = bf16[512,4096]{1,0:T(8,128)(2,1)} custom-call(bf16[2,592,512]{2,1,0:T(8,128)(2,1)S(1)} %copy-done.5, bf16[592,4096]{1,0:T(8,128)(2,1)} %get-tuple-element.440.refs_1_.refs_0_), custom_call_target="tpu_custom_call" | custom-call | flops 49660560 | bytes 167772 | tf_op jit(solution)/shard_map/weight_grad/pallas_call | solution.py:371
  296.8 13.2 %back_norm.2 = (f32[592,1024]{1,0:T(8,128)}, bf16[592,1024]{1,0:T(8,128)(2,1)S(1)}, f32[8,1024]{1,0:T(8,128)S(1)}) custom-call(bf16[592,4096]{1,0:T(8,128)(2,1)} %get-tuple-element.440.refs_1_.refs_0_, bf16[1024,4096]{1,0:T(8,128)(2,1)} %bitcast.259, f32[592,1024]{1,0:T(8,128)} %get-tuple-element.433.r_ref.refs_2_, ...), custom_call_target="tpu_custom_call" | custom-call | flops 120000000 | bytes 400000 | tf_op jit(solution)/shard_map/back_norm/pallas_call | solution.py:829
  310.0 8.1 %weight_grad.11 = (bf16[2,4,16,4096]{3,2,1,0:T(8,128)(2,1)S(1)}, bf16[2,4,16,4096]{3,2,1,0:T(8,128)(2,1)S(1)}, bf16[2,4,16,4096]{3,2,1,0:T(8,128)(2,1)S(1)}, bf16[2,4,16,4096]{3,2,1,0:T(8,128)(2,1)}) custom-call(bf16[2,592,512]{2,1,0:T(8,128)(2,1)} %copy-done.4, bf16[592,4096]{1,0:T(8,128)(2,1)} %get-tuple-element.440.refs_1_.refs_0_, ...), custom_call_target="tpu_custom_call" | custom-call | flops 49660560 | bytes 167772 | tf_op jit(solution)/shard_map/weight_grad/pallas_call | solution.py:371
  334.1 12.2 %attend_back.2 = (bf16[592,1536]{1,0:T(8,128)(2,1)S(1)}, f32[1,1536]{1,0:T(1,128)S(1)}) custom-call(bf16[592,3072]{1,0:T(8,128)(2,1)} %project.1.q_ref.k_ref.v_ref, bf16[592,3072]{1,0:T(8,128)(2,1)} %project.1.q_ref.k_ref.v_ref, bf16[592,3072]{1,0:T(8,128)(2,1)} %project.1.q_ref.k_ref.v_ref, f32[64,592]{1,0:T(8,128)S(1)} %get-tuple-element.475.l_ref, ...), custom_call_target="tpu_custom_call" | custom-call | flops 240000000 | bytes 290979 | tf_op jit(solution)/shard_map/attend_back/pallas_call | solution.py:509
  352.0 14.2 %attend_back.3 = (bf16[592,3072]{1,0:T(8,128)(2,1)}, f32[1,3072]{1,0:T(1,128)S(1)}) custom-call(bf16[592,3072]{1,0:T(8,128)(2,1)} %project.1.q_ref.k_ref.v_ref, bf16[592,3072]{1,0:T(8,128)(2,1)} %project.1.q_ref.k_ref.v_ref, bf16[592,3072]{1,0:T(8,128)(2,1)} %project.1.q_ref.k_ref.v_ref, f32[64,592]{1,0:T(8,128)S(1)} %get-tuple-element.475.l_ref, ...), custom_call_target="tpu_custom_call" | custom-call | flops 240000000 | bytes 290979 | tf_op jit(solution)/shard_map/attend_back/pallas_call | solution.py:509
  366.2 5.9 %weight_grad.13 = bf16[512,3072]{1,0:T(8,128)(2,1)} custom-call(bf16[2,592,512]{2,1,0:T(8,128)(2,1)S(1)} %by_distance.5.refs_0_, bf16[592,3072]{1,0:T(8,128)(2,1)} %get-tuple-element.534.refs_1_.refs_0_), custom_call_target="tpu_custom_call" | custom-call | flops 37245420 | bytes 125829 | tf_op jit(solution)/shard_map/weight_grad/pallas_call | solution.py:371
  379.8 12.1 %back_norm.3 = (bf16[832,1024]{1,0:T(8,128)(2,1)S(1)}, f32[8,1024]{1,0:T(8,128)S(1)}) custom-call(bf16[592,3072]{1,0:T(8,128)(2,1)} %get-tuple-element.534.refs_1_.refs_0_, bf16[1024,3072]{1,0:T(8,128)(2,1)} %bitcast.261, f32[592,1024]{1,0:T(8,128)} %get-tuple-element.396.t_ref.refs_2_, f32[1,1024]{1,0:T(1,128)S(1)} %reshape_reshape_squeeze.23.g_ref.refs_3_, ...), custom_call_target="tpu_custom_call" | custom-call | flops 120000000 | bytes 400000 | tf_op jit(solution)/shard_map/back_norm/pallas_call | solution.py:829
  401.9 6.3 %weight_grad.14 = (bf16[2,4,16,3072]{3,2,1,0:T(8,128)(2,1)S(1)}, bf16[2,4,16,3072]{3,2,1,0:T(8,128)(2,1)}, bf16[2,4,16,3072]{3,2,1,0:T(8,128)(2,1)S(1)}, bf16[2,4,16,3072]{3,2,1,0:T(8,128)(2,1)S(1)}) custom-call(bf16[2,592,512]{2,1,0:T(8,128)(2,1)} %copy-done.3, bf16[592,3072]{1,0:T(8,128)(2,1)} %get-tuple-element.534.refs_1_.refs_0_, ...), custom_call_target="tpu_custom_call" | custom-call | flops 37245420 | bytes 125829 | tf_op jit(solution)/shard_map/weight_grad/pallas_call | solution.py:371
  408.9 6.3 %collective-permute-done.60 = bf16[2,104,1024]{2,1,0:T(8,128)(2,1)} collective-permute-done((bf16[2,104,1024]{2,1,0:T(8,128)(2,1)}, bf16[2,104,1024]{2,1,0:T(8,128)(2,1)}, u32[]{:S(2)}, u32[]{:S(2)}) %collective-permute-start.60) | collective-permute-done | bytes 426016 | tf_op jit(solution)/shard_map/ppermute | solution.py:58
  425.1 16.6 %collective-permute-done.65 = bf16[2,104,1024]{2,1,0:T(8,128)(2,1)} collective-permute-done((bf16[2,104,1024]{2,1,0:T(8,128)(2,1)}, bf16[2,104,1024]{2,1,0:T(8,128)(2,1)}, u32[]{:S(2)}, u32[]{:S(2)}) %collective-permute-start.65) | collective-permute-done | bytes 426016 | tf_op jit(solution)/shard_map/ppermute | solution.py:58
  455.0 4.5 collective-permute-done.69
  459.5 5.7 %collective-permute-done.70 = bf16[4,16,3072]{2,1,0:T(8,128)(2,1)S(1)} collective-permute-done((bf16[4,16,3072]{2,1,0:T(8,128)(2,1)S(1)}, bf16[4,16,3072]{2,1,0:T(8,128)(2,1)S(1)}, u32[]{:S(2)}, u32[]{:S(2)}) %collective-permute-start.70) | collective-permute-done | bytes 393248 | tf_op jit(solution)/shard_map/ppermute | solution.py:58
  477.2 5.9 %collective-permute-done.73 = bf16[32,3072]{1,0:T(8,128)(2,1)S(1)} collective-permute-done((bf16[32,3072]{1,0:T(8,128)(2,1)S(1)}, bf16[32,3072]{1,0:T(8,128)(2,1)S(1)}, u32[]{:S(2)}, u32[]{:S(2)}) %collective-permute-start.73) | collective-permute-done | bytes 196640 | tf_op jit(solution)/shard_map/ppermute | solution.py:58
  (484 shorter events, 196.9 us)
Async XLA Ops:
  45.5 23.6 %collective-permute-start.12 = (bf16[32,5120]{1,0:T(8,128)(2,1)S(1)}, bf16[32,5120]{1,0:T(8,128)(2,1)S(1)}, u32[]{:S(2)}, u32[]{:S(2)}) collective-permute-start(bf16[32,5120]{1,0:T(8,128)(2,1)S(1)} %pad_maximum_fusion.32), channel_id=1, source_target_pairs={{0,4},{2,6},{4,0},{6,2},{1,5},{3,7},{5,1},{7,3},{8,12},{10,14},{12... | collective-permute-start | bytes 983048 | tf_op jit(solution)/shard_map/ppermute | solution.py:58
  45.5 24.1 %collective-permute-start.13 = (bf16[2,104,1024]{2,1,0:T(8,128)(2,1)S(1)}, bf16[2,104,1024]{2,1,0:T(8,128)(2,1)S(1)}, u32[]{:S(2)}, u32[]{:S(2)}) collective-permute-start(bf16[2,104,1024]{2,1,0:T(8,128)(2,1)S(1)} %pad_maximum_fusion.24), channel_id=1, source_target_pairs={{0,2},{2,4},{4,6},{6,0},{1,3},{3,5},{5,7},{7,1},{8,10},{10,12},{12... | collective-permute-start | bytes 1277960 | tf_op jit(solution)/shard_map/ppermute | solution.py:58
  45.6 23.9 %collective-permute-start.9 = (bf16[2,4,16,3328]{3,2,1,0:T(8,128)(2,1)S(1)}, bf16[2,4,16,3328]{3,2,1,0:T(8,128)(2,1)S(1)}, u32[]{:S(2)}, u32[]{:S(2)}) collective-permute-start(bf16[2,4,16,3328]{3,2,1,0:T(8,128)(2,1)S(1)} %pad_maximum_fusion.15), channel_id=1, source_target_pairs={{0,16},{16,0},{1,17},{17,1},{2,18},{18,2},{3,19},{19,3},{4,20},{20... | collective-permute-start | bytes 2555912 | tf_op jit(solution)/shard_map/ppermute | solution.py:58
  47.1 22.4 %collective-permute-start.10 = (bf16[2,4,16,3328]{3,2,1,0:T(8,128)(2,1)S(1)}, bf16[2,4,16,3328]{3,2,1,0:T(8,128)(2,1)S(1)}, u32[]{:S(2)}, u32[]{:S(2)}) collective-permute-start(bf16[2,4,16,3328]{3,2,1,0:T(8,128)(2,1)S(1)} %pad_maximum_fusion.16), channel_id=1, source_target_pairs={{0,8},{8,0},{1,9},{9,1},{2,10},{10,2},{3,11},{11,3},{4,12},{12,4},... | collective-permute-start | bytes 2555912 | tf_op jit(solution)/shard_map/ppermute | solution.py:58
  91.3 29.5 %collective-permute-start.21 = (bf16[2,4,16,5120]{3,2,1,0:T(8,128)(2,1)S(1)}, bf16[2,4,16,5120]{3,2,1,0:T(8,128)(2,1)S(1)}, u32[]{:S(2)}, u32[]{:S(2)}) collective-permute-start(bf16[2,4,16,5120]{3,2,1,0:T(8,128)(2,1)S(1)} %pad_maximum_fusion.7.refs_0_), channel_id=1, source_target_pairs={{0,16},{16,0},{1,17},{17,1},{2,18},{18,2},{3,19},{19,3},{4,20},{20... | collective-permute-start | bytes 3932168 | tf_op jit(solution)/shard_map/ppermute | solution.py:58
  92.8 28.0 %collective-permute-start.19 = (bf16[2,4,16,5120]{3,2,1,0:T(8,128)(2,1)S(1)}, bf16[2,4,16,5120]{3,2,1,0:T(8,128)(2,1)}, u32[]{:S(2)}, u32[]{:S(2)}) collective-permute-start(bf16[2,4,16,5120]{3,2,1,0:T(8,128)(2,1)S(1)} %pad_maximum_fusion.7.refs_0_), channel_id=1, source_target_pairs={{0,1},{1,0},{2,3},{3,2},{4,5},{5,4},{6,7},{7,6},{8,9},{9,8},{10,11... | collective-permute-start | bytes 3932168 | tf_op jit(solution)/shard_map/ppermute | solution.py:58
  92.8 31.5 %collective-permute-start.22 = (bf16[2,4,16,5120]{3,2,1,0:T(8,128)(2,1)}, bf16[2,4,16,5120]{3,2,1,0:T(8,128)(2,1)}, u32[]{:S(2)}, u32[]{:S(2)}) collective-permute-start(bf16[2,4,16,5120]{3,2,1,0:T(8,128)(2,1)} %pad_maximum_fusion.8.refs_4_), channel_id=1, source_target_pairs={{0,8},{8,0},{1,9},{9,1},{2,10},{10,2},{3,11},{11,3},{4,12},{12,4},... | collective-permute-start | bytes 3932168 | tf_op jit(solution)/shard_map/ppermute | solution.py:58
  93.5 30.8 %collective-permute-start.20 = (bf16[2,4,16,5120]{3,2,1,0:T(8,128)(2,1)}, bf16[2,4,16,5120]{3,2,1,0:T(8,128)(2,1)}, u32[]{:S(2)}, u32[]{:S(2)}) collective-permute-start(bf16[2,4,16,5120]{3,2,1,0:T(8,128)(2,1)} %pad_maximum_fusion.8.refs_4_), channel_id=1, source_target_pairs={{0,1},{1,0},{2,3},{3,2},{4,5},{5,4},{6,7},{7,6},{8,9},{9,8},{10,11... | collective-permute-start | bytes 3932168 | tf_op jit(solution)/shard_map/ppermute | solution.py:58
  126.1 43.9 %collective-permute-start.28 = (bf16[128,1024]{1,0:T(8,128)(2,1)S(1)}, bf16[128,1024]{1,0:T(8,128)(2,1)S(1)}, u32[]{:S(2)}, u32[]{:S(2)}) collective-permute-start(bf16[128,1024]{1,0:T(8,128)(2,1)S(1)} %copy-done.66), channel_id=1, source_target_pairs={{0,6},{2,0},{4,2},{6,4},{1,7},{3,1},{5,3},{7,5},{8,14},{10,8},{12,... | collective-permute-start | bytes 786440 | tf_op jit(solution)/shard_map/ppermute | solution.py:58
  126.2 43.9 %collective-permute-start.27 = (bf16[128,1024]{1,0:T(8,128)(2,1)S(1)}, bf16[128,1024]{1,0:T(8,128)(2,1)}, u32[]{:S(2)}, u32[]{:S(2)}) collective-permute-start(bf16[128,1024]{1,0:T(8,128)(2,1)S(1)} %copy-done.66), channel_id=1, source_target_pairs={{0,4},{2,6},{4,0},{6,2},{1,5},{3,7},{5,1},{7,3},{8,12},{10,14},{12... | collective-permute-start | bytes 786440 | tf_op jit(solution)/shard_map/ppermute | solution.py:58
  127.5 43.3 %collective-permute-start.26 = (bf16[128,1024]{1,0:T(8,128)(2,1)S(1)}, bf16[128,1024]{1,0:T(8,128)(2,1)}, u32[]{:S(2)}, u32[]{:S(2)}) collective-permute-start(bf16[128,1024]{1,0:T(8,128)(2,1)S(1)} %copy-done.66), channel_id=1, source_target_pairs={{0,2},{2,4},{4,6},{6,0},{1,3},{3,5},{5,7},{7,1},{8,10},{10,12},{12... | collective-permute-start | bytes 786440 | tf_op jit(solution)/shard_map/ppermute | solution.py:58
  143.2 29.9 %collective-permute-start.24 = (bf16[2,4,16,5120]{3,2,1,0:T(8,128)(2,1)}, bf16[2,4,16,5120]{3,2,1,0:T(8,128)(2,1)S(1)}, u32[]{:S(2)}, u32[]{:S(2)}) collective-permute-start(bf16[2,4,16,5120]{3,2,1,0:T(8,128)(2,1)} %copy-done.18), channel_id=1, source_target_pairs={{0,1},{1,0},{2,3},{3,2},{4,5},{5,4},{6,7},{7,6},{8,9},{9,8},{10,11... | collective-permute-start | bytes 3932168 | tf_op jit(solution)/shard_map/ppermute | solution.py:58
  143.2 29.9 %collective-permute-start.25 = (bf16[2,4,16,5120]{3,2,1,0:T(8,128)(2,1)}, bf16[2,4,16,5120]{3,2,1,0:T(8,128)(2,1)S(1)}, u32[]{:S(2)}, u32[]{:S(2)}) collective-permute-start(bf16[2,4,16,5120]{3,2,1,0:T(8,128)(2,1)} %collective-permute-done.22.refs_5_), channel_id=1, source_target_pairs={{0,1},{1,0},{2,3},{3,2},{4,5},{5,4},{6,7},{7,6},{8,9},{9,8},{10,11... | collective-permute-start | bytes 3932168 | tf_op jit(solution)/shard_map/ppermute | solution.py:58
  174.4 22.4 %collective-permute-start.31 = (bf16[2,104,1024]{2,1,0:T(8,128)(2,1)}, bf16[2,104,1024]{2,1,0:T(8,128)(2,1)}, u32[]{:S(2)}, u32[]{:S(2)}) collective-permute-start(bf16[2,104,1024]{2,1,0:T(8,128)(2,1)} %pad_maximum_fusion.28), channel_id=1, source_target_pairs={{0,2},{2,4},{4,6},{6,0},{1,3},{3,5},{5,7},{7,1},{8,10},{10,12},{12... | collective-permute-start | bytes 1277960 | tf_op jit(solution)/shard_map/ppermute | solution.py:58
  174.7 22.1 %collective-permute-start.32 = (bf16[2,104,1024]{2,1,0:T(8,128)(2,1)}, bf16[2,104,1024]{2,1,0:T(8,128)(2,1)}, u32[]{:S(2)}, u32[]{:S(2)}) collective-permute-start(bf16[2,104,1024]{2,1,0:T(8,128)(2,1)} %pad_maximum_fusion.30), channel_id=1, source_target_pairs={{0,6},{2,0},{4,2},{6,4},{1,7},{3,1},{5,3},{7,5},{8,14},{10,8},{12,... | collective-permute-start | bytes 1277960 | tf_op jit(solution)/shard_map/ppermute | solution.py:58
  196.8 24.6 %collective-permute-start.35 = (bf16[2,4,64,1024]{3,2,1,0:T(8,128)(2,1)S(1)}, bf16[2,4,64,1024]{3,2,1,0:T(8,128)(2,1)S(1)}, u32[]{:S(2)}, u32[]{:S(2)}) collective-permute-start(bf16[2,4,64,1024]{3,2,1,0:T(8,128)(2,1)S(1)} %pad_maximum_fusion.9.refs_0_), channel_id=1, source_target_pairs={{0,1},{1,0},{2,3},{3,2},{4,5},{5,4},{6,7},{7,6},{8,9},{9,8},{10,11... | collective-permute-start | bytes 3145736 | tf_op jit(solution)/shard_map/ppermute | solution.py:58
  196.9 25.6 %collective-permute-start.33 = (bf16[2,4,64,1024]{3,2,1,0:T(8,128)(2,1)S(1)}, bf16[2,4,64,1024]{3,2,1,0:T(8,128)(2,1)S(1)}, u32[]{:S(2)}, u32[]{:S(2)}) collective-permute-start(bf16[2,4,64,1024]{3,2,1,0:T(8,128)(2,1)S(1)} %pad_maximum_fusion.9.refs_0_), channel_id=1, source_target_pairs={{0,16},{16,0},{1,17},{17,1},{2,18},{18,2},{3,19},{19,3},{4,20},{20... | collective-permute-start | bytes 3145736 | tf_op jit(solution)/shard_map/ppermute | solution.py:58
  198.4 24.0 %collective-permute-start.36 = (bf16[2,4,64,1024]{3,2,1,0:T(8,128)(2,1)S(1)}, bf16[2,4,64,1024]{3,2,1,0:T(8,128)(2,1)S(1)}, u32[]{:S(2)}, u32[]{:S(2)}) collective-permute-start(bf16[2,4,64,1024]{3,2,1,0:T(8,128)(2,1)S(1)} %pad_maximum_fusion.10.refs_4_), channel_id=1, source_target_pairs={{0,1},{1,0},{2,3},{3,2},{4,5},{5,4},{6,7},{7,6},{8,9},{9,8},{10,11... | collective-permute-start | bytes 3145736 | tf_op jit(solution)/shard_map/ppermute | solution.py:58
  198.6 25.4 %collective-permute-start.34 = (bf16[2,4,64,1024]{3,2,1,0:T(8,128)(2,1)S(1)}, bf16[2,4,64,1024]{3,2,1,0:T(8,128)(2,1)S(1)}, u32[]{:S(2)}, u32[]{:S(2)}) collective-permute-start(bf16[2,4,64,1024]{3,2,1,0:T(8,128)(2,1)S(1)} %pad_maximum_fusion.10.refs_4_), channel_id=1, source_target_pairs={{0,8},{8,0},{1,9},{9,1},{2,10},{10,2},{3,11},{11,3},{4,12},{12,4},... | collective-permute-start | bytes 3145736 | tf_op jit(solution)/shard_map/ppermute | solution.py:58
  264.5 25.3 %collective-permute-start.41 = (bf16[2,4,64,1024]{3,2,1,0:T(8,128)(2,1)S(1)}, bf16[2,4,64,1024]{3,2,1,0:T(8,128)(2,1)}, u32[]{:S(2)}, u32[]{:S(2)}) collective-permute-start(bf16[2,4,64,1024]{3,2,1,0:T(8,128)(2,1)S(1)} %get-tuple-element.435), channel_id=1, source_target_pairs={{0,16},{16,0},{1,17},{17,1},{2,18},{18,2},{3,19},{19,3},{4,20},{20... | collective-permute-start | bytes 3145736 | tf_op jit(solution)/shard_map/ppermute | solution.py:58
  265.1 24.9 %collective-permute-start.42 = (bf16[2,4,64,1024]{3,2,1,0:T(8,128)(2,1)S(1)}, bf16[2,4,64,1024]{3,2,1,0:T(8,128)(2,1)}, u32[]{:S(2)}, u32[]{:S(2)}) collective-permute-start(bf16[2,4,64,1024]{3,2,1,0:T(8,128)(2,1)S(1)} %copy-done.75), channel_id=1, source_target_pairs={{0,8},{8,0},{1,9},{9,1},{2,10},{10,2},{3,11},{11,3},{4,12},{12,4},... | collective-permute-start | bytes 3145736 | tf_op jit(solution)/shard_map/ppermute | solution.py:58
  321.7 25.0 %collective-permute-start.48 = (bf16[2,4,16,4096]{3,2,1,0:T(8,128)(2,1)S(1)}, bf16[2,4,16,4096]{3,2,1,0:T(8,128)(2,1)S(1)}, u32[]{:S(2)}, u32[]{:S(2)}) collective-permute-start(bf16[2,4,16,4096]{3,2,1,0:T(8,128)(2,1)S(1)} %get-tuple-element.466), channel_id=1, source_target_pairs={{0,16},{16,0},{1,17},{17,1},{2,18},{18,2},{3,19},{19,3},{4,20},{20... | collective-permute-start | bytes 3145736 | tf_op jit(solution)/shard_map/ppermute | solution.py:58
  322.3 24.6 %collective-permute-start.49 = (bf16[2,4,16,4096]{3,2,1,0:T(8,128)(2,1)}, bf16[2,4,16,4096]{3,2,1,0:T(8,128)(2,1)S(1)}, u32[]{:S(2)}, u32[]{:S(2)}) collective-permute-start(bf16[2,4,16,4096]{3,2,1,0:T(8,128)(2,1)} %get-tuple-element.468), channel_id=1, source_target_pairs={{0,8},{8,0},{1,9},{9,1},{2,10},{10,2},{3,11},{11,3},{4,12},{12,4},... | collective-permute-start | bytes 3145736 | tf_op jit(solution)/shard_map/ppermute | solution.py:58
  323.0 23.3 %collective-permute-start.52 = (bf16[2,104,1024]{2,1,0:T(8,128)(2,1)}, bf16[2,104,1024]{2,1,0:T(8,128)(2,1)}, u32[]{:S(2)}, u32[]{:S(2)}) collective-permute-start(bf16[2,104,1024]{2,1,0:T(8,128)(2,1)} %get-tuple-element.673), channel_id=1, source_target_pairs={{0,2},{2,4},{4,6},{6,0},{1,3},{3,5},{5,7},{7,1},{8,10},{10,12},{12... | collective-permute-start | bytes 1277960 | tf_op jit(solution)/shard_map/ppermute | solution.py:58
  324.8 22.0 %collective-permute-start.51 = (bf16[128,1024]{1,0:T(8,128)(2,1)}, bf16[128,1024]{1,0:T(8,128)(2,1)}, u32[]{:S(2)}, u32[]{:S(2)}) collective-permute-start(bf16[128,1024]{1,0:T(8,128)(2,1)} %pad_maximum_fusion.36), channel_id=1, source_target_pairs={{0,6},{2,0},{4,2},{6,4},{1,7},{3,1},{5,3},{7,5},{8,14},{10,8},{12,... | collective-permute-start | bytes 786440 | tf_op jit(solution)/shard_map/ppermute | solution.py:58
  348.2 24.0 %collective-permute-start.55 = (bf16[512,1024]{1,0:T(8,128)(2,1)S(1)}, bf16[512,1024]{1,0:T(8,128)(2,1)S(1)}, u32[]{:S(2)}, u32[]{:S(2)}) collective-permute-start(bf16[512,1024]{1,0:T(8,128)(2,1)S(1)} %weight_grad.12), channel_id=1, source_target_pairs={{0,1},{1,0},{2,3},{3,2},{4,5},{5,4},{6,7},{7,6},{8,9},{9,8},{10,11... | collective-permute-start | bytes 3145736 | tf_op jit(solution)/shard_map/ppermute | solution.py:58
  348.3 23.9 %collective-permute-start.53 = (bf16[4,16,4096]{2,1,0:T(8,128)(2,1)}, bf16[4,16,4096]{2,1,0:T(8,128)(2,1)S(1)}, u32[]{:S(2)}, u32[]{:S(2)}) collective-permute-start(bf16[4,16,4096]{2,1,0:T(8,128)(2,1)} %get-tuple-element.496), channel_id=1, source_target_pairs={{0,8},{8,0},{1,9},{9,1},{2,10},{10,2},{3,11},{11,3},{4,12},{12,4},... | collective-permute-start | bytes 1572872 | tf_op jit(solution)/shard_map/ppermute | solution.py:58
  349.6 22.6 %collective-permute-start.54 = (bf16[4,16,4096]{2,1,0:T(8,128)(2,1)S(1)}, bf16[4,16,4096]{2,1,0:T(8,128)(2,1)S(1)}, u32[]{:S(2)}, u32[]{:S(2)}) collective-permute-start(bf16[4,16,4096]{2,1,0:T(8,128)(2,1)S(1)} %get-tuple-element.498), channel_id=1, source_target_pairs={{0,16},{16,0},{1,17},{17,1},{2,18},{18,2},{3,19},{19,3},{4,20},{20... | collective-permute-start | bytes 1572872 | tf_op jit(solution)/shard_map/ppermute | solution.py:58
  417.5 24.2 %collective-permute-start.66 = (bf16[4,104,1024]{2,1,0:T(8,128)(2,1)}, bf16[4,104,1024]{2,1,0:T(8,128)(2,1)}, u32[]{:S(2)}, u32[]{:S(2)}) collective-permute-start(bf16[4,104,1024]{2,1,0:T(8,128)(2,1)} %slice_bitcast_fusion.2), channel_id=1, source_target_pairs={{0,1},{1,0},{2,3},{3,2},{4,5},{5,4},{6,7},{7,6},{8,9},{9,8},{10,11... | collective-permute-start | bytes 2555912 | tf_op jit(solution)/shard_map/ppermute | solution.py:58
  417.5 24.2 %collective-permute-start.62 = (bf16[2,4,16,3072]{3,2,1,0:T(8,128)(2,1)}, bf16[2,4,16,3072]{3,2,1,0:T(8,128)(2,1)}, u32[]{:S(2)}, u32[]{:S(2)}) collective-permute-start(bf16[2,4,16,3072]{3,2,1,0:T(8,128)(2,1)} %get-tuple-element.557), channel_id=1, source_target_pairs={{0,16},{16,0},{1,17},{17,1},{2,18},{18,2},{3,19},{19,3},{4,20},{20... | collective-permute-start | bytes 2359304 | tf_op jit(solution)/shard_map/ppermute | solution.py:58
  418.1 23.7 %collective-permute-start.63 = (bf16[2,4,16,3072]{3,2,1,0:T(8,128)(2,1)S(1)}, bf16[2,4,16,3072]{3,2,1,0:T(8,128)(2,1)}, u32[]{:S(2)}, u32[]{:S(2)}) collective-permute-start(bf16[2,4,16,3072]{3,2,1,0:T(8,128)(2,1)S(1)} %get-tuple-element.559), channel_id=1, source_target_pairs={{0,8},{8,0},{1,9},{9,1},{2,10},{10,2},{3,11},{11,3},{4,12},{12,4},... | collective-permute-start | bytes 2359304 | tf_op jit(solution)/shard_map/ppermute | solution.py:58
  459.5 23.6 %collective-permute-start.77 = (bf16[4,104,1024]{2,1,0:T(8,128)(2,1)S(1)}, bf16[4,104,1024]{2,1,0:T(8,128)(2,1)S(1)}, u32[]{:S(2)}, u32[]{:S(2)}) collective-permute-start(bf16[4,104,1024]{2,1,0:T(8,128)(2,1)S(1)} %get-tuple-element.668), channel_id=1, source_target_pairs={{0,1},{1,0},{2,3},{3,2},{4,5},{5,4},{6,7},{7,6},{8,9},{9,8},{10,11... | collective-permute-start | bytes 2555912 | tf_op jit(solution)/shard_map/ppermute | solution.py:58
  (125 other events, 1311.4 us)

commit v8 on v7

--- a/solution.py
+++ b/solution.py
@@ -959,10 +959,9 @@
     active, slope, active_far = rise(normed_two, full_up, bu, ranks)
     if active_far is None:
         active_far = ring.by_distance(active, ring.target(ff))
-    mixed_far = ring.by_distance(mixed, target)
     two_far = ring.by_distance(normed_two, target)
-    three, three_more, three_core, active, active_far, mixed_far, two_far, cot_rest = tie(
-        three, three_more, three_core, active, active_far, mixed_far, two_far, cot_rest
+    three, three_more, three_core, active, active_far, two_far, cot_rest = tie(
+        three, three_more, three_core, active, active_far, two_far, cot_rest
     )
 
     three_more_core = ring.to_core(three_more)
@@ -978,13 +977,14 @@
 
     d = ring.kept(active_far, grad_low, share, d)
     result = slots_of(land(active, full_down, residual, bd, packing))
-    d, result = tie(d, result)
+    d, result, mixed = tie(d, result, mixed)
 
     d = ring.first(d)
+    mixed_far = ring.by_distance(mixed, target)
     back = ring.send(result, inner, -1)
     hidden_low, grad_bu = fall(grad_low, full_down, slope)
     sent = weight_grad(two_far, 1, hidden_low, share)
-    d, sent, back = tie(d, sent, back)
+    d, sent, back, mixed_far = tie(d, sent, back, mixed_far)
 
     d = ring.again(d)
     d, sent = tie(d, sent)

time: 499 us -> 500 us (level)
    unnamed x168 -> x176, local copies, waits for them, and re-layouts: 16.5 us -> 18.9 us
  transfers between devices with their start and end apart: 81 -> 81, of which waited for: 27 -> 25; matrix products, arithmetic and copies ran while one was open for 9% -> 9% of each run, Pallas kernels for 34% -> 34%
where the time goes in v8:
time: 500 us; the launch traced here: 497 us
  Pallas kernels  199 us (40%)
  waiting for transfers between devices  116 us (23%)
  starting transfers between devices  93.2 us (19%)
  other arithmetic  53.4 us (11%)
  local copies, waits for them, and re-layouts  33.2 us (7%)
    ppermute x81, waiting for transfers between devices, shifted(): lax.ppermute(array, axis, [(i, (i + step) % size) for i in range(size)])  116 us
    ppermute x81, starting transfers between devices, shifted(): lax.ppermute(array, axis, [(i, (i + step) % size) for i in range(size)])  93.2 us
    pallas_call x8, Pallas kernels, weight_grad(): pl.pallas_call(body, out_shape=[jax.ShapeDtypeStruct(shape, bf16) for sha...  45.9 us
    pallas_call x2, Pallas kernels, attend_back(): pl.pallas_call(attend_back_body, out_shape=[jax.ShapeDtypeStruct((PACKED,...  26.4 us
    pallas_call x2, Pallas kernels, back_norm(): pl.pallas_call(body, out_shape=shapes + [jax.ShapeDtypeStruct((8, width),...  25.4 us
    pallas_call x3, Pallas kernels, assemble(): pl.pallas_call(body, out_shape=[jax.ShapeDtypeStruct((planes_all, depth,...  20.9 us
    unnamed x176, local copies, waits for them, and re-layouts  18.9 us
    pallas_call x1, Pallas kernels, rise(): pl.pallas_call(body, out_shape=shapes, grid_spec=pltpu.PrefetchScalarGrid...  15.4 us
  transfers between devices with their start and end apart: 81, of which 25 were waited for; matrix products, arithmetic and copies ran while one was open for 9% of the time, Pallas kernels for 34%

profile of v8, /device:TPU:0, one launch (start us, length us, event | category | flops | bytes accessed | tf_op | source)
XLA Modules:
  0.0 497.3 jit_solution(1031965980130296955)
XLA Ops:
  2.4 5.0 %collective-permute-start.2 = (bf16[32,3328]{1,0:T(8,128)(2,1)}, bf16[32,3328]{1,0:T(8,128)(2,1)}, u32[]{:S(2)}, u32[]{:S(2)}) collective-permute-start(bf16[32,3328]{1,0:T(8,128)(2,1)} %seed.1), channel_id=1, source_target_pairs={{0,6},{2,0},{4,2},{6,4},{1,7},{3,1},{5,3},{7,5},{8,14},{10,8},{12,... | collective-permute-start | bytes 638984 | tf_op jit(solution)/shard_map/ppermute | solution.py:58
  20.0 5.8 %collective-permute-done.1 = bf16[32,3328]{1,0:T(8,128)(2,1)} collective-permute-done((bf16[32,3328]{1,0:T(8,128)(2,1)}, bf16[32,3328]{1,0:T(8,128)(2,1)}, u32[]{:S(2)}, u32[]{:S(2)}) %collective-permute-start.1) | collective-permute-done | bytes 213024 | tf_op jit(solution)/shard_map/ppermute | solution.py:58
  41.3 4.2 collective-permute-done.7
  48.6 20.4 %collective-permute-done.12 = bf16[32,5120]{1,0:T(8,128)(2,1)S(1)} collective-permute-done((bf16[32,5120]{1,0:T(8,128)(2,1)S(1)}, bf16[32,5120]{1,0:T(8,128)(2,1)S(1)}, u32[]{:S(2)}, u32[]{:S(2)}) %collective-permute-start.12) | collective-permute-done | bytes 327712 | tf_op jit(solution)/shard_map/ppermute | solution.py:58
  73.2 13.1 %collective-permute-done.16 = bf16[4,16,5120]{2,1,0:T(8,128)(2,1)S(1)} collective-permute-done((bf16[4,16,5120]{2,1,0:T(8,128)(2,1)S(1)}, bf16[4,16,5120]{2,1,0:T(8,128)(2,1)S(1)}, u32[]{:S(2)}, u32[]{:S(2)}) %collective-permute-start.16) | collective-permute-done | bytes 655392 | tf_op jit(solution)/shard_map/ppermute | solution.py:58
  98.6 5.4 %assemble.3 = (bf16[4,4,2,2,16,3072]{5,4,3,2,1,0:T(8,128)(2,1)}, bf16[4,4,2,2,16,256]{5,4,3,2,1,0:T(8,128)(2,1)S(1)}) custom-call(s32[32]{0:T(128)S(1)} %stack.422.table_ref, bf16[4,4,16,3328]{3,2,1,0:T(8,128)(2,1)} %copy-done.36, bf16[4,4,16,3328]{3,2,1,0:T(8,128)(2,1)} %copy-done.41, bf16[2,4,16,3328]{3,2,1,0:T(8,128)(2,1)S(1)} %collective-permute-done.9.refs_2_, ...), custom_call_target="tpu_custom_call" | custom-call | bytes 272629 | tf_op jit(solution)/shard_map/assemble/pallas_call | solution.py:171
  104.9 10.0 %collective-permute-done.23 = bf16[2,104,1024]{2,1,0:T(8,128)(2,1)} collective-permute-done((bf16[2,104,1024]{2,1,0:T(8,128)(2,1)}, bf16[2,104,1024]{2,1,0:T(8,128)(2,1)}, u32[]{:S(2)}, u32[]{:S(2)}) %collective-permute-start.23) | collective-permute-done | bytes 426016 | tf_op jit(solution)/shard_map/ppermute | solution.py:58
  114.9 6.0 %collective-permute-done.21.refs_1_ = bf16[2,4,16,5120]{3,2,1,0:T(8,128)(2,1)S(1)} collective-permute-done((bf16[2,4,16,5120]{3,2,1,0:T(8,128)(2,1)S(1)}, bf16[2,4,16,5120]{3,2,1,0:T(8,128)(2,1)S(1)}, u32[]{:S(2)}, u32[]{:S(2)}) %collective-permute-start.21) | collective-permute-done | bytes 1310752 | tf_op jit(solution)/shard_map/ppermute | solution.py:58
  127.5 13.8 %collective-permute-start.26 = (bf16[128,1024]{1,0:T(8,128)(2,1)S(1)}, bf16[128,1024]{1,0:T(8,128)(2,1)}, u32[]{:S(2)}, u32[]{:S(2)}) collective-permute-start(bf16[128,1024]{1,0:T(8,128)(2,1)S(1)} %copy-done.69), channel_id=1, source_target_pairs={{0,2},{2,4},{4,6},{6,0},{1,3},{3,5},{5,7},{7,1},{8,10},{10,12},{12... | collective-permute-start | bytes 786440 | tf_op jit(solution)/shard_map/ppermute | solution.py:58
  147.3 7.6 %project.1.q_ref.k_ref.v_ref = bf16[592,3072]{1,0:T(8,128)(2,1)} custom-call(bf16[592,1024]{1,0:T(8,128)(2,1)S(1)} %get-tuple-element.482.x_ref, bf16[1024,3072]{1,0:T(8,128)(2,1)} %bitcast.260, f32[1,3072]{1,0:T(1,128)S(1)} %reshape_reshape.3.b_ref), custom_call_target="tpu_custom_call" | custom-call | flops 120000000 | bytes 240000 | tf_op jit(solution)/shard_map/project/pallas_call | solution.py:625
  156.0 14.1 %attend.1 = (bf16[592,1024]{1,0:T(8,128)(2,1)S(1)}, f32[64,592]{1,0:T(8,128)S(1)}) custom-call(bf16[592,3072]{1,0:T(8,128)(2,1)} %project.1.q_ref.k_ref.v_ref, bf16[592,3072]{1,0:T(8,128)(2,1)} %project.1.q_ref.k_ref.v_ref, bf16[592,3072]{1,0:T(8,128)(2,1)} %project.1.q_ref.k_ref.v_ref), custom_call_target="tpu_custom_call" | custom-call | flops 240000000 | bytes 290979 | tf_op jit(solution)/shard_map/attend/pallas_call | solution.py:453
  179.3 8.8 %assemble.4 = (bf16[4,4,2,2,16,1024]{5,4,3,2,1,0:T(8,128)(2,1)}, bf16[4,4,2,2,16,4096]{5,4,3,2,1,0:T(8,128)(2,1)}) custom-call(s32[32]{0:T(128)S(1)} %stack.439.table_ref, bf16[2,4,16,5120]{3,2,1,0:T(8,128)(2,1)S(1)} %copy-done.8, bf16[2,4,16,5120]{3,2,1,0:T(8,128)(2,1)S(1)} %copy-done.19, bf16[2,4,16,5120]{3,2,1,0:T(8,128)(2,1)} %collective-permute-done.19.refs_2_, ...), custom_call_target="tpu_custom_call" | custom-call | bytes 419430 | tf_op jit(solution)/shard_map/assemble/pallas_call | solution.py:171
  188.0 5.1 %out_norm.1 = (f32[592,1024]{1,0:T(8,128)}, bf16[592,1024]{1,0:T(8,128)(2,1)S(1)}) custom-call(bf16[592,1024]{1,0:T(8,128)(2,1)S(1)} %copy-done.12, bf16[1024,1024]{1,0:T(8,128)(2,1)} %bitcast.262, f32[592,1024]{1,0:T(8,128)} %get-tuple-element.397.t_ref.refs_2_, f32[1,1024]{1,0:T(1,128)S(1)} %reshape_reshape_squeeze.25.b_ref, ...), custom_call_target="tpu_custom_call" | custom-call | flops 40000000 | bytes 160000 | tf_op jit(solution)/shard_map/out_norm/pallas_call | solution.py:724
  202.8 15.4 %rise.1 = (bf16[592,4096]{1,0:T(8,128)(2,1)}, f32[592,4096]{1,0:T(8,128)}, bf16[2,592,2048]{2,1,0:T(8,128)(2,1)}) custom-call(s32[32]{0:T(128)S(1)} %fusion.92.rank_ref, bf16[592,1024]{1,0:T(8,128)(2,1)S(1)} %get-tuple-element.403.x_ref, bf16[1024,4096]{1,0:T(8,128)(2,1)} %bitcast.258, f32[1,4096]{1,0:T(1,128)S(1)} %slice_bitcast_fusion.36.b_ref), custom_call_target="tpu_custom_call" | custom-call | flops 240000000 | bytes 600000 | tf_op jit(solution)/shard_map/rise/pallas_call | solution.py:572
  227.0 7.1 %weight_grad.8 = bf16[2048,1024]{1,0:T(8,128)(2,1)} custom-call(bf16[2,592,2048]{2,1,0:T(8,128)(2,1)} %get-tuple-element.411.refs_0_, bf16[592,1024]{1,0:T(8,128)(2,1)S(1)} %get-tuple-element.419.refs_1_.g_ref.refs_4_), custom_call_target="tpu_custom_call" | custom-call | flops 49660560 | bytes 167772 | tf_op jit(solution)/shard_map/weight_grad/pallas_call | solution.py:371
  239.3 6.7 %assemble.5 = bf16[4,4,2,2,64,1024]{5,4,3,2,1,0:T(8,128)(2,1)} custom-call(s32[32]{0:T(128)S(1)} %stack.439.table_ref, bf16[2,4,64,1024]{3,2,1,0:T(8,128)(2,1)S(1)} %copy-done.15, bf16[2,4,64,1024]{3,2,1,0:T(8,128)(2,1)S(1)} %copy-done.23, bf16[2,4,64,1024]{3,2,1,0:T(8,128)(2,1)S(1)} %copy-done.21, bf16[2,4,64,1024]{3,2,1,0:T(8,128)(2,1)} %copy-done.51, ...), custom_call_target="tpu_custom_call" | custom-call | bytes 335544 | tf_op jit(solution)/shard_map/assemble/pallas_call | solution.py:171
  246.0 7.7 %weight_grad.9 = (bf16[2,4,64,1024]{3,2,1,0:T(8,128)(2,1)S(1)}, bf16[2,4,64,1024]{3,2,1,0:T(8,128)(2,1)S(1)}, bf16[2,4,64,1024]{3,2,1,0:T(8,128)(2,1)S(1)}, bf16[2,4,64,1024]{3,2,1,0:T(8,128)(2,1)}) custom-call(bf16[2,592,2048]{2,1,0:T(8,128)(2,1)} %get-tuple-element.411.refs_0_, bf16[592,1024]{1,0:T(8,128)(2,1)} %copy-done, ...), custom_call_target="tpu_custom_call" | custom-call | flops 49660560 | bytes 167772 | tf_op jit(solution)/shard_map/weight_grad/pallas_call | solution.py:371
  253.7 11.4 %land.1 = bf16[832,1024]{1,0:T(8,128)(2,1)S(1)} custom-call(bf16[592,4096]{1,0:T(8,128)(2,1)} %get-tuple-element.432.a_ref, bf16[4096,1024]{1,0:T(8,128)(2,1)} %bitcast.256, f32[592,1024]{1,0:T(8,128)} %get-tuple-element.434.r_ref.refs_2_, f32[1,1024]{1,0:T(1,128)S(1)} %reshape_reshape_squeeze.29.b_ref, bf16[592,832]{1,0:T(8,128)(2,1)S(1)} %fusion.p_ref.refs_5_), custom_call_target="tpu_custom_call" | custom-call | flops 120000000 | bytes 280000 | tf_op jit(solution)/shard_map/land/pallas_call | solution.py:757
  270.6 11.0 %fall.1 = (bf16[592,4096]{1,0:T(8,128)(2,1)}, f32[1,4096]{1,0:T(1,128)S(1)}) custom-call(bf16[592,1024]{1,0:T(8,128)(2,1)S(1)} %copy-done.1, bf16[4096,1024]{1,0:T(8,128)(2,1)} %bitcast.257, f32[592,4096]{1,0:T(8,128)} %get-tuple-element.440.slope_ref), custom_call_target="tpu_custom_call" | custom-call | flops 200000000 | bytes 500000 | tf_op jit(solution)/shard_map/fall/pallas_call | solution.py:602
  281.6 7.4 %weight_grad.10 = bf16[512,4096]{1,0:T(8,128)(2,1)} custom-call(bf16[2,592,512]{2,1,0:T(8,128)(2,1)S(1)} %by_distance.3.refs_0_, bf16[592,4096]{1,0:T(8,128)(2,1)} %get-tuple-element.441.refs_1_.refs_0_), custom_call_target="tpu_custom_call" | custom-call | flops 49660560 | bytes 167772 | tf_op jit(solution)/shard_map/weight_grad/pallas_call | solution.py:371
  297.4 13.2 %back_norm.2 = (f32[592,1024]{1,0:T(8,128)}, bf16[592,1024]{1,0:T(8,128)(2,1)S(1)}, f32[8,1024]{1,0:T(8,128)S(1)}) custom-call(bf16[592,4096]{1,0:T(8,128)(2,1)} %get-tuple-element.441.refs_1_.refs_0_, bf16[1024,4096]{1,0:T(8,128)(2,1)} %bitcast.259, f32[592,1024]{1,0:T(8,128)} %get-tuple-element.434.r_ref.refs_2_, ...), custom_call_target="tpu_custom_call" | custom-call | flops 120000000 | bytes 400000 | tf_op jit(solution)/shard_map/back_norm/pallas_call | solution.py:829
  310.7 8.1 %weight_grad.11 = (bf16[2,4,16,4096]{3,2,1,0:T(8,128)(2,1)S(1)}, bf16[2,4,16,4096]{3,2,1,0:T(8,128)(2,1)S(1)}, bf16[2,4,16,4096]{3,2,1,0:T(8,128)(2,1)S(1)}, bf16[2,4,16,4096]{3,2,1,0:T(8,128)(2,1)}) custom-call(bf16[2,592,512]{2,1,0:T(8,128)(2,1)} %copy-done.4, bf16[592,4096]{1,0:T(8,128)(2,1)} %get-tuple-element.441.refs_1_.refs_0_, ...), custom_call_target="tpu_custom_call" | custom-call | flops 49660560 | bytes 167772 | tf_op jit(solution)/shard_map/weight_grad/pallas_call | solution.py:371
  335.5 12.2 %attend_back.2 = (bf16[592,1536]{1,0:T(8,128)(2,1)S(1)}, f32[1,1536]{1,0:T(1,128)S(1)}) custom-call(bf16[592,3072]{1,0:T(8,128)(2,1)} %project.1.q_ref.k_ref.v_ref, bf16[592,3072]{1,0:T(8,128)(2,1)} %project.1.q_ref.k_ref.v_ref, bf16[592,3072]{1,0:T(8,128)(2,1)} %project.1.q_ref.k_ref.v_ref, f32[64,592]{1,0:T(8,128)S(1)} %copy-done.31, ...), custom_call_target="tpu_custom_call" | custom-call | flops 240000000 | bytes 290979 | tf_op jit(solution)/shard_map/attend_back/pallas_call | solution.py:509
  354.3 14.2 %attend_back.3 = (bf16[592,3072]{1,0:T(8,128)(2,1)}, f32[1,3072]{1,0:T(1,128)S(1)}) custom-call(bf16[592,3072]{1,0:T(8,128)(2,1)} %project.1.q_ref.k_ref.v_ref, bf16[592,3072]{1,0:T(8,128)(2,1)} %project.1.q_ref.k_ref.v_ref, bf16[592,3072]{1,0:T(8,128)(2,1)} %project.1.q_ref.k_ref.v_ref, f32[64,592]{1,0:T(8,128)S(1)} %copy-done.31, ...), custom_call_target="tpu_custom_call" | custom-call | flops 240000000 | bytes 290979 | tf_op jit(solution)/shard_map/attend_back/pallas_call | solution.py:509
  368.5 5.9 %weight_grad.13 = bf16[512,3072]{1,0:T(8,128)(2,1)} custom-call(bf16[2,592,512]{2,1,0:T(8,128)(2,1)S(1)} %by_distance.5.refs_0_, bf16[592,3072]{1,0:T(8,128)(2,1)} %get-tuple-element.536.refs_1_.refs_0_), custom_call_target="tpu_custom_call" | custom-call | flops 37245420 | bytes 125829 | tf_op jit(solution)/shard_map/weight_grad/pallas_call | solution.py:371
  382.0 12.1 %back_norm.3 = (bf16[832,1024]{1,0:T(8,128)(2,1)S(1)}, f32[8,1024]{1,0:T(8,128)S(1)}) custom-call(bf16[592,3072]{1,0:T(8,128)(2,1)} %get-tuple-element.536.refs_1_.refs_0_, bf16[1024,3072]{1,0:T(8,128)(2,1)} %bitcast.261, f32[592,1024]{1,0:T(8,128)} %get-tuple-element.397.t_ref.refs_2_, f32[1,1024]{1,0:T(1,128)S(1)} %reshape_reshape_squeeze.23.g_ref.refs_3_, ...), custom_call_target="tpu_custom_call" | custom-call | flops 120000000 | bytes 400000 | tf_op jit(solution)/shard_map/back_norm/pallas_call | solution.py:829
  404.2 6.4 %weight_grad.14 = (bf16[2,4,16,3072]{3,2,1,0:T(8,128)(2,1)S(1)}, bf16[2,4,16,3072]{3,2,1,0:T(8,128)(2,1)}, bf16[2,4,16,3072]{3,2,1,0:T(8,128)(2,1)S(1)}, bf16[2,4,16,3072]{3,2,1,0:T(8,128)(2,1)S(1)}) custom-call(bf16[2,592,512]{2,1,0:T(8,128)(2,1)} %copy-done.3, bf16[592,3072]{1,0:T(8,128)(2,1)} %get-tuple-element.536.refs_1_.refs_0_, ...), custom_call_target="tpu_custom_call" | custom-call | flops 37245420 | bytes 125829 | tf_op jit(solution)/shard_map/weight_grad/pallas_call | solution.py:371
  411.1 6.3 %collective-permute-done.60 = bf16[2,104,1024]{2,1,0:T(8,128)(2,1)} collective-permute-done((bf16[2,104,1024]{2,1,0:T(8,128)(2,1)}, bf16[2,104,1024]{2,1,0:T(8,128)(2,1)}, u32[]{:S(2)}, u32[]{:S(2)}) %collective-permute-start.60) | collective-permute-done | bytes 426016 | tf_op jit(solution)/shard_map/ppermute | solution.py:58
  426.5 16.7 %collective-permute-done.65 = bf16[2,104,1024]{2,1,0:T(8,128)(2,1)} collective-permute-done((bf16[2,104,1024]{2,1,0:T(8,128)(2,1)}, bf16[2,104,1024]{2,1,0:T(8,128)(2,1)}, u32[]{:S(2)}, u32[]{:S(2)}) %collective-permute-start.65) | collective-permute-done | bytes 426016 | tf_op jit(solution)/shard_map/ppermute | solution.py:58
  456.4 4.4 collective-permute-done.69
  460.8 5.8 %collective-permute-done.70 = bf16[4,16,3072]{2,1,0:T(8,128)(2,1)S(1)} collective-permute-done((bf16[4,16,3072]{2,1,0:T(8,128)(2,1)S(1)}, bf16[4,16,3072]{2,1,0:T(8,128)(2,1)S(1)}, u32[]{:S(2)}, u32[]{:S(2)}) %collective-permute-start.70) | collective-permute-done | bytes 393248 | tf_op jit(solution)/shard_map/ppermute | solution.py:58
  478.1 5.5 %collective-permute-done.73 = bf16[32,3072]{1,0:T(8,128)(2,1)S(1)} collective-permute-done((bf16[32,3072]{1,0:T(8,128)(2,1)S(1)}, bf16[32,3072]{1,0:T(8,128)(2,1)S(1)}, u32[]{:S(2)}, u32[]{:S(2)}) %collective-permute-start.73) | collective-permute-done | bytes 196640 | tf_op jit(solution)/shard_map/ppermute | solution.py:58
  (492 shorter events, 197.8 us)
Async XLA Ops:
  45.4 23.6 %collective-permute-start.12 = (bf16[32,5120]{1,0:T(8,128)(2,1)S(1)}, bf16[32,5120]{1,0:T(8,128)(2,1)S(1)}, u32[]{:S(2)}, u32[]{:S(2)}) collective-permute-start(bf16[32,5120]{1,0:T(8,128)(2,1)S(1)} %pad_maximum_fusion.32), channel_id=1, source_target_pairs={{0,4},{2,6},{4,0},{6,2},{1,5},{3,7},{5,1},{7,3},{8,12},{10,14},{12... | collective-permute-start | bytes 983048 | tf_op jit(solution)/shard_map/ppermute | solution.py:58
  45.5 24.1 %collective-permute-start.13 = (bf16[2,104,1024]{2,1,0:T(8,128)(2,1)S(1)}, bf16[2,104,1024]{2,1,0:T(8,128)(2,1)S(1)}, u32[]{:S(2)}, u32[]{:S(2)}) collective-permute-start(bf16[2,104,1024]{2,1,0:T(8,128)(2,1)S(1)} %pad_maximum_fusion.24), channel_id=1, source_target_pairs={{0,2},{2,4},{4,6},{6,0},{1,3},{3,5},{5,7},{7,1},{8,10},{10,12},{12... | collective-permute-start | bytes 1277960 | tf_op jit(solution)/shard_map/ppermute | solution.py:58
  45.6 23.9 %collective-permute-start.9 = (bf16[2,4,16,3328]{3,2,1,0:T(8,128)(2,1)S(1)}, bf16[2,4,16,3328]{3,2,1,0:T(8,128)(2,1)S(1)}, u32[]{:S(2)}, u32[]{:S(2)}) collective-permute-start(bf16[2,4,16,3328]{3,2,1,0:T(8,128)(2,1)S(1)} %pad_maximum_fusion.15), channel_id=1, source_target_pairs={{0,16},{16,0},{1,17},{17,1},{2,18},{18,2},{3,19},{19,3},{4,20},{20... | collective-permute-start | bytes 2555912 | tf_op jit(solution)/shard_map/ppermute | solution.py:58
  47.1 22.4 %collective-permute-start.10 = (bf16[2,4,16,3328]{3,2,1,0:T(8,128)(2,1)S(1)}, bf16[2,4,16,3328]{3,2,1,0:T(8,128)(2,1)S(1)}, u32[]{:S(2)}, u32[]{:S(2)}) collective-permute-start(bf16[2,4,16,3328]{3,2,1,0:T(8,128)(2,1)S(1)} %pad_maximum_fusion.16), channel_id=1, source_target_pairs={{0,8},{8,0},{1,9},{9,1},{2,10},{10,2},{3,11},{11,3},{4,12},{12,4},... | collective-permute-start | bytes 2555912 | tf_op jit(solution)/shard_map/ppermute | solution.py:58
  91.3 29.5 %collective-permute-start.21 = (bf16[2,4,16,5120]{3,2,1,0:T(8,128)(2,1)S(1)}, bf16[2,4,16,5120]{3,2,1,0:T(8,128)(2,1)S(1)}, u32[]{:S(2)}, u32[]{:S(2)}) collective-permute-start(bf16[2,4,16,5120]{3,2,1,0:T(8,128)(2,1)S(1)} %pad_maximum_fusion.7.refs_0_), channel_id=1, source_target_pairs={{0,16},{16,0},{1,17},{17,1},{2,18},{18,2},{3,19},{19,3},{4,20},{20... | collective-permute-start | bytes 3932168 | tf_op jit(solution)/shard_map/ppermute | solution.py:58
  92.9 28.0 %collective-permute-start.19 = (bf16[2,4,16,5120]{3,2,1,0:T(8,128)(2,1)S(1)}, bf16[2,4,16,5120]{3,2,1,0:T(8,128)(2,1)}, u32[]{:S(2)}, u32[]{:S(2)}) collective-permute-start(bf16[2,4,16,5120]{3,2,1,0:T(8,128)(2,1)S(1)} %pad_maximum_fusion.7.refs_0_), channel_id=1, source_target_pairs={{0,1},{1,0},{2,3},{3,2},{4,5},{5,4},{6,7},{7,6},{8,9},{9,8},{10,11... | collective-permute-start | bytes 3932168 | tf_op jit(solution)/shard_map/ppermute | solution.py:58
  92.9 31.5 %collective-permute-start.22 = (bf16[2,4,16,5120]{3,2,1,0:T(8,128)(2,1)}, bf16[2,4,16,5120]{3,2,1,0:T(8,128)(2,1)}, u32[]{:S(2)}, u32[]{:S(2)}) collective-permute-start(bf16[2,4,16,5120]{3,2,1,0:T(8,128)(2,1)} %pad_maximum_fusion.8.refs_4_), channel_id=1, source_target_pairs={{0,8},{8,0},{1,9},{9,1},{2,10},{10,2},{3,11},{11,3},{4,12},{12,4},... | collective-permute-start | bytes 3932168 | tf_op jit(solution)/shard_map/ppermute | solution.py:58
  93.6 30.8 %collective-permute-start.20 = (bf16[2,4,16,5120]{3,2,1,0:T(8,128)(2,1)}, bf16[2,4,16,5120]{3,2,1,0:T(8,128)(2,1)}, u32[]{:S(2)}, u32[]{:S(2)}) collective-permute-start(bf16[2,4,16,5120]{3,2,1,0:T(8,128)(2,1)} %pad_maximum_fusion.8.refs_4_), channel_id=1, source_target_pairs={{0,1},{1,0},{2,3},{3,2},{4,5},{5,4},{6,7},{7,6},{8,9},{9,8},{10,11... | collective-permute-start | bytes 3932168 | tf_op jit(solution)/shard_map/ppermute | solution.py:58
  126.1 44.0 %collective-permute-start.28 = (bf16[128,1024]{1,0:T(8,128)(2,1)S(1)}, bf16[128,1024]{1,0:T(8,128)(2,1)S(1)}, u32[]{:S(2)}, u32[]{:S(2)}) collective-permute-start(bf16[128,1024]{1,0:T(8,128)(2,1)S(1)} %copy-done.69), channel_id=1, source_target_pairs={{0,6},{2,0},{4,2},{6,4},{1,7},{3,1},{5,3},{7,5},{8,14},{10,8},{12,... | collective-permute-start | bytes 786440 | tf_op jit(solution)/shard_map/ppermute | solution.py:58
  126.2 44.0 %collective-permute-start.27 = (bf16[128,1024]{1,0:T(8,128)(2,1)S(1)}, bf16[128,1024]{1,0:T(8,128)(2,1)}, u32[]{:S(2)}, u32[]{:S(2)}) collective-permute-start(bf16[128,1024]{1,0:T(8,128)(2,1)S(1)} %copy-done.69), channel_id=1, source_target_pairs={{0,4},{2,6},{4,0},{6,2},{1,5},{3,7},{5,1},{7,3},{8,12},{10,14},{12... | collective-permute-start | bytes 786440 | tf_op jit(solution)/shard_map/ppermute | solution.py:58
  127.5 43.4 %collective-permute-start.26 = (bf16[128,1024]{1,0:T(8,128)(2,1)S(1)}, bf16[128,1024]{1,0:T(8,128)(2,1)}, u32[]{:S(2)}, u32[]{:S(2)}) collective-permute-start(bf16[128,1024]{1,0:T(8,128)(2,1)S(1)} %copy-done.69), channel_id=1, source_target_pairs={{0,2},{2,4},{4,6},{6,0},{1,3},{3,5},{5,7},{7,1},{8,10},{10,12},{12... | collective-permute-start | bytes 786440 | tf_op jit(solution)/shard_map/ppermute | solution.py:58
  143.3 29.2 %collective-permute-start.24 = (bf16[2,4,16,5120]{3,2,1,0:T(8,128)(2,1)}, bf16[2,4,16,5120]{3,2,1,0:T(8,128)(2,1)S(1)}, u32[]{:S(2)}, u32[]{:S(2)}) collective-permute-start(bf16[2,4,16,5120]{3,2,1,0:T(8,128)(2,1)} %copy-done.18), channel_id=1, source_target_pairs={{0,1},{1,0},{2,3},{3,2},{4,5},{5,4},{6,7},{7,6},{8,9},{9,8},{10,11... | collective-permute-start | bytes 3932168 | tf_op jit(solution)/shard_map/ppermute | solution.py:58
  143.3 29.2 %collective-permute-start.25 = (bf16[2,4,16,5120]{3,2,1,0:T(8,128)(2,1)}, bf16[2,4,16,5120]{3,2,1,0:T(8,128)(2,1)S(1)}, u32[]{:S(2)}, u32[]{:S(2)}) collective-permute-start(bf16[2,4,16,5120]{3,2,1,0:T(8,128)(2,1)} %collective-permute-done.22.refs_5_), channel_id=1, source_target_pairs={{0,1},{1,0},{2,3},{3,2},{4,5},{5,4},{6,7},{7,6},{8,9},{9,8},{10,11... | collective-permute-start | bytes 3932168 | tf_op jit(solution)/shard_map/ppermute | solution.py:58
  173.8 22.2 %collective-permute-start.31 = (bf16[2,104,1024]{2,1,0:T(8,128)(2,1)}, bf16[2,104,1024]{2,1,0:T(8,128)(2,1)}, u32[]{:S(2)}, u32[]{:S(2)}) collective-permute-start(bf16[2,104,1024]{2,1,0:T(8,128)(2,1)} %pad_maximum_fusion.28), channel_id=1, source_target_pairs={{0,2},{2,4},{4,6},{6,0},{1,3},{3,5},{5,7},{7,1},{8,10},{10,12},{12... | collective-permute-start | bytes 1277960 | tf_op jit(solution)/shard_map/ppermute | solution.py:58
  174.1 21.9 %collective-permute-start.32 = (bf16[2,104,1024]{2,1,0:T(8,128)(2,1)}, bf16[2,104,1024]{2,1,0:T(8,128)(2,1)}, u32[]{:S(2)}, u32[]{:S(2)}) collective-permute-start(bf16[2,104,1024]{2,1,0:T(8,128)(2,1)} %pad_maximum_fusion.30), channel_id=1, source_target_pairs={{0,6},{2,0},{4,2},{6,4},{1,7},{3,1},{5,3},{7,5},{8,14},{10,8},{12,... | collective-permute-start | bytes 1277960 | tf_op jit(solution)/shard_map/ppermute | solution.py:58
  196.0 24.8 %collective-permute-start.35 = (bf16[2,4,64,1024]{3,2,1,0:T(8,128)(2,1)S(1)}, bf16[2,4,64,1024]{3,2,1,0:T(8,128)(2,1)S(1)}, u32[]{:S(2)}, u32[]{:S(2)}) collective-permute-start(bf16[2,4,64,1024]{3,2,1,0:T(8,128)(2,1)S(1)} %pad_maximum_fusion.9.refs_0_), channel_id=1, source_target_pairs={{0,1},{1,0},{2,3},{3,2},{4,5},{5,4},{6,7},{7,6},{8,9},{9,8},{10,11... | collective-permute-start | bytes 3145736 | tf_op jit(solution)/shard_map/ppermute | solution.py:58
  196.1 25.7 %collective-permute-start.33 = (bf16[2,4,64,1024]{3,2,1,0:T(8,128)(2,1)S(1)}, bf16[2,4,64,1024]{3,2,1,0:T(8,128)(2,1)S(1)}, u32[]{:S(2)}, u32[]{:S(2)}) collective-permute-start(bf16[2,4,64,1024]{3,2,1,0:T(8,128)(2,1)S(1)} %pad_maximum_fusion.9.refs_0_), channel_id=1, source_target_pairs={{0,16},{16,0},{1,17},{17,1},{2,18},{18,2},{3,19},{19,3},{4,20},{20... | collective-permute-start | bytes 3145736 | tf_op jit(solution)/shard_map/ppermute | solution.py:58
  197.7 24.1 %collective-permute-start.36 = (bf16[2,4,64,1024]{3,2,1,0:T(8,128)(2,1)S(1)}, bf16[2,4,64,1024]{3,2,1,0:T(8,128)(2,1)S(1)}, u32[]{:S(2)}, u32[]{:S(2)}) collective-permute-start(bf16[2,4,64,1024]{3,2,1,0:T(8,128)(2,1)S(1)} %pad_maximum_fusion.10.refs_4_), channel_id=1, source_target_pairs={{0,1},{1,0},{2,3},{3,2},{4,5},{5,4},{6,7},{7,6},{8,9},{9,8},{10,11... | collective-permute-start | bytes 3145736 | tf_op jit(solution)/shard_map/ppermute | solution.py:58
  197.9 25.4 %collective-permute-start.34 = (bf16[2,4,64,1024]{3,2,1,0:T(8,128)(2,1)S(1)}, bf16[2,4,64,1024]{3,2,1,0:T(8,128)(2,1)S(1)}, u32[]{:S(2)}, u32[]{:S(2)}) collective-permute-start(bf16[2,4,64,1024]{3,2,1,0:T(8,128)(2,1)S(1)} %pad_maximum_fusion.10.refs_4_), channel_id=1, source_target_pairs={{0,8},{8,0},{1,9},{9,1},{2,10},{10,2},{3,11},{11,3},{4,12},{12,4},... | collective-permute-start | bytes 3145736 | tf_op jit(solution)/shard_map/ppermute | solution.py:58
  265.1 25.2 %collective-permute-start.41 = (bf16[2,4,64,1024]{3,2,1,0:T(8,128)(2,1)S(1)}, bf16[2,4,64,1024]{3,2,1,0:T(8,128)(2,1)}, u32[]{:S(2)}, u32[]{:S(2)}) collective-permute-start(bf16[2,4,64,1024]{3,2,1,0:T(8,128)(2,1)S(1)} %get-tuple-element.436), channel_id=1, source_target_pairs={{0,16},{16,0},{1,17},{17,1},{2,18},{18,2},{3,19},{19,3},{4,20},{20... | collective-permute-start | bytes 3145736 | tf_op jit(solution)/shard_map/ppermute | solution.py:58
  265.6 24.9 %collective-permute-start.42 = (bf16[2,4,64,1024]{3,2,1,0:T(8,128)(2,1)S(1)}, bf16[2,4,64,1024]{3,2,1,0:T(8,128)(2,1)}, u32[]{:S(2)}, u32[]{:S(2)}) collective-permute-start(bf16[2,4,64,1024]{3,2,1,0:T(8,128)(2,1)S(1)} %copy-done.79), channel_id=1, source_target_pairs={{0,8},{8,0},{1,9},{9,1},{2,10},{10,2},{3,11},{11,3},{4,12},{12,4},... | collective-permute-start | bytes 3145736 | tf_op jit(solution)/shard_map/ppermute | solution.py:58
  323.1 24.9 %collective-permute-start.48 = (bf16[2,4,16,4096]{3,2,1,0:T(8,128)(2,1)S(1)}, bf16[2,4,16,4096]{3,2,1,0:T(8,128)(2,1)}, u32[]{:S(2)}, u32[]{:S(2)}) collective-permute-start(bf16[2,4,16,4096]{3,2,1,0:T(8,128)(2,1)S(1)} %get-tuple-element.468), channel_id=1, source_target_pairs={{0,16},{16,0},{1,17},{17,1},{2,18},{18,2},{3,19},{19,3},{4,20},{20... | collective-permute-start | bytes 3145736 | tf_op jit(solution)/shard_map/ppermute | solution.py:58
  323.7 24.6 %collective-permute-start.49 = (bf16[2,4,16,4096]{3,2,1,0:T(8,128)(2,1)}, bf16[2,4,16,4096]{3,2,1,0:T(8,128)(2,1)S(1)}, u32[]{:S(2)}, u32[]{:S(2)}) collective-permute-start(bf16[2,4,16,4096]{3,2,1,0:T(8,128)(2,1)} %get-tuple-element.470), channel_id=1, source_target_pairs={{0,8},{8,0},{1,9},{9,1},{2,10},{10,2},{3,11},{11,3},{4,12},{12,4},... | collective-permute-start | bytes 3145736 | tf_op jit(solution)/shard_map/ppermute | solution.py:58
  324.5 23.2 %collective-permute-start.52 = (bf16[2,104,1024]{2,1,0:T(8,128)(2,1)S(1)}, bf16[2,104,1024]{2,1,0:T(8,128)(2,1)S(1)}, u32[]{:S(2)}, u32[]{:S(2)}) collective-permute-start(bf16[2,104,1024]{2,1,0:T(8,128)(2,1)S(1)} %copy-done.67), channel_id=1, source_target_pairs={{0,2},{2,4},{4,6},{6,0},{1,3},{3,5},{5,7},{7,1},{8,10},{10,12},{12... | collective-permute-start | bytes 1277960 | tf_op jit(solution)/shard_map/ppermute | solution.py:58
  326.3 21.8 %collective-permute-start.51 = (bf16[128,1024]{1,0:T(8,128)(2,1)}, bf16[128,1024]{1,0:T(8,128)(2,1)}, u32[]{:S(2)}, u32[]{:S(2)}) collective-permute-start(bf16[128,1024]{1,0:T(8,128)(2,1)} %pad_maximum_fusion.36), channel_id=1, source_target_pairs={{0,6},{2,0},{4,2},{6,4},{1,7},{3,1},{5,3},{7,5},{8,14},{10,8},{12,... | collective-permute-start | bytes 786440 | tf_op jit(solution)/shard_map/ppermute | solution.py:58
  350.9 23.5 %collective-permute-start.55 = (bf16[512,1024]{1,0:T(8,128)(2,1)S(1)}, bf16[512,1024]{1,0:T(8,128)(2,1)S(1)}, u32[]{:S(2)}, u32[]{:S(2)}) collective-permute-start(bf16[512,1024]{1,0:T(8,128)(2,1)S(1)} %weight_grad.12), channel_id=1, source_target_pairs={{0,1},{1,0},{2,3},{3,2},{4,5},{5,4},{6,7},{7,6},{8,9},{9,8},{10,11... | collective-permute-start | bytes 3145736 | tf_op jit(solution)/shard_map/ppermute | solution.py:58
  350.9 23.5 %collective-permute-start.53 = (bf16[4,16,4096]{2,1,0:T(8,128)(2,1)S(1)}, bf16[4,16,4096]{2,1,0:T(8,128)(2,1)S(1)}, u32[]{:S(2)}, u32[]{:S(2)}) collective-permute-start(bf16[4,16,4096]{2,1,0:T(8,128)(2,1)S(1)} %get-tuple-element.498), channel_id=1, source_target_pairs={{0,8},{8,0},{1,9},{9,1},{2,10},{10,2},{3,11},{11,3},{4,12},{12,4},... | collective-permute-start | bytes 1572872 | tf_op jit(solution)/shard_map/ppermute | solution.py:58
  352.2 22.2 %collective-permute-start.54 = (bf16[4,16,4096]{2,1,0:T(8,128)(2,1)}, bf16[4,16,4096]{2,1,0:T(8,128)(2,1)S(1)}, u32[]{:S(2)}, u32[]{:S(2)}) collective-permute-start(bf16[4,16,4096]{2,1,0:T(8,128)(2,1)} %get-tuple-element.500), channel_id=1, source_target_pairs={{0,16},{16,0},{1,17},{17,1},{2,18},{18,2},{3,19},{19,3},{4,20},{20... | collective-permute-start | bytes 1572872 | tf_op jit(solution)/shard_map/ppermute | solution.py:58
  418.6 24.6 %collective-permute-start.66 = (bf16[4,104,1024]{2,1,0:T(8,128)(2,1)}, bf16[4,104,1024]{2,1,0:T(8,128)(2,1)}, u32[]{:S(2)}, u32[]{:S(2)}) collective-permute-start(bf16[4,104,1024]{2,1,0:T(8,128)(2,1)} %slice_bitcast_fusion.2), channel_id=1, source_target_pairs={{0,1},{1,0},{2,3},{3,2},{4,5},{5,4},{6,7},{7,6},{8,9},{9,8},{10,11... | collective-permute-start | bytes 2555912 | tf_op jit(solution)/shard_map/ppermute | solution.py:58
  418.6 24.5 %collective-permute-start.62 = (bf16[2,4,16,3072]{3,2,1,0:T(8,128)(2,1)}, bf16[2,4,16,3072]{3,2,1,0:T(8,128)(2,1)}, u32[]{:S(2)}, u32[]{:S(2)}) collective-permute-start(bf16[2,4,16,3072]{3,2,1,0:T(8,128)(2,1)} %get-tuple-element.559), channel_id=1, source_target_pairs={{0,16},{16,0},{1,17},{17,1},{2,18},{18,2},{3,19},{19,3},{4,20},{20... | collective-permute-start | bytes 2359304 | tf_op jit(solution)/shard_map/ppermute | solution.py:58
  419.2 24.0 %collective-permute-start.63 = (bf16[2,4,16,3072]{3,2,1,0:T(8,128)(2,1)S(1)}, bf16[2,4,16,3072]{3,2,1,0:T(8,128)(2,1)}, u32[]{:S(2)}, u32[]{:S(2)}) collective-permute-start(bf16[2,4,16,3072]{3,2,1,0:T(8,128)(2,1)S(1)} %get-tuple-element.561), channel_id=1, source_target_pairs={{0,8},{8,0},{1,9},{9,1},{2,10},{10,2},{3,11},{11,3},{4,12},{12,4},... | collective-permute-start | bytes 2359304 | tf_op jit(solution)/shard_map/ppermute | solution.py:58
  460.8 22.9 %collective-permute-start.77 = (bf16[4,104,1024]{2,1,0:T(8,128)(2,1)S(1)}, bf16[4,104,1024]{2,1,0:T(8,128)(2,1)S(1)}, u32[]{:S(2)}, u32[]{:S(2)}) collective-permute-start(bf16[4,104,1024]{2,1,0:T(8,128)(2,1)S(1)} %get-tuple-element.670), channel_id=1, source_target_pairs={{0,1},{1,0},{2,3},{3,2},{4,5},{5,4},{6,7},{7,6},{8,9},{9,8},{10,11... | collective-permute-start | bytes 2555912 | tf_op jit(solution)/shard_map/ppermute | solution.py:58
  (129 other events, 1387.5 us)
